TPU v7x, 32 devices: a whole 2x2x4 slice. The times are simulated.
32 devices in a mesh: fsdp: 8 (over z, y), dp: 4 (over x, core).
Axes of the slice: x: 2, y: 2, z: 4, core: 2. Of those that a mesh axis runs over, the one named last changes fastest.
Arguments:
- series_values: float32 [24960, 96], P(('fsdp', 'dp')), may hold values from -15 to 15
- quarter_index: int32 [128], P(('fsdp', 'dp')), may hold values from 0 to 3, as said below
- patch_weight: bfloat16 [96, 1024], P(None, 'fsdp'), may hold values from -0.625 to 0.625
- heads_in: bfloat16 [1024, 3072], P('fsdp'), may hold values from -0.1875 to 0.1875
- heads_out: bfloat16 [1024, 1024], P('fsdp'), may hold values from -0.375 to 0.375
- expand_weight: bfloat16 [1024, 2048], P('fsdp'), may hold values from -0.1875 to 0.1875
- reduce_weight: bfloat16 [2048, 1024], P('fsdp'), may hold values from -0.125 to 0.125
- norm_gains: bfloat16 [2, 1024], P(None, 'fsdp'), may hold values from 0.5 to 1.5
- bias_rows: bfloat16 [4, 1024], P(None, 'fsdp'), may hold values from -1.796875 to 1.796875
- expand_bias: bfloat16 [2048], P('fsdp'), may hold values from -1.796875 to 1.796875
- cotangent: bfloat16 [24960, 1024], P(('fsdp', 'dp')), may hold values from -6 to 6
Outputs:
- layer_output: bfloat16 [24960, 1024], P(('fsdp', 'dp'))
- series_grad: float32 [24960, 96], P(('fsdp', 'dp'))
- grad_patch: float32 [96, 1024], P(None, 'fsdp')
- grad_heads_in: float32 [1024, 3072], P('fsdp')
- grad_heads_out: float32 [1024, 1024], P('fsdp')
- grad_expand: float32 [1024, 2048], P('fsdp')
- grad_reduce: float32 [2048, 1024], P('fsdp')
- grad_gains: float32 [2, 1024], P(None, 'fsdp')
- grad_biases: float32 [4, 1024], P(None, 'fsdp')
- grad_expand_bias: float32 [2048], P('fsdp')
Inputs may be any that keep to these rules, and one draw needn't show every extreme that they name: `quarter_index`: along fsdp the quarters of one slot position run 0, 1, 2, 3 and then again from 0, closing the loop: the device at fsdp index i whose slot holds quarter q shares that long series with the same slot position at the same dp index on fsdp indices i - q to i - q + 3, modulo 8.
All inputs are finite; a program needn't handle non-finite values.
Results may differ from a plain program's by a relative error of at most 0.014.
Values may be sent and summed in bfloat16 or wider, within the bound.
No kernel may reach another device: no remote copies, remote signals or barrier semaphores. Data moves between devices by JAX's collectives and lax.ppermute only.
A program may use at most 256 MiB of HBM per device.

v0:
```python
import jax
import jax.numpy as jnp
from jax import lax
from jax.sharding import PartitionSpec as P

D = 1024
HEADS = 8
HEAD_DIM = 128
PATCH = 96
SPAN = 15
SHORT_SLOTS = 48
BLOCK_SLOTS = 48


EPSILON = 1e-05
NEG_LARGE = -1e30


def passed_along(value, axis, steps):
    count = lax.axis_size(axis)
    pairs = [(source, (source + steps) % count) for source in range(count)]
    return lax.ppermute(value, axis, pairs)


def layer_norm(inputs, gain_row, shift_row):
    center = inputs - jnp.mean(inputs, axis=-1, keepdims=True)
    spread = jnp.mean(center * center, axis=-1, keepdims=True)
    return center * lax.rsqrt(spread + EPSILON) * gain_row + shift_row


def exact_gelu(inputs):
    return jax.nn.gelu(inputs, approximate=False)


def chain_keep(quarter, offset):
    return (offset >= -quarter) & (offset <= 3 - quarter)


def block_scores(query_rows, key_rows):
    scaling = HEAD_DIM ** (-0.5)
    return (
        jnp.einsum("ihd,jhd->hij", query_rows, key_rows, preferred_element_type=jnp.float32)
        * scaling
    )


def attend(query_rows, key_rows, value_rows, allowed):
    scores = jnp.where(allowed[None], block_scores(query_rows, key_rows), NEG_LARGE)
    row_top = jnp.max(scores, axis=-1, keepdims=True)
    weights = jnp.exp(scores - row_top)
    row_total = jnp.sum(weights, axis=-1, keepdims=True)
    weights_low = (weights / row_total).astype(jnp.bfloat16)
    mixture = jnp.einsum(
        "hij,jhd->ihd", weights_low, value_rows, preferred_element_type=jnp.float32
    )
    return (mixture, row_top + jnp.log(row_total))


def attend_back(query_rows, key_rows, value_rows, allowed, log_total, grad_mixture):
    scaling = HEAD_DIM ** (-0.5)
    weights = jnp.where(allowed[None], jnp.exp(block_scores(query_rows, key_rows) - log_total), 0.0)
    grad_values = jnp.einsum(
        "hij,ihd->jhd",
        weights.astype(jnp.bfloat16),
        grad_mixture,
        preferred_element_type=jnp.float32,
    )
    grad_weights = jnp.einsum(
        "ihd,jhd->hij", grad_mixture, value_rows, preferred_element_type=jnp.float32
    )
    inner_sum = jnp.sum(weights * grad_weights, axis=-1, keepdims=True)
    grad_scores = (weights * (grad_weights - inner_sum)).astype(jnp.bfloat16)
    grad_query = (
        jnp.einsum("hij,jhd->ihd", grad_scores, key_rows, preferred_element_type=jnp.float32)
        * scaling
    )
    grad_keys = (
        jnp.einsum("hij,ihd->jhd", grad_scores, query_rows, preferred_element_type=jnp.float32)
        * scaling
    )
    return (grad_query, grad_keys, grad_values)


def body(
    series_values,
    quarter_index,
    patch_weight,
    heads_in,
    heads_out,
    expand_weight,
    reduce_weight,
    norm_gains,
    bias_rows,
    expand_bias,
    cotangent,
):
    shard_params = (
        patch_weight,
        heads_in,
        heads_out,
        expand_weight,
        reduce_weight,
        norm_gains,
        bias_rows,
        expand_bias,
    )
    gathered = (
        lax.all_gather(shard_params[0], "fsdp", axis=1, tiled=True),
        lax.all_gather(shard_params[1], "fsdp", axis=0, tiled=True),
        lax.all_gather(shard_params[2], "fsdp", axis=0, tiled=True),
        lax.all_gather(shard_params[3], "fsdp", axis=0, tiled=True),
        lax.all_gather(shard_params[4], "fsdp", axis=0, tiled=True),
        lax.all_gather(shard_params[5], "fsdp", axis=1, tiled=True),
        lax.all_gather(shard_params[6], "fsdp", axis=1, tiled=True),
        lax.all_gather(shard_params[7], "fsdp", axis=0, tiled=True),
    )
    gains_all = gathered[5].astype(jnp.float32)
    biases_all = gathered[6].astype(jnp.float32)
    expand_shift = gathered[7].astype(jnp.float32)
    row_count = series_values.shape[0]
    slot_count = row_count // SPAN
    short_rows = SHORT_SLOTS * SPAN
    long_rows = row_count - short_rows
    block_rows = BLOCK_SLOTS * SPAN
    grouped = series_values.reshape(slot_count, SPAN * PATCH)
    slot_sums = jnp.stack([jnp.sum(grouped, 1), jnp.sum(grouped * grouped, 1)], 1)
    long_sums = slot_sums[SHORT_SLOTS:]
    chain_sum = long_sums
    for shift_by in (1, 2, 3, -1, -2, -3):
        arrived = passed_along(long_sums, "fsdp", shift_by)
        chain_sum = chain_sum + jnp.where(
            chain_keep(quarter_index, -shift_by)[:, None], arrived, 0.0
        )
    totals = jnp.concatenate([slot_sums[:SHORT_SLOTS], chain_sum], 0)
    counts = jnp.where(jnp.arange(slot_count) < SHORT_SLOTS, SPAN * PATCH, 4 * SPAN * PATCH).astype(
        jnp.float32
    )
    slot_mean = totals[:, 0] / counts
    inv_spread = lax.rsqrt(totals[:, 1] / counts - slot_mean * slot_mean + EPSILON)
    normed_slots = (grouped - slot_mean[:, None]) * inv_spread[:, None]
    normed_low = normed_slots.reshape(row_count, PATCH).astype(jnp.bfloat16)
    embedded = jnp.dot(normed_low, gathered[0], preferred_element_type=jnp.float32) + biases_all[0]
    first_value, first_back = jax.vjp(layer_norm, embedded, gains_all[0], biases_all[1])
    first_norm = first_value.astype(jnp.bfloat16)
    projected = jnp.dot(first_norm, gathered[1], preferred_element_type=jnp.float32).astype(
        jnp.bfloat16
    )
    long_pairs = projected[short_rows:, D:]
    priors = []
    for shift_by in (1, 2, 3):
        priors.append(passed_along(long_pairs, "fsdp", shift_by))
    head_split = projected.reshape(row_count, 3, HEADS, HEAD_DIM)
    block_index = jnp.arange(block_rows)
    short_mask = (block_index[:, None] // SPAN == block_index[None, :] // SPAN) & (
        block_index[None, :] <= block_index[:, None]
    )
    long_index = jnp.arange(long_rows)
    same_slot = long_index[:, None] // SPAN == long_index[None, :] // SPAN
    row_quarter = jnp.repeat(quarter_index, SPAN)
    long_mask = jnp.concatenate(
        [same_slot & (long_index[None, :] <= long_index[:, None])]
        + [same_slot & (shift_by <= row_quarter)[:, None] for shift_by in (1, 2, 3)],
        1,
    )
    long_keys = jnp.concatenate(
        [head_split[short_rows:, 1]]
        + [member[:, :D].reshape(long_rows, HEADS, HEAD_DIM) for member in priors],
        0,
    )
    long_values = jnp.concatenate(
        [head_split[short_rows:, 2]]
        + [member[:, D:].reshape(long_rows, HEADS, HEAD_DIM) for member in priors],
        0,
    )
    mixtures = []
    log_totals = []
    block_number = 0
    window = slice(block_number * block_rows, (block_number + 1) * block_rows)
    mixture, log_total = attend(
        head_split[window, 0], head_split[window, 1], head_split[window, 2], short_mask
    )
    mixtures.append(mixture)
    log_totals.append(log_total)
    mixture, log_total = attend(head_split[short_rows:, 0], long_keys, long_values, long_mask)
    mixtures.append(mixture)
    log_totals.append(log_total)
    mixed_all = jnp.concatenate(mixtures, 0).reshape(row_count, D).astype(jnp.bfloat16)
    middle = embedded + jnp.dot(mixed_all, gathered[2], preferred_element_type=jnp.float32)
    second_value, second_back = jax.vjp(layer_norm, middle, gains_all[1], biases_all[2])
    second_norm = second_value.astype(jnp.bfloat16)
    pre_act = jnp.dot(second_norm, gathered[3], preferred_element_type=jnp.float32) + expand_shift
    act_value, gelu_back = jax.vjp(exact_gelu, pre_act)
    activation = act_value.astype(jnp.bfloat16)
    layer_output = (
        middle
        + jnp.dot(activation, gathered[4], preferred_element_type=jnp.float32)
        + biases_all[3]
    ).astype(jnp.bfloat16)
    matrices = (
        lax.all_gather(shard_params[0], "fsdp", axis=1, tiled=True),
        lax.all_gather(shard_params[1], "fsdp", axis=0, tiled=True),
        lax.all_gather(shard_params[2], "fsdp", axis=0, tiled=True),
        lax.all_gather(shard_params[3], "fsdp", axis=0, tiled=True),
        lax.all_gather(shard_params[4], "fsdp", axis=0, tiled=True),
        lax.all_gather(shard_params[5], "fsdp", axis=1, tiled=True),
        lax.all_gather(shard_params[6], "fsdp", axis=1, tiled=True),
        lax.all_gather(shard_params[7], "fsdp", axis=0, tiled=True),
    )
    grad_reduce = jnp.einsum("rk,rn->kn", activation, cotangent, preferred_element_type=jnp.float32)
    grad_act = jnp.einsum("rn,kn->rk", cotangent, matrices[4], preferred_element_type=jnp.float32)
    grad_pre = gelu_back(grad_act)[0].astype(jnp.bfloat16)
    grad_expand = jnp.einsum("rn,rk->nk", second_norm, grad_pre, preferred_element_type=jnp.float32)
    grad_expand_bias = jnp.sum(grad_pre.astype(jnp.float32), 0)
    grad_second = jnp.einsum("rk,nk->rn", grad_pre, matrices[3], preferred_element_type=jnp.float32)
    middle_back, gain_two, shift_two = second_back(grad_second)
    grad_middle = cotangent.astype(jnp.float32) + middle_back
    grad_branch = grad_middle.astype(jnp.bfloat16)
    grad_heads_out = jnp.einsum(
        "rk,rn->kn", mixed_all, grad_branch, preferred_element_type=jnp.float32
    )
    grad_mixture = (
        jnp.einsum("rn,kn->rk", grad_branch, matrices[2], preferred_element_type=jnp.float32)
        .astype(jnp.bfloat16)
        .reshape(row_count, HEADS, HEAD_DIM)
    )
    block_number = 0
    window = slice(block_number * block_rows, (block_number + 1) * block_rows)
    grad_query, grad_keys, grad_values = attend_back(
        head_split[window, 0],
        head_split[window, 1],
        head_split[window, 2],
        short_mask,
        log_totals[block_number],
        grad_mixture[window],
    )
    query_grads = grad_query.reshape(block_rows, D)
    key_grads = grad_keys.reshape(block_rows, D)
    value_grads = grad_values.reshape(block_rows, D)
    long_query, long_key, long_value = attend_back(
        head_split[short_rows:, 0],
        long_keys,
        long_values,
        long_mask,
        log_totals[-1],
        grad_mixture[short_rows:],
    )
    own_grads = jnp.concatenate(
        [long_key[:long_rows].reshape(long_rows, D), long_value[:long_rows].reshape(long_rows, D)],
        1,
    )
    for shift_by in (1, 2, 3):
        window = slice(shift_by * long_rows, (shift_by + 1) * long_rows)
        sent_back = jnp.concatenate(
            [long_key[window].reshape(long_rows, D), long_value[window].reshape(long_rows, D)], 1
        )
        own_grads = own_grads + passed_along(
            sent_back.astype(jnp.bfloat16), "fsdp", -shift_by
        ).astype(sent_back.dtype)
    short_grads = jnp.concatenate([query_grads, key_grads, value_grads], 1)
    long_grads_all = jnp.concatenate([long_query.reshape(long_rows, D), own_grads], 1)
    grad_projected = jnp.concatenate([short_grads, long_grads_all], 0).astype(jnp.bfloat16)
    grad_heads_in = jnp.einsum(
        "rk,rn->kn", first_norm, grad_projected, preferred_element_type=jnp.float32
    )
    grad_first = jnp.einsum(
        "rn,kn->rk", grad_projected, matrices[1], preferred_element_type=jnp.float32
    )
    embed_back, gain_one, shift_one = first_back(grad_first)
    grad_embedded = (grad_middle + embed_back).astype(jnp.bfloat16)
    grad_patch = jnp.einsum(
        "rp,rk->pk", normed_low, grad_embedded, preferred_element_type=jnp.float32
    )
    shift_zero = jnp.sum(grad_embedded.astype(jnp.float32), 0)
    grad_normed = jnp.einsum(
        "rk,pk->rp", grad_embedded, matrices[0], preferred_element_type=jnp.float32
    ).reshape(slot_count, SPAN * PATCH)
    slot_grads = jnp.stack([jnp.sum(grad_normed, 1), jnp.sum(grad_normed * normed_slots, 1)], 1)
    long_sums_grad = slot_grads[SHORT_SLOTS:]
    chain_grad = long_sums_grad
    for shift_by in (1, 2, 3, -1, -2, -3):
        arrived = passed_along(long_sums_grad, "fsdp", shift_by)
        chain_grad = chain_grad + jnp.where(
            chain_keep(quarter_index, -shift_by)[:, None], arrived, 0.0
        )
    grad_totals = jnp.concatenate([slot_grads[:SHORT_SLOTS], chain_grad], 0)
    series_grad = (
        inv_spread[:, None]
        * (
            grad_normed
            - grad_totals[:, 0:1] / counts[:, None]
            - normed_slots * grad_totals[:, 1:2] / counts[:, None]
        )
    ).reshape(row_count, PATCH)
    shift_three = jnp.sum(cotangent.astype(jnp.float32), 0)
    local_grads = (
        grad_patch,
        grad_heads_in,
        grad_heads_out,
        grad_expand,
        grad_reduce,
        jnp.stack([gain_one, gain_two]),
        jnp.stack([shift_zero, shift_one, shift_two, shift_three]),
        grad_expand_bias,
    )
    shards = (
        lax.psum_scatter(local_grads[0], "fsdp", scatter_dimension=1, tiled=True),
        lax.psum_scatter(local_grads[1], "fsdp", scatter_dimension=0, tiled=True),
        lax.psum_scatter(local_grads[2], "fsdp", scatter_dimension=0, tiled=True),
        lax.psum_scatter(local_grads[3], "fsdp", scatter_dimension=0, tiled=True),
        lax.psum_scatter(local_grads[4], "fsdp", scatter_dimension=0, tiled=True),
        lax.psum_scatter(local_grads[5], "fsdp", scatter_dimension=1, tiled=True),
        lax.psum_scatter(local_grads[6], "fsdp", scatter_dimension=1, tiled=True),
        lax.psum_scatter(local_grads[7], "fsdp", scatter_dimension=0, tiled=True),
    )
    summed = (
        lax.psum(shards[0].astype(jnp.bfloat16), "dp").astype(jnp.float32),
        lax.psum(shards[1].astype(jnp.bfloat16), "dp").astype(jnp.float32),
        lax.psum(shards[2].astype(jnp.bfloat16), "dp").astype(jnp.float32),
        lax.psum(shards[3].astype(jnp.bfloat16), "dp").astype(jnp.float32),
        lax.psum(shards[4].astype(jnp.bfloat16), "dp").astype(jnp.float32),
        lax.psum(shards[5].astype(jnp.bfloat16), "dp").astype(jnp.float32),
        lax.psum(shards[6].astype(jnp.bfloat16), "dp").astype(jnp.float32),
        lax.psum(shards[7].astype(jnp.bfloat16), "dp").astype(jnp.float32),
    )
    return (
        layer_output,
        series_grad,
        summed[0],
        summed[1],
        summed[2],
        summed[3],
        summed[4],
        summed[5],
        summed[6],
        summed[7],
    )


def solution(mesh):
    in_specs = (
        P(("fsdp", "dp"), None),
        P(("fsdp", "dp")),
        P(None, "fsdp"),
        P("fsdp", None),
        P("fsdp", None),
        P("fsdp", None),
        P("fsdp", None),
        P(None, "fsdp"),
        P(None, "fsdp"),
        P("fsdp"),
        P(("fsdp", "dp"), None),
    )
    out_specs = (
        P(("fsdp", "dp"), None),
        P(("fsdp", "dp"), None),
        P(None, "fsdp"),
        P("fsdp", None),
        P("fsdp", None),
        P("fsdp", None),
        P("fsdp", None),
        P(None, "fsdp"),
        P(None, "fsdp"),
        P("fsdp"),
    )
    return jax.shard_map(body, mesh=mesh, in_specs=in_specs, out_specs=out_specs, check_vma=False)
```

profile of v0, /device:TPU:0, one launch (start us, length us, event | category | flops | bytes accessed | tf_op | source)
XLA Modules:
  0.0 1247.5 jit_solution(16482280274859635679)
XLA Ops:
  11.0 5.1 collective-permute-start.4
  17.5 1.6 collective-permute-start.1
  19.1 3.8 collective-permute-start.5
  23.7 18.6 %all_gather.31 = bf16[2,1024]{1,0:T(2,128)(2,1)S(1)} all-gather(bf16[2,128]{1,0:T(2,128)(2,1)} %param.18), channel_id=1, replica_groups=mesh['fsdp'=8,'dp'=4] {'fsdp'}, dimensions={1}, use_global_device_ids=true | all-gather | bytes 4608 | tf_op jit(solution)/shard_map/all_gather | solution.py:113
  44.1 16.9 %all-gather = bf16[8,1,256]{2,1,0:T(2,128)(2,1)S(1)} all-gather(bf16[1,1,256]{2,1,0:T(2,128)(2,1)S(1)} %reshape.401), channel_id=1, replica_groups=mesh['fsdp'=8,'dp'=4] {'fsdp'}, dimensions={0}, use_global_device_ids=true | all-gather | bytes 4608 | tf_op jit(solution)/shard_map/all_gather | solution.py:115
  61.6 19.1 %all_gather.30 = bf16[4,1024]{1,0:T(4,128)(2,1)S(1)} all-gather(bf16[4,128]{1,0:T(4,128)(2,1)} %param.19), channel_id=1, replica_groups=mesh['fsdp'=8,'dp'=4] {'fsdp'}, dimensions={1}, use_global_device_ids=true | all-gather | bytes 9216 | tf_op jit(solution)/shard_map/all_gather | solution.py:114
  81.3 29.3 %all_gather.29 = bf16[96,1024]{1,0:T(8,128)(2,1)} all-gather(bf16[96,128]{1,0:T(8,128)(2,1)} %param.13), channel_id=1, replica_groups=mesh['fsdp'=8,'dp'=4] {'fsdp'}, dimensions={1}, use_global_device_ids=true | all-gather | bytes 221184 | tf_op jit(solution)/shard_map/all_gather | solution.py:108
  112.6 6.2 collective-permute-done
  120.6 1.6 add_reduce_fusion
  123.0 9.3 convolution_convert_fusion
  133.1 2.7 collective-permute-start.6
  138.1 2.3 fusion.84
  140.7 8.0 select_reduce_fusion
  148.7 9.8 fusion
  158.5 10.6 fusion.21
  176.3 1.6 copy.124
  177.9 3.6 all-gather.8.cloned.1.call-done
  181.5 4.0 fusion.93
  185.5 1.7 copy-done.6
  187.7 67.2 %all-gather.10.cloned.1.call-done = bf16[1024,2048]{1,0:T(8,128)(2,1)} async-done(((bf16[128,2048]{1,0:T(8,128)(2,1)}), bf16[1024,2048]{1,0:T(8,128)(2,1)}) %all-gather.10.cloned.1.call-update) | async-done | bytes 4194320 | tf_op jit(solution)/shard_map/all_gather | solution.py:111
  254.9 9.4 fusion.78
  264.3 63.9 %all-gather.12.cloned.1.call-done = bf16[2048,1024]{1,0:T(8,128)(2,1)} async-done(((bf16[256,1024]{1,0:T(8,128)(2,1)}), bf16[2048,1024]{1,0:T(8,128)(2,1)}) %all-gather.12.cloned.1.call-update) | async-done | bytes 4194320 | tf_op jit(solution)/shard_map/all_gather | solution.py:112
  328.3 22.9 %convert_reduce_fusion = (f32[2048]{0:T(1024)}, bf16[780,2048]{1,0:T(8,128)(2,1)S(1)}, f32[780,2048]{1,0:T(8,128)}) fusion(f32[780,2048]{1,0:T(8,128)} %fusion.78, f32[2048]{0:T(1024)S(1)} %bitcast.241, bf16[780,1024]{1,0:T(8,128)(2,1)} %param.21, bf16[2048,1024]{1,0:T(8,128)(2,1)} %all-gather.12.cloned.1.call-done), kind=kOutput, calls=%fused_computation.13 | convolution fusion | flops 3391363072 | bytes 21782528 | tf_op jit(solution)/shard_map/rn,kn->rk/dot_general | solution.py:210
  351.2 4.6 multiply_reduce_fusion.1
  355.8 1.9 fusion.83
  360.5 4.5 fusion.96
  365.7 9.0 fusion.77
  374.8 6.5 multiply_convert_fusion.1
  381.3 1.7 copy-done.20
  383.0 7.0 fusion.97
  390.1 1.4 copy-done.23
  391.5 3.6 convolution_convert_fusion.1
  395.2 1.5 fusion.94
  398.9 1.9 collective-permute-start.10
  402.9 2.5 collective-permute-start.9
  405.4 12.8 %multiply_reduce_fusion = (f32[8,720]{1,0:T(8,128)S(1)}, f32[8,720,720]{1,2,0:T(8,128)}) fusion(f32[8,720,720]{1,2,0:T(8,128)} %get-tuple-element.84, f32[8,720]{1,0:T(8,128)S(1)} %log_add_fusion, pred[720,720]{0,1:T(8,128)(4,1)S(1)} %copy-done.9, bf16[720,1,8,128]{3,2,1,0:T(8,128)(2,1)S(1)} %copy-done.17, bf16[780,1024]{1,0:T(8,128)(2,1)S(1)} %convolution_convert_fusion.1), kind=kOutput, calls=%fused_computation.1 | convolution fusion | flops 1082413440 | bytes 36727296 | tf_op jit(solution)/shard_map/ihd,jhd->hij/dot_general | solution.py:68
  418.2 13.4 %multiply_convert_fusion = bf16[8,720,720]{1,2,0:T(8,128)(2,1)S(1)} fusion(f32[8,720,720]{1,2,0:T(8,128)} %get-tuple-element.95, f32[8,720,720]{1,2,0:T(8,128)} %get-tuple-element.84, f32[8,720]{1,0:T(8,128)S(1)} %get-tuple-element.94, f32[8,720]{1,0:T(8,128)S(1)} %log_add_fusion, pred[720,720]{0,1:T(8,128)(4,1)S(1)} %copy-done.9), kind=kLoop, calls=%fused_computation | loop fusion | flops 24883200 | bytes 42036480 | tf_op jit(solution)/shard_map/convert_element_type | solution.py:72
  431.5 3.5 copy-done
  435.0 3.6 fusion.28
  438.6 10.9 fusion.22
  449.6 6.8 fusion.27
  460.2 2.5 fusion.38
  462.8 12.0 fusion.75
  476.7 18.5 %all-reduce = bf16[2048]{0:T(1024)(128)(2,1)S(1)} all-reduce(f32[2048]{0:T(1024)S(1)} %copy-done.72), channel_id=9, replica_groups=mesh['fsdp'=8,'dp'=4] {'fsdp'}, use_global_device_ids=true, to_apply=%region_43.44.clone | all-reduce | flops 2048 | bytes 12288
  495.3 11.5 multiply_reduce_fusion.2
  507.9 3.1 fusion.82
  514.9 9.0 add_convert_fusion.2
  523.9 1.8 convert_element_type.181
  525.7 97.9 %reduce-scatter.18.cloned.1.call-done = f32[128,2048]{1,0:T(8,128)} async-done(((f32[1024,2048]{1,0:T(8,128)}), f32[128,2048]{1,0:T(8,128)}) %reduce-scatter.18.cloned.1.call-update) | async-done | bytes 1048592 | tf_op jit(solution)/shard_map/reduce_scatter | solution.py:309
  623.6 2.1 convert_element_type.183
  625.7 148.1 %reduce-scatter.20.cloned.1.call-done = f32[256,1024]{1,0:T(8,128)} async-done(((f32[2048,1024]{1,0:T(8,128)}), f32[256,1024]{1,0:T(8,128)}) %reduce-scatter.20.cloned.1.call-update) | async-done | bytes 1048592 | tf_op jit(solution)/shard_map/reduce_scatter | solution.py:310
  773.8 2.1 convert_element_type.185
  775.9 208.0 %reduce-scatter.14.cloned.1.call-done = f32[128,3072]{1,0:T(8,128)} async-done(((f32[1024,3072]{1,0:T(8,128)}), f32[128,3072]{1,0:T(8,128)}) %reduce-scatter.14.cloned.1.call-update) | async-done | bytes 1572880 | tf_op jit(solution)/shard_map/reduce_scatter | solution.py:307
  984.0 2.4 convert_element_type.179
  988.8 2.7 collective-permute-start.15
  992.0 3.8 collective-permute-start.17
  997.5 4.6 collective-permute-done.12
  1003.5 46.2 %reduce-scatter.22.cloned.1.call-done = f32[128,2]{1,0:T(8,128)} async-done(((f32[1024,2]{1,0:T(8,128)}), f32[128,2]{1,0:T(8,128)}) %reduce-scatter.22.cloned.1.call-update) | async-done | bytes 1040
  1050.6 64.6 %reduce-scatter.24.cloned.1.call-done = f32[128,4]{1,0:T(8,128)} async-done(((f32[1024,4]{1,0:T(8,128)}), f32[128,4]{1,0:T(8,128)}) %reduce-scatter.24.cloned.1.call-update) | async-done | bytes 2064
  1116.1 64.3 %reduce-scatter.12.cloned.1.call-done = f32[96,128]{1,0:T(8,128)} async-done(((f32[96,1024]{1,0:T(8,128)}), f32[96,128]{1,0:T(8,128)}) %reduce-scatter.12.cloned.1.call-update) | async-done | bytes 49168 | tf_op jit(solution)/shard_map/reduce_scatter | solution.py:306
  1181.2 10.8 all-reduce.1
  1194.3 39.6 %all-reduce.5.cloned.1.call-done = (bf16[128,3072]{1,0:T(8,128)(2,1)}, bf16[128,1024]{1,0:T(8,128)(2,1)}, bf16[128,2048]{1,0:T(8,128)(2,1)}, bf16[256,1024]{1,0:T(8,128)(2,1)}) async-done(((bf16[128,3072]{1,0:T(8,128)(2,1)}, bf16[128,1024]{1,0:T(8,128)(2,1)}, bf16[128,2048]{1,0:T(8,128)(2,1)}, bf16[256,1024]{1,0:T(8,128)(2,1)}), (bf16[128,3072]{1,0:T(8,128)(2,1)}, bf16[128,1024]{1,0:T(8,128)(2,1)}, ...) | async-done | bytes 2097168 | tf_op jit(solution)/shard_map/psum | solution.py:317
  1233.9 1.9 convert_element_type.182
  1235.8 2.4 convert_element_type.180
  (390 shorter events, 54.5 us)
Async XLA Ops:
  7.2 113.5 %copy-start.10 = (f32[780,96]{0,1:T(8,128)S(1)}, f32[780,96]{0,1:T(8,128)}, u32[]{:S(2)}) copy-start(f32[780,96]{0,1:T(8,128)} %param.11) | copy-start | bytes 898564
  7.2 115.8 %all-gather.6.cloned.1.call-start = ((), (), s32[]{:S(2)}) async-start(), calls=%async_computation.7 | async-start | bytes 7077888 | tf_op jit(solution)/shard_map/all_gather | solution.py:109
  7.9 173.5 %all-gather.8.cloned.1.call-start = ((), (), s32[]{:S(2)}) async-start(), calls=%async_computation.8 | async-start | bytes 2359296 | tf_op jit(solution)/shard_map/all_gather | solution.py:110
  8.7 246.2 %all-gather.10.cloned.1.call-start = ((), (), s32[]{:S(2)}) async-start(), calls=%async_computation.9 | async-start | bytes 4718592 | tf_op jit(solution)/shard_map/all_gather | solution.py:111
  9.4 318.8 %all-gather.12.cloned.1.call-start = ((), (), s32[]{:S(2)}) async-start(), calls=%async_computation.10 | async-start | bytes 4718592 | tf_op jit(solution)/shard_map/all_gather | solution.py:112
  11.0 101.5 %collective-permute-start.4 = (f32[4,2]{0,1:T(2,128)S(1)}, f32[4,2]{0,1:T(2,128)S(1)}, u32[]{:S(2)}, u32[]{:S(2)}) collective-permute-start(f32[4,2]{0,1:T(2,128)S(1)} %slice.128), channel_id=1, source_target_pairs={{0,24},{4,28},{8,0},{12,4},{16,8},{20,12},{24,16},{28,20},{1,25},{... | collective-permute-start | bytes 104 | tf_op jit(solution)/shard_map/ppermute | solution.py:22
  16.1 96.5 %collective-permute-start.3 = (f32[4,2]{0,1:T(2,128)S(1)}, f32[4,2]{0,1:T(2,128)S(1)}, u32[]{:S(2)}, u32[]{:S(2)}) collective-permute-start(f32[4,2]{0,1:T(2,128)S(1)} %slice.128), channel_id=1, source_target_pairs={{0,28},{4,0},{8,4},{12,8},{16,12},{20,16},{24,20},{28,24},{1,29},{... | collective-permute-start | bytes 104 | tf_op jit(solution)/shard_map/ppermute | solution.py:22
  17.5 95.1 %collective-permute-start.2 = (f32[4,2]{0,1:T(2,128)S(1)}, f32[4,2]{0,1:T(2,128)S(1)}, u32[]{:S(2)}, u32[]{:S(2)}) collective-permute-start(f32[4,2]{0,1:T(2,128)S(1)} %slice.128), channel_id=1, source_target_pairs={{0,12},{4,16},{8,20},{12,24},{16,28},{20,0},{24,4},{28,8},{1,13},{... | collective-permute-start | bytes 104 | tf_op jit(solution)/shard_map/ppermute | solution.py:22
  17.5 95.1 %collective-permute-start.1 = (f32[4,2]{0,1:T(2,128)S(1)}, f32[4,2]{0,1:T(2,128)S(1)}, u32[]{:S(2)}, u32[]{:S(2)}) collective-permute-start(f32[4,2]{0,1:T(2,128)S(1)} %slice.128), channel_id=1, source_target_pairs={{0,8},{4,12},{8,16},{12,20},{16,24},{20,28},{24,0},{28,4},{1,9},{5... | collective-permute-start | bytes 104 | tf_op jit(solution)/shard_map/ppermute | solution.py:22
  19.1 93.5 %collective-permute-start.5 = (f32[4,2]{0,1:T(2,128)S(1)}, f32[4,2]{0,1:T(2,128)S(1)}, u32[]{:S(2)}, u32[]{:S(2)}) collective-permute-start(f32[4,2]{0,1:T(2,128)S(1)} %slice.128), channel_id=1, source_target_pairs={{0,20},{4,24},{8,28},{12,0},{16,4},{20,8},{24,12},{28,16},{1,21},{... | collective-permute-start | bytes 104 | tf_op jit(solution)/shard_map/ppermute | solution.py:22
  23.0 500.9 %reduce-scatter.16.cloned.1.call-start = ((), (), s32[]{:S(2)}) async-start(), calls=%async_computation.13 | async-start | bytes 4718592 | tf_op jit(solution)/shard_map/reduce_scatter | solution.py:308
  43.5 75.5 %copy-start.73 = (pred[4]{0:T(512)(128)(4,1)}, pred[4]{0:T(512)(128)(4,1)S(1)}, u32[]{:S(2)}) copy-start(pred[4]{0:T(512)(128)(4,1)S(1)} %get-tuple-element.71) | copy-start | bytes 16
  43.6 75.5 %copy-start.75 = (pred[4]{0:T(512)(128)(4,1)}, pred[4]{0:T(512)(128)(4,1)S(1)}, u32[]{:S(2)}) copy-start(pred[4]{0:T(512)(128)(4,1)S(1)} %get-tuple-element.72) | copy-start | bytes 16
  43.6 75.5 %copy-start.77 = (pred[4]{0:T(512)(128)(4,1)}, pred[4]{0:T(512)(128)(4,1)S(1)}, u32[]{:S(2)}) copy-start(pred[4]{0:T(512)(128)(4,1)S(1)} %get-tuple-element.73) | copy-start | bytes 16
  43.6 77.1 %copy-start.79 = (pred[4]{0:T(512)(128)(4,1)}, pred[4]{0:T(512)(128)(4,1)S(1)}, u32[]{:S(2)}) copy-start(pred[4]{0:T(512)(128)(4,1)S(1)} %get-tuple-element.74) | copy-start | bytes 16
  43.6 77.0 %copy-start.81 = (pred[4]{0:T(512)(128)(4,1)}, pred[4]{0:T(512)(128)(4,1)S(1)}, u32[]{:S(2)}) copy-start(pred[4]{0:T(512)(128)(4,1)S(1)} %get-tuple-element.75) | copy-start | bytes 16
  43.6 77.0 %copy-start.83 = (pred[4]{0:T(512)(128)(4,1)}, pred[4]{0:T(512)(128)(4,1)S(1)}, u32[]{:S(2)}) copy-start(pred[4]{0:T(512)(128)(4,1)S(1)} %get-tuple-element.76) | copy-start | bytes 16
  112.6 6.3 collective-permute-start
  122.3 59.2 %copy-start.1 = (f32[780,1024]{1,0:T(8,128)}, f32[780,1024]{1,0:T(8,128)S(1)}, u32[]{:S(2)}) copy-start(f32[780,1024]{1,0:T(8,128)S(1)} %get-tuple-element.80) | copy-start | bytes 9584644
  122.3 10.0 copy-start.57
  122.9 9.4 copy-start.59
  123.0 9.4 copy-start.64
  133.1 37.2 %collective-permute-start.8 = (bf16[60,2048]{1,0:T(8,128)(2,1)}, bf16[60,2048]{1,0:T(8,128)(2,1)}, u32[]{:S(2)}, u32[]{:S(2)}) collective-permute-start(bf16[60,2048]{1,0:T(8,128)(2,1)} %slice.173), channel_id=1, source_target_pairs={{0,12},{4,16},{8,20},{12,24},{16,28},{20,0},{24,4},{28,8},{1,13},{... | collective-permute-start | bytes 737288 | tf_op jit(solution)/shard_map/ppermute | solution.py:22
  133.1 38.4 %collective-permute-start.7 = (bf16[60,2048]{1,0:T(8,128)(2,1)}, bf16[60,2048]{1,0:T(8,128)(2,1)}, u32[]{:S(2)}, u32[]{:S(2)}) collective-permute-start(bf16[60,2048]{1,0:T(8,128)(2,1)} %slice.173), channel_id=1, source_target_pairs={{0,8},{4,12},{8,16},{12,20},{16,24},{20,28},{24,0},{28,4},{1,9},{5... | collective-permute-start | bytes 737288 | tf_op jit(solution)/shard_map/ppermute | solution.py:22
  133.1 39.6 %collective-permute-start.6 = (bf16[60,2048]{1,0:T(8,128)(2,1)}, bf16[60,2048]{1,0:T(8,128)(2,1)}, u32[]{:S(2)}, u32[]{:S(2)}) collective-permute-start(bf16[60,2048]{1,0:T(8,128)(2,1)} %slice.173), channel_id=1, source_target_pairs={{0,4},{4,8},{8,12},{12,16},{16,20},{20,24},{24,28},{28,0},{1,5},{5... | collective-permute-start | bytes 737288 | tf_op jit(solution)/shard_map/ppermute | solution.py:22
  140.7 8.0 copy-start.15
  140.7 8.0 copy-start.26
  185.5 69.4 %copy-start.70 = (f32[1,1024]{1,0:T(1,128)S(1)}, f32[1,1024]{1,0:T(1,128)}, u32[]{:S(2)}) copy-start(f32[1,1024]{1,0:T(1,128)} %get-tuple-element.62) | copy-start | bytes 12292
  185.5 69.4 %copy-start.90 = (f32[1,1024]{1,0:T(1,128)S(1)}, f32[1,1024]{1,0:T(1,128)}, u32[]{:S(2)}) copy-start(f32[1,1024]{1,0:T(1,128)} %get-tuple-element.59) | copy-start | bytes 12292
  187.7 163.4 %copy-start.66 = (f32[780]{0:T(1024)}, f32[780]{0:T(1024)S(1)}, u32[]{:S(2)}) copy-start(f32[780]{0:T(1024)S(1)} %fusion.61) | copy-start | bytes 9364
  254.9 73.3 %copy-start.61 = (f32[8,1,256]{2,1,0:T(1,128)S(1)}, f32[8,1,256]{2,1,0:T(1,128)}, u32[]{:S(2)}) copy-start(f32[8,1,256]{2,1,0:T(1,128)} %convert_element_type.195) | copy-start | bytes 24580
  328.3 22.9 %copy-start.7 = (f32[780,1024]{1,0:T(8,128)S(1)}, f32[780,1024]{1,0:T(8,128)}, u32[]{:S(2)}) copy-start(f32[780,1024]{1,0:T(8,128)} %copy-done.6) | copy-start | bytes 9584644
  328.3 22.9 %copy-start.71 = (f32[1,1024]{1,0:T(1,128)S(1)}, f32[1,1024]{1,0:T(1,128)}, u32[]{:S(2)}) copy-start(f32[1,1024]{1,0:T(1,128)} %get-tuple-element.62) | copy-start | bytes 12292
  328.3 22.9 %copy-start.91 = (bf16[1024,2048]{1,0:T(8,128)(2,1)S(1)}, bf16[1024,2048]{1,0:T(8,128)(2,1)}, u32[]{:S(2)}) copy-start(bf16[1024,2048]{1,0:T(8,128)(2,1)} %all-gather.10.cloned.1.call-done) | copy-start | bytes 12582916
  365.0 258.6 %reduce-scatter.18.cloned.1.call-start = ((), (), s32[]{:S(2)}) async-start(), calls=%async_computation.14 | async-start | bytes 9437184 | tf_op jit(solution)/shard_map/reduce_scatter | solution.py:309
  374.7 399.1 %reduce-scatter.20.cloned.1.call-start = ((), (), s32[]{:S(2)}) async-start(), calls=%async_computation.15 | async-start | bytes 9437184 | tf_op jit(solution)/shard_map/reduce_scatter | solution.py:310
  374.8 8.2 copy-start.13
  390.0 594.0 %reduce-scatter.14.cloned.1.call-start = ((), (), s32[]{:S(2)}) async-start(), calls=%async_computation.12 | async-start | bytes 14155776 | tf_op jit(solution)/shard_map/reduce_scatter | solution.py:307
  391.5 26.7 %copy-start.36 = (f32[8,720]{1,0:T(8,128)}, f32[8,720]{1,0:T(8,128)S(1)}, u32[]{:S(2)}) copy-start(f32[8,720]{1,0:T(8,128)S(1)} %log_add_fusion) | copy-start | bytes 69124
  395.1 10.3 copy-start.25
  398.9 61.2 %collective-permute-start.10 = (bf16[60,2048]{1,0:T(8,128)(2,1)S(1)}, bf16[60,2048]{1,0:T(8,128)(2,1)}, u32[]{:S(2)}, u32[]{:S(2)}) collective-permute-start(bf16[60,2048]{1,0:T(8,128)(2,1)S(1)} %pad_maximum_fusion.4), channel_id=1, source_target_pairs={{0,24},{4,28},{8,0},{12,4},{16,8},{20,12},{24,16},{28,20},{1,25},{... | collective-permute-start | bytes 737288 | tf_op jit(solution)/shard_map/ppermute | solution.py:22
  401.6 58.6 %collective-permute-start.11 = (bf16[60,2048]{1,0:T(8,128)(2,1)}, bf16[60,2048]{1,0:T(8,128)(2,1)}, u32[]{:S(2)}, u32[]{:S(2)}) collective-permute-start(bf16[60,2048]{1,0:T(8,128)(2,1)} %pad_maximum_fusion.5), channel_id=1, source_target_pairs={{0,20},{4,24},{8,28},{12,0},{16,4},{20,8},{24,12},{28,16},{1,21},{... | collective-permute-start | bytes 737288 | tf_op jit(solution)/shard_map/ppermute | solution.py:22
  402.9 57.3 %collective-permute-start.9 = (bf16[60,2048]{1,0:T(8,128)(2,1)}, bf16[60,2048]{1,0:T(8,128)(2,1)}, u32[]{:S(2)}, u32[]{:S(2)}) collective-permute-start(bf16[60,2048]{1,0:T(8,128)(2,1)} %pad_maximum_fusion.3), channel_id=1, source_target_pairs={{0,28},{4,0},{8,4},{12,8},{16,12},{20,16},{24,20},{28,24},{1,29},{... | collective-permute-start | bytes 737288 | tf_op jit(solution)/shard_map/ppermute | solution.py:22
  418.2 16.9 %copy-start.27 = (bf16[720,1,8,128]{3,2,1,0:T(8,128)(2,1)S(1)}, bf16[720,1,8,128]{3,2,1,0:T(8,128)(2,1)}, u32[]{:S(2)}) copy-start(bf16[720,1,8,128]{3,2,1,0:T(8,128)(2,1)} %copy-done.26) | copy-start | bytes 4423684
  438.6 10.9 copy-start.16
  474.8 574.8 %reduce-scatter.22.cloned.1.call-start = ((), (), s32[]{:S(2)}) async-start(), calls=%async_computation.16 | async-start | bytes 589824
  495.3 11.5 copy-start.85
  495.3 12.6 %copy-start.60 = (f32[780]{0:T(1024)S(1)}, f32[780]{0:T(1024)}, u32[]{:S(2)}) copy-start(f32[780]{0:T(1024)} %copy-done.59) | copy-start | bytes 9364
  512.2 603.0 %reduce-scatter.24.cloned.1.call-start = ((), (), s32[]{:S(2)}) async-start(), calls=%async_computation.17 | async-start | bytes 589824
  513.3 667.0 %reduce-scatter.12.cloned.1.call-start = ((), (), s32[]{:S(2)}) async-start(), calls=%async_computation.11 | async-start | bytes 442368 | tf_op jit(solution)/shard_map/reduce_scatter | solution.py:306
  514.8 719.1 %all-reduce.5.cloned.1.call-start = ((), (), s32[]{:S(2)}) async-start(), calls=%async_computation.18 | async-start | bytes 4194304 | tf_op jit(solution)/shard_map/psum | solution.py:317
  625.7 360.7 %copy-start.21 = (bf16[96,1024]{1,0:T(8,128)(2,1)S(1)}, bf16[96,1024]{1,0:T(8,128)(2,1)}, u32[]{:S(2)}) copy-start(bf16[96,1024]{1,0:T(8,128)(2,1)} %all_gather.29) | copy-start | bytes 589828
  775.9 226.2 %copy-start.74 = (pred[4]{0:T(512)(128)(4,1)S(1)}, pred[4]{0:T(512)(128)(4,1)}, u32[]{:S(2)}) copy-start(pred[4]{0:T(512)(128)(4,1)} %copy-done.73) | copy-start | bytes 16
  775.9 226.2 %copy-start.76 = (pred[4]{0:T(512)(128)(4,1)S(1)}, pred[4]{0:T(512)(128)(4,1)}, u32[]{:S(2)}) copy-start(pred[4]{0:T(512)(128)(4,1)} %copy-done.75) | copy-start | bytes 16
  775.9 226.2 %copy-start.78 = (pred[4]{0:T(512)(128)(4,1)S(1)}, pred[4]{0:T(512)(128)(4,1)}, u32[]{:S(2)}) copy-start(pred[4]{0:T(512)(128)(4,1)} %copy-done.77) | copy-start | bytes 16
  775.9 226.2 %copy-start.80 = (pred[4]{0:T(512)(128)(4,1)S(1)}, pred[4]{0:T(512)(128)(4,1)}, u32[]{:S(2)}) copy-start(pred[4]{0:T(512)(128)(4,1)} %copy-done.79) | copy-start | bytes 16
  775.9 226.2 %copy-start.82 = (pred[4]{0:T(512)(128)(4,1)S(1)}, pred[4]{0:T(512)(128)(4,1)}, u32[]{:S(2)}) copy-start(pred[4]{0:T(512)(128)(4,1)} %copy-done.81) | copy-start | bytes 16
  775.9 226.2 %copy-start.84 = (pred[4]{0:T(512)(128)(4,1)S(1)}, pred[4]{0:T(512)(128)(4,1)}, u32[]{:S(2)}) copy-start(pred[4]{0:T(512)(128)(4,1)} %copy-done.83) | copy-start | bytes 16
  987.6 8.2 collective-permute-start.16
  988.8 8.0 collective-permute-start.15
  991.5 5.4 collective-permute-start.14
  991.5 5.4 collective-permute-start.13
  992.0 5.5 collective-permute-start.17
  995.8 6.3 collective-permute-start.12
  (60 other events, 183.0 us)
Sparse Core Ops, SparseCore 0:
  10.2 104.2 all-gather.5
  116.6 64.7 all-gather.7
  183.6 71.2 all-gather.9
  256.9 71.3 all-gather.11
  365.1 107.6 reduce-scatter.15
  476.3 147.2 reduce-scatter.17
  627.2 146.5 reduce-scatter.19
  777.4 206.5 reduce-scatter.13
  987.9 61.7 reduce-scatter.21
  1053.4 61.7 reduce-scatter.23
  1118.5 61.8 reduce-scatter.11
  1183.4 50.5 all-reduce.4
where the time goes:
time: 1250 us
  waiting for transfers between devices  817 us (65%)
  matrix products  166 us (13%)
  blocking collectives  113 us (9%)
  other arithmetic  65.6 us (5%)
  local copies, waits for them, and re-layouts  38.8 us (3%)
  starting transfers between devices  29.4 us (2%)
  between operations  16.9 us (1%)
    reduce_scatter x1, waiting for transfers between devices, body(): lax.psum_scatter(local_grads[1], 'fsdp', scatter_dimension=0, tiled=True)  208 us
    reduce_scatter x1, waiting for transfers between devices, body(): lax.psum_scatter(local_grads[4], 'fsdp', scatter_dimension=0, tiled=True)  148 us
    unnamed x14, waiting for transfers between devices  113 us
    reduce_scatter x1, waiting for transfers between devices, body(): lax.psum_scatter(local_grads[3], 'fsdp', scatter_dimension=0, tiled=True)  97.9 us
    all_gather x1, waiting for transfers between devices, body(): lax.all_gather(shard_params[3], 'fsdp', axis=0, tiled=True)  67.2 us
    reduce_scatter x1, waiting for transfers between devices, body(): lax.psum_scatter(local_grads[0], 'fsdp', scatter_dimension=1, tiled=True)  64.3 us
    all_gather x1, waiting for transfers between devices, body(): lax.all_gather(shard_params[4], 'fsdp', axis=0, tiled=True)  63.9 us
    psum x1, waiting for transfers between devices, body(): lax.psum(shards[1].astype(jnp.bfloat16), 'dp').astype(jnp.float32)  39.6 us
  transfers between devices with their start and end apart: 30, of which 14 were waited for; matrix products, arithmetic and copies ran while one was open for 17% of the time, Pallas kernels for 0%

commit v1 on v0

v1 whole, which is shorter than its diff:
```python
import jax
import jax.numpy as jnp
from jax import lax
from jax.experimental import pallas as pl
from jax.experimental.pallas import tpu as pltpu
from jax.sharding import PartitionSpec as P

D = 1024
HEADS = 8
HEAD_DIM = 128
PATCH = 96
SPAN = 15
SHORT_SLOTS = 48
LONG_SLOTS = 4
CHUNK = 16 * SPAN

EPSILON = 1e-05
NEG_LARGE = -1e30
SCALE = HEAD_DIM ** (-0.5)
AXES = ("fsdp", "dp")
F32 = jnp.float32
BF16 = jnp.bfloat16


class Place:
    def __init__(self):
        self.fsdp = lax.axis_size("fsdp")
        self.dp = lax.axis_size("dp")
        self.tuned = self.fsdp == 8 and self.dp == 4
        self.f = lax.axis_index("fsdp")
        d = lax.axis_index("dp")
        self.line = self.fsdp // 2
        self.z, self.y = self.f // 2, self.f % 2
        self.x, self.c = d // 2, d % 2

    def move(self, value, line=0, pair=0, side=0, core=0):
        pairs = []
        for f in range(self.fsdp):
            for d in range(self.dp):
                z, y, x, c = f // 2, f % 2, d // 2, d % 2
                to_f = ((z + line) % self.line) * 2 + (y ^ pair)
                to_d = (x ^ side) * 2 + (c ^ core)
                pairs.append((f * self.dp + d, to_f * self.dp + to_d))
        return lax.ppermute(value, AXES, pairs)

    def along(self, value, steps):
        pairs = [(s, (s + steps) % self.fsdp) for s in range(self.fsdp)]
        return lax.ppermute(value, "fsdp", pairs)


def pick(value, index, axis):
    return lax.dynamic_index_in_dim(value, index, axis, keepdims=False)


def assemble_kernel(rows, info, own, a1, a2, a3, b1, b2, n1, n2, n3, m1, m2, out, sem):
    z, y, x, c = info[0], info[1], info[2], info[3]
    half, quarter = rows // 2, rows // 4
    jobs = []

    def add(src, src_row, dst_row, count):
        jobs.append(
            pltpu.make_async_copy(
                src.at[pl.ds(src_row, count), :],
                out.at[pl.ds(pl.multiple_of(dst_row, 16), count), :],
                sem.at[len(jobs)],
            )
        )

    add(own, 0, (z * 2 + y) * rows, rows)
    for step, (mine, other) in enumerate(((a1, n1), (a2, n2), (a3, n3)), 1):
        base = (lax.rem(z + 4 - step, 4) * 2 + y) * rows
        add(mine, 0, base + c * half, half)
        add(other, 0, base + (1 - c) * half, half)
    for step in range(4):
        base = (lax.rem(z + 4 - step, 4) * 2 + (1 - y)) * rows
        for core, side, src in ((c, x, b1), (c, 1 - x, b2), (1 - c, x, m1), (1 - c, 1 - x, m2)):
            add(src, step * quarter, base + core * half + side * quarter, quarter)
    for job in jobs:
        job.start()
    for job in jobs:
        job.wait()


def gather_weight(place, info, shard):
    rows, columns = shard.shape
    if not place.tuned:
        return lax.all_gather(shard, "fsdp", axis=0, tiled=True)
    half, quarter = rows // 2, rows // 4
    a0 = lax.dynamic_slice_in_dim(shard, place.c * half, half, 0)
    a1 = place.move(a0, line=1)
    a2 = place.move(a1, line=1)
    a3 = place.move(a2, line=1)
    piece = lambda a: lax.dynamic_slice_in_dim(a, place.x * quarter, quarter, 0)
    b1 = place.move(jnp.concatenate([piece(a) for a in (a0, a1, a2, a3)], 0), pair=1)
    b2 = place.move(b1, side=1)
    n1, n2, n3, m1, m2 = [place.move(a, core=1) for a in (a1, a2, a3, b1, b2)]
    return pl.pallas_call(
        lambda *refs: assemble_kernel(rows, *refs),
        out_shape=jax.ShapeDtypeStruct((8 * rows, columns), shard.dtype),
        in_specs=[pl.BlockSpec(memory_space=pltpu.SMEM)]
        + [pl.BlockSpec(memory_space=pl.ANY)] * 11,
        out_specs=pl.BlockSpec(memory_space=pltpu.VMEM),
        scratch_shapes=[pltpu.SemaphoreType.DMA((23,))],
        cost_estimate=pl.CostEstimate(
            flops=0, bytes_accessed=32 * rows * columns, transcendentals=0
        ),
        name="assemble",
    )(info, shard, a1, a2, a3, b1, b2, n1, n2, n3, m1, m2)


def gather_small(place, packed):
    if not place.tuned:
        return lax.all_gather(packed, "fsdp", axis=0, tiled=False)
    other = place.move(packed, pair=1)
    low = jnp.where(place.y == 0, packed, other)
    high = jnp.where(place.y == 0, other, packed)
    both = jnp.stack([low, high])
    steps = jnp.stack([both] + [place.move(both, line=k) for k in (1, 2, 3)])
    ordered = [pick(steps, (place.z + 4 - line) % 4, 0) for line in range(4)]
    return jnp.concatenate(ordered, 0)


def reduce_weight(place, grad):
    if not place.tuned:
        part = lax.psum_scatter(grad.astype(F32), "fsdp", scatter_dimension=0, tiled=True)
        return lax.psum(part.astype(BF16), "dp").astype(F32)
    rows, columns = grad.shape[0] // 8, grad.shape[1]
    half = rows // 2
    z, y, x, c = place.z, place.y, place.x, place.c
    view = grad.reshape(8, 2, half, columns)
    got = place.move(pick(view, 1 - c, 1), core=1)
    one = (pick(view, c, 1).astype(F32) + got.astype(F32)).astype(BF16)
    one = one.reshape(4, 2, half, columns)
    got = place.move(pick(one, 1 - y, 1), pair=1)
    two = (pick(one, y, 1).astype(F32) + got.astype(F32)).astype(BF16)
    three = pick(two, z, 0).astype(F32)
    for k in (1, 2, 3):
        three = three + place.move(pick(two, (z + k) % 4, 0), line=k).astype(F32)
    three = three.astype(BF16)
    four = (three.astype(F32) + place.move(three, side=1).astype(F32)).astype(BF16)
    got = place.move(four, core=1)
    low = jnp.where(c == 0, four, got)
    high = jnp.where(c == 0, got, four)
    return jnp.concatenate([low, high], 0).astype(F32)


def reduce_small(place, packed):
    if not place.tuned:
        part = lax.psum_scatter(packed, "fsdp", scatter_dimension=0, tiled=True)[0]
        return lax.psum(part, "dp")
    z, y = place.z, place.y
    packed = packed.astype(BF16)
    one = packed.astype(F32)
    for side, core in ((0, 1), (1, 0), (1, 1)):
        one = one + place.move(packed, side=side, core=core).astype(F32)
    one = one.astype(BF16).reshape(4, 2, *packed.shape[1:])
    got = place.move(pick(one, 1 - y, 1), pair=1)
    two = (pick(one, y, 1).astype(F32) + got.astype(F32)).astype(BF16)
    three = pick(two, z, 0).astype(F32)
    for k in (1, 2, 3):
        three = three + place.move(pick(two, (z + k) % 4, 0), line=k).astype(F32)
    return three


def layer_norm(inputs, gain_row, shift_row):
    center = inputs - jnp.mean(inputs, axis=-1, keepdims=True)
    spread = jnp.mean(center * center, axis=-1, keepdims=True)
    return center * lax.rsqrt(spread + EPSILON) * gain_row + shift_row


def exact_gelu(inputs):
    return jax.nn.gelu(inputs, approximate=False)


def dot_t(a, b):
    return lax.dot_general(a, b, (((1,), (1,)), ((), ())), preferred_element_type=F32)


def dot_l(a, b):
    return lax.dot_general(a, b, (((0,), (0,)), ((), ())), preferred_element_type=F32)


def dot_n(a, b):
    return lax.dot_general(a, b, (((1,), (0,)), ((), ())), preferred_element_type=F32)


def slot_of(index):
    return jnp.floor((index.astype(F32) + 0.5) * (1.0 / SPAN))


def short_bias():
    row = lax.broadcasted_iota(jnp.int32, (CHUNK, CHUNK), 0)
    column = lax.broadcasted_iota(jnp.int32, (CHUNK, CHUNK), 1)
    keep = (slot_of(row) == slot_of(column)) & (column <= row)
    return jnp.where(keep, 0.0, NEG_LARGE)


def short_forward_kernel(q_ref, k_ref, v_ref, out_ref, bias_ref):
    @pl.when(pl.program_id(0) == 0)
    def _():
        bias_ref[...] = short_bias()

    bias = bias_ref[...]
    for chunk in range(SHORT_SLOTS * SPAN // CHUNK):
        rows = pl.ds(chunk * CHUNK, CHUNK)
        scores = dot_t(q_ref[rows, :], k_ref[rows, :]) * SCALE + bias
        top = jnp.max(scores, axis=-1, keepdims=True)
        weights = jnp.exp(scores - top)
        total = jnp.sum(weights, axis=-1, keepdims=True)
        low = (weights * (1.0 / total)).astype(BF16)
        out_ref[rows, :] = dot_n(low, v_ref[rows, :]).astype(BF16)


def short_forward(projected):
    rows = projected.shape[0]
    short_rows = SHORT_SLOTS * SPAN
    block = lambda part: pl.BlockSpec((short_rows, HEAD_DIM), lambda h: (0, part * HEADS + h))
    return pl.pallas_call(
        short_forward_kernel,
        grid=(HEADS,),
        out_shape=jax.ShapeDtypeStruct((rows, D), BF16),
        in_specs=[block(0), block(1), block(2)],
        out_specs=block(0),
        scratch_shapes=[pltpu.VMEM((CHUNK, CHUNK), F32)],
        cost_estimate=pl.CostEstimate(
            flops=4 * short_rows * CHUNK * D,
            bytes_accessed=8 * rows * D,
            transcendentals=short_rows * CHUNK * HEADS,
        ),
        name="short_forward",
    )(projected, projected, projected)


def short_backward_kernel(q_ref, k_ref, v_ref, g_ref, out_ref, bias_ref):
    head = pl.program_id(0)

    @pl.when(head == 0)
    def _():
        bias_ref[...] = short_bias()

    bias = bias_ref[...]
    lanes = lambda part: pl.ds(pl.multiple_of((part * HEADS + head) * HEAD_DIM, HEAD_DIM), HEAD_DIM)
    for chunk in range(SHORT_SLOTS * SPAN // CHUNK):
        rows = pl.ds(chunk * CHUNK, CHUNK)
        query, key, grad = q_ref[rows, :], k_ref[rows, :], g_ref[rows, :]
        scores = dot_t(query, key) * SCALE + bias
        top = jnp.max(scores, axis=-1, keepdims=True)
        weights = jnp.exp(scores - top)
        probs = weights * (1.0 / jnp.sum(weights, axis=-1, keepdims=True))
        grad_probs = dot_t(grad, v_ref[rows, :])
        inner = jnp.sum(probs * grad_probs, axis=-1, keepdims=True)
        grad_scores = (probs * (grad_probs - inner)).astype(BF16)
        out_ref[rows, lanes(0)] = (dot_n(grad_scores, key) * SCALE).astype(BF16)
        out_ref[rows, lanes(1)] = (dot_l(grad_scores, query) * SCALE).astype(BF16)
        out_ref[rows, lanes(2)] = dot_l(probs.astype(BF16), grad).astype(BF16)


def short_backward(projected, grad_mixture):
    rows = projected.shape[0]
    short_rows = SHORT_SLOTS * SPAN
    block = lambda part: pl.BlockSpec((short_rows, HEAD_DIM), lambda h: (0, part * HEADS + h))
    return pl.pallas_call(
        short_backward_kernel,
        grid=(HEADS,),
        out_shape=jax.ShapeDtypeStruct((rows, 3 * D), BF16),
        in_specs=[block(0), block(1), block(2), block(0)],
        out_specs=pl.BlockSpec((rows, 3 * D), lambda h: (0, 0)),
        scratch_shapes=[pltpu.VMEM((CHUNK, CHUNK), F32)],
        cost_estimate=pl.CostEstimate(
            flops=10 * short_rows * CHUNK * D,
            bytes_accessed=14 * rows * D,
            transcendentals=short_rows * CHUNK * HEADS,
        ),
        name="short_backward",
    )(projected, projected, projected, grad_mixture)


def long_biases(quarter_ref):
    rows = LONG_SLOTS * SPAN
    row = lax.broadcasted_iota(jnp.int32, (rows, rows), 0)
    column = lax.broadcasted_iota(jnp.int32, (rows, rows), 1)
    slot = slot_of(row)
    same = slot == slot_of(column)
    quarter = jnp.zeros((rows, rows), jnp.int32)
    for index in range(LONG_SLOTS):
        quarter = jnp.where(slot == float(index), quarter_ref[index], quarter)
    keeps = [same & (column <= row)] + [same & (step <= quarter) for step in (1, 2, 3)]
    return [jnp.where(keep, 0.0, NEG_LARGE) for keep in keeps]


def long_probs(query, keys, biases):
    scores = [dot_t(query, key) * SCALE + bias for key, bias in zip(keys, biases)]
    top = scores[0]
    for member in scores[1:]:
        top = jnp.maximum(top, member)
    top = jnp.max(top, axis=-1, keepdims=True)
    weights = [jnp.exp(member - top) for member in scores]
    total = weights[0] + weights[1] + weights[2] + weights[3]
    scale = 1.0 / jnp.sum(total, axis=-1, keepdims=True)
    return [member * scale for member in weights]


def long_forward_kernel(quarter_ref, q, k0, v0, k1, v1, k2, v2, k3, v3, out_ref):
    biases = long_biases(quarter_ref)
    probs = long_probs(q[...], [k[...] for k in (k0, k1, k2, k3)], biases)
    total = None
    for member, value in zip(probs, (v0, v1, v2, v3)):
        part = dot_n(member.astype(BF16), value[...])
        total = part if total is None else total + part
    out_ref[...] = total.astype(BF16)


def long_specs(rows):
    block = lambda part: pl.BlockSpec((rows, HEAD_DIM), lambda h: (0, part * HEADS + h))
    return [block(0), block(1), block(2)] + [block(0), block(1)] * 3


def long_forward(quarter_index, own, priors):
    rows = own.shape[0]
    spread = [member for prior in priors for member in (prior, prior)]
    return pl.pallas_call(
        long_forward_kernel,
        grid=(HEADS,),
        out_shape=jax.ShapeDtypeStruct((rows, D), BF16),
        in_specs=[pl.BlockSpec(memory_space=pltpu.SMEM)] + long_specs(rows),
        out_specs=pl.BlockSpec((rows, HEAD_DIM), lambda h: (0, h)),
        cost_estimate=pl.CostEstimate(
            flops=16 * rows * rows * D, bytes_accessed=20 * rows * D, transcendentals=0
        ),
        name="long_forward",
    )(quarter_index, own, own, own, *spread)


def long_backward_kernel(
    quarter_ref, q, k0, v0, k1, v1, k2, v2, k3, v3, g, dq_ref, own_ref, s1_ref, s2_ref, s3_ref
):
    biases = long_biases(quarter_ref)
    query, grad = q[...], g[...]
    keys = [k[...] for k in (k0, k1, k2, k3)]
    probs = long_probs(query, keys, biases)
    grads = [dot_t(grad, value[...]) for value in (v0, v1, v2, v3)]
    inner = None
    for member, part in zip(probs, grads):
        inner = member * part if inner is None else inner + member * part
    inner = jnp.sum(inner, axis=-1, keepdims=True)
    total = None
    for index, out in enumerate((own_ref, s1_ref, s2_ref, s3_ref)):
        grad_scores = (probs[index] * (grads[index] - inner)).astype(BF16)
        part = dot_n(grad_scores, keys[index])
        total = part if total is None else total + part
        out[0, :, :] = (dot_l(grad_scores, query) * SCALE).astype(out.dtype)
        out[1, :, :] = dot_l(probs[index].astype(BF16), grad).astype(out.dtype)
    dq_ref[...] = (total * SCALE).astype(BF16)


def long_backward(quarter_index, own, priors, grad_mixture):
    rows = own.shape[0]
    spread = [member for prior in priors for member in (prior, prior)]
    flat = pl.BlockSpec((rows, HEAD_DIM), lambda h: (0, h))
    pair = pl.BlockSpec((2, rows, HEAD_DIM), lambda h: (0, 0, h))
    return pl.pallas_call(
        long_backward_kernel,
        grid=(HEADS,),
        out_shape=[jax.ShapeDtypeStruct((rows, D), BF16)]
        + [jax.ShapeDtypeStruct((2, rows, D), kind) for kind in (F32, BF16, BF16, BF16)],
        in_specs=[pl.BlockSpec(memory_space=pltpu.SMEM)] + long_specs(rows) + [flat],
        out_specs=[flat] + [pair] * 4,
        cost_estimate=pl.CostEstimate(
            flops=40 * rows * rows * D, bytes_accessed=40 * rows * D, transcendentals=0
        ),
        name="long_backward",
    )(quarter_index, own, own, own, *spread, grad_mixture)


def body(
    series_values,
    quarter_index,
    patch_weight,
    heads_in,
    heads_out,
    expand_weight,
    reduce_weight_shard,
    norm_gains,
    bias_rows,
    expand_bias,
    cotangent,
):
    place = Place()
    fsdp = place.fsdp
    width = patch_weight.shape[1]
    info = jnp.stack([place.z, place.y, place.x, place.c]).astype(jnp.int32)
    row_count = series_values.shape[0]
    slot_count = row_count // SPAN
    short_rows = SHORT_SLOTS * SPAN
    long_rows = row_count - short_rows

    grouped = series_values.reshape(slot_count, SPAN * PATCH)
    slot_sums = jnp.stack([jnp.sum(grouped, 1), jnp.sum(grouped * grouped, 1)], 1)
    long_sums = slot_sums[SHORT_SLOTS:]
    rows_of = lambda a: a.astype(F32).reshape(-1, width)
    pieces = [rows_of(a) for a in (patch_weight, norm_gains, bias_rows, expand_bias)]
    small = gather_small(place, jnp.concatenate(pieces, 0))
    chain = gather_small(place, long_sums)
    offset = jnp.arange(fsdp)[:, None] - place.f + quarter_index[None, :]
    member = ((offset + fsdp) % fsdp < 4).astype(F32)[:, :, None]
    chain_sum = jnp.sum(chain * member, 0)

    wide = lambda low, high: small[:, low:high].transpose(1, 0, 2).reshape(high - low, D)
    patch_all = wide(0, PATCH).astype(BF16)
    gains_all = wide(PATCH, PATCH + 2)
    biases_all = wide(PATCH + 2, PATCH + 6)
    expand_shift = small[:, PATCH + 6 :].reshape(-1)

    heads_in_all = gather_weight(place, info, heads_in)
    heads_out_all = gather_weight(place, info, heads_out)
    reduce_all = gather_weight(place, info, reduce_weight_shard)
    expand_all = gather_weight(place, info, expand_weight)

    totals = jnp.concatenate([slot_sums[:SHORT_SLOTS], chain_sum], 0)
    counts = jnp.where(jnp.arange(slot_count) < SHORT_SLOTS, SPAN * PATCH, 4 * SPAN * PATCH).astype(
        F32
    )
    slot_mean = totals[:, 0] / counts
    inv_spread = lax.rsqrt(totals[:, 1] / counts - slot_mean * slot_mean + EPSILON)
    normed_slots = (grouped - slot_mean[:, None]) * inv_spread[:, None]
    normed_low = normed_slots.reshape(row_count, PATCH).astype(BF16)
    embedded = dot_n(normed_low, patch_all) + biases_all[0]
    first_value, first_back = jax.vjp(layer_norm, embedded, gains_all[0], biases_all[1])
    first_norm = first_value.astype(BF16)
    projected = dot_n(first_norm, heads_in_all).astype(BF16)

    own_long = projected[short_rows:]
    long_pairs = own_long[:, D:]
    priors = [place.along(long_pairs, step) for step in (1, 2, 3)]
    mixed_short = short_forward(projected)
    mixed_long = long_forward(quarter_index, own_long, priors)
    mixed_all = lax.dynamic_update_slice(mixed_short, mixed_long, (short_rows, 0))
    middle = embedded + dot_n(mixed_all, heads_out_all)
    second_value, second_back = jax.vjp(layer_norm, middle, gains_all[1], biases_all[2])
    second_norm = second_value.astype(BF16)

    pre_act = dot_n(second_norm, expand_all) + expand_shift
    act_value, gelu_back = jax.vjp(exact_gelu, pre_act)
    activation = act_value.astype(BF16)
    layer_output = (middle + dot_n(activation, reduce_all) + biases_all[3]).astype(BF16)

    grad_reduce = reduce_weight(place, dot_l(activation, cotangent).astype(BF16))
    grad_act = dot_t(cotangent, reduce_all)
    grad_pre = gelu_back(grad_act)[0].astype(BF16)
    grad_expand = reduce_weight(place, dot_l(second_norm, grad_pre).astype(BF16))
    grad_expand_bias = jnp.sum(grad_pre.astype(F32), 0)
    grad_second = dot_t(grad_pre, expand_all)
    middle_back, gain_two, shift_two = second_back(grad_second)
    grad_middle = cotangent.astype(F32) + middle_back
    grad_branch = grad_middle.astype(BF16)
    grad_heads_out = reduce_weight(place, dot_l(mixed_all, grad_branch).astype(BF16))
    grad_mixture = dot_t(grad_branch, heads_out_all).astype(BF16)

    long_query, own_grads, *sent = long_backward(
        quarter_index, own_long, priors, grad_mixture[short_rows:]
    )
    for step, sent_back in zip((1, 2, 3), sent):
        own_grads = own_grads + place.along(sent_back, -step).astype(F32)
    own_grads = own_grads.astype(BF16)
    grad_short = short_backward(projected, grad_mixture)
    grad_long = jnp.concatenate([long_query, own_grads[0], own_grads[1]], 1)
    grad_projected = lax.dynamic_update_slice(grad_short, grad_long, (short_rows, 0))
    grad_heads_in = reduce_weight(place, dot_l(first_norm, grad_projected).astype(BF16))
    grad_first = dot_t(grad_projected, heads_in_all)
    embed_back, gain_one, shift_one = first_back(grad_first)
    grad_embedded = (grad_middle + embed_back).astype(BF16)
    grad_patch = dot_l(normed_low, grad_embedded)
    shift_zero = jnp.sum(grad_embedded.astype(F32), 0)
    grad_normed = dot_t(grad_embedded, patch_all).reshape(slot_count, SPAN * PATCH)
    slot_grads = jnp.stack([jnp.sum(grad_normed, 1), jnp.sum(grad_normed * normed_slots, 1)], 1)
    chain_grads = gather_small(place, slot_grads[SHORT_SLOTS:])
    chain_grad = jnp.sum(chain_grads * member, 0)
    grad_totals = jnp.concatenate([slot_grads[:SHORT_SLOTS], chain_grad], 0)
    series_grad = (
        inv_spread[:, None]
        * (
            grad_normed
            - grad_totals[:, 0:1] / counts[:, None]
            - normed_slots * grad_totals[:, 1:2] / counts[:, None]
        )
    ).reshape(row_count, PATCH)
    shift_three = jnp.sum(cotangent.astype(F32), 0)

    split = lambda a: a.reshape(-1, fsdp, width).transpose(1, 0, 2)
    packed = jnp.concatenate(
        [
            split(grad_patch),
            split(jnp.stack([gain_one, gain_two, shift_zero, shift_one, shift_two, shift_three])),
            grad_expand_bias.reshape(fsdp, -1, width),
        ],
        1,
    )
    small_grads = reduce_small(place, packed)
    return (
        layer_output,
        series_grad,
        small_grads[:PATCH],
        grad_heads_in,
        grad_heads_out,
        grad_expand,
        grad_reduce,
        small_grads[PATCH : PATCH + 2],
        small_grads[PATCH + 2 : PATCH + 6],
        small_grads[PATCH + 6 :].reshape(-1),
    )


def solution(mesh):
    in_specs = (
        P(("fsdp", "dp"), None),
        P(("fsdp", "dp")),
        P(None, "fsdp"),
        P("fsdp", None),
        P("fsdp", None),
        P("fsdp", None),
        P("fsdp", None),
        P(None, "fsdp"),
        P(None, "fsdp"),
        P("fsdp"),
        P(("fsdp", "dp"), None),
    )
    out_specs = (
        P(("fsdp", "dp"), None),
        P(("fsdp", "dp"), None),
        P(None, "fsdp"),
        P("fsdp", None),
        P("fsdp", None),
        P("fsdp", None),
        P("fsdp", None),
        P(None, "fsdp"),
        P(None, "fsdp"),
        P("fsdp"),
    )
    return jax.shard_map(body, mesh=mesh, in_specs=in_specs, out_specs=out_specs, check_vma=False)
```

time: 1250 us -> 554 us (0.44)
  waiting for transfers between devices: 817 us -> 227 us
  blocking collectives: 113 us -> 0 us
  matrix products: 166 us -> 91.7 us
  Pallas kernels: 0 us -> 63.5 us
  starting transfers between devices: 29.4 us -> 85.2 us
  other arithmetic: 65.6 us -> 34.3 us
  between operations: 16.9 us -> 2.66 us
    reduce_scatter x5 -> x0, waiting for transfers between devices: 518 us -> none  [the longest x1 208 us: body(): lax.psum_scatter(local_grads[1], 'fsdp', scatter_dimension=0, tiled=True)]
    ppermute x18 -> x93, waiting for transfers between devices: 11.5 us -> 227 us  [the longest x87 227 us: move(): return lax.ppermute(value, AXES, pairs)]
    all_gather x4 -> x0, waiting for transfers between devices: 135 us -> none  [the longest x1 67.2 us: body(): lax.all_gather(shard_params[3], 'fsdp', axis=0, tiled=True)]
    unnamed x14 -> x0, waiting for transfers between devices: 113 us -> none
    all_gather x4 -> x0, blocking collectives: 83.8 us -> none  [the longest x1 29.3 us: body(): lax.all_gather(shard_params[0], 'fsdp', axis=1, tiled=True)]
    dot_general x27 -> x15, matrix products: 166 us -> 91.7 us  [the longest x5 38.3 us: dot_n(): lax.dot_general(a, b, (((1,), (0,)), ((), ())), preferred_element_type=F32)]
    pallas_call x0 -> x8, Pallas kernels: none -> 63.5 us  [the longest x4 20 us: gather_weight(): pl.pallas_call(lambda *refs: assemble_kernel(rows, *refs), out_shape=jax....]
    ppermute x18 -> x93, starting transfers between devices: 28.8 us -> 85.2 us  [the longest x87 76.9 us: move(): return lax.ppermute(value, AXES, pairs)]
  transfers between devices with their start and end apart: 30 -> 93, of which waited for: 14 -> 37; matrix products, arithmetic and copies ran while one was open for 17% -> 16% of each run, Pallas kernels for 0% -> 9%
where the time goes in v1:
time: 554 us; the launch traced here: 544 us
  waiting for transfers between devices  227 us (41%)
  matrix products  91.7 us (17%)
  starting transfers between devices  85.2 us (15%)
  Pallas kernels  63.5 us (11%)
  local copies, waits for them, and re-layouts  39.2 us (7%)
  other arithmetic  34.3 us (6%)
    ppermute x87, waiting for transfers between devices, move(): return lax.ppermute(value, AXES, pairs)  227 us
    ppermute x87, starting transfers between devices, move(): return lax.ppermute(value, AXES, pairs)  76.9 us
    dot_general x5, matrix products, dot_n(): lax.dot_general(a, b, (((1,), (0,)), ((), ())), preferred_element_type=F32)  38.3 us
    dot_general x5, matrix products, dot_t(): lax.dot_general(a, b, (((1,), (1,)), ((), ())), preferred_element_type=F32)  26.8 us
    dot_general x5, matrix products, dot_l(): lax.dot_general(a, b, (((0,), (0,)), ((), ())), preferred_element_type=F32)  26.6 us
    pallas_call x4, Pallas kernels, gather_weight(): pl.pallas_call(lambda *refs: assemble_kernel(rows, *refs), out_shape=jax....  20 us
    pallas_call x1, Pallas kernels, short_backward(): pl.pallas_call(short_backward_kernel, grid=(HEADS,), out_shape=jax.ShapeD...  18.5 us
    squeeze x17, local copies, waits for them, and re-layouts, pick(): return lax.dynamic_index_in_dim(value, index, axis, keepdims=False)  11.2 us
  transfers between devices with their start and end apart: 93, of which 37 were waited for; matrix products, arithmetic and copies ran while one was open for 16% of the time, Pallas kernels for 9%

profile of v1, /device:TPU:0, one launch (start us, length us, event | category | flops | bytes accessed | tf_op | source)
XLA Modules:
  0.0 543.8 jit_solution(12862776529251467123)
XLA Ops:
  2.4 3.0 collective-permute-start
  21.2 2.2 collective-permute-start.3
  26.7 3.4 collective-permute-start.5
  30.6 10.1 %collective-permute-done.6 = f32[2,104,128]{2,1,0:T(8,128)S(1)} collective-permute-done((f32[2,104,128]{2,1,0:T(8,128)S(1)}, f32[2,104,128]{2,1,0:T(8,128)S(1)}, u32[]{:S(2)}, u32[]{:S(2)}) %collective-permute-start.6) | collective-permute-done | bytes 106528 | tf_op jit(solution)/shard_map/ppermute | solution.py:44
  40.7 2.7 collective-permute-start.22
  43.7 10.7 %collective-permute-done.22.refs_3_ = bf16[64,1024]{1,0:T(8,128)(2,1)S(1)} collective-permute-done((bf16[64,1024]{1,0:T(8,128)(2,1)S(1)}, bf16[64,1024]{1,0:T(8,128)(2,1)S(1)}, u32[]{:S(2)}, u32[]{:S(2)}) %collective-permute-start.22) | collective-permute-done | bytes 131104 | tf_op jit(solution)/shard_map/ppermute | solution.py:44
  54.4 8.4 %collective-permute-done.9.refs_3_ = bf16[64,3072]{1,0:T(8,128)(2,1)S(1)} collective-permute-done((bf16[64,3072]{1,0:T(8,128)(2,1)S(1)}, bf16[64,3072]{1,0:T(8,128)(2,1)S(1)}, u32[]{:S(2)}, u32[]{:S(2)}) %collective-permute-start.9) | collective-permute-done | bytes 393248 | tf_op jit(solution)/shard_map/ppermute | solution.py:44
  62.9 10.9 %collective-permute-done.10.refs_4_ = bf16[64,3072]{1,0:T(8,128)(2,1)S(1)} collective-permute-done((bf16[64,3072]{1,0:T(8,128)(2,1)S(1)}, bf16[64,3072]{1,0:T(8,128)(2,1)S(1)}, u32[]{:S(2)}, u32[]{:S(2)}) %collective-permute-start.10) | collective-permute-done | bytes 393248 | tf_op jit(solution)/shard_map/ppermute | solution.py:44
  76.3 10.3 %collective-permute-done.32.refs_3_ = bf16[64,2048]{1,0:T(8,128)(2,1)S(1)} collective-permute-done((bf16[64,2048]{1,0:T(8,128)(2,1)S(1)}, bf16[64,2048]{1,0:T(8,128)(2,1)S(1)}, u32[]{:S(2)}, u32[]{:S(2)}) %collective-permute-start.32) | collective-permute-done | bytes 262176 | tf_op jit(solution)/shard_map/ppermute | solution.py:44
  86.6 5.6 %collective-permute-done.42.refs_3_ = bf16[128,1024]{1,0:T(8,128)(2,1)S(1)} collective-permute-done((bf16[128,1024]{1,0:T(8,128)(2,1)S(1)}, bf16[128,1024]{1,0:T(8,128)(2,1)S(1)}, u32[]{:S(2)}, u32[]{:S(2)}) %collective-permute-start.42) | collective-permute-done | bytes 262176 | tf_op jit(solution)/shard_map/ppermute | solution.py:44
  94.3 3.5 collective-permute-done.33.refs_4_
  98.4 4.7 collective-permute-done.43.refs_4_
  108.4 2.5 collective-permute-done.12.refs_6_
  113.1 7.5 %collective-permute-done.44.refs_5_ = bf16[256,1024]{1,0:T(8,128)(2,1)} collective-permute-done((bf16[256,1024]{1,0:T(8,128)(2,1)S(1)}, bf16[256,1024]{1,0:T(8,128)(2,1)}, u32[]{:S(2)}, u32[]{:S(2)}) %collective-permute-start.44) | collective-permute-done | bytes 524320 | tf_op jit(solution)/shard_map/ppermute | solution.py:44
  122.0 9.2 %collective-permute-done.34.refs_5_ = bf16[128,2048]{1,0:T(8,128)(2,1)} collective-permute-done((bf16[128,2048]{1,0:T(8,128)(2,1)S(1)}, bf16[128,2048]{1,0:T(8,128)(2,1)}, u32[]{:S(2)}, u32[]{:S(2)}) %collective-permute-start.34) | collective-permute-done | bytes 524320 | tf_op jit(solution)/shard_map/ppermute | solution.py:44
  134.5 6.2 %assemble.4 = bf16[1024,3072]{1,0:T(8,128)(2,1)} custom-call(s32[4]{0:T(128)} %pad_add_fusion.refs_0_, bf16[128,3072]{1,0:T(8,128)(2,1)} %refs_1_.4, bf16[64,3072]{1,0:T(8,128)(2,1)} %copy-done.22, bf16[64,3072]{1,0:T(8,128)(2,1)} %copy-done.23, bf16[64,3072]{1,0:T(8,128)(2,1)} %copy-done.24, bf16[128,3072]{1,0:T(8,128)(2,1)} %copy-done.25, ...), custom_call_target="tpu_custom_call" | custom-call | bytes 12582912 | tf_op jit(solution)/shard_map/assemble/pallas_call | solution.py:97
  140.7 9.8 %collective-permute-done.25.refs_6_ = bf16[128,1024]{1,0:T(8,128)(2,1)} collective-permute-done((bf16[128,1024]{1,0:T(8,128)(2,1)}, bf16[128,1024]{1,0:T(8,128)(2,1)}, u32[]{:S(2)}, u32[]{:S(2)}) %collective-permute-start.25) | collective-permute-done | bytes 262176 | tf_op jit(solution)/shard_map/ppermute | solution.py:44
  151.7 8.7 %convolution_convert_fusion.1.q_ref.k_ref.v_ref = bf16[780,3072]{1,0:T(8,128)(2,1)S(1)} fusion(bf16[1024,3072]{1,0:T(8,128)(2,1)} %assemble.4, f32[780,1024]{1,0:T(8,128)S(1)} %get-tuple-element.103, f32[1024]{0:T(1024)S(1)} %bitcast.329, f32[1024]{0:T(1024)S(1)} %bitcast.315, f32[780]{0:T(1024)S(1)} %fusion.61, f32[780]{0:T(1024)S(1)} %broadcast_multiply_fusion.1, ...), kind=kOutput, calls=%fused_computation.28 | convolution fusion | flops 4914524160 | bytes 14297184 | tf_op jit(solution)/shard_map/dot_general | solution.py:184
  163.4 3.2 collective-permute-start.18
  167.4 3.7 assemble.5
  171.1 5.1 assemble.7
  176.2 5.0 assemble.6
  183.0 10.6 %short_forward.1 = bf16[780,1024]{1,0:T(8,128)(2,1)} custom-call(bf16[780,3072]{1,0:T(8,128)(2,1)} %copy-done, bf16[780,3072]{1,0:T(8,128)(2,1)} %copy-done, bf16[780,3072]{1,0:T(8,128)(2,1)} %copy-done), custom_call_target="tpu_custom_call" | custom-call | flops 707788800 | bytes 6389760 | tf_op jit(solution)/shard_map/short_forward/pallas_call | solution.py:218
  194.3 6.7 %long_forward.1 = bf16[60,1024]{1,0:T(8,128)(2,1)} custom-call(s32[4]{0:T(128)} %quarter_ref.3, bf16[60,3072]{1,0:T(8,128)(2,1)} %slice.120.q.k0.v0, bf16[60,3072]{1,0:T(8,128)(2,1)} %slice.120.q.k0.v0, bf16[60,3072]{1,0:T(8,128)(2,1)} %slice.120.q.k0.v0, bf16[60,2048]{1,0:T(8,128)(2,1)} %collective-permute-done.18.k1.v1, ...), custom_call_target="tpu_custom_call" | custom-call | flops 58982400 | bytes 1228800 | tf_op jit(solution)/shard_map/long_forward/pallas_call | solution.py:321
  202.6 4.2 fusion.86
  207.3 20.1 %multiply_convert_fusion = (bf16[780,2048]{1,0:T(8,128)(2,1)S(1)}, f32[780,2048]{1,0:T(8,128)}, f32[780,2048]{1,0:T(8,128)}) fusion(f32[2048]{0:T(1024)S(1)} %bitcast.325, bf16[1024,2048]{1,0:T(8,128)(2,1)S(1)} %copy-done.13, f32[780,1024]{1,0:T(8,128)S(1)} %get-tuple-element.105, f32[1024]{0:T(1024)S(1)} %bitcast.332, f32[1024]{0:T(1024)S(1)} %bitcast.319, ...), kind=kOutput, calls=%fused_computation.11 | convolution fusion | flops 3380981760 | bytes 23386208 | tf_op jit(solution)/shard_map/dot_general | solution.py:184
  227.4 9.3 %fusion.87 = (bf16[2048]{0:T(1024)(128)(2,1)}, bf16[780,2048]{1,0:T(8,128)(2,1)S(1)}) fusion(f32[780,2048]{1,0:T(8,128)} %get-tuple-element.37, bf16[2048,1024]{1,0:T(8,128)(2,1)S(1)} %copy-done.12, bf16[780,1024]{1,0:T(8,128)(2,1)S(1)} %copy-done.4, f32[780,2048]{1,0:T(8,128)} %get-tuple-element.106, f32[2048]{0:T(1024)S(1)} %bitcast.326), kind=kOutput, calls=%fused_computation.264 | convolution fusion | flops 3297114112 | bytes 21778432 | tf_op jit(solution)/shard_map/dot_general | solution.py:176
  236.7 4.1 multiply_reduce_fusion
  240.8 6.7 %convolution_convert_fusion.3 = bf16[1024,2048]{1,0:T(8,128)(2,1)} fusion(bf16[780,2048]{1,0:T(8,128)(2,1)S(1)} %get-tuple-element.111, f32[780,1024]{1,0:T(8,128)S(1)} %get-tuple-element.105, f32[1024]{0:T(1024)S(1)} %bitcast.333, f32[1024]{0:T(1024)S(1)} %bitcast.321, f32[780]{0:T(1024)S(1)} %fusion.62, f32[780]{0:T(1024)S(1)} %broadcast_multiply_fusion), kind=kOutput, calls=%fused_computation.36 | convolution fusion | flops 3277647872 | bytes 10598496 | tf_op jit(solution)/shard_map/dot_general | solution.py:180
  252.1 3.7 convolution_convert_fusion.4
  255.7 6.2 %convolution_convert_fusion.2 = bf16[2048,1024]{1,0:T(8,128)(2,1)} fusion(bf16[780,2048]{1,0:T(8,128)(2,1)S(1)} %get-tuple-element.36, bf16[780,1024]{1,0:T(8,128)(2,1)S(1)} %copy-done.4), kind=kOutput, calls=%fused_computation.35 | convolution fusion | flops 3273654272 | bytes 8986624 | tf_op jit(solution)/shard_map/dot_general | solution.py:180
  261.9 4.6 add_convert_fusion.1
  268.4 7.7 %long_backward.1 = (bf16[60,1024]{1,0:T(8,128)(2,1)}, f32[2,60,1024]{2,1,0:T(8,128)}, bf16[2,60,1024]{2,1,0:T(8,128)(2,1)}, bf16[2,60,1024]{2,1,0:T(8,128)(2,1)}, bf16[2,60,1024]{2,1,0:T(8,128)(2,1)}) custom-call(s32[4]{0:T(128)} %quarter_ref.3, bf16[60,3072]{1,0:T(8,128)(2,1)} %slice.120.q.k0.v0, bf16[60,3072]{1,0:T(8,128)(2,1)} %slice.120.q.k0.v0, ...), custom_call_target="tpu_custom_call" | custom-call | flops 147456000 | bytes 2457600 | tf_op jit(solution)/shard_map/long_backward/pallas_call | solution.py:361
  281.0 2.3 dynamic-slice_bitcast_fusion.6
  283.3 3.1 dynamic-slice_bitcast_fusion.1
  288.3 18.5 %short_backward.1 = bf16[780,3072]{1,0:T(8,128)(2,1)} custom-call(bf16[780,3072]{1,0:T(8,128)(2,1)} %copy-done, bf16[780,3072]{1,0:T(8,128)(2,1)} %copy-done, bf16[780,3072]{1,0:T(8,128)(2,1)} %copy-done, bf16[780,1024]{1,0:T(8,128)(2,1)} %copy-done.17), custom_call_target="tpu_custom_call" | custom-call | flops 1769472000 | bytes 11182080 | tf_op jit(solution)/shard_map/short_backward/pallas_call | solution.py:262
  310.0 10.2 %multiply_reduce_fusion.1 = (bf16[1024]{0:T(1024)(128)(2,1)S(1)}, f32[780]{0:T(1024)S(1)}, bf16[1024]{0:T(1024)(128)(2,1)S(1)}, f32[780,1024]{1,0:T(8,128)S(1)}) fusion(f32[780,1024]{1,0:T(8,128)} %copy-done.1, f32[780]{0:T(1024)S(1)} %fusion.61, f32[780]{0:T(1024)S(1)} %broadcast_multiply_fusion.1, f32[1024]{0:T(1024)S(1)} %bitcast.310, ...), kind=kOutput, calls=%fused_computation.38 | convolution fusion | flops 4914521088 | bytes 17495184 | tf_op jit(solution)/shard_map/dot_general | solution.py:176
  320.2 9.6 %convolution_convert_fusion = bf16[1024,3072]{1,0:T(8,128)(2,1)} fusion(bf16[780,3072]{1,0:T(8,128)(2,1)S(1)} %copy-done.8, f32[780,1024]{1,0:T(8,128)S(1)} %copy-done.2, f32[1024]{0:T(1024)S(1)} %bitcast.330, f32[1024]{0:T(1024)S(1)} %bitcast.317, f32[780]{0:T(1024)S(1)} %fusion.61, f32[780]{0:T(1024)S(1)} %broadcast_multiply_fusion.1, f32[1024]{0:T(1024)S(1)} %bitcast.311), kind=kOutput, calls=%fused_computation.27 | convolution fusion | flops 4915273728 | bytes 14297184 | tf_op jit(solution)/shard_map/dot_general | solution.py:180
  335.5 2.3 collective-permute-start.54
  342.0 2.4 dynamic-slice_bitcast_fusion
  345.7 3.9 collective-permute-done.56
  350.6 2.6 collective-permute-done.57
  354.1 5.8 %collective-permute-done.60 = bf16[8,104,128]{2,1,0:T(8,128)(2,1)S(1)} collective-permute-done((bf16[8,104,128]{2,1,0:T(8,128)(2,1)S(1)}, bf16[8,104,128]{2,1,0:T(8,128)(2,1)S(1)}, u32[]{:S(2)}, u32[]{:S(2)}) %collective-permute-start.60) | collective-permute-done | bytes 213024 | tf_op jit(solution)/shard_map/ppermute | solution.py:44
  364.0 13.2 %collective-permute-done.61 = bf16[4,104,128]{2,1,0:T(8,128)(2,1)S(1)} collective-permute-done((bf16[4,104,128]{2,1,0:T(8,128)(2,1)S(1)}, bf16[4,104,128]{2,1,0:T(8,128)(2,1)S(1)}, u32[]{:S(2)}, u32[]{:S(2)}) %collective-permute-start.61) | collective-permute-done | bytes 106528 | tf_op jit(solution)/shard_map/ppermute | solution.py:44
  384.1 2.3 collective-permute-start.76
  389.5 3.9 collective-permute-start.64
  404.8 3.2 fusion.15
  408.6 3.0 fusion.14
  412.9 3.1 fusion.13
  417.1 17.1 %collective-permute-done.80 = bf16[4,64,2048]{2,1,0:T(8,128)(2,1)S(1)} collective-permute-done((bf16[4,64,2048]{2,1,0:T(8,128)(2,1)S(1)}, bf16[4,64,2048]{2,1,0:T(8,128)(2,1)S(1)}, u32[]{:S(2)}, u32[]{:S(2)}) %collective-permute-start.80) | collective-permute-done | bytes 1048608 | tf_op jit(solution)/shard_map/ppermute | solution.py:44
  434.6 3.4 collective-permute-start.81
  439.6 17.0 %collective-permute-done.87 = bf16[4,128,1024]{2,1,0:T(8,128)(2,1)S(1)} collective-permute-done((bf16[4,128,1024]{2,1,0:T(8,128)(2,1)S(1)}, bf16[4,128,1024]{2,1,0:T(8,128)(2,1)S(1)}, u32[]{:S(2)}, u32[]{:S(2)}) %collective-permute-start.87) | collective-permute-done | bytes 1048608 | tf_op jit(solution)/shard_map/ppermute | solution.py:44
  457.1 3.4 collective-permute-start.88
  464.3 3.9 collective-permute-done.88
  468.2 4.7 collective-permute-done.90
  472.9 9.6 %collective-permute-done.89 = bf16[128,1024]{1,0:T(8,128)(2,1)S(1)} collective-permute-done((bf16[128,1024]{1,0:T(8,128)(2,1)S(1)}, bf16[128,1024]{1,0:T(8,128)(2,1)S(1)}, u32[]{:S(2)}, u32[]{:S(2)}) %collective-permute-start.89) | collective-permute-done | bytes 262176 | tf_op jit(solution)/shard_map/ppermute | solution.py:44
  482.7 2.6 collective-permute-start.91
  485.3 4.2 collective-permute-done.66
  490.2 3.4 collective-permute-start.67
  495.9 8.2 %collective-permute-done.67 = bf16[64,3072]{1,0:T(8,128)(2,1)S(1)} collective-permute-done((bf16[64,3072]{1,0:T(8,128)(2,1)S(1)}, bf16[64,3072]{1,0:T(8,128)(2,1)S(1)}, u32[]{:S(2)}, u32[]{:S(2)}) %collective-permute-start.67) | collective-permute-done | bytes 393248 | tf_op jit(solution)/shard_map/ppermute | solution.py:44
  504.1 7.5 %collective-permute-done.69 = bf16[64,3072]{1,0:T(8,128)(2,1)S(1)} collective-permute-done((bf16[64,3072]{1,0:T(8,128)(2,1)S(1)}, bf16[64,3072]{1,0:T(8,128)(2,1)S(1)}, u32[]{:S(2)}, u32[]{:S(2)}) %collective-permute-start.69) | collective-permute-done | bytes 393248 | tf_op jit(solution)/shard_map/ppermute | solution.py:44
  511.6 16.1 %collective-permute-done.68 = bf16[64,3072]{1,0:T(8,128)(2,1)S(1)} collective-permute-done((bf16[64,3072]{1,0:T(8,128)(2,1)S(1)}, bf16[64,3072]{1,0:T(8,128)(2,1)S(1)}, u32[]{:S(2)}, u32[]{:S(2)}) %collective-permute-start.68) | collective-permute-done | bytes 393248 | tf_op jit(solution)/shard_map/ppermute | solution.py:44
  527.9 2.6 collective-permute-start.70
  530.6 9.2 %collective-permute-done.70 = bf16[64,3072]{1,0:T(8,128)(2,1)S(1)} collective-permute-done((bf16[64,3072]{1,0:T(8,128)(2,1)S(1)}, bf16[64,3072]{1,0:T(8,128)(2,1)S(1)}, u32[]{:S(2)}, u32[]{:S(2)}) %collective-permute-start.70) | collective-permute-done | bytes 393248 | tf_op jit(solution)/shard_map/ppermute | solution.py:44
  (445 shorter events, 118.6 us)
Async XLA Ops:
  2.4 14.3 %collective-permute-start = (f32[4,2]{0,1:T(2,128)S(1)}, f32[4,2]{0,1:T(2,128)S(1)}, u32[]{:S(2)}, u32[]{:S(2)}) collective-permute-start(f32[4,2]{0,1:T(2,128)S(1)} %slice.90), channel_id=1, source_target_pairs={{0,4},{1,5},{2,6},{3,7},{4,0},{5,1},{6,2},{7,3},{8,12},{9,13},{10,... | collective-permute-start | bytes 104 | tf_op jit(solution)/shard_map/ppermute | solution.py:44
  6.2 19.2 %collective-permute-start.4 = (f32[104,128]{1,0:T(8,128)S(1)}, f32[104,128]{1,0:T(8,128)S(1)}, u32[]{:S(2)}, u32[]{:S(2)}) collective-permute-start(f32[104,128]{1,0:T(8,128)S(1)} %maximum_convert_fusion.4), channel_id=1, source_target_pairs={{0,4},{1,5},{2,6},{3,7},{4,0},{5,1},{6,2},{7,3},{8,12},{9,13},{10,... | collective-permute-start | bytes 159752 | tf_op jit(solution)/shard_map/ppermute | solution.py:44
  7.2 23.0 %collective-permute-start.21 = (bf16[64,1024]{1,0:T(8,128)(2,1)S(1)}, bf16[64,1024]{1,0:T(8,128)(2,1)S(1)}, u32[]{:S(2)}, u32[]{:S(2)}) collective-permute-start(bf16[64,1024]{1,0:T(8,128)(2,1)S(1)} %constant_dynamic-slice_fusion.18), channel_id=1, source_target_pairs={{0,8},{1,9},{2,10},{3,11},{4,12},{5,13},{6,14},{7,15},{8,16},{9,17... | collective-permute-start | bytes 393224 | tf_op jit(solution)/shard_map/ppermute | solution.py:44
  10.2 65.2 %collective-permute-start.31 = (bf16[64,2048]{1,0:T(8,128)(2,1)S(1)}, bf16[64,2048]{1,0:T(8,128)(2,1)S(1)}, u32[]{:S(2)}, u32[]{:S(2)}) collective-permute-start(bf16[64,2048]{1,0:T(8,128)(2,1)S(1)} %constant_dynamic-slice_fusion.13), channel_id=1, source_target_pairs={{0,8},{1,9},{2,10},{3,11},{4,12},{5,13},{6,14},{7,15},{8,16},{9,17... | collective-permute-start | bytes 786440 | tf_op jit(solution)/shard_map/ppermute | solution.py:44
  23.4 20.1 %collective-permute-start.8 = (bf16[64,3072]{1,0:T(8,128)(2,1)S(1)}, bf16[64,3072]{1,0:T(8,128)(2,1)S(1)}, u32[]{:S(2)}, u32[]{:S(2)}) collective-permute-start(bf16[64,3072]{1,0:T(8,128)(2,1)S(1)} %constant_dynamic-slice_fusion.23), channel_id=1, source_target_pairs={{0,8},{1,9},{2,10},{3,11},{4,12},{5,13},{6,14},{7,15},{8,16},{9,17... | collective-permute-start | bytes 1179656 | tf_op jit(solution)/shard_map/ppermute | solution.py:44
  25.5 15.2 %collective-permute-start.6 = (f32[2,104,128]{2,1,0:T(8,128)S(1)}, f32[2,104,128]{2,1,0:T(8,128)S(1)}, u32[]{:S(2)}, u32[]{:S(2)}) collective-permute-start(f32[2,104,128]{2,1,0:T(8,128)S(1)} %get-tuple-element.73), channel_id=1, source_target_pairs={{0,16},{1,17},{2,18},{3,19},{4,20},{5,21},{6,22},{7,23},{8,24},{9,... | collective-permute-start | bytes 319496 | tf_op jit(solution)/shard_map/ppermute | solution.py:44
  26.7 13.9 %collective-permute-start.5 = (f32[2,104,128]{2,1,0:T(8,128)S(1)}, f32[2,104,128]{2,1,0:T(8,128)S(1)}, u32[]{:S(2)}, u32[]{:S(2)}) collective-permute-start(f32[2,104,128]{2,1,0:T(8,128)S(1)} %get-tuple-element.73), channel_id=1, source_target_pairs={{0,8},{1,9},{2,10},{3,11},{4,12},{5,13},{6,14},{7,15},{8,16},{9,17... | collective-permute-start | bytes 319496 | tf_op jit(solution)/shard_map/ppermute | solution.py:44
  40.6 34.9 %collective-permute-start.41 = (bf16[128,1024]{1,0:T(8,128)(2,1)S(1)}, bf16[128,1024]{1,0:T(8,128)(2,1)S(1)}, u32[]{:S(2)}, u32[]{:S(2)}) collective-permute-start(bf16[128,1024]{1,0:T(8,128)(2,1)S(1)} %constant_dynamic-slice_fusion.8), channel_id=1, source_target_pairs={{0,8},{1,9},{2,10},{3,11},{4,12},{5,13},{6,14},{7,15},{8,16},{9,17... | collective-permute-start | bytes 786440 | tf_op jit(solution)/shard_map/ppermute | solution.py:44
  40.6 35.2 %collective-permute-start.26 = (bf16[64,1024]{1,0:T(8,128)(2,1)S(1)}, bf16[64,1024]{1,0:T(8,128)(2,1)S(1)}, u32[]{:S(2)}, u32[]{:S(2)}) collective-permute-start(bf16[64,1024]{1,0:T(8,128)(2,1)S(1)} %collective-permute-done.21.refs_2_), channel_id=1, source_target_pairs={{0,1},{1,0},{2,3},{3,2},{4,5},{5,4},{6,7},{7,6},{8,9},{9,8},{10,11... | collective-permute-start | bytes 393224 | tf_op jit(solution)/shard_map/ppermute | solution.py:44
  40.7 13.8 %collective-permute-start.22 = (bf16[64,1024]{1,0:T(8,128)(2,1)S(1)}, bf16[64,1024]{1,0:T(8,128)(2,1)S(1)}, u32[]{:S(2)}, u32[]{:S(2)}) collective-permute-start(bf16[64,1024]{1,0:T(8,128)(2,1)S(1)} %collective-permute-done.21.refs_2_), channel_id=1, source_target_pairs={{0,8},{1,9},{2,10},{3,11},{4,12},{5,13},{6,14},{7,15},{8,16},{9,17... | collective-permute-start | bytes 393224 | tf_op jit(solution)/shard_map/ppermute | solution.py:44
  43.5 19.3 %collective-permute-start.9 = (bf16[64,3072]{1,0:T(8,128)(2,1)S(1)}, bf16[64,3072]{1,0:T(8,128)(2,1)S(1)}, u32[]{:S(2)}, u32[]{:S(2)}) collective-permute-start(bf16[64,3072]{1,0:T(8,128)(2,1)S(1)} %collective-permute-done.8.refs_2_), channel_id=1, source_target_pairs={{0,8},{1,9},{2,10},{3,11},{4,12},{5,13},{6,14},{7,15},{8,16},{9,17... | collective-permute-start | bytes 1179656 | tf_op jit(solution)/shard_map/ppermute | solution.py:44
  54.4 21.3 %collective-permute-start.23 = (bf16[64,1024]{1,0:T(8,128)(2,1)S(1)}, bf16[64,1024]{1,0:T(8,128)(2,1)S(1)}, u32[]{:S(2)}, u32[]{:S(2)}) collective-permute-start(bf16[64,1024]{1,0:T(8,128)(2,1)S(1)} %collective-permute-done.22.refs_3_), channel_id=1, source_target_pairs={{0,8},{1,9},{2,10},{3,11},{4,12},{5,13},{6,14},{7,15},{8,16},{9,17... | collective-permute-start | bytes 393224 | tf_op jit(solution)/shard_map/ppermute | solution.py:44
  73.9 18.4 %collective-permute-start.11 = (bf16[128,3072]{1,0:T(8,128)(2,1)S(1)}, bf16[128,3072]{1,0:T(8,128)(2,1)S(1)}, u32[]{:S(2)}, u32[]{:S(2)}) collective-permute-start(bf16[128,3072]{1,0:T(8,128)(2,1)S(1)} %pad_maximum_fusion), channel_id=1, source_target_pairs={{0,4},{1,5},{2,6},{3,7},{4,0},{5,1},{6,2},{7,3},{8,12},{9,13},{10,... | collective-permute-start | bytes 2359304 | tf_op jit(solution)/shard_map/ppermute | solution.py:44
  75.5 18.3 %collective-permute-start.27 = (bf16[64,1024]{1,0:T(8,128)(2,1)S(1)}, bf16[64,1024]{1,0:T(8,128)(2,1)}, u32[]{:S(2)}, u32[]{:S(2)}) collective-permute-start(bf16[64,1024]{1,0:T(8,128)(2,1)S(1)} %collective-permute-done.22.refs_3_), channel_id=1, source_target_pairs={{0,1},{1,0},{2,3},{3,2},{4,5},{5,4},{6,7},{7,6},{8,9},{9,8},{10,11... | collective-permute-start | bytes 393224 | tf_op jit(solution)/shard_map/ppermute | solution.py:44
  75.6 11.0 %collective-permute-start.32 = (bf16[64,2048]{1,0:T(8,128)(2,1)S(1)}, bf16[64,2048]{1,0:T(8,128)(2,1)S(1)}, u32[]{:S(2)}, u32[]{:S(2)}) collective-permute-start(bf16[64,2048]{1,0:T(8,128)(2,1)S(1)} %collective-permute-done.31.refs_2_), channel_id=1, source_target_pairs={{0,8},{1,9},{2,10},{3,11},{4,12},{5,13},{6,14},{7,15},{8,16},{9,17... | collective-permute-start | bytes 786440 | tf_op jit(solution)/shard_map/ppermute | solution.py:44
  75.7 16.5 %collective-permute-start.42 = (bf16[128,1024]{1,0:T(8,128)(2,1)S(1)}, bf16[128,1024]{1,0:T(8,128)(2,1)S(1)}, u32[]{:S(2)}, u32[]{:S(2)}) collective-permute-start(bf16[128,1024]{1,0:T(8,128)(2,1)S(1)} %collective-permute-done.41.refs_2_), channel_id=1, source_target_pairs={{0,8},{1,9},{2,10},{3,11},{4,12},{5,13},{6,14},{7,15},{8,16},{9,17... | collective-permute-start | bytes 786440 | tf_op jit(solution)/shard_map/ppermute | solution.py:44
  75.9 18.0 %collective-permute-start.28 = (bf16[64,1024]{1,0:T(8,128)(2,1)S(1)}, bf16[64,1024]{1,0:T(8,128)(2,1)S(1)}, u32[]{:S(2)}, u32[]{:S(2)}) collective-permute-start(bf16[64,1024]{1,0:T(8,128)(2,1)S(1)} %collective-permute-done.23.refs_4_), channel_id=1, source_target_pairs={{0,1},{1,0},{2,3},{3,2},{4,5},{5,4},{6,7},{7,6},{8,9},{9,8},{10,11... | collective-permute-start | bytes 393224 | tf_op jit(solution)/shard_map/ppermute | solution.py:44
  86.6 11.2 %collective-permute-start.33 = (bf16[64,2048]{1,0:T(8,128)(2,1)S(1)}, bf16[64,2048]{1,0:T(8,128)(2,1)S(1)}, u32[]{:S(2)}, u32[]{:S(2)}) collective-permute-start(bf16[64,2048]{1,0:T(8,128)(2,1)S(1)} %collective-permute-done.32.refs_3_), channel_id=1, source_target_pairs={{0,8},{1,9},{2,10},{3,11},{4,12},{5,13},{6,14},{7,15},{8,16},{9,17... | collective-permute-start | bytes 786440 | tf_op jit(solution)/shard_map/ppermute | solution.py:44
  92.3 18.5 %collective-permute-start.12 = (bf16[128,3072]{1,0:T(8,128)(2,1)S(1)}, bf16[128,3072]{1,0:T(8,128)(2,1)S(1)}, u32[]{:S(2)}, u32[]{:S(2)}) collective-permute-start(bf16[128,3072]{1,0:T(8,128)(2,1)S(1)} %collective-permute-done.11.refs_5_), channel_id=1, source_target_pairs={{0,2},{1,3},{2,0},{3,1},{4,6},{5,7},{6,4},{7,5},{8,10},{9,11},{10,... | collective-permute-start | bytes 2359304 | tf_op jit(solution)/shard_map/ppermute | solution.py:44
  105.7 14.9 %collective-permute-start.44 = (bf16[256,1024]{1,0:T(8,128)(2,1)S(1)}, bf16[256,1024]{1,0:T(8,128)(2,1)}, u32[]{:S(2)}, u32[]{:S(2)}) collective-permute-start(bf16[256,1024]{1,0:T(8,128)(2,1)S(1)} %pad_maximum_fusion.2), channel_id=1, source_target_pairs={{0,4},{1,5},{2,6},{3,7},{4,0},{5,1},{6,2},{7,3},{8,12},{9,13},{10,... | collective-permute-start | bytes 1572872 | tf_op jit(solution)/shard_map/ppermute | solution.py:44
  106.2 25.0 %collective-permute-start.34 = (bf16[128,2048]{1,0:T(8,128)(2,1)S(1)}, bf16[128,2048]{1,0:T(8,128)(2,1)}, u32[]{:S(2)}, u32[]{:S(2)}) collective-permute-start(bf16[128,2048]{1,0:T(8,128)(2,1)S(1)} %pad_maximum_fusion.1), channel_id=1, source_target_pairs={{0,4},{1,5},{2,6},{3,7},{4,0},{5,1},{6,2},{7,3},{8,12},{9,13},{10,... | collective-permute-start | bytes 1572872 | tf_op jit(solution)/shard_map/ppermute | solution.py:44
  107.9 25.5 %collective-permute-start.16 = (bf16[128,3072]{1,0:T(8,128)(2,1)S(1)}, bf16[128,3072]{1,0:T(8,128)(2,1)S(1)}, u32[]{:S(2)}, u32[]{:S(2)}) collective-permute-start(bf16[128,3072]{1,0:T(8,128)(2,1)S(1)} %collective-permute-done.11.refs_5_), channel_id=1, source_target_pairs={{0,1},{1,0},{2,3},{3,2},{4,5},{5,4},{6,7},{7,6},{8,9},{9,8},{10,11... | collective-permute-start | bytes 2359304 | tf_op jit(solution)/shard_map/ppermute | solution.py:44
  110.8 22.6 %collective-permute-start.17 = (bf16[128,3072]{1,0:T(8,128)(2,1)S(1)}, bf16[128,3072]{1,0:T(8,128)(2,1)S(1)}, u32[]{:S(2)}, u32[]{:S(2)}) collective-permute-start(bf16[128,3072]{1,0:T(8,128)(2,1)S(1)} %collective-permute-done.12.refs_6_), channel_id=1, source_target_pairs={{0,1},{1,0},{2,3},{3,2},{4,5},{5,4},{6,7},{7,6},{8,9},{9,8},{10,11... | collective-permute-start | bytes 2359304 | tf_op jit(solution)/shard_map/ppermute | solution.py:44
  111.7 20.9 %collective-permute-start.15 = (bf16[64,3072]{1,0:T(8,128)(2,1)S(1)}, bf16[64,3072]{1,0:T(8,128)(2,1)S(1)}, u32[]{:S(2)}, u32[]{:S(2)}) collective-permute-start(bf16[64,3072]{1,0:T(8,128)(2,1)S(1)} %collective-permute-done.10.refs_4_), channel_id=1, source_target_pairs={{0,1},{1,0},{2,3},{3,2},{4,5},{5,4},{6,7},{7,6},{8,9},{9,8},{10,11... | collective-permute-start | bytes 1179656 | tf_op jit(solution)/shard_map/ppermute | solution.py:44
  120.6 30.5 %collective-permute-start.45 = (bf16[256,1024]{1,0:T(8,128)(2,1)}, bf16[256,1024]{1,0:T(8,128)(2,1)}, u32[]{:S(2)}, u32[]{:S(2)}) collective-permute-start(bf16[256,1024]{1,0:T(8,128)(2,1)} %collective-permute-done.44.refs_5_), channel_id=1, source_target_pairs={{0,2},{1,3},{2,0},{3,1},{4,6},{5,7},{6,4},{7,5},{8,10},{9,11},{10,... | collective-permute-start | bytes 1572872 | tf_op jit(solution)/shard_map/ppermute | solution.py:44
  131.3 20.3 %collective-permute-start.35 = (bf16[128,2048]{1,0:T(8,128)(2,1)}, bf16[128,2048]{1,0:T(8,128)(2,1)}, u32[]{:S(2)}, u32[]{:S(2)}) collective-permute-start(bf16[128,2048]{1,0:T(8,128)(2,1)} %collective-permute-done.34.refs_5_), channel_id=1, source_target_pairs={{0,2},{1,3},{2,0},{3,1},{4,6},{5,7},{6,4},{7,5},{8,10},{9,11},{10,... | collective-permute-start | bytes 1572872 | tf_op jit(solution)/shard_map/ppermute | solution.py:44
  132.7 17.9 %collective-permute-start.25 = (bf16[128,1024]{1,0:T(8,128)(2,1)}, bf16[128,1024]{1,0:T(8,128)(2,1)}, u32[]{:S(2)}, u32[]{:S(2)}) collective-permute-start(bf16[128,1024]{1,0:T(8,128)(2,1)} %collective-permute-done.24.refs_5_), channel_id=1, source_target_pairs={{0,2},{1,3},{2,0},{3,1},{4,6},{5,7},{6,4},{7,5},{8,10},{9,11},{10,... | collective-permute-start | bytes 786440 | tf_op jit(solution)/shard_map/ppermute | solution.py:44
  133.4 17.2 %collective-permute-start.38 = (bf16[64,2048]{1,0:T(8,128)(2,1)S(1)}, bf16[64,2048]{1,0:T(8,128)(2,1)}, u32[]{:S(2)}, u32[]{:S(2)}) collective-permute-start(bf16[64,2048]{1,0:T(8,128)(2,1)S(1)} %collective-permute-done.33.refs_4_), channel_id=1, source_target_pairs={{0,1},{1,0},{2,3},{3,2},{4,5},{5,4},{6,7},{7,6},{8,9},{9,8},{10,11... | collective-permute-start | bytes 786440 | tf_op jit(solution)/shard_map/ppermute | solution.py:44
  133.5 17.6 %collective-permute-start.48 = (bf16[128,1024]{1,0:T(8,128)(2,1)}, bf16[128,1024]{1,0:T(8,128)(2,1)}, u32[]{:S(2)}, u32[]{:S(2)}) collective-permute-start(bf16[128,1024]{1,0:T(8,128)(2,1)} %collective-permute-done.43.refs_4_), channel_id=1, source_target_pairs={{0,1},{1,0},{2,3},{3,2},{4,5},{5,4},{6,7},{7,6},{8,9},{9,8},{10,11... | collective-permute-start | bytes 786440 | tf_op jit(solution)/shard_map/ppermute | solution.py:44
  150.5 12.7 %collective-permute-start.30 = (bf16[128,1024]{1,0:T(8,128)(2,1)}, bf16[128,1024]{1,0:T(8,128)(2,1)}, u32[]{:S(2)}, u32[]{:S(2)}) collective-permute-start(bf16[128,1024]{1,0:T(8,128)(2,1)} %collective-permute-done.25.refs_6_), channel_id=1, source_target_pairs={{0,1},{1,0},{2,3},{3,2},{4,5},{5,4},{6,7},{7,6},{8,9},{9,8},{10,11... | collective-permute-start | bytes 786440 | tf_op jit(solution)/shard_map/ppermute | solution.py:44
  150.5 12.7 %collective-permute-start.49 = (bf16[256,1024]{1,0:T(8,128)(2,1)}, bf16[256,1024]{1,0:T(8,128)(2,1)}, u32[]{:S(2)}, u32[]{:S(2)}) collective-permute-start(bf16[256,1024]{1,0:T(8,128)(2,1)} %collective-permute-done.44.refs_5_), channel_id=1, source_target_pairs={{0,1},{1,0},{2,3},{3,2},{4,5},{5,4},{6,7},{7,6},{8,9},{9,8},{10,11... | collective-permute-start | bytes 1572872 | tf_op jit(solution)/shard_map/ppermute | solution.py:44
  151.1 25.1 %collective-permute-start.39 = (bf16[128,2048]{1,0:T(8,128)(2,1)}, bf16[128,2048]{1,0:T(8,128)(2,1)}, u32[]{:S(2)}, u32[]{:S(2)}) collective-permute-start(bf16[128,2048]{1,0:T(8,128)(2,1)} %collective-permute-done.34.refs_5_), channel_id=1, source_target_pairs={{0,1},{1,0},{2,3},{3,2},{4,5},{5,4},{6,7},{7,6},{8,9},{9,8},{10,11... | collective-permute-start | bytes 1572872 | tf_op jit(solution)/shard_map/ppermute | solution.py:44
  151.1 12.2 %collective-permute-start.50 = (bf16[256,1024]{1,0:T(8,128)(2,1)}, bf16[256,1024]{1,0:T(8,128)(2,1)}, u32[]{:S(2)}, u32[]{:S(2)}) collective-permute-start(bf16[256,1024]{1,0:T(8,128)(2,1)} %collective-permute-done.45.refs_6_), channel_id=1, source_target_pairs={{0,1},{1,0},{2,3},{3,2},{4,5},{5,4},{6,7},{7,6},{8,9},{9,8},{10,11... | collective-permute-start | bytes 1572872 | tf_op jit(solution)/shard_map/ppermute | solution.py:44
  151.6 24.6 %collective-permute-start.40 = (bf16[128,2048]{1,0:T(8,128)(2,1)}, bf16[128,2048]{1,0:T(8,128)(2,1)}, u32[]{:S(2)}, u32[]{:S(2)}) collective-permute-start(bf16[128,2048]{1,0:T(8,128)(2,1)} %collective-permute-done.35.refs_6_), channel_id=1, source_target_pairs={{0,1},{1,0},{2,3},{3,2},{4,5},{5,4},{6,7},{7,6},{8,9},{9,8},{10,11... | collective-permute-start | bytes 1572872 | tf_op jit(solution)/shard_map/ppermute | solution.py:44
  163.3 30.4 %collective-permute-start.20 = (bf16[60,2048]{1,0:T(8,128)(2,1)}, bf16[60,2048]{1,0:T(8,128)(2,1)S(1)}, u32[]{:S(2)}, u32[]{:S(2)}) collective-permute-start(bf16[60,2048]{1,0:T(8,128)(2,1)} %slice.121), channel_id=1, source_target_pairs={{0,12},{4,16},{8,20},{12,24},{16,28},{20,0},{24,4},{28,8},{1,13},{... | collective-permute-start | bytes 737288 | tf_op jit(solution)/shard_map/ppermute | solution.py:48
  163.3 30.3 %collective-permute-start.19 = (bf16[60,2048]{1,0:T(8,128)(2,1)}, bf16[60,2048]{1,0:T(8,128)(2,1)}, u32[]{:S(2)}, u32[]{:S(2)}) collective-permute-start(bf16[60,2048]{1,0:T(8,128)(2,1)} %slice.121), channel_id=1, source_target_pairs={{0,8},{4,12},{8,16},{12,20},{16,24},{20,28},{24,0},{28,4},{1,9},{5... | collective-permute-start | bytes 737288 | tf_op jit(solution)/shard_map/ppermute | solution.py:48
  163.4 30.3 %collective-permute-start.18 = (bf16[60,2048]{1,0:T(8,128)(2,1)}, bf16[60,2048]{1,0:T(8,128)(2,1)}, u32[]{:S(2)}, u32[]{:S(2)}) collective-permute-start(bf16[60,2048]{1,0:T(8,128)(2,1)} %slice.121), channel_id=1, source_target_pairs={{0,4},{4,8},{8,12},{12,16},{16,20},{20,24},{24,28},{28,0},{1,5},{5... | collective-permute-start | bytes 737288 | tf_op jit(solution)/shard_map/ppermute | solution.py:48
  276.0 30.8 %collective-permute-start.51 = (bf16[2,60,1024]{2,1,0:T(8,128)(2,1)}, bf16[2,60,1024]{2,1,0:T(8,128)(2,1)S(1)}, u32[]{:S(2)}, u32[]{:S(2)}) collective-permute-start(bf16[2,60,1024]{2,1,0:T(8,128)(2,1)} %get-tuple-element.17), channel_id=1, source_target_pairs={{0,28},{4,0},{8,4},{12,8},{16,12},{20,16},{24,20},{28,24},{1,29},{... | collective-permute-start | bytes 737288 | tf_op jit(solution)/shard_map/ppermute | solution.py:48
  277.6 29.2 %collective-permute-start.52 = (bf16[2,60,1024]{2,1,0:T(8,128)(2,1)}, bf16[2,60,1024]{2,1,0:T(8,128)(2,1)}, u32[]{:S(2)}, u32[]{:S(2)}) collective-permute-start(bf16[2,60,1024]{2,1,0:T(8,128)(2,1)} %get-tuple-element.18), channel_id=1, source_target_pairs={{0,24},{4,28},{8,0},{12,4},{16,8},{20,12},{24,16},{28,20},{1,25},{... | collective-permute-start | bytes 737288 | tf_op jit(solution)/shard_map/ppermute | solution.py:48
  279.6 27.3 %collective-permute-start.53 = (bf16[2,60,1024]{2,1,0:T(8,128)(2,1)}, bf16[2,60,1024]{2,1,0:T(8,128)(2,1)}, u32[]{:S(2)}, u32[]{:S(2)}) collective-permute-start(bf16[2,60,1024]{2,1,0:T(8,128)(2,1)} %get-tuple-element.19), channel_id=1, source_target_pairs={{0,20},{4,24},{8,28},{12,0},{16,4},{20,8},{24,12},{28,16},{1,21},{... | collective-permute-start | bytes 737288 | tf_op jit(solution)/shard_map/ppermute | solution.py:48
  283.3 76.7 %collective-permute-start.72 = (bf16[8,64,1024]{2,1,0:T(8,128)(2,1)}, bf16[8,64,1024]{2,1,0:T(8,128)(2,1)}, u32[]{:S(2)}, u32[]{:S(2)}) collective-permute-start(bf16[8,64,1024]{2,1,0:T(8,128)(2,1)} %dynamic-slice_bitcast_fusion.6), channel_id=1, source_target_pairs={{0,1},{1,0},{2,3},{3,2},{4,5},{5,4},{6,7},{7,6},{8,9},{9,8},{10,11... | collective-permute-start | bytes 3145736 | tf_op jit(solution)/shard_map/ppermute | solution.py:44
  287.8 116.9 %collective-permute-start.79 = (bf16[8,64,2048]{2,1,0:T(8,128)(2,1)}, bf16[8,64,2048]{2,1,0:T(8,128)(2,1)}, u32[]{:S(2)}, u32[]{:S(2)}) collective-permute-start(bf16[8,64,2048]{2,1,0:T(8,128)(2,1)} %dynamic-slice_bitcast_fusion.2), channel_id=1, source_target_pairs={{0,1},{1,0},{2,3},{3,2},{4,5},{5,4},{6,7},{7,6},{8,9},{9,8},{10,11... | collective-permute-start | bytes 6291464 | tf_op jit(solution)/shard_map/ppermute | solution.py:44
  340.5 12.8 %collective-permute-start.59 = (bf16[8,104,128]{2,1,0:T(8,128)(2,1)S(1)}, bf16[8,104,128]{2,1,0:T(8,128)(2,1)S(1)}, u32[]{:S(2)}, u32[]{:S(2)}) collective-permute-start(bf16[8,104,128]{2,1,0:T(8,128)(2,1)S(1)} %pad_maximum_fusion.6), channel_id=1, source_target_pairs={{0,2},{1,3},{2,0},{3,1},{4,6},{5,7},{6,4},{7,5},{8,10},{9,11},{10,... | collective-permute-start | bytes 638984 | tf_op jit(solution)/shard_map/ppermute | solution.py:44
  353.3 55.4 %collective-permute-start.86 = (bf16[8,128,1024]{2,1,0:T(8,128)(2,1)}, bf16[8,128,1024]{2,1,0:T(8,128)(2,1)}, u32[]{:S(2)}, u32[]{:S(2)}) collective-permute-start(bf16[8,128,1024]{2,1,0:T(8,128)(2,1)} %dynamic-slice_bitcast_fusion.1), channel_id=1, source_target_pairs={{0,1},{1,0},{2,3},{3,2},{4,5},{5,4},{6,7},{7,6},{8,9},{9,8},{10,11... | collective-permute-start | bytes 6291464 | tf_op jit(solution)/shard_map/ppermute | solution.py:44
  354.0 58.8 %collective-permute-start.65 = (bf16[8,64,3072]{2,1,0:T(8,128)(2,1)S(1)}, bf16[8,64,3072]{2,1,0:T(8,128)(2,1)}, u32[]{:S(2)}, u32[]{:S(2)}) collective-permute-start(bf16[8,64,3072]{2,1,0:T(8,128)(2,1)S(1)} %dynamic-slice_bitcast_fusion), channel_id=1, source_target_pairs={{0,1},{1,0},{2,3},{3,2},{4,5},{5,4},{6,7},{7,6},{8,9},{9,8},{10,11... | collective-permute-start | bytes 9437192 | tf_op jit(solution)/shard_map/ppermute | solution.py:44
  361.8 16.3 %collective-permute-start.73 = (bf16[4,64,1024]{2,1,0:T(8,128)(2,1)S(1)}, bf16[4,64,1024]{2,1,0:T(8,128)(2,1)S(1)}, u32[]{:S(2)}, u32[]{:S(2)}) collective-permute-start(bf16[4,64,1024]{2,1,0:T(8,128)(2,1)S(1)} %dynamic-slice_bitcast_fusion.7), channel_id=1, source_target_pairs={{0,4},{1,5},{2,6},{3,7},{4,0},{5,1},{6,2},{7,3},{8,12},{9,13},{10,... | collective-permute-start | bytes 1572872 | tf_op jit(solution)/shard_map/ppermute | solution.py:44
  361.9 15.4 %collective-permute-start.61 = (bf16[4,104,128]{2,1,0:T(8,128)(2,1)S(1)}, bf16[4,104,128]{2,1,0:T(8,128)(2,1)S(1)}, u32[]{:S(2)}, u32[]{:S(2)}) collective-permute-start(bf16[4,104,128]{2,1,0:T(8,128)(2,1)S(1)} %dynamic-slice_bitcast_fusion.20), channel_id=1, source_target_pairs={{0,4},{1,5},{2,6},{3,7},{4,0},{5,1},{6,2},{7,3},{8,12},{9,13},{10,... | collective-permute-start | bytes 319496 | tf_op jit(solution)/shard_map/ppermute | solution.py:44
  408.1 26.1 %collective-permute-start.80 = (bf16[4,64,2048]{2,1,0:T(8,128)(2,1)S(1)}, bf16[4,64,2048]{2,1,0:T(8,128)(2,1)S(1)}, u32[]{:S(2)}, u32[]{:S(2)}) collective-permute-start(bf16[4,64,2048]{2,1,0:T(8,128)(2,1)S(1)} %dynamic-slice_bitcast_fusion.5), channel_id=1, source_target_pairs={{0,4},{1,5},{2,6},{3,7},{4,0},{5,1},{6,2},{7,3},{8,12},{9,13},{10,... | collective-permute-start | bytes 3145736 | tf_op jit(solution)/shard_map/ppermute | solution.py:44
  411.7 44.9 %collective-permute-start.87 = (bf16[4,128,1024]{2,1,0:T(8,128)(2,1)S(1)}, bf16[4,128,1024]{2,1,0:T(8,128)(2,1)S(1)}, u32[]{:S(2)}, u32[]{:S(2)}) collective-permute-start(bf16[4,128,1024]{2,1,0:T(8,128)(2,1)S(1)} %dynamic-slice_bitcast_fusion.4), channel_id=1, source_target_pairs={{0,4},{1,5},{2,6},{3,7},{4,0},{5,1},{6,2},{7,3},{8,12},{9,13},{10,... | collective-permute-start | bytes 3145736 | tf_op jit(solution)/shard_map/ppermute | solution.py:44
  416.1 73.4 %collective-permute-start.66 = (bf16[4,64,3072]{2,1,0:T(8,128)(2,1)S(1)}, bf16[4,64,3072]{2,1,0:T(8,128)(2,1)S(1)}, u32[]{:S(2)}, u32[]{:S(2)}) collective-permute-start(bf16[4,64,3072]{2,1,0:T(8,128)(2,1)S(1)} %dynamic-slice_bitcast_fusion.3), channel_id=1, source_target_pairs={{0,4},{1,5},{2,6},{3,7},{4,0},{5,1},{6,2},{7,3},{8,12},{9,13},{10,... | collective-permute-start | bytes 4718600 | tf_op jit(solution)/shard_map/ppermute | solution.py:44
  434.6 25.9 %collective-permute-start.81 = (bf16[64,2048]{1,0:T(8,128)(2,1)S(1)}, bf16[64,2048]{1,0:T(8,128)(2,1)S(1)}, u32[]{:S(2)}, u32[]{:S(2)}) collective-permute-start(bf16[64,2048]{1,0:T(8,128)(2,1)S(1)} %get-tuple-element.47), channel_id=1, source_target_pairs={{0,8},{1,9},{2,10},{3,11},{4,12},{5,13},{6,14},{7,15},{8,16},{9,17... | collective-permute-start | bytes 786440 | tf_op jit(solution)/shard_map/ppermute | solution.py:44
  438.1 23.1 %collective-permute-start.83 = (bf16[64,2048]{1,0:T(8,128)(2,1)S(1)}, bf16[64,2048]{1,0:T(8,128)(2,1)S(1)}, u32[]{:S(2)}, u32[]{:S(2)}) collective-permute-start(bf16[64,2048]{1,0:T(8,128)(2,1)S(1)} %get-tuple-element.48), channel_id=1, source_target_pairs={{0,24},{1,25},{2,26},{3,27},{4,28},{5,29},{6,30},{7,31},{8,0},{9,1... | collective-permute-start | bytes 786440 | tf_op jit(solution)/shard_map/ppermute | solution.py:44
  438.5 23.8 %collective-permute-start.82 = (bf16[64,2048]{1,0:T(8,128)(2,1)S(1)}, bf16[64,2048]{1,0:T(8,128)(2,1)S(1)}, u32[]{:S(2)}, u32[]{:S(2)}) collective-permute-start(bf16[64,2048]{1,0:T(8,128)(2,1)S(1)} %get-tuple-element.49), channel_id=1, source_target_pairs={{0,16},{1,17},{2,18},{3,19},{4,20},{5,21},{6,22},{7,23},{8,24},{9,... | collective-permute-start | bytes 786440 | tf_op jit(solution)/shard_map/ppermute | solution.py:44
  457.1 11.1 %collective-permute-start.88 = (bf16[128,1024]{1,0:T(8,128)(2,1)S(1)}, bf16[128,1024]{1,0:T(8,128)(2,1)S(1)}, u32[]{:S(2)}, u32[]{:S(2)}) collective-permute-start(bf16[128,1024]{1,0:T(8,128)(2,1)S(1)} %get-tuple-element.44), channel_id=1, source_target_pairs={{0,8},{1,9},{2,10},{3,11},{4,12},{5,13},{6,14},{7,15},{8,16},{9,17... | collective-permute-start | bytes 786440 | tf_op jit(solution)/shard_map/ppermute | solution.py:44
  460.6 12.4 %collective-permute-start.90 = (bf16[128,1024]{1,0:T(8,128)(2,1)S(1)}, bf16[128,1024]{1,0:T(8,128)(2,1)S(1)}, u32[]{:S(2)}, u32[]{:S(2)}) collective-permute-start(bf16[128,1024]{1,0:T(8,128)(2,1)S(1)} %get-tuple-element.45), channel_id=1, source_target_pairs={{0,24},{1,25},{2,26},{3,27},{4,28},{5,29},{6,30},{7,31},{8,0},{9,1... | collective-permute-start | bytes 786440 | tf_op jit(solution)/shard_map/ppermute | solution.py:44
  461.2 21.3 %collective-permute-start.89 = (bf16[128,1024]{1,0:T(8,128)(2,1)S(1)}, bf16[128,1024]{1,0:T(8,128)(2,1)S(1)}, u32[]{:S(2)}, u32[]{:S(2)}) collective-permute-start(bf16[128,1024]{1,0:T(8,128)(2,1)S(1)} %get-tuple-element.46), channel_id=1, source_target_pairs={{0,16},{1,17},{2,18},{3,19},{4,20},{5,21},{6,22},{7,23},{8,24},{9,... | collective-permute-start | bytes 786440 | tf_op jit(solution)/shard_map/ppermute | solution.py:44
  462.4 32.7 %collective-permute-start.84 = (bf16[64,2048]{1,0:T(8,128)(2,1)S(1)}, bf16[64,2048]{1,0:T(8,128)(2,1)S(1)}, u32[]{:S(2)}, u32[]{:S(2)}) collective-permute-start(bf16[64,2048]{1,0:T(8,128)(2,1)S(1)} %fusion.38), channel_id=1, source_target_pairs={{0,2},{1,3},{2,0},{3,1},{4,6},{5,7},{6,4},{7,5},{8,10},{9,11},{10,... | collective-permute-start | bytes 786440 | tf_op jit(solution)/shard_map/ppermute | solution.py:44
  482.7 12.6 %collective-permute-start.91 = (bf16[128,1024]{1,0:T(8,128)(2,1)S(1)}, bf16[128,1024]{1,0:T(8,128)(2,1)S(1)}, u32[]{:S(2)}, u32[]{:S(2)}) collective-permute-start(bf16[128,1024]{1,0:T(8,128)(2,1)S(1)} %fusion.35), channel_id=1, source_target_pairs={{0,2},{1,3},{2,0},{3,1},{4,6},{5,7},{6,4},{7,5},{8,10},{9,11},{10,... | collective-permute-start | bytes 786440 | tf_op jit(solution)/shard_map/ppermute | solution.py:44
  490.2 13.9 %collective-permute-start.67 = (bf16[64,3072]{1,0:T(8,128)(2,1)S(1)}, bf16[64,3072]{1,0:T(8,128)(2,1)S(1)}, u32[]{:S(2)}, u32[]{:S(2)}) collective-permute-start(bf16[64,3072]{1,0:T(8,128)(2,1)S(1)} %get-tuple-element.41), channel_id=1, source_target_pairs={{0,8},{1,9},{2,10},{3,11},{4,12},{5,13},{6,14},{7,15},{8,16},{9,17... | collective-permute-start | bytes 1179656 | tf_op jit(solution)/shard_map/ppermute | solution.py:44
  493.6 18.0 %collective-permute-start.69 = (bf16[64,3072]{1,0:T(8,128)(2,1)S(1)}, bf16[64,3072]{1,0:T(8,128)(2,1)S(1)}, u32[]{:S(2)}, u32[]{:S(2)}) collective-permute-start(bf16[64,3072]{1,0:T(8,128)(2,1)S(1)} %get-tuple-element.42), channel_id=1, source_target_pairs={{0,24},{1,25},{2,26},{3,27},{4,28},{5,29},{6,30},{7,31},{8,0},{9,1... | collective-permute-start | bytes 1179656 | tf_op jit(solution)/shard_map/ppermute | solution.py:44
  494.1 33.6 %collective-permute-start.68 = (bf16[64,3072]{1,0:T(8,128)(2,1)S(1)}, bf16[64,3072]{1,0:T(8,128)(2,1)S(1)}, u32[]{:S(2)}, u32[]{:S(2)}) collective-permute-start(bf16[64,3072]{1,0:T(8,128)(2,1)S(1)} %get-tuple-element.43), channel_id=1, source_target_pairs={{0,16},{1,17},{2,18},{3,19},{4,20},{5,21},{6,22},{7,23},{8,24},{9,... | collective-permute-start | bytes 1179656 | tf_op jit(solution)/shard_map/ppermute | solution.py:44
  495.2 35.3 %collective-permute-start.85 = (bf16[64,2048]{1,0:T(8,128)(2,1)S(1)}, bf16[64,2048]{1,0:T(8,128)(2,1)S(1)}, u32[]{:S(2)}, u32[]{:S(2)}) collective-permute-start(bf16[64,2048]{1,0:T(8,128)(2,1)S(1)} %add_convert_fusion.6), channel_id=1, source_target_pairs={{0,1},{1,0},{2,3},{3,2},{4,5},{5,4},{6,7},{7,6},{8,9},{9,8},{10,11... | collective-permute-start | bytes 786440 | tf_op jit(solution)/shard_map/ppermute | solution.py:44
  495.4 44.6 %collective-permute-start.92 = (bf16[128,1024]{1,0:T(8,128)(2,1)S(1)}, bf16[128,1024]{1,0:T(8,128)(2,1)S(1)}, u32[]{:S(2)}, u32[]{:S(2)}) collective-permute-start(bf16[128,1024]{1,0:T(8,128)(2,1)S(1)} %add_convert_fusion.5), channel_id=1, source_target_pairs={{0,1},{1,0},{2,3},{3,2},{4,5},{5,4},{6,7},{7,6},{8,9},{9,8},{10,11... | collective-permute-start | bytes 786440 | tf_op jit(solution)/shard_map/ppermute | solution.py:44
  527.9 11.9 %collective-permute-start.70 = (bf16[64,3072]{1,0:T(8,128)(2,1)S(1)}, bf16[64,3072]{1,0:T(8,128)(2,1)S(1)}, u32[]{:S(2)}, u32[]{:S(2)}) collective-permute-start(bf16[64,3072]{1,0:T(8,128)(2,1)S(1)} %fusion.32), channel_id=1, source_target_pairs={{0,2},{1,3},{2,0},{3,1},{4,6},{5,7},{6,4},{7,5},{8,10},{9,11},{10,... | collective-permute-start | bytes 1179656 | tf_op jit(solution)/shard_map/ppermute | solution.py:44
  (103 other events, 1546.6 us)

commit v2 on v1

--- a/solution.py
+++ b/solution.py
@@ -13,6 +13,9 @@
 SHORT_SLOTS = 48
 LONG_SLOTS = 4
 CHUNK = 16 * SPAN
+GROUPS = 2
+GROUP = HEADS // GROUPS
+WIDE = 3 * GROUP * HEAD_DIM
 
 EPSILON = 1e-05
 NEG_LARGE = -1e30
@@ -52,9 +55,46 @@
     return lax.dynamic_index_in_dim(value, index, axis, keepdims=False)
 
 
-def assemble_kernel(rows, info, own, a1, a2, a3, b1, b2, n1, n2, n3, m1, m2, out, sem):
+class Chain:
+    def __init__(self, place, stages):
+        self.place, self.stages, self.result = place, stages, None
+        self.sends = self.take(None)
+
+    def take(self, got):
+        try:
+            return self.stages.send(got)
+        except StopIteration as end:
+            self.result = end.value
+            return []
+
+    def launch(self, arrays):
+        if self.sends:
+            got = [self.place.move(a, **where) for a, (_, where) in zip(arrays, self.sends)]
+            self.sends = self.take(got)
+
+    def finish(self):
+        while self.sends:
+            self.launch([a for a, _ in self.sends])
+        return self.result
+
+
+def tied(value, *chains):
+    pending = [[a for a, _ in chain.sends] for chain in chains]
+    if not any(pending):
+        return value
+    value, pending = lax.optimization_barrier((value, pending))
+    for chain, arrays in zip(chains, pending):
+        chain.launch(arrays)
+    return value
+
+
+def assemble_kernel(rows, info, own, *refs):
     z, y, x, c = info[0], info[1], info[2], info[3]
     half, quarter = rows // 2, rows // 4
+    *parts, out, sem = refs
+    near, far = parts[:6], parts[6:]
+    count = len(far) // 4
+    each = 4 // count
     jobs = []
 
     def add(src, src_row, dst_row, count):
@@ -67,45 +107,74 @@
         )
 
     add(own, 0, (z * 2 + y) * rows, rows)
-    for step, (mine, other) in enumerate(((a1, n1), (a2, n2), (a3, n3)), 1):
+    for step in (1, 2, 3):
         base = (lax.rem(z + 4 - step, 4) * 2 + y) * rows
-        add(mine, 0, base + c * half, half)
-        add(other, 0, base + (1 - c) * half, half)
+        add(near[step - 1], 0, base + c * half, half)
+        add(near[step + 2], 0, base + (1 - c) * half, half)
     for step in range(4):
         base = (lax.rem(z + 4 - step, 4) * 2 + (1 - y)) * rows
-        for core, side, src in ((c, x, b1), (c, 1 - x, b2), (1 - c, x, m1), (1 - c, 1 - x, m2)):
-            add(src, step * quarter, base + core * half + side * quarter, quarter)
+        for kind, (core, side) in enumerate(((c, x), (c, 1 - x), (1 - c, x), (1 - c, 1 - x))):
+            src = far[kind * count + step // each]
+            add(src, (step % each) * quarter, base + core * half + side * quarter, quarter)
     for job in jobs:
         job.start()
     for job in jobs:
         job.wait()
 
 
-def gather_weight(place, info, shard):
+def assemble(info, shard, near, far):
     rows, columns = shard.shape
-    if not place.tuned:
-        return lax.all_gather(shard, "fsdp", axis=0, tiled=True)
-    half, quarter = rows // 2, rows // 4
-    a0 = lax.dynamic_slice_in_dim(shard, place.c * half, half, 0)
-    a1 = place.move(a0, line=1)
-    a2 = place.move(a1, line=1)
-    a3 = place.move(a2, line=1)
-    piece = lambda a: lax.dynamic_slice_in_dim(a, place.x * quarter, quarter, 0)
-    b1 = place.move(jnp.concatenate([piece(a) for a in (a0, a1, a2, a3)], 0), pair=1)
-    b2 = place.move(b1, side=1)
-    n1, n2, n3, m1, m2 = [place.move(a, core=1) for a in (a1, a2, a3, b1, b2)]
+    parts = list(near) + list(far)
     return pl.pallas_call(
         lambda *refs: assemble_kernel(rows, *refs),
         out_shape=jax.ShapeDtypeStruct((8 * rows, columns), shard.dtype),
         in_specs=[pl.BlockSpec(memory_space=pltpu.SMEM)]
-        + [pl.BlockSpec(memory_space=pl.ANY)] * 11,
+        + [pl.BlockSpec(memory_space=pl.ANY)] * (1 + len(parts)),
         out_specs=pl.BlockSpec(memory_space=pltpu.VMEM),
         scratch_shapes=[pltpu.SemaphoreType.DMA((23,))],
         cost_estimate=pl.CostEstimate(
             flops=0, bytes_accessed=32 * rows * columns, transcendentals=0
         ),
         name="assemble",
-    )(info, shard, a1, a2, a3, b1, b2, n1, n2, n3, m1, m2)
+    )(info, shard, *parts)
+
+
+def gather_stages(place, info, shard):
+    if not place.tuned:
+        return lax.all_gather(shard, "fsdp", axis=0, tiled=True)
+    half, quarter = shard.shape[0] // 2, shard.shape[0] // 4
+    own = lax.dynamic_slice_in_dim(shard, place.c * half, half, 0)
+    piece = lambda a: lax.dynamic_slice_in_dim(a, place.x * quarter, quarter, 0)
+    a = yield [(own, dict(line=k)) for k in (1, 2, 3)]
+    mine = jnp.concatenate([piece(m) for m in (own, *a)], 0)
+    b1, *n = yield [(mine, dict(pair=1))] + [(m, dict(core=1)) for m in a]
+    b2, m1 = yield [(b1, dict(side=1)), (b1, dict(core=1))]
+    (m2,) = yield [(b2, dict(core=1))]
+    return assemble(info, shard, [*a, *n], [b1, b2, m1, m2])
+
+
+def gather_first(place, info, shard, chains):
+    if not place.tuned:
+        return lax.all_gather(shard, "fsdp", axis=0, tiled=True)
+    half, quarter = shard.shape[0] // 2, shard.shape[0] // 4
+    own = lax.dynamic_slice_in_dim(shard, place.c * half, half, 0)
+    piece = lambda a: lax.dynamic_slice_in_dim(a, place.x * quarter, quarter, 0)
+    move = place.move
+    a1 = move(own, line=1)
+    b01 = move(jnp.concatenate([piece(own), piece(a1)], 0), pair=1)
+    a2 = move(a1, line=1)
+    n1 = move(a1, core=1)
+    a2 = tied(a2, chains[0])
+    a3 = move(a2, line=1)
+    x01 = move(b01, side=1)
+    n2, m01 = move(a2, core=1), move(b01, core=1)
+    a3 = tied(a3, chains[1])
+    b23 = move(jnp.concatenate([piece(a2), piece(a3)], 0), pair=1)
+    n3, w01 = move(a3, core=1), move(x01, core=1)
+    b23 = tied(b23, chains[2])
+    x23, m23 = move(b23, side=1), move(b23, core=1)
+    w23 = move(x23, core=1)
+    return assemble(info, shard, [a1, a2, a3, n1, n2, n3], [b01, b23, x01, x23, m01, m23, w01, w23])
 
 
 def gather_small(place, packed):
@@ -120,27 +189,40 @@
     return jnp.concatenate(ordered, 0)
 
 
-def reduce_weight(place, grad):
+def plus(a, *others):
+    total = a.astype(F32)
+    for other in others:
+        total = total + other.astype(F32)
+    return total.astype(BF16)
+
+
+def reduce_stages(place, grad, side_first):
     if not place.tuned:
         part = lax.psum_scatter(grad.astype(F32), "fsdp", scatter_dimension=0, tiled=True)
         return lax.psum(part.astype(BF16), "dp").astype(F32)
     rows, columns = grad.shape[0] // 8, grad.shape[1]
-    half = rows // 2
+    half, quarter = rows // 2, rows // 4
     z, y, x, c = place.z, place.y, place.x, place.c
-    view = grad.reshape(8, 2, half, columns)
-    got = place.move(pick(view, 1 - c, 1), core=1)
-    one = (pick(view, c, 1).astype(F32) + got.astype(F32)).astype(BF16)
-    one = one.reshape(4, 2, half, columns)
-    got = place.move(pick(one, 1 - y, 1), pair=1)
-    two = (pick(one, y, 1).astype(F32) + got.astype(F32)).astype(BF16)
-    three = pick(two, z, 0).astype(F32)
-    for k in (1, 2, 3):
-        three = three + place.move(pick(two, (z + k) % 4, 0), line=k).astype(F32)
-    three = three.astype(BF16)
-    four = (three.astype(F32) + place.move(three, side=1).astype(F32)).astype(BF16)
-    got = place.move(four, core=1)
-    low = jnp.where(c == 0, four, got)
-    high = jnp.where(c == 0, got, four)
+    value = grad.reshape(8, 2, half, columns)
+    (got,) = yield [(pick(value, 1 - c, 1), dict(core=1))]
+    value = plus(pick(value, c, 1), got)
+    if side_first:
+        value = value.reshape(8, 2, quarter, columns)
+        (got,) = yield [(pick(value, 1 - x, 1), dict(side=1))]
+        value = plus(pick(value, x, 1), got)
+    value = value.reshape(4, 2, *value.shape[1:])
+    (got,) = yield [(pick(value, 1 - y, 1), dict(pair=1))]
+    value = plus(pick(value, y, 1), got)
+    got = yield [(pick(value, (z + k) % 4, 0), dict(line=k)) for k in (1, 2, 3)]
+    value = plus(pick(value, z, 0), *got)
+    (got,) = yield [(value, dict(side=1))]
+    if side_first:
+        low, high = jnp.where(x == 0, value, got), jnp.where(x == 0, got, value)
+        value = jnp.concatenate([low, high], 0)
+    else:
+        value = plus(value, got)
+    (got,) = yield [(value, dict(core=1))]
+    low, high = jnp.where(c == 0, value, got), jnp.where(c == 0, got, value)
     return jnp.concatenate([low, high], 0).astype(F32)
 
 
@@ -211,16 +293,21 @@
         out_ref[rows, :] = dot_n(low, v_ref[rows, :]).astype(BF16)
 
 
+def block_of(rows, part):
+    return pl.BlockSpec(
+        (rows, HEAD_DIM), lambda h: (0, (h // GROUP) * 3 * GROUP + part * GROUP + h % GROUP)
+    )
+
+
 def short_forward(projected):
     rows = projected.shape[0]
     short_rows = SHORT_SLOTS * SPAN
-    block = lambda part: pl.BlockSpec((short_rows, HEAD_DIM), lambda h: (0, part * HEADS + h))
     return pl.pallas_call(
         short_forward_kernel,
         grid=(HEADS,),
         out_shape=jax.ShapeDtypeStruct((rows, D), BF16),
-        in_specs=[block(0), block(1), block(2)],
-        out_specs=block(0),
+        in_specs=[block_of(short_rows, part) for part in range(3)],
+        out_specs=pl.BlockSpec((short_rows, HEAD_DIM), lambda h: (0, h)),
         scratch_shapes=[pltpu.VMEM((CHUNK, CHUNK), F32)],
         cost_estimate=pl.CostEstimate(
             flops=4 * short_rows * CHUNK * D,
@@ -239,7 +326,7 @@
         bias_ref[...] = short_bias()
 
     bias = bias_ref[...]
-    lanes = lambda part: pl.ds(pl.multiple_of((part * HEADS + head) * HEAD_DIM, HEAD_DIM), HEAD_DIM)
+    lanes = lambda part: pl.ds(pl.multiple_of((part * GROUP + head) * HEAD_DIM, HEAD_DIM), HEAD_DIM)
     for chunk in range(SHORT_SLOTS * SPAN // CHUNK):
         rows = pl.ds(chunk * CHUNK, CHUNK)
         query, key, grad = q_ref[rows, :], k_ref[rows, :], g_ref[rows, :]
@@ -255,21 +342,21 @@
         out_ref[rows, lanes(2)] = dot_l(probs.astype(BF16), grad).astype(BF16)
 
 
-def short_backward(projected, grad_mixture):
+def short_backward(projected, grad_mixture, group):
     rows = projected.shape[0]
     short_rows = SHORT_SLOTS * SPAN
-    block = lambda part: pl.BlockSpec((short_rows, HEAD_DIM), lambda h: (0, part * HEADS + h))
+    block = lambda first: pl.BlockSpec((short_rows, HEAD_DIM), lambda h: (0, first + h))
     return pl.pallas_call(
         short_backward_kernel,
-        grid=(HEADS,),
-        out_shape=jax.ShapeDtypeStruct((rows, 3 * D), BF16),
-        in_specs=[block(0), block(1), block(2), block(0)],
-        out_specs=pl.BlockSpec((rows, 3 * D), lambda h: (0, 0)),
+        grid=(GROUP,),
+        out_shape=jax.ShapeDtypeStruct((rows, WIDE), BF16),
+        in_specs=[block((group * 3 + part) * GROUP) for part in range(3)] + [block(group * GROUP)],
+        out_specs=pl.BlockSpec((rows, WIDE), lambda h: (0, 0)),
         scratch_shapes=[pltpu.VMEM((CHUNK, CHUNK), F32)],
         cost_estimate=pl.CostEstimate(
-            flops=10 * short_rows * CHUNK * D,
-            bytes_accessed=14 * rows * D,
-            transcendentals=short_rows * CHUNK * HEADS,
+            flops=10 * short_rows * CHUNK * D // GROUPS,
+            bytes_accessed=14 * rows * D // GROUPS,
+            transcendentals=short_rows * CHUNK * GROUP,
         ),
         name="short_backward",
     )(projected, projected, projected, grad_mixture)
@@ -311,8 +398,10 @@
 
 
 def long_specs(rows):
-    block = lambda part: pl.BlockSpec((rows, HEAD_DIM), lambda h: (0, part * HEADS + h))
-    return [block(0), block(1), block(2)] + [block(0), block(1)] * 3
+    sent = lambda part: pl.BlockSpec(
+        (rows, HEAD_DIM), lambda h: (0, (h // GROUP) * 2 * GROUP + part * GROUP + h % GROUP)
+    )
+    return [block_of(rows, part) for part in range(3)] + [sent(0), sent(1)] * 3
 
 
 def long_forward(quarter_index, own, priors):
@@ -396,11 +485,13 @@
 
     grouped = series_values.reshape(slot_count, SPAN * PATCH)
     slot_sums = jnp.stack([jnp.sum(grouped, 1), jnp.sum(grouped * grouped, 1)], 1)
-    long_sums = slot_sums[SHORT_SLOTS:]
     rows_of = lambda a: a.astype(F32).reshape(-1, width)
+    sums_row = slot_sums[SHORT_SLOTS:].reshape(1, 2 * LONG_SLOTS)
+    sums_row = jnp.pad(sums_row, ((0, 7), (0, width - 2 * LONG_SLOTS)))
     pieces = [rows_of(a) for a in (patch_weight, norm_gains, bias_rows, expand_bias)]
-    small = gather_small(place, jnp.concatenate(pieces, 0))
-    chain = gather_small(place, long_sums)
+    small_rows = sum(piece.shape[0] for piece in pieces)
+    small = gather_small(place, jnp.concatenate(pieces + [sums_row], 0))
+    chain = small[:, small_rows, : 2 * LONG_SLOTS].reshape(fsdp, LONG_SLOTS, 2)
     offset = jnp.arange(fsdp)[:, None] - place.f + quarter_index[None, :]
     member = ((offset + fsdp) % fsdp < 4).astype(F32)[:, :, None]
     chain_sum = jnp.sum(chain * member, 0)
@@ -409,12 +500,19 @@
     patch_all = wide(0, PATCH).astype(BF16)
     gains_all = wide(PATCH, PATCH + 2)
     biases_all = wide(PATCH + 2, PATCH + 6)
-    expand_shift = small[:, PATCH + 6 :].reshape(-1)
-
-    heads_in_all = gather_weight(place, info, heads_in)
-    heads_out_all = gather_weight(place, info, heads_out)
-    reduce_all = gather_weight(place, info, reduce_weight_shard)
-    expand_all = gather_weight(place, info, expand_weight)
+    expand_shift = small[:, PATCH + 6 : small_rows].reshape(-1)
+
+    mixed_columns = heads_in.reshape(-1, 3, GROUPS, GROUP * HEAD_DIM).transpose(0, 2, 1, 3)
+    gather_out, gather_expand, gather_reduce = [
+        Chain(place, gather_stages(place, info, shard))
+        for shard in (heads_out, expand_weight, reduce_weight_shard)
+    ]
+    heads_in_all = gather_first(
+        place,
+        info,
+        mixed_columns.reshape(-1, 3 * D),
+        (gather_out, gather_expand, gather_reduce),
+    )
 
     totals = jnp.concatenate([slot_sums[:SHORT_SLOTS], chain_sum], 0)
     counts = jnp.where(jnp.arange(slot_count) < SHORT_SLOTS, SPAN * PATCH, 4 * SPAN * PATCH).astype(
@@ -427,34 +525,54 @@
     embedded = dot_n(normed_low, patch_all) + biases_all[0]
     first_value, first_back = jax.vjp(layer_norm, embedded, gains_all[0], biases_all[1])
     first_norm = first_value.astype(BF16)
+    heads_in_all = tied(heads_in_all, gather_out)
     projected = dot_n(first_norm, heads_in_all).astype(BF16)
+    projected = tied(projected, gather_out, gather_expand)
 
     own_long = projected[short_rows:]
-    long_pairs = own_long[:, D:]
+    group_columns = lambda g, low, high: slice(
+        (g * 3 + low) * GROUP * HEAD_DIM, (g * 3 + high) * GROUP * HEAD_DIM
+    )
+    long_pairs = jnp.concatenate([own_long[:, group_columns(g, 1, 3)] for g in range(GROUPS)], 1)
     priors = [place.along(long_pairs, step) for step in (1, 2, 3)]
     mixed_short = short_forward(projected)
+    own_long, mixed_short = tied((own_long, mixed_short), gather_out, gather_expand)
     mixed_long = long_forward(quarter_index, own_long, priors)
+    heads_out_all = gather_out.finish()
+    heads_out_all, mixed_long = tied((heads_out_all, mixed_long), gather_expand, gather_reduce)
     mixed_all = lax.dynamic_update_slice(mixed_short, mixed_long, (short_rows, 0))
     middle = embedded + dot_n(mixed_all, heads_out_all)
     second_value, second_back = jax.vjp(layer_norm, middle, gains_all[1], biases_all[2])
     second_norm = second_value.astype(BF16)
 
+    expand_all = gather_expand.finish()
     pre_act = dot_n(second_norm, expand_all) + expand_shift
     act_value, gelu_back = jax.vjp(exact_gelu, pre_act)
-    activation = act_value.astype(BF16)
-    layer_output = (middle + dot_n(activation, reduce_all) + biases_all[3]).astype(BF16)
-
-    grad_reduce = reduce_weight(place, dot_l(activation, cotangent).astype(BF16))
+    activation = tied(act_value.astype(BF16), gather_reduce)
+    grad_reduce = Chain(
+        place, reduce_stages(place, dot_l(activation, cotangent).astype(BF16), False)
+    )
+    cotangent = tied(cotangent, gather_reduce, grad_reduce)
+    reduce_all = gather_reduce.finish()
+
     grad_act = dot_t(cotangent, reduce_all)
-    grad_pre = gelu_back(grad_act)[0].astype(BF16)
-    grad_expand = reduce_weight(place, dot_l(second_norm, grad_pre).astype(BF16))
+    grad_pre = tied(gelu_back(grad_act)[0].astype(BF16), grad_reduce)
+    grad_expand = Chain(
+        place, reduce_stages(place, dot_l(second_norm, grad_pre).astype(BF16), True)
+    )
     grad_expand_bias = jnp.sum(grad_pre.astype(F32), 0)
+    expand_all = tied(expand_all, grad_expand)
     grad_second = dot_t(grad_pre, expand_all)
     middle_back, gain_two, shift_two = second_back(grad_second)
     grad_middle = cotangent.astype(F32) + middle_back
-    grad_branch = grad_middle.astype(BF16)
-    grad_heads_out = reduce_weight(place, dot_l(mixed_all, grad_branch).astype(BF16))
+    grad_branch = tied(grad_middle.astype(BF16), grad_expand)
+    grad_heads_out = Chain(
+        place, reduce_stages(place, dot_l(mixed_all, grad_branch).astype(BF16), False)
+    )
+    heads_out_all = tied(heads_out_all, grad_heads_out)
     grad_mixture = dot_t(grad_branch, heads_out_all).astype(BF16)
+    grad_mixture, activation = tied((grad_mixture, activation), grad_reduce, grad_heads_out)
+    layer_output = (middle + dot_n(activation, reduce_all) + biases_all[3]).astype(BF16)
 
     long_query, own_grads, *sent = long_backward(
         quarter_index, own_long, priors, grad_mixture[short_rows:]
@@ -462,13 +580,24 @@
     for step, sent_back in zip((1, 2, 3), sent):
         own_grads = own_grads + place.along(sent_back, -step).astype(F32)
     own_grads = own_grads.astype(BF16)
-    grad_short = short_backward(projected, grad_mixture)
-    grad_long = jnp.concatenate([long_query, own_grads[0], own_grads[1]], 1)
-    grad_projected = lax.dynamic_update_slice(grad_short, grad_long, (short_rows, 0))
-    grad_heads_in = reduce_weight(place, dot_l(first_norm, grad_projected).astype(BF16))
-    grad_first = dot_t(grad_projected, heads_in_all)
+
+    def grad_group(g, grad_mixture):
+        columns = slice(g * GROUP * HEAD_DIM, (g + 1) * GROUP * HEAD_DIM)
+        grad_long = jnp.concatenate([a[:, columns] for a in (long_query, *own_grads)], 1)
+        short = short_backward(projected, grad_mixture, g)
+        return lax.dynamic_update_slice(short, grad_long, (short_rows, 0))
+
+    grad_mixture, long_query = tied((grad_mixture, long_query), grad_expand)
+    low_grad = tied(grad_group(0, grad_mixture), grad_reduce, grad_heads_out)
+    grad_low = Chain(place, reduce_stages(place, dot_l(first_norm, low_grad).astype(BF16), False))
+    grad_mixture = tied(grad_mixture, grad_low, grad_expand)
+    high_grad = tied(grad_group(1, grad_mixture), grad_low, grad_reduce)
+    grad_high = Chain(place, reduce_stages(place, dot_l(first_norm, high_grad).astype(BF16), True))
+    heads_in_all = tied(heads_in_all, grad_high, grad_expand, grad_heads_out)
+    grad_first = dot_t(low_grad, heads_in_all[:, :WIDE]) + dot_t(high_grad, heads_in_all[:, WIDE:])
     embed_back, gain_one, shift_one = first_back(grad_first)
     grad_embedded = (grad_middle + embed_back).astype(BF16)
+    grad_embedded = tied(grad_embedded, grad_high, grad_low, grad_expand, grad_heads_out)
     grad_patch = dot_l(normed_low, grad_embedded)
     shift_zero = jnp.sum(grad_embedded.astype(F32), 0)
     grad_normed = dot_t(grad_embedded, patch_all).reshape(slot_count, SPAN * PATCH)
@@ -496,14 +625,16 @@
         1,
     )
     small_grads = reduce_small(place, packed)
+    grouped_grads = jnp.stack([grad_low.finish(), grad_high.finish()], 1)
+    grad_heads_in = grouped_grads.reshape(-1, GROUPS, 3, GROUP * HEAD_DIM).transpose(0, 2, 1, 3)
     return (
         layer_output,
         series_grad,
         small_grads[:PATCH],
-        grad_heads_in,
-        grad_heads_out,
-        grad_expand,
-        grad_reduce,
+        grad_heads_in.reshape(-1, 3 * D),
+        grad_heads_out.finish(),
+        grad_expand.finish(),
+        grad_reduce.finish(),
         small_grads[PATCH : PATCH + 2],
         small_grads[PATCH + 2 : PATCH + 6],
         small_grads[PATCH + 6 :].reshape(-1),

time: 554 us -> 544 us (0.982)
  the two profiles are of different devices: /device:TPU:0 before, /device:TPU:29 now
where the time goes in v2:
time: 544 us; the launch traced here: 535 us
  waiting for transfers between devices  131 us (24%)
  starting transfers between devices  124 us (23%)
  matrix products  91.3 us (17%)
  local copies, waits for them, and re-layouts  66.7 us (12%)
  Pallas kernels  65.8 us (12%)
  other arithmetic  53.1 us (10%)
    ppermute x96, starting transfers between devices, move(): return lax.ppermute(value, AXES, pairs)  119 us
    ppermute x96, waiting for transfers between devices, move(): return lax.ppermute(value, AXES, pairs)  106 us
    dot_general x5, matrix products, dot_n(): lax.dot_general(a, b, (((1,), (0,)), ((), ())), preferred_element_type=F32)  41.6 us
    dot_general x6, matrix products, dot_t(): lax.dot_general(a, b, (((1,), (1,)), ((), ())), preferred_element_type=F32)  27 us
    ppermute x6, waiting for transfers between devices, along(): return lax.ppermute(value, 'fsdp', pairs)  24.6 us
    dot_general x6, matrix products, dot_l(): lax.dot_general(a, b, (((0,), (0,)), ((), ())), preferred_element_type=F32)  22.7 us
    unnamed x207, local copies, waits for them, and re-layouts  22.5 us
    convert_element_type x20, other arithmetic, plus(): return total.astype(BF16)  21.7 us
  transfers between devices with their start and end apart: 102, of which 28 were waited for; matrix products, arithmetic and copies ran while one was open for 30% of the time, Pallas kernels for 12%

profile of v2, /device:TPU:29, one launch (start us, length us, event | category | flops | bytes accessed | tf_op | source)
XLA Modules:
  0.0 534.5 jit_solution(3357004992054344511)
XLA Ops:
  15.5 4.7 collective-permute-done.1
  20.1 6.9 %collective-permute-done.2 = f32[2,112,128]{2,1,0:T(8,128)S(1)} collective-permute-done((f32[2,112,128]{2,1,0:T(8,128)S(1)}, f32[2,112,128]{2,1,0:T(8,128)S(1)}, u32[]{:S(2)}, u32[]{:S(2)}) %collective-permute-start.2) | collective-permute-done | bytes 114720 | tf_op jit(solution)/shard_map/ppermute | solution.py:47
  35.7 7.1 %collective-permute-done.5.refs_3_ = bf16[64,3072]{1,0:T(8,128)(2,1)S(1)} collective-permute-done((bf16[64,3072]{1,0:T(8,128)(2,1)}, bf16[64,3072]{1,0:T(8,128)(2,1)S(1)}, u32[]{:S(2)}, u32[]{:S(2)}) %collective-permute-start.5) | collective-permute-done | bytes 393248 | tf_op jit(solution)/shard_map/ppermute | solution.py:47
  42.8 3.9 collective-permute-start.6
  51.3 2.6 collective-permute-done.6.refs_4_
  55.3 2.9 collective-permute-done.20.refs_4_
  58.2 4.2 collective-permute-start.22
  62.4 11.1 %collective-permute-start.24 = (bf16[64,2048]{1,0:T(8,128)(2,1)S(1)}, bf16[64,2048]{1,0:T(8,128)(2,1)S(1)}, u32[]{:S(2)}, u32[]{:S(2)}) collective-permute-start(bf16[64,2048]{1,0:T(8,128)(2,1)S(1)} %copy-done.69), channel_id=1, source_target_pairs={{0,24},{1,25},{2,26},{3,27},{4,28},{5,29},{6,30},{7,31},{8,0},{9,1... | collective-permute-start | bytes 786440 | tf_op jit(solution)/shard_map/ppermute | solution.py:47
  76.1 3.2 collective-permute-start.23
  79.3 3.9 collective-permute-done.24.refs_4_
  84.5 3.6 collective-permute-start.8
  88.7 7.0 %collective-permute-done.23.refs_3_ = bf16[64,2048]{1,0:T(8,128)(2,1)S(1)} collective-permute-done((bf16[64,2048]{1,0:T(8,128)(2,1)S(1)}, bf16[64,2048]{1,0:T(8,128)(2,1)S(1)}, u32[]{:S(2)}, u32[]{:S(2)}) %collective-permute-start.23) | collective-permute-done | bytes 262176 | tf_op jit(solution)/shard_map/ppermute | solution.py:47
  98.5 2.3 collective-permute-start.36
  101.7 6.2 %assemble.4 = bf16[1024,3072]{1,0:T(8,128)(2,1)} custom-call(s32[4]{0:T(128)} %pad_add_fusion.refs_0_, bf16[128,3072]{1,0:T(8,128)(2,1)} %copy-done.12, bf16[64,3072]{1,0:T(8,128)(2,1)} %collective-permute-done.4.refs_2_, bf16[64,3072]{1,0:T(8,128)(2,1)} %copy-done.44, bf16[64,3072]{1,0:T(8,128)(2,1)} %copy-done.45, bf16[64,3072]{1,0:T(8,128)(2,1)} %copy-done.55, ...), custom_call_target="tpu_custom_call" | custom-call | bytes 12582912 | tf_op jit(solution)/shard_map/assemble/pallas_call | solution.py:128
  108.9 8.7 %convolution_convert_fusion.q_ref.k_ref.v_ref = bf16[780,3072]{1,0:T(8,128)(2,1)S(1)} fusion(bf16[1024,3072]{1,0:T(8,128)(2,1)} %assemble.4, f32[780,1024]{1,0:T(8,128)S(1)} %get-tuple-element.295, f32[1024]{0:T(1024)S(1)} %copy-done.91, f32[1024]{0:T(1024)S(1)} %copy-done.85, f32[780]{0:T(1024)S(1)} %fusion.68, f32[780]{0:T(1024)S(1)} %broadcast_multiply_fusion.1, ...), kind=kOutput, calls=%fused_computation.17 | convolution fusion | flops 4914524160 | bytes 14297184 | tf_op jit(solution)/shard_map/dot_general | solution.py:266
  120.6 4.1 collective-permute-done.25.refs_9_
  127.0 10.6 %short_forward.1 = bf16[780,1024]{1,0:T(8,128)(2,1)} custom-call(bf16[780,3072]{1,0:T(8,128)(2,1)} %copy-done, bf16[780,3072]{1,0:T(8,128)(2,1)} %copy-done, bf16[780,3072]{1,0:T(8,128)(2,1)} %copy-done), custom_call_target="tpu_custom_call" | custom-call | flops 707788800 | bytes 6389760 | tf_op jit(solution)/shard_map/short_forward/pallas_call | solution.py:305
  139.4 2.3 collective-permute-start.27
  150.8 4.5 collective-permute-done.34.k3.v3
  158.9 6.8 %long_forward.1 = bf16[60,1024]{1,0:T(8,128)(2,1)} custom-call(s32[4]{0:T(128)} %quarter_ref.3, bf16[60,3072]{1,0:T(8,128)(2,1)} %slice.125.q.k0.v0, bf16[60,3072]{1,0:T(8,128)(2,1)} %slice.125.q.k0.v0, bf16[60,3072]{1,0:T(8,128)(2,1)} %slice.125.q.k0.v0, bf16[60,2048]{1,0:T(8,128)(2,1)} %copy-done.15, bf16[60,2048]{1,0:T(8,128)(2,1)} %copy-done.15, ...), custom_call_target="tpu_custom_call" | custom-call | flops 58982400 | bytes 1228800 | tf_op jit(solution)/shard_map/long_forward/pallas_call | solution.py:410
  166.8 3.7 assemble.5
  171.4 4.0 fusion.89
  177.6 7.5 %collective-permute-start.44 = (bf16[256,1024]{1,0:T(8,128)(2,1)}, bf16[256,1024]{1,0:T(8,128)(2,1)}, u32[]{:S(2)}, u32[]{:S(2)}) collective-permute-start(bf16[256,1024]{1,0:T(8,128)(2,1)} %pad_maximum_fusion.1), channel_id=1, source_target_pairs={{0,4},{1,5},{2,6},{3,7},{4,0},{5,1},{6,2},{7,3},{8,12},{9,13},{10,... | collective-permute-start | bytes 1572872 | tf_op jit(solution)/shard_map/ppermute | solution.py:47
  185.1 4.9 assemble.6
  190.1 22.5 %multiply_convert_fusion = (bf16[780,2048]{1,0:T(8,128)(2,1)S(1)}, f32[780,2048]{1,0:T(8,128)}, f32[780,2048]{1,0:T(8,128)}) fusion(f32[2048]{0:T(1024)S(1)} %bitcast.350, bf16[1024,2048]{1,0:T(8,128)(2,1)} %assemble.6, f32[780,1024]{1,0:T(8,128)} %copy-done.6, f32[1024]{0:T(1024)S(1)} %copy-done.95, f32[1024]{0:T(1024)S(1)} %copy-done.88, ...), kind=kOutput, calls=%fused_computation.3 | convolution fusion | flops 3380981760 | bytes 23386208 | tf_op jit(solution)/shard_map/dot_general | solution.py:266
  213.9 5.4 %convolution_convert_fusion.4 = bf16[2048,1024]{1,0:T(8,128)(2,1)S(1)} fusion(bf16[780,2048]{1,0:T(8,128)(2,1)S(1)} %get-tuple-element.147, bf16[780,1024]{1,0:T(8,128)(2,1)S(1)} %copy-done.3), kind=kOutput, calls=%fused_computation.27 | convolution fusion | flops 3273654272 | bytes 8986624 | tf_op jit(solution)/shard_map/dot_general | solution.py:262
  222.8 3.0 collective-permute-done.45.refs_9_
  228.3 3.4 collective-permute-done.46.refs_5_
  234.1 5.1 assemble.7
  239.2 11.9 %add_convert_fusion = bf16[780,2048]{1,0:T(8,128)(2,1)S(1)} fusion(f32[780,2048]{1,0:T(8,128)} %get-tuple-element.221, f32[780,2048]{1,0:T(8,128)} %get-tuple-element.298, f32[2048]{0:T(1024)S(1)} %bitcast.351, bf16[780,1024]{1,0:T(8,128)(2,1)} %param.21, bf16[2048,1024]{1,0:T(8,128)(2,1)} %assemble.7), kind=kOutput, calls=%fused_computation.2 | convolution fusion | flops 3295518720 | bytes 21774336 | tf_op jit(solution)/shard_map/dot_general | solution.py:258
  251.1 3.7 fusion.7
  257.2 5.5 %convolution_convert_fusion.3 = bf16[1024,2048]{1,0:T(8,128)(2,1)S(1)} fusion(bf16[780,2048]{1,0:T(8,128)(2,1)S(1)} %add_convert_fusion, f32[780,1024]{1,0:T(8,128)S(1)} %copy-done.7, f32[1024]{0:T(1024)S(1)} %copy-done.95, f32[1024]{0:T(1024)S(1)} %copy-done.88, f32[780]{0:T(1024)S(1)} %fusion.69, f32[780]{0:T(1024)S(1)} %broadcast_multiply_fusion), kind=kOutput, calls=%fused_computation.26 | convolution fusion | flops 3277647872 | bytes 10598496 | tf_op jit(solution)/shard_map/dot_general | solution.py:262
  264.9 4.1 multiply_reduce_fusion
  274.3 2.4 convolution_convert_fusion.5
  282.6 2.4 reduce.11
  297.9 3.0 collective-permute-start.59
  301.6 8.0 %long_backward.1 = (bf16[60,1024]{1,0:T(8,128)(2,1)}, f32[2,60,1024]{2,1,0:T(8,128)}, bf16[2,60,1024]{2,1,0:T(8,128)(2,1)}, bf16[2,60,1024]{2,1,0:T(8,128)(2,1)}, bf16[2,60,1024]{2,1,0:T(8,128)(2,1)}) custom-call(s32[4]{0:T(128)} %quarter_ref.3, bf16[60,3072]{1,0:T(8,128)(2,1)} %slice.125.q.k0.v0, bf16[60,3072]{1,0:T(8,128)(2,1)} %slice.125.q.k0.v0, ...), custom_call_target="tpu_custom_call" | custom-call | flops 147456000 | bytes 2457600 | tf_op jit(solution)/shard_map/long_backward/pallas_call | solution.py:450
  315.0 10.2 %short_backward.2 = bf16[780,1536]{1,0:T(8,128)(2,1)} custom-call(bf16[780,3072]{1,0:T(8,128)(2,1)} %copy-done, bf16[780,3072]{1,0:T(8,128)(2,1)} %copy-done, bf16[780,3072]{1,0:T(8,128)(2,1)} %copy-done, bf16[780,1024]{1,0:T(8,128)(2,1)} %copy-done.11), custom_call_target="tpu_custom_call" | custom-call | flops 884736000 | bytes 5591040 | tf_op jit(solution)/shard_map/short_backward/pallas_call | solution.py:349
  326.2 3.2 collective-permute-start.60
  329.6 19.3 %collective-permute-done.58 = bf16[2,60,1024]{2,1,0:T(8,128)(2,1)} collective-permute-done((bf16[2,60,1024]{2,1,0:T(8,128)(2,1)}, bf16[2,60,1024]{2,1,0:T(8,128)(2,1)}, u32[]{:S(2)}, u32[]{:S(2)}) %collective-permute-start.58) | collective-permute-done | bytes 245792 | tf_op jit(solution)/shard_map/ppermute | solution.py:51
  355.4 6.7 %collective-permute-done.63 = bf16[4,32,2048]{2,1,0:T(8,128)(2,1)S(1)} collective-permute-done((bf16[4,32,2048]{2,1,0:T(8,128)(2,1)}, bf16[4,32,2048]{2,1,0:T(8,128)(2,1)S(1)}, u32[]{:S(2)}, u32[]{:S(2)}) %collective-permute-start.63) | collective-permute-done | bytes 524320 | tf_op jit(solution)/shard_map/ppermute | solution.py:47
  363.8 4.0 convolution_convert_fusion.2
  370.7 4.6 add_convert_fusion.2
  377.5 10.2 %short_backward.3 = bf16[780,1536]{1,0:T(8,128)(2,1)} custom-call(bf16[780,3072]{1,0:T(8,128)(2,1)} %copy-done, bf16[780,3072]{1,0:T(8,128)(2,1)} %copy-done, bf16[780,3072]{1,0:T(8,128)(2,1)} %copy-done, bf16[780,1024]{1,0:T(8,128)(2,1)} %copy-done.11), custom_call_target="tpu_custom_call" | custom-call | flops 884736000 | bytes 5591040 | tf_op jit(solution)/shard_map/short_backward/pallas_call | solution.py:349
  394.3 9.3 %collective-permute-done.70 = bf16[64,1024]{1,0:T(8,128)(2,1)S(1)} collective-permute-done((bf16[64,1024]{1,0:T(8,128)(2,1)}, bf16[64,1024]{1,0:T(8,128)(2,1)S(1)}, u32[]{:S(2)}, u32[]{:S(2)}) %collective-permute-start.70) | collective-permute-done | bytes 131104 | tf_op jit(solution)/shard_map/ppermute | solution.py:47
  405.7 2.5 fusion.9
  409.4 4.4 convolution_convert_fusion.1
  416.4 2.7 fusion.10
  419.1 3.5 multiply_reduce_fusion.1
  429.6 4.5 collective-permute-done.73
  444.1 3.0 fusion.80
  449.3 2.4 collective-permute-done.76
  455.4 3.2 collective-permute-start.87
  463.2 4.8 collective-permute-start.82
  468.0 6.5 %collective-permute-done.88 = bf16[64,1536]{1,0:T(8,128)(2,1)S(1)} collective-permute-done((bf16[64,1536]{1,0:T(8,128)(2,1)}, bf16[64,1536]{1,0:T(8,128)(2,1)S(1)}, u32[]{:S(2)}, u32[]{:S(2)}) %collective-permute-start.88) | collective-permute-done | bytes 196640 | tf_op jit(solution)/shard_map/ppermute | solution.py:47
  474.5 2.8 collective-permute-start.100
  482.4 2.9 collective-permute-done.83
  485.4 3.2 collective-permute-start.85
  488.6 8.1 %collective-permute-done.92 = bf16[8,32,1536]{2,1,0:T(8,128)(2,1)S(1)} collective-permute-done((bf16[8,32,1536]{2,1,0:T(8,128)(2,1)}, bf16[8,32,1536]{2,1,0:T(8,128)(2,1)S(1)}, u32[]{:S(2)}, u32[]{:S(2)}) %collective-permute-start.92) | collective-permute-done | bytes 786464 | tf_op jit(solution)/shard_map/ppermute | solution.py:47
  498.1 8.2 %collective-permute-done.93 = bf16[4,32,1536]{2,1,0:T(8,128)(2,1)S(1)} collective-permute-done((bf16[4,32,1536]{2,1,0:T(8,128)(2,1)S(1)}, bf16[4,32,1536]{2,1,0:T(8,128)(2,1)S(1)}, u32[]{:S(2)}, u32[]{:S(2)}) %collective-permute-start.93) | collective-permute-done | bytes 393248 | tf_op jit(solution)/shard_map/ppermute | solution.py:47
  506.6 6.0 %collective-permute-start.95 = (bf16[32,1536]{1,0:T(8,128)(2,1)S(1)}, bf16[32,1536]{1,0:T(8,128)(2,1)S(1)}, u32[]{:S(2)}, u32[]{:S(2)}) collective-permute-start(bf16[32,1536]{1,0:T(8,128)(2,1)S(1)} %get-tuple-element.254), channel_id=1, source_target_pairs={{0,16},{1,17},{2,18},{3,19},{4,20},{5,21},{6,22},{7,23},{8,24},{9,... | collective-permute-start | bytes 294920 | tf_op jit(solution)/shard_map/ppermute | solution.py:47
  514.4 7.0 %collective-permute-done.95 = bf16[32,1536]{1,0:T(8,128)(2,1)S(1)} collective-permute-done((bf16[32,1536]{1,0:T(8,128)(2,1)S(1)}, bf16[32,1536]{1,0:T(8,128)(2,1)S(1)}, u32[]{:S(2)}, u32[]{:S(2)}) %collective-permute-start.95) | collective-permute-done | bytes 98336 | tf_op jit(solution)/shard_map/ppermute | solution.py:47
  525.0 2.5 collective-permute-start.98
  531.3 3.0 copy.122
  (557 shorter events, 176.1 us)
Async XLA Ops:
  7.6 25.9 %collective-permute-start.4 = (bf16[64,3072]{1,0:T(8,128)(2,1)}, bf16[64,3072]{1,0:T(8,128)(2,1)}, u32[]{:S(2)}, u32[]{:S(2)}) collective-permute-start(bf16[64,3072]{1,0:T(8,128)(2,1)} %constant_dynamic-slice_fusion.23), channel_id=1, source_target_pairs={{0,8},{1,9},{2,10},{3,11},{4,12},{5,13},{6,14},{7,15},{8,16},{9,17... | collective-permute-start | bytes 1179656 | tf_op jit(solution)/shard_map/ppermute | solution.py:47
  13.2 13.8 %collective-permute-start.2 = (f32[2,112,128]{2,1,0:T(8,128)S(1)}, f32[2,112,128]{2,1,0:T(8,128)S(1)}, u32[]{:S(2)}, u32[]{:S(2)}) collective-permute-start(f32[2,112,128]{2,1,0:T(8,128)S(1)} %get-tuple-element.270), channel_id=1, source_target_pairs={{0,16},{1,17},{2,18},{3,19},{4,20},{5,21},{6,22},{7,23},{8,24},{9,... | collective-permute-start | bytes 344072 | tf_op jit(solution)/shard_map/ppermute | solution.py:47
  14.6 12.4 %collective-permute-start.3 = (f32[2,112,128]{2,1,0:T(8,128)S(1)}, f32[2,112,128]{2,1,0:T(8,128)S(1)}, u32[]{:S(2)}, u32[]{:S(2)}) collective-permute-start(f32[2,112,128]{2,1,0:T(8,128)S(1)} %get-tuple-element.270), channel_id=1, source_target_pairs={{0,24},{1,25},{2,26},{3,27},{4,28},{5,29},{6,30},{7,31},{8,0},{9,1... | collective-permute-start | bytes 344072 | tf_op jit(solution)/shard_map/ppermute | solution.py:47
  46.7 26.9 %collective-permute-start.10 = (bf16[64,3072]{1,0:T(8,128)(2,1)S(1)}, bf16[64,3072]{1,0:T(8,128)(2,1)S(1)}, u32[]{:S(2)}, u32[]{:S(2)}) collective-permute-start(bf16[64,3072]{1,0:T(8,128)(2,1)S(1)} %pad_maximum_fusion.4), channel_id=1, source_target_pairs={{0,4},{1,5},{2,6},{3,7},{4,0},{5,1},{6,2},{7,3},{8,12},{9,13},{10,... | collective-permute-start | bytes 1179656 | tf_op jit(solution)/shard_map/ppermute | solution.py:47
  48.0 14.4 %collective-permute-start.19 = (bf16[64,1024]{1,0:T(8,128)(2,1)S(1)}, bf16[64,1024]{1,0:T(8,128)(2,1)S(1)}, u32[]{:S(2)}, u32[]{:S(2)}) collective-permute-start(bf16[64,1024]{1,0:T(8,128)(2,1)S(1)} %copy-done.71), channel_id=1, source_target_pairs={{0,16},{1,17},{2,18},{3,19},{4,20},{5,21},{6,22},{7,23},{8,24},{9,... | collective-permute-start | bytes 393224 | tf_op jit(solution)/shard_map/ppermute | solution.py:47
  49.5 24.9 %collective-permute-start.18 = (bf16[64,1024]{1,0:T(8,128)(2,1)S(1)}, bf16[64,1024]{1,0:T(8,128)(2,1)S(1)}, u32[]{:S(2)}, u32[]{:S(2)}) collective-permute-start(bf16[64,1024]{1,0:T(8,128)(2,1)S(1)} %copy-done.71), channel_id=1, source_target_pairs={{0,8},{1,9},{2,10},{3,11},{4,12},{5,13},{6,14},{7,15},{8,16},{9,17... | collective-permute-start | bytes 393224 | tf_op jit(solution)/shard_map/ppermute | solution.py:47
  54.0 21.7 %collective-permute-start.11 = (bf16[64,3072]{1,0:T(8,128)(2,1)S(1)}, bf16[64,3072]{1,0:T(8,128)(2,1)S(1)}, u32[]{:S(2)}, u32[]{:S(2)}) collective-permute-start(bf16[64,3072]{1,0:T(8,128)(2,1)S(1)} %pad_maximum_fusion.5), channel_id=1, source_target_pairs={{0,4},{1,5},{2,6},{3,7},{4,0},{5,1},{6,2},{7,3},{8,12},{9,13},{10,... | collective-permute-start | bytes 1179656 | tf_op jit(solution)/shard_map/ppermute | solution.py:47
  58.2 17.9 %collective-permute-start.22 = (bf16[64,2048]{1,0:T(8,128)(2,1)S(1)}, bf16[64,2048]{1,0:T(8,128)(2,1)S(1)}, u32[]{:S(2)}, u32[]{:S(2)}) collective-permute-start(bf16[64,2048]{1,0:T(8,128)(2,1)S(1)} %copy-done.69), channel_id=1, source_target_pairs={{0,8},{1,9},{2,10},{3,11},{4,12},{5,13},{6,14},{7,15},{8,16},{9,17... | collective-permute-start | bytes 786440 | tf_op jit(solution)/shard_map/ppermute | solution.py:47
  62.4 20.9 %collective-permute-start.24 = (bf16[64,2048]{1,0:T(8,128)(2,1)S(1)}, bf16[64,2048]{1,0:T(8,128)(2,1)S(1)}, u32[]{:S(2)}, u32[]{:S(2)}) collective-permute-start(bf16[64,2048]{1,0:T(8,128)(2,1)S(1)} %copy-done.69), channel_id=1, source_target_pairs={{0,24},{1,25},{2,26},{3,27},{4,28},{5,29},{6,30},{7,31},{8,0},{9,1... | collective-permute-start | bytes 786440 | tf_op jit(solution)/shard_map/ppermute | solution.py:47
  74.4 13.7 %collective-permute-start.12 = (bf16[64,3072]{1,0:T(8,128)(2,1)S(1)}, bf16[64,3072]{1,0:T(8,128)(2,1)S(1)}, u32[]{:S(2)}, u32[]{:S(2)}) collective-permute-start(bf16[64,3072]{1,0:T(8,128)(2,1)S(1)} %collective-permute-done.10.refs_8_), channel_id=1, source_target_pairs={{0,2},{1,3},{2,0},{3,1},{4,6},{5,7},{6,4},{7,5},{8,10},{9,11},{10,... | collective-permute-start | bytes 1179656 | tf_op jit(solution)/shard_map/ppermute | solution.py:47
  75.7 12.6 %collective-permute-start.14 = (bf16[64,3072]{1,0:T(8,128)(2,1)S(1)}, bf16[64,3072]{1,0:T(8,128)(2,1)S(1)}, u32[]{:S(2)}, u32[]{:S(2)}) collective-permute-start(bf16[64,3072]{1,0:T(8,128)(2,1)S(1)} %collective-permute-done.10.refs_8_), channel_id=1, source_target_pairs={{0,1},{1,0},{2,3},{3,2},{4,5},{5,4},{6,7},{7,6},{8,9},{9,8},{10,11... | collective-permute-start | bytes 1179656 | tf_op jit(solution)/shard_map/ppermute | solution.py:47
  76.1 19.6 %collective-permute-start.23 = (bf16[64,2048]{1,0:T(8,128)(2,1)S(1)}, bf16[64,2048]{1,0:T(8,128)(2,1)S(1)}, u32[]{:S(2)}, u32[]{:S(2)}) collective-permute-start(bf16[64,2048]{1,0:T(8,128)(2,1)S(1)} %copy-done.69), channel_id=1, source_target_pairs={{0,16},{1,17},{2,18},{3,19},{4,20},{5,21},{6,22},{7,23},{8,24},{9,... | collective-permute-start | bytes 786440 | tf_op jit(solution)/shard_map/ppermute | solution.py:47
  83.3 13.0 %collective-permute-start.13 = (bf16[64,3072]{1,0:T(8,128)(2,1)S(1)}, bf16[64,3072]{1,0:T(8,128)(2,1)S(1)}, u32[]{:S(2)}, u32[]{:S(2)}) collective-permute-start(bf16[64,3072]{1,0:T(8,128)(2,1)S(1)} %collective-permute-done.11.refs_9_), channel_id=1, source_target_pairs={{0,2},{1,3},{2,0},{3,1},{4,6},{5,7},{6,4},{7,5},{8,10},{9,11},{10,... | collective-permute-start | bytes 1179656 | tf_op jit(solution)/shard_map/ppermute | solution.py:47
  84.5 12.8 %collective-permute-start.8 = (bf16[64,3072]{1,0:T(8,128)(2,1)S(1)}, bf16[64,3072]{1,0:T(8,128)(2,1)S(1)}, u32[]{:S(2)}, u32[]{:S(2)}) collective-permute-start(bf16[64,3072]{1,0:T(8,128)(2,1)S(1)} %collective-permute-done.5.refs_3_), channel_id=1, source_target_pairs={{0,1},{1,0},{2,3},{3,2},{4,5},{5,4},{6,7},{7,6},{8,9},{9,8},{10,11... | collective-permute-start | bytes 1179656 | tf_op jit(solution)/shard_map/ppermute | solution.py:47
  97.3 44.3 %collective-permute-start.38 = (bf16[128,1024]{1,0:T(8,128)(2,1)}, bf16[128,1024]{1,0:T(8,128)(2,1)}, u32[]{:S(2)}, u32[]{:S(2)}) collective-permute-start(bf16[128,1024]{1,0:T(8,128)(2,1)} %constant_dynamic-slice_fusion.16), channel_id=1, source_target_pairs={{0,24},{1,25},{2,26},{3,27},{4,28},{5,29},{6,30},{7,31},{8,0},{9,1... | collective-permute-start | bytes 786440 | tf_op jit(solution)/shard_map/ppermute | solution.py:47
  97.4 46.0 %collective-permute-start.37 = (bf16[128,1024]{1,0:T(8,128)(2,1)}, bf16[128,1024]{1,0:T(8,128)(2,1)}, u32[]{:S(2)}, u32[]{:S(2)}) collective-permute-start(bf16[128,1024]{1,0:T(8,128)(2,1)} %constant_dynamic-slice_fusion.16), channel_id=1, source_target_pairs={{0,16},{1,17},{2,18},{3,19},{4,20},{5,21},{6,22},{7,23},{8,24},{9,... | collective-permute-start | bytes 786440 | tf_op jit(solution)/shard_map/ppermute | solution.py:47
  98.5 45.3 %collective-permute-start.36 = (bf16[128,1024]{1,0:T(8,128)(2,1)}, bf16[128,1024]{1,0:T(8,128)(2,1)}, u32[]{:S(2)}, u32[]{:S(2)}) collective-permute-start(bf16[128,1024]{1,0:T(8,128)(2,1)} %constant_dynamic-slice_fusion.16), channel_id=1, source_target_pairs={{0,8},{1,9},{2,10},{3,11},{4,12},{5,13},{6,14},{7,15},{8,16},{9,17... | collective-permute-start | bytes 786440 | tf_op jit(solution)/shard_map/ppermute | solution.py:47
  117.7 21.7 %collective-permute-start.26 = (bf16[128,2048]{1,0:T(8,128)(2,1)}, bf16[128,2048]{1,0:T(8,128)(2,1)}, u32[]{:S(2)}, u32[]{:S(2)}) collective-permute-start(bf16[128,2048]{1,0:T(8,128)(2,1)} %pad_maximum_fusion), channel_id=1, source_target_pairs={{0,4},{1,5},{2,6},{3,7},{4,0},{5,1},{6,2},{7,3},{8,12},{9,13},{10,... | collective-permute-start | bytes 1572872 | tf_op jit(solution)/shard_map/ppermute | solution.py:47
  125.5 22.6 %collective-permute-start.32 = (bf16[60,2048]{1,0:T(8,128)(2,1)}, bf16[60,2048]{1,0:T(8,128)(2,1)S(1)}, u32[]{:S(2)}, u32[]{:S(2)}) collective-permute-start(bf16[60,2048]{1,0:T(8,128)(2,1)} %pad_maximum_fusion.7), channel_id=1, source_target_pairs={{0,4},{4,8},{8,12},{12,16},{16,20},{20,24},{24,28},{28,0},{1,5},{5... | collective-permute-start | bytes 737288 | tf_op jit(solution)/shard_map/ppermute | solution.py:51
  143.8 26.7 %collective-permute-start.35 = (bf16[128,2048]{1,0:T(8,128)(2,1)}, bf16[128,2048]{1,0:T(8,128)(2,1)}, u32[]{:S(2)}, u32[]{:S(2)}) collective-permute-start(bf16[128,2048]{1,0:T(8,128)(2,1)} %collective-permute-done.26.refs_8_), channel_id=1, source_target_pairs={{0,2},{1,3},{2,0},{3,1},{4,6},{5,7},{6,4},{7,5},{8,10},{9,11},{10,... | collective-permute-start | bytes 1572872 | tf_op jit(solution)/shard_map/ppermute | solution.py:47
  147.1 19.2 %collective-permute-start.30 = (bf16[128,1024]{1,0:T(8,128)(2,1)}, bf16[128,1024]{1,0:T(8,128)(2,1)}, u32[]{:S(2)}, u32[]{:S(2)}) collective-permute-start(bf16[128,1024]{1,0:T(8,128)(2,1)} %copy-done.66), channel_id=1, source_target_pairs={{0,1},{1,0},{2,3},{3,2},{4,5},{5,4},{6,7},{7,6},{8,9},{9,8},{10,11... | collective-permute-start | bytes 786440 | tf_op jit(solution)/shard_map/ppermute | solution.py:47
  148.1 18.3 %collective-permute-start.31 = (bf16[128,1024]{1,0:T(8,128)(2,1)}, bf16[128,1024]{1,0:T(8,128)(2,1)}, u32[]{:S(2)}, u32[]{:S(2)}) collective-permute-start(bf16[128,1024]{1,0:T(8,128)(2,1)} %copy-done.67), channel_id=1, source_target_pairs={{0,1},{1,0},{2,3},{3,2},{4,5},{5,4},{6,7},{7,6},{8,9},{9,8},{10,11... | collective-permute-start | bytes 786440 | tf_op jit(solution)/shard_map/ppermute | solution.py:47
  149.8 15.9 %collective-permute-start.28 = (bf16[64,1024]{1,0:T(8,128)(2,1)}, bf16[64,1024]{1,0:T(8,128)(2,1)}, u32[]{:S(2)}, u32[]{:S(2)}) collective-permute-start(bf16[64,1024]{1,0:T(8,128)(2,1)} %copy-done.64), channel_id=1, source_target_pairs={{0,1},{1,0},{2,3},{3,2},{4,5},{5,4},{6,7},{7,6},{8,9},{9,8},{10,11... | collective-permute-start | bytes 393224 | tf_op jit(solution)/shard_map/ppermute | solution.py:47
  165.7 11.9 %collective-permute-start.39 = (bf16[64,2048]{1,0:T(8,128)(2,1)}, bf16[64,2048]{1,0:T(8,128)(2,1)}, u32[]{:S(2)}, u32[]{:S(2)}) collective-permute-start(bf16[64,2048]{1,0:T(8,128)(2,1)} %copy-done.48), channel_id=1, source_target_pairs={{0,1},{1,0},{2,3},{3,2},{4,5},{5,4},{6,7},{7,6},{8,9},{9,8},{10,11... | collective-permute-start | bytes 786440 | tf_op jit(solution)/shard_map/ppermute | solution.py:47
  165.8 19.4 %collective-permute-start.40 = (bf16[64,2048]{1,0:T(8,128)(2,1)}, bf16[64,2048]{1,0:T(8,128)(2,1)}, u32[]{:S(2)}, u32[]{:S(2)}) collective-permute-start(bf16[64,2048]{1,0:T(8,128)(2,1)} %copy-done.50), channel_id=1, source_target_pairs={{0,1},{1,0},{2,3},{3,2},{4,5},{5,4},{6,7},{7,6},{8,9},{9,8},{10,11... | collective-permute-start | bytes 786440 | tf_op jit(solution)/shard_map/ppermute | solution.py:47
  166.3 18.9 %collective-permute-start.41 = (bf16[64,2048]{1,0:T(8,128)(2,1)}, bf16[64,2048]{1,0:T(8,128)(2,1)}, u32[]{:S(2)}, u32[]{:S(2)}) collective-permute-start(bf16[64,2048]{1,0:T(8,128)(2,1)} %copy-done.49), channel_id=1, source_target_pairs={{0,1},{1,0},{2,3},{3,2},{4,5},{5,4},{6,7},{7,6},{8,9},{9,8},{10,11... | collective-permute-start | bytes 786440 | tf_op jit(solution)/shard_map/ppermute | solution.py:47
  166.4 18.8 %collective-permute-start.42 = (bf16[128,2048]{1,0:T(8,128)(2,1)}, bf16[128,2048]{1,0:T(8,128)(2,1)}, u32[]{:S(2)}, u32[]{:S(2)}) collective-permute-start(bf16[128,2048]{1,0:T(8,128)(2,1)} %collective-permute-done.26.refs_8_), channel_id=1, source_target_pairs={{0,1},{1,0},{2,3},{3,2},{4,5},{5,4},{6,7},{7,6},{8,9},{9,8},{10,11... | collective-permute-start | bytes 1572872 | tf_op jit(solution)/shard_map/ppermute | solution.py:47
  170.5 14.6 %collective-permute-start.43 = (bf16[128,2048]{1,0:T(8,128)(2,1)}, bf16[128,2048]{1,0:T(8,128)(2,1)}, u32[]{:S(2)}, u32[]{:S(2)}) collective-permute-start(bf16[128,2048]{1,0:T(8,128)(2,1)} %collective-permute-done.35.refs_9_), channel_id=1, source_target_pairs={{0,1},{1,0},{2,3},{3,2},{4,5},{5,4},{6,7},{7,6},{8,9},{9,8},{10,11... | collective-permute-start | bytes 1572872 | tf_op jit(solution)/shard_map/ppermute | solution.py:47
  177.6 35.0 %collective-permute-start.44 = (bf16[256,1024]{1,0:T(8,128)(2,1)}, bf16[256,1024]{1,0:T(8,128)(2,1)}, u32[]{:S(2)}, u32[]{:S(2)}) collective-permute-start(bf16[256,1024]{1,0:T(8,128)(2,1)} %pad_maximum_fusion.1), channel_id=1, source_target_pairs={{0,4},{1,5},{2,6},{3,7},{4,0},{5,1},{6,2},{7,3},{8,12},{9,13},{10,... | collective-permute-start | bytes 1572872 | tf_op jit(solution)/shard_map/ppermute | solution.py:47
  212.6 13.2 %collective-permute-start.45 = (bf16[256,1024]{1,0:T(8,128)(2,1)}, bf16[256,1024]{1,0:T(8,128)(2,1)}, u32[]{:S(2)}, u32[]{:S(2)}) collective-permute-start(bf16[256,1024]{1,0:T(8,128)(2,1)} %collective-permute-done.44.refs_8_), channel_id=1, source_target_pairs={{0,2},{1,3},{2,0},{3,1},{4,6},{5,7},{6,4},{7,5},{8,10},{9,11},{10,... | collective-permute-start | bytes 1572872 | tf_op jit(solution)/shard_map/ppermute | solution.py:47
  225.8 25.3 %collective-permute-start.51 = (bf16[8,128,1024]{2,1,0:T(8,128)(2,1)}, bf16[8,128,1024]{2,1,0:T(8,128)(2,1)}, u32[]{:S(2)}, u32[]{:S(2)}) collective-permute-start(bf16[8,128,1024]{2,1,0:T(8,128)(2,1)} %dynamic-slice_bitcast_fusion.1), channel_id=1, source_target_pairs={{0,1},{1,0},{2,3},{3,2},{4,5},{5,4},{6,7},{7,6},{8,9},{9,8},{10,11... | collective-permute-start | bytes 6291464 | tf_op jit(solution)/shard_map/ppermute | solution.py:47
  263.3 24.9 %collective-permute-start.53 = (bf16[4,128,1024]{2,1,0:T(8,128)(2,1)}, bf16[4,128,1024]{2,1,0:T(8,128)(2,1)}, u32[]{:S(2)}, u32[]{:S(2)}) collective-permute-start(bf16[4,128,1024]{2,1,0:T(8,128)(2,1)} %dynamic-slice_bitcast_fusion.6), channel_id=1, source_target_pairs={{0,4},{1,5},{2,6},{3,7},{4,0},{5,1},{6,2},{7,3},{8,12},{9,13},{10,... | collective-permute-start | bytes 3145736 | tf_op jit(solution)/shard_map/ppermute | solution.py:47
  279.1 14.8 %collective-permute-start.54 = (bf16[8,64,1024]{2,1,0:T(8,128)(2,1)}, bf16[8,64,1024]{2,1,0:T(8,128)(2,1)}, u32[]{:S(2)}, u32[]{:S(2)}) collective-permute-start(bf16[8,64,1024]{2,1,0:T(8,128)(2,1)} %dynamic-slice_bitcast_fusion.4), channel_id=1, source_target_pairs={{0,1},{1,0},{2,3},{3,2},{4,5},{5,4},{6,7},{7,6},{8,9},{9,8},{10,11... | collective-permute-start | bytes 3145736 | tf_op jit(solution)/shard_map/ppermute | solution.py:47
  286.2 24.9 %collective-permute-start.55 = (bf16[8,32,2048]{2,1,0:T(8,128)(2,1)}, bf16[8,32,2048]{2,1,0:T(8,128)(2,1)}, u32[]{:S(2)}, u32[]{:S(2)}) collective-permute-start(bf16[8,32,2048]{2,1,0:T(8,128)(2,1)} %dynamic-slice_bitcast_fusion.5), channel_id=1, source_target_pairs={{0,2},{1,3},{2,0},{3,1},{4,6},{5,7},{6,4},{7,5},{8,10},{9,11},{10,... | collective-permute-start | bytes 3145736 | tf_op jit(solution)/shard_map/ppermute | solution.py:47
  297.9 55.4 %collective-permute-start.62 = (bf16[4,64,1024]{2,1,0:T(8,128)(2,1)}, bf16[4,64,1024]{2,1,0:T(8,128)(2,1)}, u32[]{:S(2)}, u32[]{:S(2)}) collective-permute-start(bf16[4,64,1024]{2,1,0:T(8,128)(2,1)} %dynamic-slice_bitcast_fusion.10), channel_id=1, source_target_pairs={{0,4},{1,5},{2,6},{3,7},{4,0},{5,1},{6,2},{7,3},{8,12},{9,13},{10,... | collective-permute-start | bytes 1572872 | tf_op jit(solution)/shard_map/ppermute | solution.py:47
  297.9 54.0 %collective-permute-start.59 = (bf16[128,1024]{1,0:T(8,128)(2,1)}, bf16[128,1024]{1,0:T(8,128)(2,1)}, u32[]{:S(2)}, u32[]{:S(2)}) collective-permute-start(bf16[128,1024]{1,0:T(8,128)(2,1)} %get-tuple-element.157), channel_id=1, source_target_pairs={{0,8},{1,9},{2,10},{3,11},{4,12},{5,13},{6,14},{7,15},{8,16},{9,17... | collective-permute-start | bytes 786440 | tf_op jit(solution)/shard_map/ppermute | solution.py:47
  309.6 16.6 %collective-permute-start.56 = (bf16[2,60,1024]{2,1,0:T(8,128)(2,1)}, bf16[2,60,1024]{2,1,0:T(8,128)(2,1)}, u32[]{:S(2)}, u32[]{:S(2)}) collective-permute-start(bf16[2,60,1024]{2,1,0:T(8,128)(2,1)} %get-tuple-element.154), channel_id=1, source_target_pairs={{0,28},{4,0},{8,4},{12,8},{16,12},{20,16},{24,20},{28,24},{1,29},{... | collective-permute-start | bytes 737288 | tf_op jit(solution)/shard_map/ppermute | solution.py:51
  311.1 18.4 %collective-permute-start.57 = (bf16[2,60,1024]{2,1,0:T(8,128)(2,1)}, bf16[2,60,1024]{2,1,0:T(8,128)(2,1)}, u32[]{:S(2)}, u32[]{:S(2)}) collective-permute-start(bf16[2,60,1024]{2,1,0:T(8,128)(2,1)} %get-tuple-element.155), channel_id=1, source_target_pairs={{0,24},{4,28},{8,0},{12,4},{16,8},{20,12},{24,16},{28,20},{1,25},{... | collective-permute-start | bytes 737288 | tf_op jit(solution)/shard_map/ppermute | solution.py:51
  311.1 37.9 %collective-permute-start.58 = (bf16[2,60,1024]{2,1,0:T(8,128)(2,1)}, bf16[2,60,1024]{2,1,0:T(8,128)(2,1)}, u32[]{:S(2)}, u32[]{:S(2)}) collective-permute-start(bf16[2,60,1024]{2,1,0:T(8,128)(2,1)} %get-tuple-element.156), channel_id=1, source_target_pairs={{0,20},{4,24},{8,28},{12,0},{16,4},{20,8},{24,12},{28,16},{1,21},{... | collective-permute-start | bytes 737288 | tf_op jit(solution)/shard_map/ppermute | solution.py:51
  326.2 25.7 %collective-permute-start.60 = (bf16[128,1024]{1,0:T(8,128)(2,1)}, bf16[128,1024]{1,0:T(8,128)(2,1)S(1)}, u32[]{:S(2)}, u32[]{:S(2)}) collective-permute-start(bf16[128,1024]{1,0:T(8,128)(2,1)} %get-tuple-element.158), channel_id=1, source_target_pairs={{0,16},{1,17},{2,18},{3,19},{4,20},{5,21},{6,22},{7,23},{8,24},{9,... | collective-permute-start | bytes 786440 | tf_op jit(solution)/shard_map/ppermute | solution.py:47
  329.4 22.5 %collective-permute-start.61 = (bf16[128,1024]{1,0:T(8,128)(2,1)S(1)}, bf16[128,1024]{1,0:T(8,128)(2,1)S(1)}, u32[]{:S(2)}, u32[]{:S(2)}) collective-permute-start(bf16[128,1024]{1,0:T(8,128)(2,1)S(1)} %get-tuple-element.159), channel_id=1, source_target_pairs={{0,24},{1,25},{2,26},{3,27},{4,28},{5,29},{6,30},{7,31},{8,0},{9,1... | collective-permute-start | bytes 786440 | tf_op jit(solution)/shard_map/ppermute | solution.py:47
  349.0 13.1 %collective-permute-start.63 = (bf16[4,32,2048]{2,1,0:T(8,128)(2,1)}, bf16[4,32,2048]{2,1,0:T(8,128)(2,1)S(1)}, u32[]{:S(2)}, u32[]{:S(2)}) collective-permute-start(bf16[4,32,2048]{2,1,0:T(8,128)(2,1)} %dynamic-slice_bitcast_fusion.9), channel_id=1, source_target_pairs={{0,4},{1,5},{2,6},{3,7},{4,0},{5,1},{6,2},{7,3},{8,12},{9,13},{10,... | collective-permute-start | bytes 1572872 | tf_op jit(solution)/shard_map/ppermute | solution.py:47
  369.2 36.4 %collective-permute-start.64 = (bf16[8,64,1536]{2,1,0:T(8,128)(2,1)}, bf16[8,64,1536]{2,1,0:T(8,128)(2,1)}, u32[]{:S(2)}, u32[]{:S(2)}) collective-permute-start(bf16[8,64,1536]{2,1,0:T(8,128)(2,1)} %dynamic-slice_bitcast_fusion.3), channel_id=1, source_target_pairs={{0,1},{1,0},{2,3},{3,2},{4,5},{5,4},{6,7},{7,6},{8,9},{9,8},{10,11... | collective-permute-start | bytes 4718600 | tf_op jit(solution)/shard_map/ppermute | solution.py:47
  375.3 29.3 %collective-permute-start.65 = (bf16[128,1024]{1,0:T(8,128)(2,1)S(1)}, bf16[128,1024]{1,0:T(8,128)(2,1)}, u32[]{:S(2)}, u32[]{:S(2)}) collective-permute-start(bf16[128,1024]{1,0:T(8,128)(2,1)S(1)} %fusion.36), channel_id=1, source_target_pairs={{0,2},{1,3},{2,0},{3,1},{4,6},{5,7},{6,4},{7,5},{8,10},{9,11},{10,... | collective-permute-start | bytes 786440 | tf_op jit(solution)/shard_map/ppermute | solution.py:47
  376.1 13.2 %collective-permute-start.66 = (bf16[32,2048]{1,0:T(8,128)(2,1)}, bf16[32,2048]{1,0:T(8,128)(2,1)}, u32[]{:S(2)}, u32[]{:S(2)}) collective-permute-start(bf16[32,2048]{1,0:T(8,128)(2,1)} %get-tuple-element.167), channel_id=1, source_target_pairs={{0,8},{1,9},{2,10},{3,11},{4,12},{5,13},{6,14},{7,15},{8,16},{9,17... | collective-permute-start | bytes 393224 | tf_op jit(solution)/shard_map/ppermute | solution.py:47
  376.1 15.3 %collective-permute-start.67 = (bf16[32,2048]{1,0:T(8,128)(2,1)}, bf16[32,2048]{1,0:T(8,128)(2,1)}, u32[]{:S(2)}, u32[]{:S(2)}) collective-permute-start(bf16[32,2048]{1,0:T(8,128)(2,1)} %get-tuple-element.168), channel_id=1, source_target_pairs={{0,16},{1,17},{2,18},{3,19},{4,20},{5,21},{6,22},{7,23},{8,24},{9,... | collective-permute-start | bytes 393224 | tf_op jit(solution)/shard_map/ppermute | solution.py:47
  376.1 15.6 %collective-permute-start.68 = (bf16[32,2048]{1,0:T(8,128)(2,1)}, bf16[32,2048]{1,0:T(8,128)(2,1)}, u32[]{:S(2)}, u32[]{:S(2)}) collective-permute-start(bf16[32,2048]{1,0:T(8,128)(2,1)} %get-tuple-element.169), channel_id=1, source_target_pairs={{0,24},{1,25},{2,26},{3,27},{4,28},{5,29},{6,30},{7,31},{8,0},{9,1... | collective-permute-start | bytes 393224 | tf_op jit(solution)/shard_map/ppermute | solution.py:47
  391.4 12.2 %collective-permute-start.70 = (bf16[64,1024]{1,0:T(8,128)(2,1)}, bf16[64,1024]{1,0:T(8,128)(2,1)S(1)}, u32[]{:S(2)}, u32[]{:S(2)}) collective-permute-start(bf16[64,1024]{1,0:T(8,128)(2,1)} %get-tuple-element.171), channel_id=1, source_target_pairs={{0,16},{1,17},{2,18},{3,19},{4,20},{5,21},{6,22},{7,23},{8,24},{9,... | collective-permute-start | bytes 393224 | tf_op jit(solution)/shard_map/ppermute | solution.py:47
  408.2 20.2 %collective-permute-start.101 = (bf16[128,1024]{1,0:T(8,128)(2,1)S(1)}, bf16[128,1024]{1,0:T(8,128)(2,1)S(1)}, u32[]{:S(2)}, u32[]{:S(2)}) collective-permute-start(bf16[128,1024]{1,0:T(8,128)(2,1)S(1)} %add_convert_fusion.5), channel_id=1, source_target_pairs={{0,1},{1,0},{2,3},{3,2},{4,5},{5,4},{6,7},{7,6},{8,9},{9,8},{10,11... | collective-permute-start | bytes 786440 | tf_op jit(solution)/shard_map/ppermute | solution.py:47
  414.0 13.8 %collective-permute-start.75 = (bf16[64,1024]{1,0:T(8,128)(2,1)S(1)}, bf16[64,1024]{1,0:T(8,128)(2,1)S(1)}, u32[]{:S(2)}, u32[]{:S(2)}) collective-permute-start(bf16[64,1024]{1,0:T(8,128)(2,1)S(1)} %fusion.43), channel_id=1, source_target_pairs={{0,2},{1,3},{2,0},{3,1},{4,6},{5,7},{6,4},{7,5},{8,10},{9,11},{10,... | collective-permute-start | bytes 393224 | tf_op jit(solution)/shard_map/ppermute | solution.py:47
  414.8 12.1 %collective-permute-start.74 = (bf16[32,2048]{1,0:T(8,128)(2,1)S(1)}, bf16[32,2048]{1,0:T(8,128)(2,1)S(1)}, u32[]{:S(2)}, u32[]{:S(2)}) collective-permute-start(bf16[32,2048]{1,0:T(8,128)(2,1)S(1)} %fusion.46), channel_id=1, source_target_pairs={{0,2},{1,3},{2,0},{3,1},{4,6},{5,7},{6,4},{7,5},{8,10},{9,11},{10,... | collective-permute-start | bytes 393224 | tf_op jit(solution)/shard_map/ppermute | solution.py:47
  415.5 18.5 %collective-permute-start.73 = (bf16[4,64,1536]{2,1,0:T(8,128)(2,1)S(1)}, bf16[4,64,1536]{2,1,0:T(8,128)(2,1)S(1)}, u32[]{:S(2)}, u32[]{:S(2)}) collective-permute-start(bf16[4,64,1536]{2,1,0:T(8,128)(2,1)S(1)} %dynamic-slice_bitcast_fusion.8), channel_id=1, source_target_pairs={{0,4},{1,5},{2,6},{3,7},{4,0},{5,1},{6,2},{7,3},{8,12},{9,13},{10,... | collective-permute-start | bytes 2359304 | tf_op jit(solution)/shard_map/ppermute | solution.py:47
  415.5 19.6 %collective-permute-start.72 = (bf16[8,64,1536]{2,1,0:T(8,128)(2,1)S(1)}, bf16[8,64,1536]{2,1,0:T(8,128)(2,1)S(1)}, u32[]{:S(2)}, u32[]{:S(2)}) collective-permute-start(bf16[8,64,1536]{2,1,0:T(8,128)(2,1)S(1)} %dynamic-slice_bitcast_fusion.2), channel_id=1, source_target_pairs={{0,1},{1,0},{2,3},{3,2},{4,5},{5,4},{6,7},{7,6},{8,9},{9,8},{10,11... | collective-permute-start | bytes 4718600 | tf_op jit(solution)/shard_map/ppermute | solution.py:47
  441.9 37.2 %collective-permute-start.80 = (bf16[8,104,128]{2,1,0:T(8,128)(2,1)}, bf16[8,104,128]{2,1,0:T(8,128)(2,1)}, u32[]{:S(2)}, u32[]{:S(2)}) collective-permute-start(bf16[8,104,128]{2,1,0:T(8,128)(2,1)} %pad_maximum_fusion.9), channel_id=1, source_target_pairs={{0,1},{1,0},{2,3},{3,2},{4,5},{5,4},{6,7},{7,6},{8,9},{9,8},{10,11... | collective-permute-start | bytes 638984 | tf_op jit(solution)/shard_map/ppermute | solution.py:47
  443.4 36.6 %collective-permute-start.81 = (bf16[8,104,128]{2,1,0:T(8,128)(2,1)}, bf16[8,104,128]{2,1,0:T(8,128)(2,1)}, u32[]{:S(2)}, u32[]{:S(2)}) collective-permute-start(bf16[8,104,128]{2,1,0:T(8,128)(2,1)} %pad_maximum_fusion.9), channel_id=1, source_target_pairs={{0,2},{1,3},{2,0},{3,1},{4,6},{5,7},{6,4},{7,5},{8,10},{9,11},{10,... | collective-permute-start | bytes 638984 | tf_op jit(solution)/shard_map/ppermute | solution.py:47
  447.1 14.3 %collective-permute-start.99 = (bf16[64,1024]{1,0:T(8,128)(2,1)}, bf16[64,1024]{1,0:T(8,128)(2,1)S(1)}, u32[]{:S(2)}, u32[]{:S(2)}) collective-permute-start(bf16[64,1024]{1,0:T(8,128)(2,1)} %add_convert_fusion.9), channel_id=1, source_target_pairs={{0,1},{1,0},{2,3},{3,2},{4,5},{5,4},{6,7},{7,6},{8,9},{9,8},{10,11... | collective-permute-start | bytes 393224 | tf_op jit(solution)/shard_map/ppermute | solution.py:47
  458.6 15.9 %collective-permute-start.88 = (bf16[64,1536]{1,0:T(8,128)(2,1)}, bf16[64,1536]{1,0:T(8,128)(2,1)S(1)}, u32[]{:S(2)}, u32[]{:S(2)}) collective-permute-start(bf16[64,1536]{1,0:T(8,128)(2,1)} %get-tuple-element.180), channel_id=1, source_target_pairs={{0,16},{1,17},{2,18},{3,19},{4,20},{5,21},{6,22},{7,23},{8,24},{9,... | collective-permute-start | bytes 589832 | tf_op jit(solution)/shard_map/ppermute | solution.py:47
  461.4 15.9 %collective-permute-start.89 = (bf16[64,1536]{1,0:T(8,128)(2,1)}, bf16[64,1536]{1,0:T(8,128)(2,1)S(1)}, u32[]{:S(2)}, u32[]{:S(2)}) collective-permute-start(bf16[64,1536]{1,0:T(8,128)(2,1)} %get-tuple-element.181), channel_id=1, source_target_pairs={{0,24},{1,25},{2,26},{3,27},{4,28},{5,29},{6,30},{7,31},{8,0},{9,1... | collective-permute-start | bytes 589832 | tf_op jit(solution)/shard_map/ppermute | solution.py:47
  463.2 16.7 %collective-permute-start.82 = (bf16[8,104,128]{2,1,0:T(8,128)(2,1)}, bf16[8,104,128]{2,1,0:T(8,128)(2,1)S(1)}, u32[]{:S(2)}, u32[]{:S(2)}) collective-permute-start(bf16[8,104,128]{2,1,0:T(8,128)(2,1)} %pad_maximum_fusion.9), channel_id=1, source_target_pairs={{0,3},{1,2},{2,1},{3,0},{4,7},{5,6},{6,5},{7,4},{8,11},{9,10},{10,... | collective-permute-start | bytes 638984 | tf_op jit(solution)/shard_map/ppermute | solution.py:47
  477.4 19.3 %collective-permute-start.92 = (bf16[8,32,1536]{2,1,0:T(8,128)(2,1)}, bf16[8,32,1536]{2,1,0:T(8,128)(2,1)S(1)}, u32[]{:S(2)}, u32[]{:S(2)}) collective-permute-start(bf16[8,32,1536]{2,1,0:T(8,128)(2,1)} %dynamic-slice_bitcast_fusion.7), channel_id=1, source_target_pairs={{0,2},{1,3},{2,0},{3,1},{4,6},{5,7},{6,4},{7,5},{8,10},{9,11},{10,... | collective-permute-start | bytes 2359304 | tf_op jit(solution)/shard_map/ppermute | solution.py:47
  479.2 43.0 %collective-permute-start.90 = (bf16[64,1536]{1,0:T(8,128)(2,1)S(1)}, bf16[64,1536]{1,0:T(8,128)(2,1)S(1)}, u32[]{:S(2)}, u32[]{:S(2)}) collective-permute-start(bf16[64,1536]{1,0:T(8,128)(2,1)S(1)} %fusion.39), channel_id=1, source_target_pairs={{0,2},{1,3},{2,0},{3,1},{4,6},{5,7},{6,4},{7,5},{8,10},{9,11},{10,... | collective-permute-start | bytes 589832 | tf_op jit(solution)/shard_map/ppermute | solution.py:47
  485.3 12.8 %collective-permute-start.84 = (bf16[104,128]{1,0:T(8,128)(2,1)S(1)}, bf16[104,128]{1,0:T(8,128)(2,1)S(1)}, u32[]{:S(2)}, u32[]{:S(2)}) collective-permute-start(bf16[104,128]{1,0:T(8,128)(2,1)S(1)} %get-tuple-element.273), channel_id=1, source_target_pairs={{0,8},{1,9},{2,10},{3,11},{4,12},{5,13},{6,14},{7,15},{8,16},{9,17... | collective-permute-start | bytes 79880 | tf_op jit(solution)/shard_map/ppermute | solution.py:47
  485.4 12.7 %collective-permute-start.85 = (bf16[104,128]{1,0:T(8,128)(2,1)S(1)}, bf16[104,128]{1,0:T(8,128)(2,1)S(1)}, u32[]{:S(2)}, u32[]{:S(2)}) collective-permute-start(bf16[104,128]{1,0:T(8,128)(2,1)S(1)} %get-tuple-element.275), channel_id=1, source_target_pairs={{0,16},{1,17},{2,18},{3,19},{4,20},{5,21},{6,22},{7,23},{8,24},{9,... | collective-permute-start | bytes 79880 | tf_op jit(solution)/shard_map/ppermute | solution.py:47
  506.6 14.8 %collective-permute-start.95 = (bf16[32,1536]{1,0:T(8,128)(2,1)S(1)}, bf16[32,1536]{1,0:T(8,128)(2,1)S(1)}, u32[]{:S(2)}, u32[]{:S(2)}) collective-permute-start(bf16[32,1536]{1,0:T(8,128)(2,1)S(1)} %get-tuple-element.254), channel_id=1, source_target_pairs={{0,16},{1,17},{2,18},{3,19},{4,20},{5,21},{6,22},{7,23},{8,24},{9,... | collective-permute-start | bytes 294920 | tf_op jit(solution)/shard_map/ppermute | solution.py:47
  (138 other events, 1360.3 us)

commit v3 on v2

--- a/solution.py
+++ b/solution.py
@@ -139,21 +139,21 @@
     )(info, shard, *parts)
 
 
-def gather_stages(place, info, shard):
-    if not place.tuned:
-        return lax.all_gather(shard, "fsdp", axis=0, tiled=True)
-    half, quarter = shard.shape[0] // 2, shard.shape[0] // 4
-    own = lax.dynamic_slice_in_dim(shard, place.c * half, half, 0)
-    piece = lambda a: lax.dynamic_slice_in_dim(a, place.x * quarter, quarter, 0)
-    a = yield [(own, dict(line=k)) for k in (1, 2, 3)]
-    mine = jnp.concatenate([piece(m) for m in (own, *a)], 0)
-    b1, *n = yield [(mine, dict(pair=1))] + [(m, dict(core=1)) for m in a]
-    b2, m1 = yield [(b1, dict(side=1)), (b1, dict(core=1))]
-    (m2,) = yield [(b2, dict(core=1))]
-    return assemble(info, shard, [*a, *n], [b1, b2, m1, m2])
-
-
-def gather_first(place, info, shard, chains):
+def gather_rest(place, heads_out, expand, reduce):
+    dp = place.dp
+    wide = heads_out.shape[1]
+    pieces = [heads_out, reduce] + [expand[:, i : i + wide] for i in range(0, expand.shape[1], wide)]
+    mine = lambda a: pick(a.reshape(dp, -1, wide), lax.axis_index("dp"), 0)
+    every = lax.all_gather(jnp.concatenate([mine(a) for a in pieces], 0), AXES, axis=0)
+    whole, low = [], 0
+    for a in pieces:
+        high = low + a.shape[0] // dp
+        whole.append(every[:, low:high].reshape(-1, wide))
+        low = high
+    return whole[0], jnp.concatenate(whole[2:], 1), whole[1]
+
+
+def gather_first(place, info, shard):
     if not place.tuned:
         return lax.all_gather(shard, "fsdp", axis=0, tiled=True)
     half, quarter = shard.shape[0] // 2, shard.shape[0] // 4
@@ -164,29 +164,19 @@
     b01 = move(jnp.concatenate([piece(own), piece(a1)], 0), pair=1)
     a2 = move(a1, line=1)
     n1 = move(a1, core=1)
-    a2 = tied(a2, chains[0])
     a3 = move(a2, line=1)
     x01 = move(b01, side=1)
     n2, m01 = move(a2, core=1), move(b01, core=1)
-    a3 = tied(a3, chains[1])
     b23 = move(jnp.concatenate([piece(a2), piece(a3)], 0), pair=1)
     n3, w01 = move(a3, core=1), move(x01, core=1)
-    b23 = tied(b23, chains[2])
     x23, m23 = move(b23, side=1), move(b23, core=1)
     w23 = move(x23, core=1)
     return assemble(info, shard, [a1, a2, a3, n1, n2, n3], [b01, b23, x01, x23, m01, m23, w01, w23])
 
 
 def gather_small(place, packed):
-    if not place.tuned:
-        return lax.all_gather(packed, "fsdp", axis=0, tiled=False)
-    other = place.move(packed, pair=1)
-    low = jnp.where(place.y == 0, packed, other)
-    high = jnp.where(place.y == 0, other, packed)
-    both = jnp.stack([low, high])
-    steps = jnp.stack([both] + [place.move(both, line=k) for k in (1, 2, 3)])
-    ordered = [pick(steps, (place.z + 4 - line) % 4, 0) for line in range(4)]
-    return jnp.concatenate(ordered, 0)
+    copies = jnp.broadcast_to(packed, (place.fsdp,) + packed.shape)
+    return lax.all_to_all(copies, "fsdp", 0, 0, tiled=True)
 
 
 def plus(a, *others):
@@ -196,18 +186,21 @@
     return total.astype(BF16)
 
 
-def reduce_stages(place, grad, side_first):
+def reduce_stages(place, grads, side_first):
     if not place.tuned:
-        part = lax.psum_scatter(grad.astype(F32), "fsdp", scatter_dimension=0, tiled=True)
-        return lax.psum(part.astype(BF16), "dp").astype(F32)
-    rows, columns = grad.shape[0] // 8, grad.shape[1]
-    half, quarter = rows // 2, rows // 4
+        parts = [
+            lax.psum_scatter(g.astype(F32), "fsdp", scatter_dimension=0, tiled=True) for g in grads
+        ]
+        return [lax.psum(part.astype(BF16), "dp").astype(F32) for part in parts]
     z, y, x, c = place.z, place.y, place.x, place.c
-    value = grad.reshape(8, 2, half, columns)
-    (got,) = yield [(pick(value, 1 - c, 1), dict(core=1))]
-    value = plus(pick(value, c, 1), got)
+    columns = grads[0].shape[1]
+    views = [g.reshape(8, 2, -1, columns) for g in grads]
+    got = yield [(pick(view, 1 - c, 1), dict(core=1)) for view in views]
+    value = [plus(pick(view, c, 1), other) for view, other in zip(views, got)]
+    value = value[0] if len(value) == 1 else jnp.concatenate(value, 1)
+    half = value.shape[1]
     if side_first:
-        value = value.reshape(8, 2, quarter, columns)
+        value = value.reshape(8, 2, half // 2, columns)
         (got,) = yield [(pick(value, 1 - x, 1), dict(side=1))]
         value = plus(pick(value, x, 1), got)
     value = value.reshape(4, 2, *value.shape[1:])
@@ -223,25 +216,17 @@
         value = plus(value, got)
     (got,) = yield [(value, dict(core=1))]
     low, high = jnp.where(c == 0, value, got), jnp.where(c == 0, got, value)
-    return jnp.concatenate([low, high], 0).astype(F32)
-
-
-def reduce_small(place, packed):
-    if not place.tuned:
-        part = lax.psum_scatter(packed, "fsdp", scatter_dimension=0, tiled=True)[0]
-        return lax.psum(part, "dp")
-    z, y = place.z, place.y
-    packed = packed.astype(BF16)
-    one = packed.astype(F32)
-    for side, core in ((0, 1), (1, 0), (1, 1)):
-        one = one + place.move(packed, side=side, core=core).astype(F32)
-    one = one.astype(BF16).reshape(4, 2, *packed.shape[1:])
-    got = place.move(pick(one, 1 - y, 1), pair=1)
-    two = (pick(one, y, 1).astype(F32) + got.astype(F32)).astype(BF16)
-    three = pick(two, z, 0).astype(F32)
-    for k in (1, 2, 3):
-        three = three + place.move(pick(two, (z + k) % 4, 0), line=k).astype(F32)
-    return three
+    results, row = [], 0
+    for view in views:
+        rows = slice(row, row + view.shape[2])
+        results.append(jnp.concatenate([low[rows], high[rows]], 0).astype(F32))
+        row += view.shape[2]
+    return results
+
+
+def sum_replicas(place, part):
+    copies = jnp.broadcast_to(part, (place.dp,) + part.shape)
+    return jnp.sum(lax.all_to_all(copies, "dp", 0, 0, tiled=True), 0)
 
 
 def layer_norm(inputs, gain_row, shift_row):
@@ -299,8 +284,7 @@
     )
 
 
-def short_forward(projected):
-    rows = projected.shape[0]
+def short_forward(projected, rows):
     short_rows = SHORT_SLOTS * SPAN
     return pl.pallas_call(
         short_forward_kernel,
@@ -343,7 +327,7 @@
 
 
 def short_backward(projected, grad_mixture, group):
-    rows = projected.shape[0]
+    rows = grad_mixture.shape[0]
     short_rows = SHORT_SLOTS * SPAN
     block = lambda first: pl.BlockSpec((short_rows, HEAD_DIM), lambda h: (0, first + h))
     return pl.pallas_call(
@@ -503,15 +487,9 @@
     expand_shift = small[:, PATCH + 6 : small_rows].reshape(-1)
 
     mixed_columns = heads_in.reshape(-1, 3, GROUPS, GROUP * HEAD_DIM).transpose(0, 2, 1, 3)
-    gather_out, gather_expand, gather_reduce = [
-        Chain(place, gather_stages(place, info, shard))
-        for shard in (heads_out, expand_weight, reduce_weight_shard)
-    ]
-    heads_in_all = gather_first(
-        place,
-        info,
-        mixed_columns.reshape(-1, 3 * D),
-        (gather_out, gather_expand, gather_reduce),
+    heads_in_all = gather_first(place, info, mixed_columns.reshape(-1, 3 * D))
+    heads_out_all, expand_all, reduce_all = gather_rest(
+        place, heads_out, expand_weight, reduce_weight_shard
     )
 
     totals = jnp.concatenate([slot_sums[:SHORT_SLOTS], chain_sum], 0)
@@ -525,53 +503,48 @@
     embedded = dot_n(normed_low, patch_all) + biases_all[0]
     first_value, first_back = jax.vjp(layer_norm, embedded, gains_all[0], biases_all[1])
     first_norm = first_value.astype(BF16)
-    heads_in_all = tied(heads_in_all, gather_out)
-    projected = dot_n(first_norm, heads_in_all).astype(BF16)
-    projected = tied(projected, gather_out, gather_expand)
-
-    own_long = projected[short_rows:]
+    own_long = dot_n(first_norm[short_rows:], heads_in_all).astype(BF16)
+
     group_columns = lambda g, low, high: slice(
         (g * 3 + low) * GROUP * HEAD_DIM, (g * 3 + high) * GROUP * HEAD_DIM
     )
     long_pairs = jnp.concatenate([own_long[:, group_columns(g, 1, 3)] for g in range(GROUPS)], 1)
     priors = [place.along(long_pairs, step) for step in (1, 2, 3)]
-    mixed_short = short_forward(projected)
-    own_long, mixed_short = tied((own_long, mixed_short), gather_out, gather_expand)
+    first_norm_short, heads_in_all = lax.optimization_barrier(
+        (first_norm[:short_rows], heads_in_all, long_pairs)
+    )[:2]
+    projected = dot_n(first_norm_short, heads_in_all).astype(BF16)
+    projected, priors = lax.optimization_barrier((projected, priors))
+    mixed_short = short_forward(projected, row_count)
     mixed_long = long_forward(quarter_index, own_long, priors)
-    heads_out_all = gather_out.finish()
-    heads_out_all, mixed_long = tied((heads_out_all, mixed_long), gather_expand, gather_reduce)
     mixed_all = lax.dynamic_update_slice(mixed_short, mixed_long, (short_rows, 0))
     middle = embedded + dot_n(mixed_all, heads_out_all)
     second_value, second_back = jax.vjp(layer_norm, middle, gains_all[1], biases_all[2])
     second_norm = second_value.astype(BF16)
 
-    expand_all = gather_expand.finish()
     pre_act = dot_n(second_norm, expand_all) + expand_shift
     act_value, gelu_back = jax.vjp(exact_gelu, pre_act)
-    activation = tied(act_value.astype(BF16), gather_reduce)
+    activation = act_value.astype(BF16)
     grad_reduce = Chain(
-        place, reduce_stages(place, dot_l(activation, cotangent).astype(BF16), False)
-    )
-    cotangent = tied(cotangent, gather_reduce, grad_reduce)
-    reduce_all = gather_reduce.finish()
+        place, reduce_stages(place, [dot_l(activation, cotangent).astype(BF16)], False)
+    )
+    cotangent = tied(cotangent, grad_reduce)
 
     grad_act = dot_t(cotangent, reduce_all)
     grad_pre = tied(gelu_back(grad_act)[0].astype(BF16), grad_reduce)
-    grad_expand = Chain(
-        place, reduce_stages(place, dot_l(second_norm, grad_pre).astype(BF16), True)
-    )
+    grad_expand = dot_l(second_norm, grad_pre).astype(BF16)
     grad_expand_bias = jnp.sum(grad_pre.astype(F32), 0)
-    expand_all = tied(expand_all, grad_expand)
     grad_second = dot_t(grad_pre, expand_all)
     middle_back, gain_two, shift_two = second_back(grad_second)
     grad_middle = cotangent.astype(F32) + middle_back
-    grad_branch = tied(grad_middle.astype(BF16), grad_expand)
-    grad_heads_out = Chain(
-        place, reduce_stages(place, dot_l(mixed_all, grad_branch).astype(BF16), False)
-    )
-    heads_out_all = tied(heads_out_all, grad_heads_out)
+    grad_branch = grad_middle.astype(BF16)
+    grad_heads_out = dot_l(mixed_all, grad_branch).astype(BF16)
+    grad_rest = Chain(
+        place, reduce_stages(place, [grad_expand[:, :D], grad_expand[:, D:], grad_heads_out], True)
+    )
+    heads_out_all = tied(heads_out_all, grad_rest)
     grad_mixture = dot_t(grad_branch, heads_out_all).astype(BF16)
-    grad_mixture, activation = tied((grad_mixture, activation), grad_reduce, grad_heads_out)
+    grad_mixture, activation = tied((grad_mixture, activation), grad_rest, grad_reduce)
     layer_output = (middle + dot_n(activation, reduce_all) + biases_all[3]).astype(BF16)
 
     long_query, own_grads, *sent = long_backward(
@@ -587,23 +560,41 @@
         short = short_backward(projected, grad_mixture, g)
         return lax.dynamic_update_slice(short, grad_long, (short_rows, 0))
 
-    grad_mixture, long_query = tied((grad_mixture, long_query), grad_expand)
-    low_grad = tied(grad_group(0, grad_mixture), grad_reduce, grad_heads_out)
-    grad_low = Chain(place, reduce_stages(place, dot_l(first_norm, low_grad).astype(BF16), False))
-    grad_mixture = tied(grad_mixture, grad_low, grad_expand)
-    high_grad = tied(grad_group(1, grad_mixture), grad_low, grad_reduce)
-    grad_high = Chain(place, reduce_stages(place, dot_l(first_norm, high_grad).astype(BF16), True))
-    heads_in_all = tied(heads_in_all, grad_high, grad_expand, grad_heads_out)
+    low_grad = tied(grad_group(0, grad_mixture), grad_reduce)
+    grad_low = Chain(place, reduce_stages(place, [dot_l(first_norm, low_grad).astype(BF16)], False))
+    grad_mixture = tied(grad_mixture, grad_low)
+    high_grad = tied(grad_group(1, grad_mixture), grad_low, grad_reduce, grad_rest)
+    grad_high = Chain(
+        place, reduce_stages(place, [dot_l(first_norm, high_grad).astype(BF16)], True)
+    )
+    heads_in_all = tied(heads_in_all, grad_high)
     grad_first = dot_t(low_grad, heads_in_all[:, :WIDE]) + dot_t(high_grad, heads_in_all[:, WIDE:])
     embed_back, gain_one, shift_one = first_back(grad_first)
     grad_embedded = (grad_middle + embed_back).astype(BF16)
-    grad_embedded = tied(grad_embedded, grad_high, grad_low, grad_expand, grad_heads_out)
+    grad_embedded = tied(grad_embedded, grad_high)
     grad_patch = dot_l(normed_low, grad_embedded)
     shift_zero = jnp.sum(grad_embedded.astype(F32), 0)
     grad_normed = dot_t(grad_embedded, patch_all).reshape(slot_count, SPAN * PATCH)
     slot_grads = jnp.stack([jnp.sum(grad_normed, 1), jnp.sum(grad_normed * normed_slots, 1)], 1)
-    chain_grads = gather_small(place, slot_grads[SHORT_SLOTS:])
+    shift_three = jnp.sum(cotangent.astype(F32), 0)
+    split = lambda a: a.reshape(-1, fsdp, width).transpose(1, 0, 2)
+    chain_row = slot_grads[SHORT_SLOTS:].reshape(1, 2 * LONG_SLOTS)
+    chain_row = jnp.pad(chain_row, ((0, 7), (0, width - 2 * LONG_SLOTS)))
+    packed = jnp.concatenate(
+        [
+            split(grad_patch),
+            split(jnp.stack([gain_one, gain_two, shift_zero, shift_one, shift_two, shift_three])),
+            grad_expand_bias.reshape(fsdp, -1, width),
+            jnp.broadcast_to(chain_row, (fsdp,) + chain_row.shape),
+        ],
+        1,
+    )
+    packed = tied(packed, grad_low, grad_rest)
+    parts = lax.all_to_all(packed, "fsdp", 0, 0, tiled=True)
+    chain_grads = parts[:, small_rows, : 2 * LONG_SLOTS].reshape(fsdp, LONG_SLOTS, 2)
     chain_grad = jnp.sum(chain_grads * member, 0)
+    small_sums = tied(jnp.sum(parts[:, :small_rows], 0), grad_high, grad_low, grad_rest)
+    small_grads = sum_replicas(place, small_sums)
     grad_totals = jnp.concatenate([slot_grads[:SHORT_SLOTS], chain_grad], 0)
     series_grad = (
         inv_spread[:, None]
@@ -613,28 +604,17 @@
             - normed_slots * grad_totals[:, 1:2] / counts[:, None]
         )
     ).reshape(row_count, PATCH)
-    shift_three = jnp.sum(cotangent.astype(F32), 0)
-
-    split = lambda a: a.reshape(-1, fsdp, width).transpose(1, 0, 2)
-    packed = jnp.concatenate(
-        [
-            split(grad_patch),
-            split(jnp.stack([gain_one, gain_two, shift_zero, shift_one, shift_two, shift_three])),
-            grad_expand_bias.reshape(fsdp, -1, width),
-        ],
-        1,
-    )
-    small_grads = reduce_small(place, packed)
-    grouped_grads = jnp.stack([grad_low.finish(), grad_high.finish()], 1)
+    grouped_grads = jnp.stack([grad_low.finish()[0], grad_high.finish()[0]], 1)
     grad_heads_in = grouped_grads.reshape(-1, GROUPS, 3, GROUP * HEAD_DIM).transpose(0, 2, 1, 3)
+    expand_low, expand_high, grad_heads_out = grad_rest.finish()
     return (
         layer_output,
         series_grad,
         small_grads[:PATCH],
         grad_heads_in.reshape(-1, 3 * D),
-        grad_heads_out.finish(),
-        grad_expand.finish(),
-        grad_reduce.finish(),
+        grad_heads_out,
+        jnp.concatenate([expand_low, expand_high], 1),
+        grad_reduce.finish()[0],
         small_grads[PATCH : PATCH + 2],
         small_grads[PATCH + 2 : PATCH + 6],
         small_grads[PATCH + 6 :].reshape(-1),

time: 544 us -> 518 us (0.952)
  the two profiles are of different devices: /device:TPU:29 before, /device:TPU:0 now
where the time goes in v3:
time: 518 us; the launch traced here: 510 us
  waiting for transfers between devices  153 us (30%)
  starting transfers between devices  92.7 us (18%)
  matrix products  89.7 us (17%)
  local copies, waits for them, and re-layouts  60 us (12%)
  Pallas kernels  51.9 us (10%)
  other arithmetic  47.2 us (9%)
  between operations  16 us (3%)
    ppermute x46, waiting for transfers between devices, move(): return lax.ppermute(value, AXES, pairs)  134 us
    ppermute x46, starting transfers between devices, move(): return lax.ppermute(value, AXES, pairs)  62.2 us
    dot_general x6, matrix products, dot_n(): lax.dot_general(a, b, (((1,), (0,)), ((), ())), preferred_element_type=F32)  39.1 us
    dot_general x6, matrix products, dot_t(): lax.dot_general(a, b, (((1,), (1,)), ((), ())), preferred_element_type=F32)  27 us
    dot_general x6, matrix products, dot_l(): lax.dot_general(a, b, (((0,), (0,)), ((), ())), preferred_element_type=F32)  23.6 us
    convert_element_type x18, other arithmetic, plus(): return total.astype(BF16)  21.4 us
    pallas_call x2, Pallas kernels, short_backward(): pl.pallas_call(short_backward_kernel, grid=(GROUP,), out_shape=jax.ShapeD...  20.3 us
    unnamed x196, local copies, waits for them, and re-layouts  19.9 us
  transfers between devices with their start and end apart: 56, of which 22 were waited for; matrix products, arithmetic and copies ran while one was open for 21% of the time, Pallas kernels for 9%

profile of v3, /device:TPU:0, one launch (start us, length us, event | category | flops | bytes accessed | tf_op | source)
XLA Modules:
  0.0 510.3 jit_solution(1213521080111294915)
XLA Ops:
  11.0 3.1 collective-permute-start
  15.7 4.8 all-to-all-start
  20.6 5.4 %collective-permute-done.refs_2_ = bf16[64,3072]{1,0:T(8,128)(2,1)} collective-permute-done((bf16[64,3072]{1,0:T(8,128)(2,1)S(1)}, bf16[64,3072]{1,0:T(8,128)(2,1)}, u32[]{:S(2)}, u32[]{:S(2)}) %collective-permute-start) | collective-permute-done | bytes 393248 | tf_op jit(solution)/shard_map/ppermute | solution.py:47
  28.8 3.6 collective-permute-start.1
  33.0 6.9 %collective-permute-done.6.refs_8_ = bf16[64,3072]{1,0:T(8,128)(2,1)} collective-permute-done((bf16[64,3072]{1,0:T(8,128)(2,1)S(1)}, bf16[64,3072]{1,0:T(8,128)(2,1)}, u32[]{:S(2)}, u32[]{:S(2)}) %collective-permute-start.6) | collective-permute-done | bytes 393248 | tf_op jit(solution)/shard_map/ppermute | solution.py:47
  41.4 6.6 %collective-permute-done.1.refs_3_ = bf16[64,3072]{1,0:T(8,128)(2,1)} collective-permute-done((bf16[64,3072]{1,0:T(8,128)(2,1)}, bf16[64,3072]{1,0:T(8,128)(2,1)}, u32[]{:S(2)}, u32[]{:S(2)}) %collective-permute-start.1) | collective-permute-done | bytes 393248 | tf_op jit(solution)/shard_map/ppermute | solution.py:47
  53.1 13.1 %collective-permute-done.2.refs_4_ = bf16[64,3072]{1,0:T(8,128)(2,1)S(1)} collective-permute-done((bf16[64,3072]{1,0:T(8,128)(2,1)}, bf16[64,3072]{1,0:T(8,128)(2,1)S(1)}, u32[]{:S(2)}, u32[]{:S(2)}) %collective-permute-start.2) | collective-permute-done | bytes 393248 | tf_op jit(solution)/shard_map/ppermute | solution.py:47
  72.3 4.9 collective-permute-done.7.refs_9_
  79.9 12.4 %collective-permute-done.9.refs_11_ = bf16[64,3072]{1,0:T(8,128)(2,1)S(1)} collective-permute-done((bf16[64,3072]{1,0:T(8,128)(2,1)}, bf16[64,3072]{1,0:T(8,128)(2,1)S(1)}, u32[]{:S(2)}, u32[]{:S(2)}) %collective-permute-start.9) | collective-permute-done | bytes 393248 | tf_op jit(solution)/shard_map/ppermute | solution.py:47
  95.9 6.4 %assemble.1 = bf16[1024,3072]{1,0:T(8,128)(2,1)} custom-call(s32[4]{0:T(128)} %pad_add_fusion.refs_0_, bf16[128,3072]{1,0:T(8,128)(2,1)} %copy-done.27, bf16[64,3072]{1,0:T(8,128)(2,1)} %collective-permute-done.refs_2_, bf16[64,3072]{1,0:T(8,128)(2,1)} %collective-permute-done.1.refs_3_, bf16[64,3072]{1,0:T(8,128)(2,1)} %copy-done.54, ...), custom_call_target="tpu_custom_call" | custom-call | bytes 12582912 | tf_op jit(solution)/shard_map/assemble/pallas_call | solution.py:128
  102.3 4.2 convolution_convert_fusion.5.q.k0.v0
  107.3 9.1 %collective-permute-start.16 = (bf16[60,2048]{1,0:T(8,128)(2,1)S(1)}, bf16[60,2048]{1,0:T(8,128)(2,1)S(1)}, u32[]{:S(2)}, u32[]{:S(2)}) collective-permute-start(bf16[60,2048]{1,0:T(8,128)(2,1)S(1)} %pad_maximum_fusion.9), channel_id=1, source_target_pairs={{0,12},{4,16},{8,20},{12,24},{16,28},{20,0},{24,4},{28,8},{1,13},{... | collective-permute-start | bytes 737288 | tf_op jit(solution)/shard_map/ppermute | solution.py:51
  116.4 7.2 %collective-permute-start.15 = (bf16[60,2048]{1,0:T(8,128)(2,1)S(1)}, bf16[60,2048]{1,0:T(8,128)(2,1)}, u32[]{:S(2)}, u32[]{:S(2)}) collective-permute-start(bf16[60,2048]{1,0:T(8,128)(2,1)S(1)} %pad_maximum_fusion.9), channel_id=1, source_target_pairs={{0,8},{4,12},{8,16},{12,20},{16,24},{20,28},{24,0},{28,4},{1,9},{5... | collective-permute-start | bytes 737288 | tf_op jit(solution)/shard_map/ppermute | solution.py:51
  123.9 6.3 %convolution_convert_fusion.q_ref.k_ref.v_ref = bf16[720,3072]{1,0:T(8,128)(2,1)} fusion(bf16[720,1024]{1,0:T(8,128)(2,1)S(1)} %slice-done.2, bf16[1024,3072]{1,0:T(8,128)(2,1)S(1)} %copy-done.6), kind=kOutput, calls=%fused_computation.18 | convolution fusion | flops 4532060160 | bytes 12189696 | tf_op jit(solution)/shard_map/dot_general | solution.py:251
  130.2 16.5 %collective-permute-done.16.k3.v3 = bf16[60,2048]{1,0:T(8,128)(2,1)S(1)} collective-permute-done((bf16[60,2048]{1,0:T(8,128)(2,1)S(1)}, bf16[60,2048]{1,0:T(8,128)(2,1)S(1)}, u32[]{:S(2)}, u32[]{:S(2)}) %collective-permute-start.16) | collective-permute-done | bytes 245792 | tf_op jit(solution)/shard_map/ppermute | solution.py:51
  147.4 6.8 %long_forward.1 = bf16[60,1024]{1,0:T(8,128)(2,1)} custom-call(s32[4]{0:T(128)} %quarter_ref.3, bf16[60,3072]{1,0:T(8,128)(2,1)} %copy-done.7, bf16[60,3072]{1,0:T(8,128)(2,1)} %copy-done.7, bf16[60,3072]{1,0:T(8,128)(2,1)} %copy-done.7, bf16[60,2048]{1,0:T(8,128)(2,1)} %collective-permute-done.14.k1.v1, bf16[60,2048]{1,0:T(8,128)(2,1)} %collective-permute-done.14.k1.v1, ...), custom_call_target="tpu_custom_call" | custom-call | flops 58982400 | bytes 1228800 | tf_op jit(solution)/shard_map/long_forward/pallas_call | solution.py:394
  154.2 10.6 %short_forward.1 = bf16[780,1024]{1,0:T(8,128)(2,1)} custom-call(bf16[720,3072]{1,0:T(8,128)(2,1)} %convolution_convert_fusion.q_ref.k_ref.v_ref, bf16[720,3072]{1,0:T(8,128)(2,1)} %convolution_convert_fusion.q_ref.k_ref.v_ref, bf16[720,3072]{1,0:T(8,128)(2,1)} %convolution_convert_fusion.q_ref.k_ref.v_ref), custom_call_target="tpu_custom_call" | custom-call | flops 707788800 | bytes 6389760 | tf_op jit(solution)/shard_map/short_forward/pallas_call | solution.py:289
  165.5 3.9 fusion.73
  169.4 2.0 fusion.83
  172.2 20.2 %multiply_convert_fusion = (bf16[780,2048]{1,0:T(8,128)(2,1)S(1)}, f32[780,2048]{1,0:T(8,128)}, f32[780,2048]{1,0:T(8,128)}) fusion(f32[2048]{0:T(1024)S(1)} %bitcast.309, bf16[1024,1024]{1,0:T(8,128)(2,1)S(1)} %bitcast.294, bf16[1024,1024]{1,0:T(8,128)(2,1)S(1)} %bitcast.292, f32[780,1024]{1,0:T(8,128)S(1)} %get-tuple-element.218, f32[1024]{0:T(1024)S(1)} %copy-done.87, ...), kind=kOutput, calls=%fused_computation.4 | convolution fusion | flops 3389370368 | bytes 23386208 | tf_op jit(solution)/shard_map/dot_general | solution.py:251
  192.4 4.8 convolution_convert_fusion.4
  197.2 2.0 copy-done.29
  200.8 2.6 slice.232
  203.5 10.8 %add_convert_fusion = bf16[780,2048]{1,0:T(8,128)(2,1)S(1)} fusion(f32[780,2048]{1,0:T(8,128)} %get-tuple-element.151, f32[780,2048]{1,0:T(8,128)} %get-tuple-element.219, f32[2048]{0:T(1024)S(1)} %bitcast.310, bf16[780,1024]{1,0:T(8,128)(2,1)S(1)} %copy-done.21, bf16[2048,1024]{1,0:T(8,128)(2,1)S(1)} %bitcast.278), kind=kOutput, calls=%fused_computation.3 | convolution fusion | flops 3295518720 | bytes 21774336 | tf_op jit(solution)/shard_map/dot_general | solution.py:243
  214.3 3.8 fusion.6
  220.5 4.8 multiply_reduce_fusion
  225.2 5.5 %convolution_convert_fusion.3 = bf16[1024,2048]{1,0:T(8,128)(2,1)S(1)} fusion(bf16[780,2048]{1,0:T(8,128)(2,1)S(1)} %add_convert_fusion, f32[780,1024]{1,0:T(8,128)S(1)} %copy-done.9, f32[1024]{0:T(1024)S(1)} %copy-done.87, f32[1024]{0:T(1024)S(1)} %copy-done.79, f32[780]{0:T(1024)S(1)} %fusion.59, f32[780]{0:T(1024)S(1)} %broadcast_multiply_fusion), kind=kOutput, calls=%fused_computation.28 | convolution fusion | flops 3277647872 | bytes 10598496 | tf_op jit(solution)/shard_map/dot_general | solution.py:247
  236.3 2.4 convolution_convert_fusion.6
  243.1 2.7 convert_reduce_fusion
  245.9 3.4 convolution_convert_fusion.7.g_ref
  249.3 2.2 fusion.19
  257.1 13.8 %collective-permute-done.21 = bf16[4,128,1024]{2,1,0:T(8,128)(2,1)S(1)} collective-permute-done((bf16[4,128,1024]{2,1,0:T(8,128)(2,1)S(1)}, bf16[4,128,1024]{2,1,0:T(8,128)(2,1)S(1)}, u32[]{:S(2)}, u32[]{:S(2)}) %collective-permute-start.21) | collective-permute-done | bytes 1048608 | tf_op jit(solution)/shard_map/ppermute | solution.py:47
  273.8 7.8 %long_backward.1 = (bf16[60,1024]{1,0:T(8,128)(2,1)}, f32[2,60,1024]{2,1,0:T(8,128)}, bf16[2,60,1024]{2,1,0:T(8,128)(2,1)}, bf16[2,60,1024]{2,1,0:T(8,128)(2,1)}, bf16[2,60,1024]{2,1,0:T(8,128)(2,1)}) custom-call(s32[4]{0:T(128)} %quarter_ref.3, bf16[60,3072]{1,0:T(8,128)(2,1)} %copy-done.7, bf16[60,3072]{1,0:T(8,128)(2,1)} %copy-done.7, ...), custom_call_target="tpu_custom_call" | custom-call | flops 147456000 | bytes 2457600 | tf_op jit(solution)/shard_map/long_backward/pallas_call | solution.py:434
  282.7 10.2 %short_backward.2 = bf16[780,1536]{1,0:T(8,128)(2,1)} custom-call(bf16[720,3072]{1,0:T(8,128)(2,1)} %convolution_convert_fusion.q_ref.k_ref.v_ref, bf16[720,3072]{1,0:T(8,128)(2,1)} %convolution_convert_fusion.q_ref.k_ref.v_ref, bf16[720,3072]{1,0:T(8,128)(2,1)} %convolution_convert_fusion.q_ref.k_ref.v_ref, bf16[780,1024]{1,0:T(8,128)(2,1)} %copy-done.20), custom_call_target="tpu_custom_call" | custom-call | flops 884736000 | bytes 5591040 | tf_op jit(solution)/shard_map/short_backward/pallas_call | solution.py:333
  293.9 4.3 collective-permute-start.26
  304.6 2.4 collective-permute-done.25
  307.0 14.1 %collective-permute-done.26 = bf16[128,1024]{1,0:T(8,128)(2,1)S(1)} collective-permute-done((bf16[128,1024]{1,0:T(8,128)(2,1)}, bf16[128,1024]{1,0:T(8,128)(2,1)S(1)}, u32[]{:S(2)}, u32[]{:S(2)}) %collective-permute-start.26) | collective-permute-done | bytes 262176 | tf_op jit(solution)/shard_map/ppermute | solution.py:47
  322.3 5.5 %convolution_convert_fusion.2 = bf16[1024,1536]{1,0:T(8,128)(2,1)S(1)} fusion(bf16[780,1024]{1,0:T(8,128)(2,1)S(1)} %copy-done.25, bf16[780,1536]{1,0:T(8,128)(2,1)} %maximum_dynamic-update-slice_fusion), kind=kOutput, calls=%fused_computation.27 | convolution fusion | flops 2455240704 | bytes 7139328 | tf_op jit(solution)/shard_map/dot_general | solution.py:247
  329.3 4.7 add_convert_fusion.2
  334.4 10.2 %short_backward.3 = bf16[780,1536]{1,0:T(8,128)(2,1)} custom-call(bf16[720,3072]{1,0:T(8,128)(2,1)} %convolution_convert_fusion.q_ref.k_ref.v_ref, bf16[720,3072]{1,0:T(8,128)(2,1)} %convolution_convert_fusion.q_ref.k_ref.v_ref, bf16[720,3072]{1,0:T(8,128)(2,1)} %convolution_convert_fusion.q_ref.k_ref.v_ref, bf16[780,1024]{1,0:T(8,128)(2,1)} %copy-done.20), custom_call_target="tpu_custom_call" | custom-call | flops 884736000 | bytes 5591040 | tf_op jit(solution)/shard_map/short_backward/pallas_call | solution.py:333
  347.8 2.7 fusion.8
  350.7 2.0 fusion.9
  353.0 2.0 collective-permute-start.33
  355.1 4.0 convolution_convert_fusion.1
  359.4 2.7 fusion.10
  362.1 3.9 multiply_reduce_fusion.1
  368.4 21.2 %collective-permute-done.33 = bf16[4,96,1024]{2,1,0:T(8,128)(2,1)S(1)} collective-permute-done((bf16[4,96,1024]{2,1,0:T(8,128)(2,1)S(1)}, bf16[4,96,1024]{2,1,0:T(8,128)(2,1)S(1)}, u32[]{:S(2)}, u32[]{:S(2)}) %collective-permute-start.33) | collective-permute-done | bytes 786464 | tf_op jit(solution)/shard_map/ppermute | solution.py:47
  401.6 7.3 %collective-permute-start.35 = (bf16[64,1536]{1,0:T(8,128)(2,1)}, bf16[64,1536]{1,0:T(8,128)(2,1)}, u32[]{:S(2)}, u32[]{:S(2)}) collective-permute-start(bf16[64,1536]{1,0:T(8,128)(2,1)} %get-tuple-element.95), channel_id=1, source_target_pairs={{0,8},{1,9},{2,10},{3,11},{4,12},{5,13},{6,14},{7,15},{8,16},{9,17... | collective-permute-start | bytes 589832 | tf_op jit(solution)/shard_map/ppermute | solution.py:47
  408.9 3.3 collective-permute-start.36
  415.5 4.3 all-to-all-start.1
  419.8 2.0 collective-permute-start.38
  421.8 2.3 collective-permute-start.39
  425.1 9.8 %collective-permute-start.40 = (bf16[96,1024]{1,0:T(8,128)(2,1)}, bf16[96,1024]{1,0:T(8,128)(2,1)S(1)}, u32[]{:S(2)}, u32[]{:S(2)}) collective-permute-start(bf16[96,1024]{1,0:T(8,128)(2,1)} %get-tuple-element.100), channel_id=1, source_target_pairs={{0,24},{1,25},{2,26},{3,27},{4,28},{5,29},{6,30},{7,31},{8,0},{9,1... | collective-permute-start | bytes 589832 | tf_op jit(solution)/shard_map/ppermute | solution.py:47
  437.7 13.9 %collective-permute-done.39 = bf16[96,1024]{1,0:T(8,128)(2,1)S(1)} collective-permute-done((bf16[96,1024]{1,0:T(8,128)(2,1)}, bf16[96,1024]{1,0:T(8,128)(2,1)S(1)}, u32[]{:S(2)}, u32[]{:S(2)}) %collective-permute-start.39) | collective-permute-done | bytes 196640 | tf_op jit(solution)/shard_map/ppermute | solution.py:47
  456.3 3.8 all-to-all-start.2
  460.2 2.1 collective-permute-start.41
  463.7 2.5 all-to-all-done.2
  468.0 2.4 collective-permute-done.41
  470.5 3.5 collective-permute-done.49
  475.3 4.7 collective-permute-start.44
  483.2 2.2 collective-permute-done.46
  485.4 3.7 collective-permute-done.45
  490.0 3.8 collective-permute-done.47
  500.3 3.0 copy.125
  (435 shorter events, 109.2 us)
Async XLA Ops:
  7.2 158.3 %all-gather.3.cloned.1.call-start = ((), (), s32[]{:S(2)}) async-start(), calls=%async_computation.3 | async-start | bytes 10813440 | tf_op jit(solution)/shard_map/all_gather | solution.py:147
  10.9 59.5 %copy-start.27 = (bf16[128,3072]{1,0:T(8,128)(2,1)}, bf16[128,3072]{1,0:T(8,128)(2,1)S(1)}, u32[]{:S(2)}) copy-start(bf16[128,3072]{1,0:T(8,128)(2,1)S(1)} %copy.112.refs_1_) | copy-start | bytes 2359300
  11.0 15.1 %collective-permute-start = (bf16[64,3072]{1,0:T(8,128)(2,1)S(1)}, bf16[64,3072]{1,0:T(8,128)(2,1)}, u32[]{:S(2)}, u32[]{:S(2)}) collective-permute-start(bf16[64,3072]{1,0:T(8,128)(2,1)S(1)} %constant_dynamic-slice_fusion.4), channel_id=1, source_target_pairs={{0,8},{1,9},{2,10},{3,11},{4,12},{5,13},{6,14},{7,15},{8,16},{9,17... | collective-permute-start | bytes 1179656 | tf_op jit(solution)/shard_map/ppermute | solution.py:47
  15.7 34.7 %all-to-all-start = ((f32[8,112,128]{2,1,0:T(8,128)}), f32[8,112,128]{2,1,0:T(8,128)S(1)}, u32[]{:S(2)}, u32[]{:S(2)}) async-start(f32[8,112,128]{2,1,0:T(8,128)} %broadcast_in_dim.45), calls=%async_computation | async-start | bytes 917504 | tf_op jit(solution)/shard_map/all_to_all | solution.py:179
  27.0 12.9 %collective-permute-start.6 = (bf16[64,3072]{1,0:T(8,128)(2,1)S(1)}, bf16[64,3072]{1,0:T(8,128)(2,1)}, u32[]{:S(2)}, u32[]{:S(2)}) collective-permute-start(bf16[64,3072]{1,0:T(8,128)(2,1)S(1)} %pad_maximum_fusion.5), channel_id=1, source_target_pairs={{0,4},{1,5},{2,6},{3,7},{4,0},{5,1},{6,2},{7,3},{8,12},{9,13},{10,... | collective-permute-start | bytes 1179656 | tf_op jit(solution)/shard_map/ppermute | solution.py:47
  28.8 19.3 %collective-permute-start.1 = (bf16[64,3072]{1,0:T(8,128)(2,1)}, bf16[64,3072]{1,0:T(8,128)(2,1)}, u32[]{:S(2)}, u32[]{:S(2)}) collective-permute-start(bf16[64,3072]{1,0:T(8,128)(2,1)} %collective-permute-done.refs_2_), channel_id=1, source_target_pairs={{0,8},{1,9},{2,10},{3,11},{4,12},{5,13},{6,14},{7,15},{8,16},{9,17... | collective-permute-start | bytes 1179656 | tf_op jit(solution)/shard_map/ppermute | solution.py:47
  33.0 46.2 %collective-permute-start.3 = (bf16[64,3072]{1,0:T(8,128)(2,1)}, bf16[64,3072]{1,0:T(8,128)(2,1)}, u32[]{:S(2)}, u32[]{:S(2)}) collective-permute-start(bf16[64,3072]{1,0:T(8,128)(2,1)} %collective-permute-done.refs_2_), channel_id=1, source_target_pairs={{0,1},{1,0},{2,3},{3,2},{4,5},{5,4},{6,7},{7,6},{8,9},{9,8},{10,11... | collective-permute-start | bytes 1179656 | tf_op jit(solution)/shard_map/ppermute | solution.py:47
  40.0 39.9 %collective-permute-start.10 = (bf16[64,3072]{1,0:T(8,128)(2,1)}, bf16[64,3072]{1,0:T(8,128)(2,1)}, u32[]{:S(2)}, u32[]{:S(2)}) collective-permute-start(bf16[64,3072]{1,0:T(8,128)(2,1)} %collective-permute-done.6.refs_8_), channel_id=1, source_target_pairs={{0,1},{1,0},{2,3},{3,2},{4,5},{5,4},{6,7},{7,6},{8,9},{9,8},{10,11... | collective-permute-start | bytes 1179656 | tf_op jit(solution)/shard_map/ppermute | solution.py:47
  40.0 39.4 %collective-permute-start.8 = (bf16[64,3072]{1,0:T(8,128)(2,1)}, bf16[64,3072]{1,0:T(8,128)(2,1)}, u32[]{:S(2)}, u32[]{:S(2)}) collective-permute-start(bf16[64,3072]{1,0:T(8,128)(2,1)} %collective-permute-done.6.refs_8_), channel_id=1, source_target_pairs={{0,2},{1,3},{2,0},{3,1},{4,6},{5,7},{6,4},{7,5},{8,10},{9,11},{10,... | collective-permute-start | bytes 1179656 | tf_op jit(solution)/shard_map/ppermute | solution.py:47
  48.1 46.1 %collective-permute-start.4 = (bf16[64,3072]{1,0:T(8,128)(2,1)}, bf16[64,3072]{1,0:T(8,128)(2,1)}, u32[]{:S(2)}, u32[]{:S(2)}) collective-permute-start(bf16[64,3072]{1,0:T(8,128)(2,1)} %collective-permute-done.1.refs_3_), channel_id=1, source_target_pairs={{0,1},{1,0},{2,3},{3,2},{4,5},{5,4},{6,7},{7,6},{8,9},{9,8},{10,11... | collective-permute-start | bytes 1179656 | tf_op jit(solution)/shard_map/ppermute | solution.py:47
  48.1 18.2 %collective-permute-start.2 = (bf16[64,3072]{1,0:T(8,128)(2,1)}, bf16[64,3072]{1,0:T(8,128)(2,1)S(1)}, u32[]{:S(2)}, u32[]{:S(2)}) collective-permute-start(bf16[64,3072]{1,0:T(8,128)(2,1)} %collective-permute-done.1.refs_3_), channel_id=1, source_target_pairs={{0,8},{1,9},{2,10},{3,11},{4,12},{5,13},{6,14},{7,15},{8,16},{9,17... | collective-permute-start | bytes 1179656 | tf_op jit(solution)/shard_map/ppermute | solution.py:47
  67.1 10.1 %collective-permute-start.7 = (bf16[64,3072]{1,0:T(8,128)(2,1)}, bf16[64,3072]{1,0:T(8,128)(2,1)}, u32[]{:S(2)}, u32[]{:S(2)}) collective-permute-start(bf16[64,3072]{1,0:T(8,128)(2,1)} %pad_maximum_fusion.6), channel_id=1, source_target_pairs={{0,4},{1,5},{2,6},{3,7},{4,0},{5,1},{6,2},{7,3},{8,12},{9,13},{10,... | collective-permute-start | bytes 1179656 | tf_op jit(solution)/shard_map/ppermute | solution.py:47
  72.3 97.1 %copy-start.2 = (f32[780,1024]{1,0:T(8,128)}, f32[780,1024]{1,0:T(8,128)S(1)}, u32[]{:S(2)}) copy-start(f32[780,1024]{1,0:T(8,128)S(1)} %get-tuple-element.216) | copy-start | bytes 9584644
  77.2 15.2 %collective-permute-start.9 = (bf16[64,3072]{1,0:T(8,128)(2,1)}, bf16[64,3072]{1,0:T(8,128)(2,1)S(1)}, u32[]{:S(2)}, u32[]{:S(2)}) collective-permute-start(bf16[64,3072]{1,0:T(8,128)(2,1)} %collective-permute-done.7.refs_9_), channel_id=1, source_target_pairs={{0,2},{1,3},{2,0},{3,1},{4,6},{5,7},{6,4},{7,5},{8,10},{9,11},{10,... | collective-permute-start | bytes 1179656 | tf_op jit(solution)/shard_map/ppermute | solution.py:47
  79.3 15.0 %collective-permute-start.5 = (bf16[64,3072]{1,0:T(8,128)(2,1)S(1)}, bf16[64,3072]{1,0:T(8,128)(2,1)S(1)}, u32[]{:S(2)}, u32[]{:S(2)}) collective-permute-start(bf16[64,3072]{1,0:T(8,128)(2,1)S(1)} %copy-done.55), channel_id=1, source_target_pairs={{0,1},{1,0},{2,3},{3,2},{4,5},{5,4},{6,7},{7,6},{8,9},{9,8},{10,11... | collective-permute-start | bytes 1179656 | tf_op jit(solution)/shard_map/ppermute | solution.py:47
  79.4 14.9 %collective-permute-start.12 = (bf16[64,3072]{1,0:T(8,128)(2,1)}, bf16[64,3072]{1,0:T(8,128)(2,1)S(1)}, u32[]{:S(2)}, u32[]{:S(2)}) collective-permute-start(bf16[64,3072]{1,0:T(8,128)(2,1)} %collective-permute-done.8.refs_10_), channel_id=1, source_target_pairs={{0,1},{1,0},{2,3},{3,2},{4,5},{5,4},{6,7},{7,6},{8,9},{9,8},{10,11... | collective-permute-start | bytes 1179656 | tf_op jit(solution)/shard_map/ppermute | solution.py:47
  79.9 15.2 %collective-permute-start.11 = (bf16[64,3072]{1,0:T(8,128)(2,1)}, bf16[64,3072]{1,0:T(8,128)(2,1)S(1)}, u32[]{:S(2)}, u32[]{:S(2)}) collective-permute-start(bf16[64,3072]{1,0:T(8,128)(2,1)} %collective-permute-done.7.refs_9_), channel_id=1, source_target_pairs={{0,1},{1,0},{2,3},{3,2},{4,5},{5,4},{6,7},{7,6},{8,9},{9,8},{10,11... | collective-permute-start | bytes 1179656 | tf_op jit(solution)/shard_map/ppermute | solution.py:47
  92.3 3.6 collective-permute-start.13
  107.3 39.4 %collective-permute-start.16 = (bf16[60,2048]{1,0:T(8,128)(2,1)S(1)}, bf16[60,2048]{1,0:T(8,128)(2,1)S(1)}, u32[]{:S(2)}, u32[]{:S(2)}) collective-permute-start(bf16[60,2048]{1,0:T(8,128)(2,1)S(1)} %pad_maximum_fusion.9), channel_id=1, source_target_pairs={{0,12},{4,16},{8,20},{12,24},{16,28},{20,0},{24,4},{28,8},{1,13},{... | collective-permute-start | bytes 737288 | tf_op jit(solution)/shard_map/ppermute | solution.py:51
  116.4 30.3 %collective-permute-start.15 = (bf16[60,2048]{1,0:T(8,128)(2,1)S(1)}, bf16[60,2048]{1,0:T(8,128)(2,1)}, u32[]{:S(2)}, u32[]{:S(2)}) collective-permute-start(bf16[60,2048]{1,0:T(8,128)(2,1)S(1)} %pad_maximum_fusion.9), channel_id=1, source_target_pairs={{0,8},{4,12},{8,16},{12,20},{16,24},{20,28},{24,0},{28,4},{1,9},{5... | collective-permute-start | bytes 737288 | tf_op jit(solution)/shard_map/ppermute | solution.py:51
  123.6 23.1 %collective-permute-start.14 = (bf16[60,2048]{1,0:T(8,128)(2,1)S(1)}, bf16[60,2048]{1,0:T(8,128)(2,1)}, u32[]{:S(2)}, u32[]{:S(2)}) collective-permute-start(bf16[60,2048]{1,0:T(8,128)(2,1)S(1)} %pad_maximum_fusion.9), channel_id=1, source_target_pairs={{0,4},{4,8},{8,12},{12,16},{16,20},{20,24},{24,28},{28,0},{1,5},{5... | collective-permute-start | bytes 737288 | tf_op jit(solution)/shard_map/ppermute | solution.py:51
  200.7 13.6 %collective-permute-start.17 = (bf16[8,128,1024]{2,1,0:T(8,128)(2,1)}, bf16[8,128,1024]{2,1,0:T(8,128)(2,1)}, u32[]{:S(2)}, u32[]{:S(2)}) collective-permute-start(bf16[8,128,1024]{2,1,0:T(8,128)(2,1)} %dynamic-slice_bitcast_fusion), channel_id=1, source_target_pairs={{0,1},{1,0},{2,3},{3,2},{4,5},{5,4},{6,7},{7,6},{8,9},{9,8},{10,11... | collective-permute-start | bytes 6291464 | tf_op jit(solution)/shard_map/ppermute | solution.py:47
  241.2 8.1 %collective-permute-start.18 = (bf16[8,64,1024]{2,1,0:T(8,128)(2,1)}, bf16[8,64,1024]{2,1,0:T(8,128)(2,1)}, u32[]{:S(2)}, u32[]{:S(2)}) collective-permute-start(bf16[8,64,1024]{2,1,0:T(8,128)(2,1)} %dynamic-slice_bitcast_fusion.6), channel_id=1, source_target_pairs={{0,1},{1,0},{2,3},{3,2},{4,5},{5,4},{6,7},{7,6},{8,9},{9,8},{10,11... | collective-permute-start | bytes 3145736 | tf_op jit(solution)/shard_map/ppermute | solution.py:47
  241.6 10.0 %collective-permute-start.19 = (bf16[8,64,1024]{2,1,0:T(8,128)(2,1)}, bf16[8,64,1024]{2,1,0:T(8,128)(2,1)}, u32[]{:S(2)}, u32[]{:S(2)}) collective-permute-start(bf16[8,64,1024]{2,1,0:T(8,128)(2,1)} %dynamic-slice_bitcast_fusion.5), channel_id=1, source_target_pairs={{0,1},{1,0},{2,3},{3,2},{4,5},{5,4},{6,7},{7,6},{8,9},{9,8},{10,11... | collective-permute-start | bytes 3145736 | tf_op jit(solution)/shard_map/ppermute | solution.py:47
  242.6 10.8 %collective-permute-start.20 = (bf16[8,64,1024]{2,1,0:T(8,128)(2,1)}, bf16[8,64,1024]{2,1,0:T(8,128)(2,1)S(1)}, u32[]{:S(2)}, u32[]{:S(2)}) collective-permute-start(bf16[8,64,1024]{2,1,0:T(8,128)(2,1)} %dynamic-slice_bitcast_fusion.4), channel_id=1, source_target_pairs={{0,1},{1,0},{2,3},{3,2},{4,5},{5,4},{6,7},{7,6},{8,9},{9,8},{10,11... | collective-permute-start | bytes 3145736 | tf_op jit(solution)/shard_map/ppermute | solution.py:47
  245.8 25.1 %collective-permute-start.21 = (bf16[4,128,1024]{2,1,0:T(8,128)(2,1)S(1)}, bf16[4,128,1024]{2,1,0:T(8,128)(2,1)S(1)}, u32[]{:S(2)}, u32[]{:S(2)}) collective-permute-start(bf16[4,128,1024]{2,1,0:T(8,128)(2,1)S(1)} %copy-done.53), channel_id=1, source_target_pairs={{0,4},{1,5},{2,6},{3,7},{4,0},{5,1},{6,2},{7,3},{8,12},{9,13},{10,... | collective-permute-start | bytes 3145736 | tf_op jit(solution)/shard_map/ppermute | solution.py:47
  249.3 23.9 %copy-start.20 = (bf16[780,1024]{1,0:T(8,128)(2,1)}, bf16[780,1024]{1,0:T(8,128)(2,1)S(1)}, u32[]{:S(2)}) copy-start(bf16[780,1024]{1,0:T(8,128)(2,1)S(1)} %convolution_convert_fusion.7.g_ref) | copy-start | bytes 4792324
  281.6 17.5 %collective-permute-start.22 = (bf16[2,60,1024]{2,1,0:T(8,128)(2,1)}, bf16[2,60,1024]{2,1,0:T(8,128)(2,1)}, u32[]{:S(2)}, u32[]{:S(2)}) collective-permute-start(bf16[2,60,1024]{2,1,0:T(8,128)(2,1)} %get-tuple-element.76), channel_id=1, source_target_pairs={{0,28},{4,0},{8,4},{12,8},{16,12},{20,16},{24,20},{28,24},{1,29},{... | collective-permute-start | bytes 737288 | tf_op jit(solution)/shard_map/ppermute | solution.py:51
  281.7 18.6 %collective-permute-start.23 = (bf16[2,60,1024]{2,1,0:T(8,128)(2,1)}, bf16[2,60,1024]{2,1,0:T(8,128)(2,1)}, u32[]{:S(2)}, u32[]{:S(2)}) collective-permute-start(bf16[2,60,1024]{2,1,0:T(8,128)(2,1)} %get-tuple-element.77), channel_id=1, source_target_pairs={{0,24},{4,28},{8,0},{12,4},{16,8},{20,12},{24,16},{28,20},{1,25},{... | collective-permute-start | bytes 737288 | tf_op jit(solution)/shard_map/ppermute | solution.py:51
  282.7 18.5 %collective-permute-start.24 = (bf16[2,60,1024]{2,1,0:T(8,128)(2,1)}, bf16[2,60,1024]{2,1,0:T(8,128)(2,1)}, u32[]{:S(2)}, u32[]{:S(2)}) collective-permute-start(bf16[2,60,1024]{2,1,0:T(8,128)(2,1)} %get-tuple-element.78), channel_id=1, source_target_pairs={{0,20},{4,24},{8,28},{12,0},{16,4},{20,8},{24,12},{28,16},{1,21},{... | collective-permute-start | bytes 737288 | tf_op jit(solution)/shard_map/ppermute | solution.py:51
  292.8 29.4 %copy-start.25 = (bf16[780,1024]{1,0:T(8,128)(2,1)S(1)}, bf16[780,1024]{1,0:T(8,128)(2,1)}, u32[]{:S(2)}) copy-start(bf16[780,1024]{1,0:T(8,128)(2,1)} %copy-done.24) | copy-start | bytes 4792324
  292.8 14.2 %collective-permute-start.25 = (bf16[128,1024]{1,0:T(8,128)(2,1)}, bf16[128,1024]{1,0:T(8,128)(2,1)S(1)}, u32[]{:S(2)}, u32[]{:S(2)}) collective-permute-start(bf16[128,1024]{1,0:T(8,128)(2,1)} %get-tuple-element.79), channel_id=1, source_target_pairs={{0,8},{1,9},{2,10},{3,11},{4,12},{5,13},{6,14},{7,15},{8,16},{9,17... | collective-permute-start | bytes 786440 | tf_op jit(solution)/shard_map/ppermute | solution.py:47
  293.9 27.2 %collective-permute-start.26 = (bf16[128,1024]{1,0:T(8,128)(2,1)}, bf16[128,1024]{1,0:T(8,128)(2,1)S(1)}, u32[]{:S(2)}, u32[]{:S(2)}) collective-permute-start(bf16[128,1024]{1,0:T(8,128)(2,1)} %get-tuple-element.80), channel_id=1, source_target_pairs={{0,16},{1,17},{2,18},{3,19},{4,20},{5,21},{6,22},{7,23},{8,24},{9,... | collective-permute-start | bytes 786440 | tf_op jit(solution)/shard_map/ppermute | solution.py:47
  299.1 22.0 %collective-permute-start.27 = (bf16[128,1024]{1,0:T(8,128)(2,1)S(1)}, bf16[128,1024]{1,0:T(8,128)(2,1)S(1)}, u32[]{:S(2)}, u32[]{:S(2)}) collective-permute-start(bf16[128,1024]{1,0:T(8,128)(2,1)S(1)} %get-tuple-element.81), channel_id=1, source_target_pairs={{0,24},{1,25},{2,26},{3,27},{4,28},{5,29},{6,30},{7,31},{8,0},{9,1... | collective-permute-start | bytes 786440 | tf_op jit(solution)/shard_map/ppermute | solution.py:47
  300.3 47.5 %collective-permute-start.30 = (bf16[8,96,1024]{2,1,0:T(8,128)(2,1)}, bf16[8,96,1024]{2,1,0:T(8,128)(2,1)}, u32[]{:S(2)}, u32[]{:S(2)}) collective-permute-start(bf16[8,96,1024]{2,1,0:T(8,128)(2,1)} %dynamic-slice_bitcast_fusion.3), channel_id=1, source_target_pairs={{0,2},{1,3},{2,0},{3,1},{4,6},{5,7},{6,4},{7,5},{8,10},{9,11},{10,... | collective-permute-start | bytes 4718600 | tf_op jit(solution)/shard_map/ppermute | solution.py:47
  329.3 21.3 %collective-permute-start.28 = (bf16[8,64,1536]{2,1,0:T(8,128)(2,1)}, bf16[8,64,1536]{2,1,0:T(8,128)(2,1)}, u32[]{:S(2)}, u32[]{:S(2)}) collective-permute-start(bf16[8,64,1536]{2,1,0:T(8,128)(2,1)} %dynamic-slice_bitcast_fusion.2), channel_id=1, source_target_pairs={{0,1},{1,0},{2,3},{3,2},{4,5},{5,4},{6,7},{7,6},{8,9},{9,8},{10,11... | collective-permute-start | bytes 4718600 | tf_op jit(solution)/shard_map/ppermute | solution.py:47
  334.0 12.1 %collective-permute-start.29 = (bf16[128,1024]{1,0:T(8,128)(2,1)S(1)}, bf16[128,1024]{1,0:T(8,128)(2,1)}, u32[]{:S(2)}, u32[]{:S(2)}) collective-permute-start(bf16[128,1024]{1,0:T(8,128)(2,1)S(1)} %fusion.35), channel_id=1, source_target_pairs={{0,2},{1,3},{2,0},{3,1},{4,6},{5,7},{6,4},{7,5},{8,10},{9,11},{10,... | collective-permute-start | bytes 786440 | tf_op jit(solution)/shard_map/ppermute | solution.py:47
  352.7 59.4 %collective-permute-start.51 = (bf16[128,1024]{1,0:T(8,128)(2,1)}, bf16[128,1024]{1,0:T(8,128)(2,1)}, u32[]{:S(2)}, u32[]{:S(2)}) collective-permute-start(bf16[128,1024]{1,0:T(8,128)(2,1)} %add_convert_fusion.5), channel_id=1, source_target_pairs={{0,1},{1,0},{2,3},{3,2},{4,5},{5,4},{6,7},{7,6},{8,9},{9,8},{10,11... | collective-permute-start | bytes 786440 | tf_op jit(solution)/shard_map/ppermute | solution.py:47
  353.0 37.8 %collective-permute-start.32 = (bf16[4,64,1536]{2,1,0:T(8,128)(2,1)S(1)}, bf16[4,64,1536]{2,1,0:T(8,128)(2,1)S(1)}, u32[]{:S(2)}, u32[]{:S(2)}) collective-permute-start(bf16[4,64,1536]{2,1,0:T(8,128)(2,1)S(1)} %dynamic-slice_bitcast_fusion.10), channel_id=1, source_target_pairs={{0,4},{1,5},{2,6},{3,7},{4,0},{5,1},{6,2},{7,3},{8,12},{9,13},{10,... | collective-permute-start | bytes 2359304 | tf_op jit(solution)/shard_map/ppermute | solution.py:47
  353.0 36.6 %collective-permute-start.33 = (bf16[4,96,1024]{2,1,0:T(8,128)(2,1)S(1)}, bf16[4,96,1024]{2,1,0:T(8,128)(2,1)S(1)}, u32[]{:S(2)}, u32[]{:S(2)}) collective-permute-start(bf16[4,96,1024]{2,1,0:T(8,128)(2,1)S(1)} %dynamic-slice_bitcast_fusion.9), channel_id=1, source_target_pairs={{0,4},{1,5},{2,6},{3,7},{4,0},{5,1},{6,2},{7,3},{8,12},{9,13},{10,... | collective-permute-start | bytes 2359304 | tf_op jit(solution)/shard_map/ppermute | solution.py:47
  366.1 25.8 %collective-permute-start.31 = (bf16[8,64,1536]{2,1,0:T(8,128)(2,1)S(1)}, bf16[8,64,1536]{2,1,0:T(8,128)(2,1)S(1)}, u32[]{:S(2)}, u32[]{:S(2)}) collective-permute-start(bf16[8,64,1536]{2,1,0:T(8,128)(2,1)S(1)} %dynamic-slice_bitcast_fusion.1), channel_id=1, source_target_pairs={{0,1},{1,0},{2,3},{3,2},{4,5},{5,4},{6,7},{7,6},{8,9},{9,8},{10,11... | collective-permute-start | bytes 4718600 | tf_op jit(solution)/shard_map/ppermute | solution.py:47
  368.4 24.8 %copy-start.4 = (bf16[780,1024]{1,0:T(8,128)(2,1)}, bf16[780,1024]{1,0:T(8,128)(2,1)S(1)}, u32[]{:S(2)}) copy-start(bf16[780,1024]{1,0:T(8,128)(2,1)S(1)} %get-tuple-element.90) | copy-start | bytes 4792324
  401.6 20.3 %collective-permute-start.35 = (bf16[64,1536]{1,0:T(8,128)(2,1)}, bf16[64,1536]{1,0:T(8,128)(2,1)}, u32[]{:S(2)}, u32[]{:S(2)}) collective-permute-start(bf16[64,1536]{1,0:T(8,128)(2,1)} %get-tuple-element.95), channel_id=1, source_target_pairs={{0,8},{1,9},{2,10},{3,11},{4,12},{5,13},{6,14},{7,15},{8,16},{9,17... | collective-permute-start | bytes 589832 | tf_op jit(solution)/shard_map/ppermute | solution.py:47
  408.9 16.2 %collective-permute-start.36 = (bf16[64,1536]{1,0:T(8,128)(2,1)}, bf16[64,1536]{1,0:T(8,128)(2,1)}, u32[]{:S(2)}, u32[]{:S(2)}) collective-permute-start(bf16[64,1536]{1,0:T(8,128)(2,1)} %get-tuple-element.96), channel_id=1, source_target_pairs={{0,16},{1,17},{2,18},{3,19},{4,20},{5,21},{6,22},{7,23},{8,24},{9,... | collective-permute-start | bytes 589832 | tf_op jit(solution)/shard_map/ppermute | solution.py:47
  412.2 22.7 %collective-permute-start.37 = (bf16[64,1536]{1,0:T(8,128)(2,1)}, bf16[64,1536]{1,0:T(8,128)(2,1)}, u32[]{:S(2)}, u32[]{:S(2)}) collective-permute-start(bf16[64,1536]{1,0:T(8,128)(2,1)} %get-tuple-element.97), channel_id=1, source_target_pairs={{0,24},{1,25},{2,26},{3,27},{4,28},{5,29},{6,30},{7,31},{8,0},{9,1... | collective-permute-start | bytes 589832 | tf_op jit(solution)/shard_map/ppermute | solution.py:47
  413.2 38.5 %collective-permute-start.34 = (bf16[8,32,1536]{2,1,0:T(8,128)(2,1)}, bf16[8,32,1536]{2,1,0:T(8,128)(2,1)}, u32[]{:S(2)}, u32[]{:S(2)}) collective-permute-start(bf16[8,32,1536]{2,1,0:T(8,128)(2,1)} %dynamic-slice_bitcast_fusion.8), channel_id=1, source_target_pairs={{0,2},{1,3},{2,0},{3,1},{4,6},{5,7},{6,4},{7,5},{8,10},{9,11},{10,... | collective-permute-start | bytes 2359304 | tf_op jit(solution)/shard_map/ppermute | solution.py:47
  415.5 37.6 %copy-start.80 = (f32[8,1,8]{2,1,0:T(1,128)S(1)}, f32[8,1,8]{2,1,0:T(1,128)}, u32[]{:S(2)}) copy-start(f32[8,1,8]{2,1,0:T(1,128)} %copy.121) | copy-start | bytes 772
  415.5 38.5 %copy-start.83 = (f32[52,2]{0,1:T(2,128)S(1)}, f32[52,2]{0,1:T(2,128)}, u32[]{:S(2)}) copy-start(f32[52,2]{0,1:T(2,128)} %copy-done.82) | copy-start | bytes 1252
  415.5 37.6 %all-to-all-start.1 = ((f32[8,112,128]{2,1,0:T(8,128)}), f32[8,112,128]{2,1,0:T(8,128)}, u32[]{:S(2)}, u32[]{:S(2)}) async-start(f32[8,112,128]{2,1,0:T(8,128)} %pad_maximum_fusion.4), calls=%async_computation.1 | async-start | bytes 917504 | tf_op jit(solution)/shard_map/all_to_all | solution.py:593
  419.8 17.9 %collective-permute-start.38 = (bf16[96,1024]{1,0:T(8,128)(2,1)}, bf16[96,1024]{1,0:T(8,128)(2,1)S(1)}, u32[]{:S(2)}, u32[]{:S(2)}) collective-permute-start(bf16[96,1024]{1,0:T(8,128)(2,1)} %get-tuple-element.98), channel_id=1, source_target_pairs={{0,8},{1,9},{2,10},{3,11},{4,12},{5,13},{6,14},{7,15},{8,16},{9,17... | collective-permute-start | bytes 589832 | tf_op jit(solution)/shard_map/ppermute | solution.py:47
  421.8 29.7 %collective-permute-start.39 = (bf16[96,1024]{1,0:T(8,128)(2,1)}, bf16[96,1024]{1,0:T(8,128)(2,1)S(1)}, u32[]{:S(2)}, u32[]{:S(2)}) collective-permute-start(bf16[96,1024]{1,0:T(8,128)(2,1)} %get-tuple-element.99), channel_id=1, source_target_pairs={{0,16},{1,17},{2,18},{3,19},{4,20},{5,21},{6,22},{7,23},{8,24},{9,... | collective-permute-start | bytes 589832 | tf_op jit(solution)/shard_map/ppermute | solution.py:47
  425.1 26.5 %collective-permute-start.40 = (bf16[96,1024]{1,0:T(8,128)(2,1)}, bf16[96,1024]{1,0:T(8,128)(2,1)S(1)}, u32[]{:S(2)}, u32[]{:S(2)}) collective-permute-start(bf16[96,1024]{1,0:T(8,128)(2,1)} %get-tuple-element.100), channel_id=1, source_target_pairs={{0,24},{1,25},{2,26},{3,27},{4,28},{5,29},{6,30},{7,31},{8,0},{9,1... | collective-permute-start | bytes 589832 | tf_op jit(solution)/shard_map/ppermute | solution.py:47
  436.8 26.1 %copy-start.52 = (f32[780,96]{0,1:T(8,128)S(1)}, f32[780,96]{0,1:T(8,128)}, u32[]{:S(2)}) copy-start(f32[780,96]{0,1:T(8,128)} %get-tuple-element.222) | copy-start | bytes 898564
  456.3 9.9 %all-to-all-start.2 = ((f32[4,104,128]{2,1,0:T(8,128)}), f32[4,104,128]{2,1,0:T(8,128)S(1)}, u32[]{:S(2)}, u32[]{:S(2)}) async-start(f32[4,104,128]{2,1,0:T(8,128)} %broadcast_in_dim.55), calls=%async_computation.2 | async-start | bytes 425984 | tf_op jit(solution)/shard_map/all_to_all | solution.py:229
  460.2 10.2 %collective-permute-start.41 = (bf16[64,1536]{1,0:T(8,128)(2,1)S(1)}, bf16[64,1536]{1,0:T(8,128)(2,1)S(1)}, u32[]{:S(2)}, u32[]{:S(2)}) collective-permute-start(bf16[64,1536]{1,0:T(8,128)(2,1)S(1)} %copy-done.57), channel_id=1, source_target_pairs={{0,2},{1,3},{2,0},{3,1},{4,6},{5,7},{6,4},{7,5},{8,10},{9,11},{10,... | collective-permute-start | bytes 589832 | tf_op jit(solution)/shard_map/ppermute | solution.py:47
  462.2 11.8 %collective-permute-start.49 = (bf16[96,1024]{1,0:T(8,128)(2,1)S(1)}, bf16[96,1024]{1,0:T(8,128)(2,1)S(1)}, u32[]{:S(2)}, u32[]{:S(2)}) collective-permute-start(bf16[96,1024]{1,0:T(8,128)(2,1)S(1)} %fusion.38), channel_id=1, source_target_pairs={{0,2},{1,3},{2,0},{3,1},{4,6},{5,7},{6,4},{7,5},{8,10},{9,11},{10,... | collective-permute-start | bytes 589832 | tf_op jit(solution)/shard_map/ppermute | solution.py:47
  462.3 11.9 %collective-permute-start.43 = (bf16[4,32,1536]{2,1,0:T(8,128)(2,1)S(1)}, bf16[4,32,1536]{2,1,0:T(8,128)(2,1)}, u32[]{:S(2)}, u32[]{:S(2)}) collective-permute-start(bf16[4,32,1536]{2,1,0:T(8,128)(2,1)S(1)} %dynamic-slice_bitcast_fusion.11), channel_id=1, source_target_pairs={{0,4},{1,5},{2,6},{3,7},{4,0},{5,1},{6,2},{7,3},{8,12},{9,13},{10,... | collective-permute-start | bytes 1179656 | tf_op jit(solution)/shard_map/ppermute | solution.py:47
  470.4 11.1 %collective-permute-start.42 = (bf16[64,1536]{1,0:T(8,128)(2,1)S(1)}, bf16[64,1536]{1,0:T(8,128)(2,1)S(1)}, u32[]{:S(2)}, u32[]{:S(2)}) collective-permute-start(bf16[64,1536]{1,0:T(8,128)(2,1)S(1)} %add_convert_fusion.7), channel_id=1, source_target_pairs={{0,1},{1,0},{2,3},{3,2},{4,5},{5,4},{6,7},{7,6},{8,9},{9,8},{10,11... | collective-permute-start | bytes 589832 | tf_op jit(solution)/shard_map/ppermute | solution.py:47
  474.1 15.7 %collective-permute-start.50 = (bf16[192,1024]{1,0:T(8,128)(2,1)S(1)}, bf16[192,1024]{1,0:T(8,128)(2,1)S(1)}, u32[]{:S(2)}, u32[]{:S(2)}) collective-permute-start(bf16[192,1024]{1,0:T(8,128)(2,1)S(1)} %pad_maximum_fusion.7), channel_id=1, source_target_pairs={{0,1},{1,0},{2,3},{3,2},{4,5},{5,4},{6,7},{7,6},{8,9},{9,8},{10,11... | collective-permute-start | bytes 1179656 | tf_op jit(solution)/shard_map/ppermute | solution.py:47
  475.3 7.9 %collective-permute-start.44 = (bf16[32,1536]{1,0:T(8,128)(2,1)S(1)}, bf16[32,1536]{1,0:T(8,128)(2,1)S(1)}, u32[]{:S(2)}, u32[]{:S(2)}) collective-permute-start(bf16[32,1536]{1,0:T(8,128)(2,1)S(1)} %get-tuple-element.190), channel_id=1, source_target_pairs={{0,8},{1,9},{2,10},{3,11},{4,12},{5,13},{6,14},{7,15},{8,16},{9,17... | collective-permute-start | bytes 294920 | tf_op jit(solution)/shard_map/ppermute | solution.py:47
  480.1 5.3 %collective-permute-start.46 = (bf16[32,1536]{1,0:T(8,128)(2,1)S(1)}, bf16[32,1536]{1,0:T(8,128)(2,1)S(1)}, u32[]{:S(2)}, u32[]{:S(2)}) collective-permute-start(bf16[32,1536]{1,0:T(8,128)(2,1)S(1)} %get-tuple-element.191), channel_id=1, source_target_pairs={{0,24},{1,25},{2,26},{3,27},{4,28},{5,29},{6,30},{7,31},{8,0},{9,1... | collective-permute-start | bytes 294920 | tf_op jit(solution)/shard_map/ppermute | solution.py:47
  480.1 9.0 %collective-permute-start.45 = (bf16[32,1536]{1,0:T(8,128)(2,1)S(1)}, bf16[32,1536]{1,0:T(8,128)(2,1)S(1)}, u32[]{:S(2)}, u32[]{:S(2)}) collective-permute-start(bf16[32,1536]{1,0:T(8,128)(2,1)S(1)} %get-tuple-element.192), channel_id=1, source_target_pairs={{0,16},{1,17},{2,18},{3,19},{4,20},{5,21},{6,22},{7,23},{8,24},{9,... | collective-permute-start | bytes 294920 | tf_op jit(solution)/shard_map/ppermute | solution.py:47
  489.1 4.7 collective-permute-start.47
  493.8 2.0 collective-permute-start.48
  (88 other events, 519.0 us)
Sparse Core Ops, SparseCore 0:
  11.4 125.2 all-gather.2

commit v4 on v3

--- a/solution.py
+++ b/solution.py
@@ -3,7 +3,7 @@
 from jax import lax
 from jax.experimental import pallas as pl
 from jax.experimental.pallas import tpu as pltpu
-from jax.sharding import PartitionSpec as P
+from jax.sharding import Mesh, PartitionSpec as P
 
 D = 1024
 HEADS = 8
@@ -20,35 +20,34 @@
 EPSILON = 1e-05
 NEG_LARGE = -1e30
 SCALE = HEAD_DIM ** (-0.5)
-AXES = ("fsdp", "dp")
 F32 = jnp.float32
 BF16 = jnp.bfloat16
 
 
 class Place:
-    def __init__(self):
-        self.fsdp = lax.axis_size("fsdp")
-        self.dp = lax.axis_size("dp")
-        self.tuned = self.fsdp == 8 and self.dp == 4
-        self.f = lax.axis_index("fsdp")
-        d = lax.axis_index("dp")
-        self.line = self.fsdp // 2
-        self.z, self.y = self.f // 2, self.f % 2
-        self.x, self.c = d // 2, d % 2
-
-    def move(self, value, line=0, pair=0, side=0, core=0):
-        pairs = []
-        for f in range(self.fsdp):
-            for d in range(self.dp):
-                z, y, x, c = f // 2, f % 2, d // 2, d % 2
-                to_f = ((z + line) % self.line) * 2 + (y ^ pair)
-                to_d = (x ^ side) * 2 + (c ^ core)
-                pairs.append((f * self.dp + d, to_f * self.dp + to_d))
-        return lax.ppermute(value, AXES, pairs)
+    def __init__(self, tuned):
+        self.tuned = tuned
+        self.fsdp_axes = ("z", "y") if tuned else ("fsdp",)
+        self.dp_axes = ("x", "c") if tuned else ("dp",)
+
+    def enter(self):
+        self.fsdp = lax.axis_size(self.fsdp_axes)
+        self.dp = lax.axis_size(self.dp_axes)
+        self.f = lax.axis_index(self.fsdp_axes)
+        self.d = lax.axis_index(self.dp_axes)
 
     def along(self, value, steps):
         pairs = [(s, (s + steps) % self.fsdp) for s in range(self.fsdp)]
-        return lax.ppermute(value, "fsdp", pairs)
+        return lax.ppermute(value, self.fsdp_axes, pairs)
+
+    def move(self, value, axes):
+        if axes == "core":
+            return lax.ppermute(value, "c", [(0, 1), (1, 0)])
+        return lax.all_to_all(value, axes, 0, 0, tiled=True)
+
+
+def copies(value, count):
+    return jnp.broadcast_to(value, (count,) + value.shape)
 
 
 def pick(value, index, axis):
@@ -69,7 +68,7 @@
 
     def launch(self, arrays):
         if self.sends:
-            got = [self.place.move(a, **where) for a, (_, where) in zip(arrays, self.sends)]
+            got = [self.place.move(a, axes) for a, (_, axes) in zip(arrays, self.sends)]
             self.sends = self.take(got)
 
     def finish(self):
@@ -88,145 +87,96 @@
     return value
 
 
-def assemble_kernel(rows, info, own, *refs):
-    z, y, x, c = info[0], info[1], info[2], info[3]
-    half, quarter = rows // 2, rows // 4
-    *parts, out, sem = refs
-    near, far = parts[:6], parts[6:]
-    count = len(far) // 4
-    each = 4 // count
+def assemble_kernel(spans, info, own, other, *refs):
+    *outs, sem = refs
+    core = info[0]
     jobs = []
-
-    def add(src, src_row, dst_row, count):
-        jobs.append(
-            pltpu.make_async_copy(
-                src.at[pl.ds(src_row, count), :],
-                out.at[pl.ds(pl.multiple_of(dst_row, 16), count), :],
-                sem.at[len(jobs)],
-            )
-        )
-
-    add(own, 0, (z * 2 + y) * rows, rows)
-    for step in (1, 2, 3):
-        base = (lax.rem(z + 4 - step, 4) * 2 + y) * rows
-        add(near[step - 1], 0, base + c * half, half)
-        add(near[step + 2], 0, base + (1 - c) * half, half)
-    for step in range(4):
-        base = (lax.rem(z + 4 - step, 4) * 2 + (1 - y)) * rows
-        for kind, (core, side) in enumerate(((c, x), (c, 1 - x), (1 - c, x), (1 - c, 1 - x))):
-            src = far[kind * count + step // each]
-            add(src, (step % each) * quarter, base + core * half + side * quarter, quarter)
+    for src, side in ((own, core), (other, 1 - core)):
+        for y in range(2):
+            for x in range(2):
+                for row, rows, out, column in spans:
+                    width = src.shape[4]
+                    jobs.append(
+                        pltpu.make_async_copy(
+                            src.at[y, x, :, pl.ds(row, rows), :],
+                            outs[out].at[:, y, x, side, :, pl.ds(column, width)],
+                            sem.at[len(jobs)],
+                        )
+                    )
     for job in jobs:
         job.start()
     for job in jobs:
         job.wait()
 
 
-def assemble(info, shard, near, far):
-    rows, columns = shard.shape
-    parts = list(near) + list(far)
-    return pl.pallas_call(
-        lambda *refs: assemble_kernel(rows, *refs),
-        out_shape=jax.ShapeDtypeStruct((8 * rows, columns), shard.dtype),
+def gather_stages(place, *shards):
+    if not place.tuned:
+        return [lax.all_gather(shard, "fsdp", axis=0, tiled=True) for shard in shards]
+    width = min(shard.shape[1] for shard in shards)
+    pieces, spans, row = [], [], 0
+    for out, shard in enumerate(shards):
+        rows = shard.shape[0] // 4
+        mine = pick(shard.reshape(4, rows, shard.shape[1]), place.d, 0)
+        for column in range(0, shard.shape[1], width):
+            pieces.append(mine[:, column : column + width])
+            spans.append((row, rows, out, column))
+            row += rows
+    mine = jnp.concatenate(pieces, 0)
+    (mine,) = yield [(copies(mine, 4), "z")]
+    (mine,) = yield [(copies(mine, 4), ("y", "x"))]
+    mine = mine.reshape(2, 2, *mine.shape[1:])
+    (other,) = yield [(mine, "core")]
+    whole = pl.pallas_call(
+        lambda *refs: assemble_kernel(spans, *refs),
+        out_shape=[
+            jax.ShapeDtypeStruct((4, 2, 2, 2, shard.shape[0] // 4, shard.shape[1]), shard.dtype)
+            for shard in shards
+        ],
         in_specs=[pl.BlockSpec(memory_space=pltpu.SMEM)]
-        + [pl.BlockSpec(memory_space=pl.ANY)] * (1 + len(parts)),
-        out_specs=pl.BlockSpec(memory_space=pltpu.VMEM),
-        scratch_shapes=[pltpu.SemaphoreType.DMA((23,))],
+        + [pl.BlockSpec(memory_space=pl.ANY)] * 2,
+        out_specs=[pl.BlockSpec(memory_space=pltpu.VMEM)] * len(shards),
+        scratch_shapes=[pltpu.SemaphoreType.DMA((8 * len(spans),))],
         cost_estimate=pl.CostEstimate(
-            flops=0, bytes_accessed=32 * rows * columns, transcendentals=0
+            flops=0, bytes_accessed=128 * row * width, transcendentals=0
         ),
         name="assemble",
-    )(info, shard, *parts)
-
-
-def gather_rest(place, heads_out, expand, reduce):
-    dp = place.dp
-    wide = heads_out.shape[1]
-    pieces = [heads_out, reduce] + [expand[:, i : i + wide] for i in range(0, expand.shape[1], wide)]
-    mine = lambda a: pick(a.reshape(dp, -1, wide), lax.axis_index("dp"), 0)
-    every = lax.all_gather(jnp.concatenate([mine(a) for a in pieces], 0), AXES, axis=0)
-    whole, low = [], 0
-    for a in pieces:
-        high = low + a.shape[0] // dp
-        whole.append(every[:, low:high].reshape(-1, wide))
-        low = high
-    return whole[0], jnp.concatenate(whole[2:], 1), whole[1]
-
-
-def gather_first(place, info, shard):
-    if not place.tuned:
-        return lax.all_gather(shard, "fsdp", axis=0, tiled=True)
-    half, quarter = shard.shape[0] // 2, shard.shape[0] // 4
-    own = lax.dynamic_slice_in_dim(shard, place.c * half, half, 0)
-    piece = lambda a: lax.dynamic_slice_in_dim(a, place.x * quarter, quarter, 0)
-    move = place.move
-    a1 = move(own, line=1)
-    b01 = move(jnp.concatenate([piece(own), piece(a1)], 0), pair=1)
-    a2 = move(a1, line=1)
-    n1 = move(a1, core=1)
-    a3 = move(a2, line=1)
-    x01 = move(b01, side=1)
-    n2, m01 = move(a2, core=1), move(b01, core=1)
-    b23 = move(jnp.concatenate([piece(a2), piece(a3)], 0), pair=1)
-    n3, w01 = move(a3, core=1), move(x01, core=1)
-    x23, m23 = move(b23, side=1), move(b23, core=1)
-    w23 = move(x23, core=1)
-    return assemble(info, shard, [a1, a2, a3, n1, n2, n3], [b01, b23, x01, x23, m01, m23, w01, w23])
+    )(lax.axis_index("c").reshape(1), mine, other)
+    return [a.reshape(8 * shard.shape[0], shard.shape[1]) for a, shard in zip(whole, shards)]
 
 
 def gather_small(place, packed):
-    copies = jnp.broadcast_to(packed, (place.fsdp,) + packed.shape)
-    return lax.all_to_all(copies, "fsdp", 0, 0, tiled=True)
-
-
-def plus(a, *others):
-    total = a.astype(F32)
-    for other in others:
-        total = total + other.astype(F32)
-    return total.astype(BF16)
-
-
-def reduce_stages(place, grads, side_first):
+    return place.move(copies(packed, place.fsdp), place.fsdp_axes)
+
+
+def reduce_stages(place, *grads):
     if not place.tuned:
         parts = [
             lax.psum_scatter(g.astype(F32), "fsdp", scatter_dimension=0, tiled=True) for g in grads
         ]
         return [lax.psum(part.astype(BF16), "dp").astype(F32) for part in parts]
-    z, y, x, c = place.z, place.y, place.x, place.c
+    core = lax.axis_index("c")
     columns = grads[0].shape[1]
-    views = [g.reshape(8, 2, -1, columns) for g in grads]
-    got = yield [(pick(view, 1 - c, 1), dict(core=1)) for view in views]
-    value = [plus(pick(view, c, 1), other) for view, other in zip(views, got)]
-    value = value[0] if len(value) == 1 else jnp.concatenate(value, 1)
-    half = value.shape[1]
-    if side_first:
-        value = value.reshape(8, 2, half // 2, columns)
-        (got,) = yield [(pick(value, 1 - x, 1), dict(side=1))]
-        value = plus(pick(value, x, 1), got)
-    value = value.reshape(4, 2, *value.shape[1:])
-    (got,) = yield [(pick(value, 1 - y, 1), dict(pair=1))]
-    value = plus(pick(value, y, 1), got)
-    got = yield [(pick(value, (z + k) % 4, 0), dict(line=k)) for k in (1, 2, 3)]
-    value = plus(pick(value, z, 0), *got)
-    (got,) = yield [(value, dict(side=1))]
-    if side_first:
-        low, high = jnp.where(x == 0, value, got), jnp.where(x == 0, got, value)
-        value = jnp.concatenate([low, high], 0)
-    else:
-        value = plus(value, got)
-    (got,) = yield [(value, dict(core=1))]
-    low, high = jnp.where(c == 0, value, got), jnp.where(c == 0, got, value)
+    total = lambda a: jnp.sum(a.astype(F32), 0).astype(BF16)
+    views = [g.reshape(4, 2, 2, 2, -1, columns) for g in grads]
+    got = yield [(pick(view, 1 - core, 3), "core") for view in views]
+    value = [
+        (pick(view, core, 3).astype(F32) + other.astype(F32)).astype(BF16).transpose(1, 2, 0, 3, 4)
+        for view, other in zip(views, got)
+    ]
+    value = value[0] if len(value) == 1 else jnp.concatenate(value, 3)
+    (got,) = yield [(value.reshape(4, *value.shape[2:]), ("y", "x"))]
+    (got,) = yield [(total(got), "z")]
+    (got,) = yield [(copies(total(got), 4), ("x", "c"))]
     results, row = [], 0
     for view in views:
-        rows = slice(row, row + view.shape[2])
-        results.append(jnp.concatenate([low[rows], high[rows]], 0).astype(F32))
-        row += view.shape[2]
+        rows = view.shape[4]
+        results.append(got[:, row : row + rows].reshape(4 * rows, columns).astype(F32))
+        row += rows
     return results
 
 
 def sum_replicas(place, part):
-    copies = jnp.broadcast_to(part, (place.dp,) + part.shape)
-    return jnp.sum(lax.all_to_all(copies, "dp", 0, 0, tiled=True), 0)
+    return jnp.sum(place.move(copies(part, place.dp), place.dp_axes), 0)
 
 
 def layer_norm(inputs, gain_row, shift_row):
@@ -382,10 +332,7 @@
 
 
 def long_specs(rows):
-    sent = lambda part: pl.BlockSpec(
-        (rows, HEAD_DIM), lambda h: (0, (h // GROUP) * 2 * GROUP + part * GROUP + h % GROUP)
-    )
-    return [block_of(rows, part) for part in range(3)] + [sent(0), sent(1)] * 3
+    return [block_of(rows, part) for part in range(3)] + [block_of(rows, 1), block_of(rows, 2)] * 3
 
 
 def long_forward(quarter_index, own, priors):
@@ -446,6 +393,7 @@
 
 
 def body(
+    place,
     series_values,
     quarter_index,
     patch_weight,
@@ -458,10 +406,9 @@
     expand_bias,
     cotangent,
 ):
-    place = Place()
+    place.enter()
     fsdp = place.fsdp
     width = patch_weight.shape[1]
-    info = jnp.stack([place.z, place.y, place.x, place.c]).astype(jnp.int32)
     row_count = series_values.shape[0]
     slot_count = row_count // SPAN
     short_rows = SHORT_SLOTS * SPAN
@@ -487,10 +434,18 @@
     expand_shift = small[:, PATCH + 6 : small_rows].reshape(-1)
 
     mixed_columns = heads_in.reshape(-1, 3, GROUPS, GROUP * HEAD_DIM).transpose(0, 2, 1, 3)
-    heads_in_all = gather_first(place, info, mixed_columns.reshape(-1, 3 * D))
-    heads_out_all, expand_all, reduce_all = gather_rest(
-        place, heads_out, expand_weight, reduce_weight_shard
-    )
+    gather_in, gather_out, gather_rest = [
+        Chain(place, gather_stages(place, *shards))
+        for shards in (
+            (mixed_columns.reshape(-1, 3 * D),),
+            (heads_out,),
+            (expand_weight, reduce_weight_shard),
+        )
+    ]
+    gather_in.launch([a for a, _ in gather_in.sends])
+    tied((), gather_in, gather_out, gather_rest)
+    tied((), gather_in, gather_out)
+    (heads_in_all,) = gather_in.finish()
 
     totals = jnp.concatenate([slot_sums[:SHORT_SLOTS], chain_sum], 0)
     counts = jnp.where(jnp.arange(slot_count) < SHORT_SLOTS, SPAN * PATCH, 4 * SPAN * PATCH).astype(
@@ -503,31 +458,28 @@
     embedded = dot_n(normed_low, patch_all) + biases_all[0]
     first_value, first_back = jax.vjp(layer_norm, embedded, gains_all[0], biases_all[1])
     first_norm = first_value.astype(BF16)
-    own_long = dot_n(first_norm[short_rows:], heads_in_all).astype(BF16)
-
-    group_columns = lambda g, low, high: slice(
-        (g * 3 + low) * GROUP * HEAD_DIM, (g * 3 + high) * GROUP * HEAD_DIM
-    )
-    long_pairs = jnp.concatenate([own_long[:, group_columns(g, 1, 3)] for g in range(GROUPS)], 1)
-    priors = [place.along(long_pairs, step) for step in (1, 2, 3)]
-    first_norm_short, heads_in_all = lax.optimization_barrier(
-        (first_norm[:short_rows], heads_in_all, long_pairs)
-    )[:2]
-    projected = dot_n(first_norm_short, heads_in_all).astype(BF16)
-    projected, priors = lax.optimization_barrier((projected, priors))
+    heads_in_all = tied(heads_in_all, gather_out, gather_rest)
+    long_norm = first_norm[short_rows:]
+    prior_norms = [place.along(long_norm, step) for step in (1, 2, 3)]
+
+    projected = dot_n(first_norm, heads_in_all).astype(BF16)
+    own_long = projected[short_rows:]
+    prior_all = dot_n(jnp.concatenate(prior_norms, 0), heads_in_all).astype(BF16)
+    priors = [prior_all[i * long_rows : (i + 1) * long_rows] for i in range(3)]
     mixed_short = short_forward(projected, row_count)
     mixed_long = long_forward(quarter_index, own_long, priors)
+    (heads_out_all,) = gather_out.finish()
+    heads_out_all, mixed_long = tied((heads_out_all, mixed_long), gather_rest)
     mixed_all = lax.dynamic_update_slice(mixed_short, mixed_long, (short_rows, 0))
     middle = embedded + dot_n(mixed_all, heads_out_all)
     second_value, second_back = jax.vjp(layer_norm, middle, gains_all[1], biases_all[2])
     second_norm = second_value.astype(BF16)
 
+    expand_all, reduce_all = gather_rest.finish()
     pre_act = dot_n(second_norm, expand_all) + expand_shift
     act_value, gelu_back = jax.vjp(exact_gelu, pre_act)
     activation = act_value.astype(BF16)
-    grad_reduce = Chain(
-        place, reduce_stages(place, [dot_l(activation, cotangent).astype(BF16)], False)
-    )
+    grad_reduce = Chain(place, reduce_stages(place, dot_l(activation, cotangent).astype(BF16)))
     cotangent = tied(cotangent, grad_reduce)
 
     grad_act = dot_t(cotangent, reduce_all)
@@ -540,7 +492,7 @@
     grad_branch = grad_middle.astype(BF16)
     grad_heads_out = dot_l(mixed_all, grad_branch).astype(BF16)
     grad_rest = Chain(
-        place, reduce_stages(place, [grad_expand[:, :D], grad_expand[:, D:], grad_heads_out], True)
+        place, reduce_stages(place, grad_expand[:, :D], grad_expand[:, D:], grad_heads_out)
     )
     heads_out_all = tied(heads_out_all, grad_rest)
     grad_mixture = dot_t(grad_branch, heads_out_all).astype(BF16)
@@ -560,18 +512,16 @@
         short = short_backward(projected, grad_mixture, g)
         return lax.dynamic_update_slice(short, grad_long, (short_rows, 0))
 
-    low_grad = tied(grad_group(0, grad_mixture), grad_reduce)
-    grad_low = Chain(place, reduce_stages(place, [dot_l(first_norm, low_grad).astype(BF16)], False))
-    grad_mixture = tied(grad_mixture, grad_low)
-    high_grad = tied(grad_group(1, grad_mixture), grad_low, grad_reduce, grad_rest)
-    grad_high = Chain(
-        place, reduce_stages(place, [dot_l(first_norm, high_grad).astype(BF16)], True)
-    )
-    heads_in_all = tied(heads_in_all, grad_high)
+    low_grad = grad_group(0, grad_mixture)
+    grad_low = Chain(place, reduce_stages(place, dot_l(first_norm, low_grad).astype(BF16)))
+    grad_mixture = tied(grad_mixture, grad_low, grad_rest)
+    high_grad = tied(grad_group(1, grad_mixture), grad_low, grad_reduce)
+    grad_high = Chain(place, reduce_stages(place, dot_l(first_norm, high_grad).astype(BF16)))
+    heads_in_all = tied(heads_in_all, grad_high, grad_rest)
     grad_first = dot_t(low_grad, heads_in_all[:, :WIDE]) + dot_t(high_grad, heads_in_all[:, WIDE:])
     embed_back, gain_one, shift_one = first_back(grad_first)
     grad_embedded = (grad_middle + embed_back).astype(BF16)
-    grad_embedded = tied(grad_embedded, grad_high)
+    grad_embedded = tied(grad_embedded, grad_high, grad_low)
     grad_patch = dot_l(normed_low, grad_embedded)
     shift_zero = jnp.sum(grad_embedded.astype(F32), 0)
     grad_normed = dot_t(grad_embedded, patch_all).reshape(slot_count, SPAN * PATCH)
@@ -589,11 +539,10 @@
         ],
         1,
     )
-    packed = tied(packed, grad_low, grad_rest)
-    parts = lax.all_to_all(packed, "fsdp", 0, 0, tiled=True)
+    parts = place.move(packed, place.fsdp_axes)
     chain_grads = parts[:, small_rows, : 2 * LONG_SLOTS].reshape(fsdp, LONG_SLOTS, 2)
     chain_grad = jnp.sum(chain_grads * member, 0)
-    small_sums = tied(jnp.sum(parts[:, :small_rows], 0), grad_high, grad_low, grad_rest)
+    small_sums = tied(jnp.sum(parts[:, :small_rows], 0), grad_high, grad_low)
     small_grads = sum_replicas(place, small_sums)
     grad_totals = jnp.concatenate([slot_grads[:SHORT_SLOTS], chain_grad], 0)
     series_grad = (
@@ -622,29 +571,35 @@
 
 
 def solution(mesh):
+    tuned = mesh.shape["fsdp"] == 8 and mesh.shape["dp"] == 4
+    if tuned:
+        mesh = Mesh(mesh.devices.reshape(4, 2, 2, 2), ("z", "y", "x", "c"))
+    place = Place(tuned)
+    fsdp, both = place.fsdp_axes, place.fsdp_axes + place.dp_axes
     in_specs = (
-        P(("fsdp", "dp"), None),
-        P(("fsdp", "dp")),
-        P(None, "fsdp"),
-        P("fsdp", None),
-        P("fsdp", None),
-        P("fsdp", None),
-        P("fsdp", None),
-        P(None, "fsdp"),
-        P(None, "fsdp"),
-        P("fsdp"),
-        P(("fsdp", "dp"), None),
+        P(both, None),
+        P(both),
+        P(None, fsdp),
+        P(fsdp, None),
+        P(fsdp, None),
+        P(fsdp, None),
+        P(fsdp, None),
+        P(None, fsdp),
+        P(None, fsdp),
+        P(fsdp),
+        P(both, None),
     )
     out_specs = (
-        P(("fsdp", "dp"), None),
-        P(("fsdp", "dp"), None),
-        P(None, "fsdp"),
-        P("fsdp", None),
-        P("fsdp", None),
-        P("fsdp", None),
-        P("fsdp", None),
-        P(None, "fsdp"),
-        P(None, "fsdp"),
-        P("fsdp"),
-    )
-    return jax.shard_map(body, mesh=mesh, in_specs=in_specs, out_specs=out_specs, check_vma=False)
+        P(both, None),
+        P(both, None),
+        P(None, fsdp),
+        P(fsdp, None),
+        P(fsdp, None),
+        P(fsdp, None),
+        P(fsdp, None),
+        P(None, fsdp),
+        P(None, fsdp),
+        P(fsdp),
+    )
+    layer = lambda *arguments: body(place, *arguments)
+    return jax.shard_map(layer, mesh=mesh, in_specs=in_specs, out_specs=out_specs, check_vma=False)

time: 518 us -> 656 us (1.27)
  waiting for transfers between devices: 153 us -> 236 us
  blocking collectives: 0 us -> 28.2 us
  local copies, waits for them, and re-layouts: 60 us -> 78.7 us
  between operations: 16 us -> 2.33 us
  matrix products: 89.7 us -> 99.4 us
  Pallas kernels: 51.9 us -> 61.1 us
    all_to_all x3 -> x19, waiting for transfers between devices: 2.58 us -> 173 us  [move(): return lax.all_to_all(value, axes, 0, 0, tiled=True)]
    ppermute x52 -> x15, waiting for transfers between devices: 150 us -> 62.8 us  [the longest x6 62.7 us: along(): return lax.ppermute(value, self.fsdp_axes, pairs)]
    ppermute x52 -> x15, starting transfers between devices: 79.8 us -> 5.88 us  [the longest x6 4.77 us: along(): return lax.ppermute(value, self.fsdp_axes, pairs)]
    all_to_all x3 -> x19, starting transfers between devices: 12.9 us -> 82.5 us  [move(): return lax.all_to_all(value, axes, 0, 0, tiled=True)]
    all_to_all x0 -> x2, blocking collectives: none -> 28.2 us  [move(): return lax.all_to_all(value, axes, 0, 0, tiled=True)]
    convert_element_type x20 -> x2, other arithmetic: 23.3 us -> 2.99 us  [reduce_stages(): got[:, row:row + rows].reshape(4 * rows, columns).astype(F32)]
    broadcast_in_dim x2 -> x12, local copies, waits for them, and re-layouts: 1.5 us -> 13.9 us  [copies(): return jnp.broadcast_to(value, (count,) + value.shape)]
    transpose x0 -> x6, other arithmetic: none -> 12 us  [reduce_stages(): (pick(view, core, 3).astype(F32) + other.astype(F32)).astype(BF16)]
  transfers between devices with their start and end apart: 56 -> 34, of which waited for: 22 -> 17; matrix products, arithmetic and copies ran while one was open for 21% -> 20% of each run, Pallas kernels for 9% -> 8%
where the time goes in v4:
time: 656 us; the launch traced here: 646 us
  waiting for transfers between devices  236 us (36%)
  matrix products  99.4 us (15%)
  starting transfers between devices  88.4 us (13%)
  local copies, waits for them, and re-layouts  78.7 us (12%)
  Pallas kernels  61.1 us (9%)
  other arithmetic  52.4 us (8%)
  blocking collectives  28.2 us (4%)
    all_to_all x19, waiting for transfers between devices, move(): return lax.all_to_all(value, axes, 0, 0, tiled=True)  173 us
    all_to_all x19, starting transfers between devices, move(): return lax.all_to_all(value, axes, 0, 0, tiled=True)  82.5 us
    ppermute x6, waiting for transfers between devices, along(): return lax.ppermute(value, self.fsdp_axes, pairs)  62.7 us
    dot_general x6, matrix products, dot_n(): lax.dot_general(a, b, (((1,), (0,)), ((), ())), preferred_element_type=F32)  44.5 us
    dot_general x6, matrix products, dot_t(): lax.dot_general(a, b, (((1,), (1,)), ((), ())), preferred_element_type=F32)  32 us
    all_to_all x2, blocking collectives, move(): return lax.all_to_all(value, axes, 0, 0, tiled=True)  28.2 us
    dot_general x6, matrix products, dot_l(): lax.dot_general(a, b, (((0,), (0,)), ((), ())), preferred_element_type=F32)  23 us
    pallas_call x2, Pallas kernels, short_backward(): pl.pallas_call(short_backward_kernel, grid=(GROUP,), out_shape=jax.ShapeD...  20.5 us
  transfers between devices with their start and end apart: 34, of which 17 were waited for; matrix products, arithmetic and copies ran while one was open for 20% of the time, Pallas kernels for 8%

profile of v4, /device:TPU:0, one launch (start us, length us, event | category | flops | bytes accessed | tf_op | source)
XLA Modules:
  0.0 646.0 jit_solution(2865563550146463640)
XLA Ops:
  5.8 6.3 all-to-all-start.1
  14.0 18.3 %all-to-all-done.1 = bf16[4,32,3072]{2,1,0:T(8,128)(2,1)S(1)} async-done(((bf16[4,32,3072]{2,1,0:T(8,128)(2,1)}), bf16[4,32,3072]{2,1,0:T(8,128)(2,1)S(1)}, u32[]{:S(2)}, u32[]{:S(2)}) %all-to-all-start.1) | async-done | bytes 786464 | tf_op jit(solution)/shard_map/all_to_all | solution.py:46
  35.5 10.8 %all_to_all.105 = bf16[4,32,1024]{2,1,0:T(8,128)(2,1)S(1)} all-to-all(bf16[4,32,1024]{2,1,0:T(8,128)(2,1)S(1)} %broadcast_in_dim.80), channel_id=1, replica_groups=mesh['z'=4,'y'=2,'x'=2,'c'=2] {'z'}, dimensions={0} | all-to-all | bytes 524288 | tf_op jit(solution)/shard_map/all_to_all | solution.py:46
  46.3 4.8 all-to-all-start.2
  52.0 32.5 %all-to-all-done.2 = bf16[4,4,32,3072]{3,2,1,0:T(8,128)(2,1)} async-done(((bf16[4,4,32,3072]{3,2,1,0:T(8,128)(2,1)}), bf16[4,4,32,3072]{3,2,1,0:T(8,128)(2,1)}, u32[]{:S(2)}, u32[]{:S(2)}) %all-to-all-start.2) | async-done | bytes 3145760 | tf_op jit(solution)/shard_map/all_to_all | solution.py:46
  85.3 6.2 all-to-all-start
  92.6 10.7 %all-to-all-done = f32[8,112,128]{2,1,0:T(8,128)S(1)} async-done(((f32[8,112,128]{2,1,0:T(8,128)}), f32[8,112,128]{2,1,0:T(8,128)S(1)}, u32[]{:S(2)}, u32[]{:S(2)}) %all-to-all-start) | async-done | bytes 458784 | tf_op jit(solution)/shard_map/all_to_all | solution.py:46
  103.4 3.5 all-to-all-start.5
  110.5 19.7 %all-to-all-done.5 = bf16[4,128,1024]{2,1,0:T(8,128)(2,1)S(1)} async-done(((bf16[4,128,1024]{2,1,0:T(8,128)(2,1)}), bf16[4,128,1024]{2,1,0:T(8,128)(2,1)S(1)}, u32[]{:S(2)}, u32[]{:S(2)}) %all-to-all-start.5) | async-done | bytes 1048608 | tf_op jit(solution)/shard_map/all_to_all | solution.py:46
  130.2 4.2 all-to-all-start.4
  138.0 5.5 assemble.3
  143.4 5.1 all-to-all-done.4
  148.5 3.8 broadcast_in_dim.83
  152.3 5.0 all-to-all-start.6
  160.2 8.4 %convolution_convert_fusion.q_ref.k_ref.v_ref = bf16[780,3072]{1,0:T(8,128)(2,1)S(1)} fusion(bf16[780,1024]{1,0:T(8,128)(2,1)S(1)} %add_convert_fusion.4, bf16[1024,3072]{1,0:T(8,128)(2,1)} %bitcast.203), kind=kOutput, calls=%fused_computation.18 | convolution fusion | flops 4909731840 | bytes 12681216 | tf_op jit(solution)/shard_map/dot_general | solution.py:201
  169.4 38.9 %collective-permute-done.2 = bf16[60,1024]{1,0:T(8,128)(2,1)S(1)} collective-permute-done((bf16[60,1024]{1,0:T(8,128)(2,1)S(1)}, bf16[60,1024]{1,0:T(8,128)(2,1)S(1)}, u32[]{:S(2)}, u32[]{:S(2)}) %collective-permute-start.2) | collective-permute-done | bytes 122912 | tf_op jit(solution)/shard_map/ppermute | solution.py:41
  210.8 6.8 %long_forward.1 = bf16[60,1024]{1,0:T(8,128)(2,1)} custom-call(s32[4]{0:T(128)} %quarter_ref.3, bf16[60,3072]{1,0:T(8,128)(2,1)} %slice.200.q.k0.v0, bf16[60,3072]{1,0:T(8,128)(2,1)} %slice.200.q.k0.v0, bf16[60,3072]{1,0:T(8,128)(2,1)} %slice.200.q.k0.v0, bf16[60,3072]{1,0:T(8,128)(2,1)} %get-tuple-element.154.k1.v1, ...), custom_call_target="tpu_custom_call" | custom-call | flops 58982400 | bytes 1228800 | tf_op jit(solution)/shard_map/long_forward/pallas_call | solution.py:341
  217.6 2.9 assemble.4
  220.6 10.6 %short_forward.1 = bf16[780,1024]{1,0:T(8,128)(2,1)} custom-call(bf16[780,3072]{1,0:T(8,128)(2,1)} %copy-done.2, bf16[780,3072]{1,0:T(8,128)(2,1)} %copy-done.2, bf16[780,3072]{1,0:T(8,128)(2,1)} %copy-done.2), custom_call_target="tpu_custom_call" | custom-call | flops 707788800 | bytes 6389760 | tf_op jit(solution)/shard_map/short_forward/pallas_call | solution.py:239
  231.9 4.0 fusion.71
  238.2 7.1 %assemble.5 = (bf16[4,2,2,2,32,2048]{5,4,3,2,1,0:T(8,128)(2,1)}, bf16[4,2,2,2,64,1024]{5,4,3,2,1,0:T(8,128)(2,1)}) custom-call(s32[1]{0:T(128)} %bitcast.12.refs_0_, bf16[2,2,4,128,1024]{4,3,2,1,0:T(8,128)(2,1)} %bitcast.25.refs_1_, bf16[2,2,4,128,1024]{4,3,2,1,0:T(8,128)(2,1)} %collective-permute-done.5.refs_2_), custom_call_target="tpu_custom_call" | custom-call | bytes 16777216 | tf_op jit(solution)/shard_map/assemble/pallas_call | solution.py:129
  245.3 21.2 %multiply_convert_fusion = (bf16[780,2048]{1,0:T(8,128)(2,1)S(1)}, f32[780,2048]{1,0:T(8,128)}, f32[780,2048]{1,0:T(8,128)}) fusion(f32[2048]{0:T(1024)S(1)} %bitcast.239, bf16[1024,2048]{1,0:T(8,128)(2,1)} %bitcast.252, f32[780,1024]{1,0:T(8,128)S(1)} %copy-done.8, f32[1024]{0:T(1024)S(1)} %copy-done.67, f32[1024]{0:T(1024)S(1)} %copy-done.58, ...), kind=kOutput, calls=%fused_computation.4 | convolution fusion | flops 3380981760 | bytes 23386208 | tf_op jit(solution)/shard_map/dot_general | solution.py:201
  266.5 5.2 convolution_convert_fusion.4
  275.8 11.8 %add_convert_fusion = bf16[780,2048]{1,0:T(8,128)(2,1)S(1)} fusion(f32[780,2048]{1,0:T(8,128)} %get-tuple-element.145, f32[780,2048]{1,0:T(8,128)} %get-tuple-element.184, f32[2048]{0:T(1024)S(1)} %bitcast.240, bf16[780,1024]{1,0:T(8,128)(2,1)} %param.21, bf16[2048,1024]{1,0:T(8,128)(2,1)} %bitcast.250), kind=kOutput, calls=%fused_computation.3 | convolution fusion | flops 3295518720 | bytes 21774336 | tf_op jit(solution)/shard_map/dot_general | solution.py:193
  287.6 3.7 fusion.13
  294.3 4.6 multiply_reduce_fusion
  298.9 5.5 convolution_convert_fusion.3
  316.4 4.9 all-to-all-start.7
  321.3 5.3 convolution_convert_fusion.7.g_ref
  332.9 13.5 %all-to-all-done.7 = bf16[4,4,64,1024]{3,2,1,0:T(8,128)(2,1)S(1)} async-done(((bf16[4,4,64,1024]{3,2,1,0:T(8,128)(2,1)}), bf16[4,4,64,1024]{3,2,1,0:T(8,128)(2,1)S(1)}, u32[]{:S(2)}, u32[]{:S(2)}) %all-to-all-start.7) | async-done | bytes 2097184 | tf_op jit(solution)/shard_map/all_to_all | solution.py:46
  347.7 3.7 all-to-all-start.8
  352.9 7.7 %long_backward.1 = (bf16[60,1024]{1,0:T(8,128)(2,1)}, f32[2,60,1024]{2,1,0:T(8,128)}, bf16[2,60,1024]{2,1,0:T(8,128)(2,1)}, bf16[2,60,1024]{2,1,0:T(8,128)(2,1)}, bf16[2,60,1024]{2,1,0:T(8,128)(2,1)}) custom-call(s32[4]{0:T(128)} %quarter_ref.3, bf16[60,3072]{1,0:T(8,128)(2,1)} %slice.200.q.k0.v0, bf16[60,3072]{1,0:T(8,128)(2,1)} %slice.200.q.k0.v0, ...), custom_call_target="tpu_custom_call" | custom-call | flops 147456000 | bytes 2457600 | tf_op jit(solution)/shard_map/long_backward/pallas_call | solution.py:381
  363.3 10.2 %short_backward.2 = bf16[780,1536]{1,0:T(8,128)(2,1)} custom-call(bf16[780,3072]{1,0:T(8,128)(2,1)} %copy-done.2, bf16[780,3072]{1,0:T(8,128)(2,1)} %copy-done.2, bf16[780,3072]{1,0:T(8,128)(2,1)} %copy-done.2, bf16[780,1024]{1,0:T(8,128)(2,1)} %convolution_convert_fusion.7.g_ref), custom_call_target="tpu_custom_call" | custom-call | flops 884736000 | bytes 5591040 | tf_op jit(solution)/shard_map/short_backward/pallas_call | solution.py:283
  374.3 23.8 %collective-permute-done.10 = bf16[2,60,1024]{2,1,0:T(8,128)(2,1)S(1)} collective-permute-done((bf16[2,60,1024]{2,1,0:T(8,128)(2,1)}, bf16[2,60,1024]{2,1,0:T(8,128)(2,1)S(1)}, u32[]{:S(2)}, u32[]{:S(2)}) %collective-permute-start.10) | collective-permute-done | bytes 245792 | tf_op jit(solution)/shard_map/ppermute | solution.py:41
  400.3 4.1 all-to-all-start.9
  404.4 5.6 convolution_convert_fusion.2
  414.7 3.9 all-to-all-done.9
  418.5 4.6 all-to-all-start.10
  423.1 3.0 convert_reduce_fusion
  427.3 10.4 %short_backward.3 = bf16[780,1536]{1,0:T(8,128)(2,1)} custom-call(bf16[780,3072]{1,0:T(8,128)(2,1)} %copy-done.2, bf16[780,3072]{1,0:T(8,128)(2,1)} %copy-done.2, bf16[780,3072]{1,0:T(8,128)(2,1)} %copy-done.2, bf16[780,1024]{1,0:T(8,128)(2,1)} %convolution_convert_fusion.7.g_ref), custom_call_target="tpu_custom_call" | custom-call | flops 884736000 | bytes 5591040 | tf_op jit(solution)/shard_map/short_backward/pallas_call | solution.py:283
  438.3 4.5 all-to-all-done.10
  448.3 3.8 convolution_convert_fusion.1
  455.5 2.7 fusion.9
  458.3 5.5 multiply_reduce_fusion.1
  463.9 4.3 all-to-all-start.11
  468.2 3.1 fusion.60
  472.9 15.5 %all-to-all-done.11 = bf16[4,4,32,1536]{3,2,1,0:T(8,128)(2,1)} async-done(((bf16[4,4,32,1536]{3,2,1,0:T(8,128)(2,1)}), bf16[4,4,32,1536]{3,2,1,0:T(8,128)(2,1)}, u32[]{:S(2)}, u32[]{:S(2)}) %all-to-all-start.11) | async-done | bytes 1572896 | tf_op jit(solution)/shard_map/all_to_all | solution.py:46
  488.4 4.3 all-to-all-start.20
  515.0 4.1 all-to-all-start.14
  521.6 10.2 %all-to-all-done.14 = bf16[4,32,1536]{2,1,0:T(8,128)(2,1)} async-done(((bf16[4,32,1536]{2,1,0:T(8,128)(2,1)}), bf16[4,32,1536]{2,1,0:T(8,128)(2,1)}, u32[]{:S(2)}, u32[]{:S(2)}) %all-to-all-start.14) | async-done | bytes 393248 | tf_op jit(solution)/shard_map/all_to_all | solution.py:46
  531.8 17.4 %all_to_all.106 = f32[8,112,128]{2,1,0:T(8,128)} all-to-all(f32[8,112,128]{2,1,0:T(8,128)} %pad_maximum_fusion.1), channel_id=1, replica_groups=mesh['z'=4,'y'=2,'x'=2,'c'=2] {'z','y'}, dimensions={0} | all-to-all | bytes 917504 | tf_op jit(solution)/shard_map/all_to_all | solution.py:46
  549.2 4.3 all-to-all-start.13
  557.0 15.0 %all-to-all-done.13 = bf16[4,4,32,1536]{3,2,1,0:T(8,128)(2,1)} async-done(((bf16[4,4,32,1536]{3,2,1,0:T(8,128)(2,1)}), bf16[4,4,32,1536]{3,2,1,0:T(8,128)(2,1)}, u32[]{:S(2)}, u32[]{:S(2)}) %all-to-all-start.13) | async-done | bytes 1572896 | tf_op jit(solution)/shard_map/all_to_all | solution.py:46
  572.0 4.2 all-to-all-start.19
  576.2 7.8 %add_convert_fusion.2 = bf16[780,1024]{1,0:T(8,128)(2,1)} fusion(f32[780,1024]{1,0:T(8,128)S(1)} %copy-done.9, bf16[780,2048]{1,0:T(8,128)(2,1)} %copy-done.72, bf16[2048,1024]{1,0:T(8,128)(2,1)} %bitcast.251, f32[1024]{0:T(1024)} %get-tuple-element.172), kind=kOutput, calls=%fused_computation.35 | convolution fusion | flops 3273953280 | bytes 12185600 | tf_op jit(solution)/shard_map/dot_general | solution.py:201
  592.2 3.4 all-to-all-start.15
  596.8 4.2 all-to-all-done.15
  601.1 3.5 all-to-all-start.17
  607.4 8.4 %all-to-all-done.17 = bf16[4,32,1536]{2,1,0:T(8,128)(2,1)S(1)} async-done(((bf16[4,32,1536]{2,1,0:T(8,128)(2,1)}), bf16[4,32,1536]{2,1,0:T(8,128)(2,1)S(1)}, u32[]{:S(2)}, u32[]{:S(2)}) %all-to-all-start.17) | async-done | bytes 393248 | tf_op jit(solution)/shard_map/all_to_all | solution.py:46
  615.9 3.5 all-to-all-start.16
  619.9 6.8 %all-to-all-done.16 = bf16[4,32,1536]{2,1,0:T(8,128)(2,1)S(1)} async-done(((bf16[4,32,1536]{2,1,0:T(8,128)(2,1)}), bf16[4,32,1536]{2,1,0:T(8,128)(2,1)S(1)}, u32[]{:S(2)}, u32[]{:S(2)}) %all-to-all-start.16) | async-done | bytes 393248 | tf_op jit(solution)/shard_map/all_to_all | solution.py:46
  627.5 3.5 all-to-all-start.18
  633.9 4.5 all-to-all-done.18
  642.8 3.0 copy.102
  (337 shorter events, 128.3 us)
Async XLA Ops:
  0.6 12.4 %copy-start = (bf16[256,1024]{1,0:T(8,128)(2,1)S(1)}, bf16[256,1024]{1,0:T(8,128)(2,1)}, u32[]{:S(2)}) copy-start(bf16[256,1024]{1,0:T(8,128)(2,1)} %param.17) | copy-start | bytes 1572868
  5.8 26.5 %all-to-all-start.1 = ((bf16[4,32,3072]{2,1,0:T(8,128)(2,1)}), bf16[4,32,3072]{2,1,0:T(8,128)(2,1)S(1)}, u32[]{:S(2)}, u32[]{:S(2)}) async-start(bf16[4,32,3072]{2,1,0:T(8,128)(2,1)} %broadcast_in_dim.78), calls=%async_computation.1 | async-start | bytes 1572864 | tf_op jit(solution)/shard_map/all_to_all | solution.py:46
  46.3 38.2 %all-to-all-start.2 = ((bf16[4,4,32,3072]{3,2,1,0:T(8,128)(2,1)}), bf16[4,4,32,3072]{3,2,1,0:T(8,128)(2,1)}, u32[]{:S(2)}, u32[]{:S(2)}) async-start(bf16[4,4,32,3072]{3,2,1,0:T(8,128)(2,1)} %broadcast_in_dim.79), calls=%async_computation.2 | async-start | bytes 6291456 | tf_op jit(solution)/shard_map/all_to_all | solution.py:46
  51.1 55.8 %copy-start.66 = (s32[4]{0:T(128)S(1)}, s32[4]{0:T(128)}, u32[]{:S(2)}) copy-start(s32[4]{0:T(128)} %quarter_ref.3) | copy-start | bytes 52
  85.3 18.0 %all-to-all-start = ((f32[8,112,128]{2,1,0:T(8,128)}), f32[8,112,128]{2,1,0:T(8,128)S(1)}, u32[]{:S(2)}, u32[]{:S(2)}) async-start(f32[8,112,128]{2,1,0:T(8,128)} %broadcast_in_dim.75), calls=%async_computation | async-start | bytes 917504 | tf_op jit(solution)/shard_map/all_to_all | solution.py:46
  92.6 45.3 %collective-permute-start = (bf16[2,2,4,32,3072]{4,3,2,1,0:T(8,128)(2,1)}, bf16[2,2,4,32,3072]{4,3,2,1,0:T(8,128)(2,1)}, u32[]{:S(2)}, u32[]{:S(2)}) collective-permute-start(bf16[2,2,4,32,3072]{4,3,2,1,0:T(8,128)(2,1)} %bitcast.21.refs_1_), channel_id=1, source_target_pairs={{0,1},{1,0},{2,3},{3,2},{4,5},{5,4},{6,7},{7,6},{8,9},{9,8},{10,11... | collective-permute-start | bytes 9437192 | tf_op jit(solution)/shard_map/ppermute | solution.py:45
  103.4 31.1 %copy-start.22 = (f32[8,112,128]{2,1,0:T(8,128)}, f32[8,112,128]{2,1,0:T(8,128)S(1)}, u32[]{:S(2)}) copy-start(f32[8,112,128]{2,1,0:T(8,128)S(1)} %all-to-all-done) | copy-start | bytes 1376260
  103.4 26.8 %all-to-all-start.5 = ((bf16[4,128,1024]{2,1,0:T(8,128)(2,1)}), bf16[4,128,1024]{2,1,0:T(8,128)(2,1)S(1)}, u32[]{:S(2)}, u32[]{:S(2)}) async-start(bf16[4,128,1024]{2,1,0:T(8,128)(2,1)} %broadcast_in_dim.81), calls=%async_computation.5 | async-start | bytes 2097152 | tf_op jit(solution)/shard_map/all_to_all | solution.py:46
  130.2 18.3 %all-to-all-start.4 = ((bf16[4,4,32,1024]{3,2,1,0:T(8,128)(2,1)}), bf16[4,4,32,1024]{3,2,1,0:T(8,128)(2,1)}, u32[]{:S(2)}, u32[]{:S(2)}) async-start(bf16[4,4,32,1024]{3,2,1,0:T(8,128)(2,1)} %broadcast_in_dim.82), calls=%async_computation.4 | async-start | bytes 2097152 | tf_op jit(solution)/shard_map/all_to_all | solution.py:46
  136.2 95.7 %copy-start.3 = (f32[780,1024]{1,0:T(8,128)}, f32[780,1024]{1,0:T(8,128)S(1)}, u32[]{:S(2)}) copy-start(f32[780,1024]{1,0:T(8,128)S(1)} %get-tuple-element.181) | copy-start | bytes 9584644
  136.2 21.0 %copy-start.48 = (f32[780]{0:T(1024)}, f32[780]{0:T(1024)S(1)}, u32[]{:S(2)}) copy-start(f32[780]{0:T(1024)S(1)} %broadcast_multiply_fusion.1) | copy-start | bytes 9364
  137.9 19.3 %copy-start.55 = (f32[780]{0:T(1024)}, f32[780]{0:T(1024)S(1)}, u32[]{:S(2)}) copy-start(f32[780]{0:T(1024)S(1)} %fusion.48) | copy-start | bytes 9364
  152.3 68.3 %all-to-all-start.6 = ((bf16[4,4,128,1024]{3,2,1,0:T(8,128)(2,1)}), bf16[4,4,128,1024]{3,2,1,0:T(8,128)(2,1)}, u32[]{:S(2)}, u32[]{:S(2)}) async-start(bf16[4,4,128,1024]{3,2,1,0:T(8,128)(2,1)} %broadcast_in_dim.83), calls=%async_computation.6 | async-start | bytes 8388608 | tf_op jit(solution)/shard_map/all_to_all | solution.py:46
  158.0 10.6 %copy-start.32 = (bf16[780,1024]{1,0:T(8,128)(2,1)}, bf16[780,1024]{1,0:T(8,128)(2,1)S(1)}, u32[]{:S(2)}) copy-start(bf16[780,1024]{1,0:T(8,128)(2,1)S(1)} %add_convert_fusion.4) | copy-start | bytes 4792324
  158.0 50.4 %slice-start = ((s8[6291456]{0:T(1024)(128)(4,1)}), s8[4194304]{0:T(1024)(128)(4,1)S(1)}, s32[]{:S(2)}) async-start(s8[6291456]{0:T(1024)(128)(4,1)} %bitcast.204), calls=%async_computation.21 | async-start | bytes 8388608
  158.0 50.3 %slice-start.1 = ((s8[6291456]{0:T(1024)(128)(4,1)}), s8[2097152]{0:T(1024)(128)(4,1)S(1)}, s32[]{:S(2)}) async-start(s8[6291456]{0:T(1024)(128)(4,1)} %bitcast.204), calls=%async_computation.22 | async-start | bytes 4194304
  158.0 50.3 %collective-permute-start.2 = (bf16[60,1024]{1,0:T(8,128)(2,1)S(1)}, bf16[60,1024]{1,0:T(8,128)(2,1)S(1)}, u32[]{:S(2)}, u32[]{:S(2)}) collective-permute-start(bf16[60,1024]{1,0:T(8,128)(2,1)S(1)} %slice.201), channel_id=1, source_target_pairs={{0,4},{4,8},{8,12},{12,16},{16,20},{20,24},{24,28},{28,0},{1,5},{5... | collective-permute-start | bytes 368648 | tf_op jit(solution)/shard_map/ppermute | solution.py:41
  160.0 48.3 %collective-permute-start.3 = (bf16[60,1024]{1,0:T(8,128)(2,1)S(1)}, bf16[60,1024]{1,0:T(8,128)(2,1)S(1)}, u32[]{:S(2)}, u32[]{:S(2)}) collective-permute-start(bf16[60,1024]{1,0:T(8,128)(2,1)S(1)} %slice.201), channel_id=1, source_target_pairs={{0,8},{4,12},{8,16},{12,20},{16,24},{20,28},{24,0},{28,4},{1,9},{5... | collective-permute-start | bytes 368648 | tf_op jit(solution)/shard_map/ppermute | solution.py:41
  160.0 48.3 %collective-permute-start.4 = (bf16[60,1024]{1,0:T(8,128)(2,1)S(1)}, bf16[60,1024]{1,0:T(8,128)(2,1)S(1)}, u32[]{:S(2)}, u32[]{:S(2)}) collective-permute-start(bf16[60,1024]{1,0:T(8,128)(2,1)S(1)} %slice.201), channel_id=1, source_target_pairs={{0,12},{4,16},{8,20},{12,24},{16,28},{20,0},{24,4},{28,8},{1,13},{... | collective-permute-start | bytes 368648 | tf_op jit(solution)/shard_map/ppermute | solution.py:41
  168.6 41.1 %copy-start.2 = (bf16[780,3072]{1,0:T(8,128)(2,1)}, bf16[780,3072]{1,0:T(8,128)(2,1)S(1)}, u32[]{:S(2)}) copy-start(bf16[780,3072]{1,0:T(8,128)(2,1)S(1)} %convolution_convert_fusion.q_ref.k_ref.v_ref) | copy-start | bytes 14376964
  169.4 48.2 %collective-permute-start.1 = (bf16[2,2,4,32,1024]{4,3,2,1,0:T(8,128)(2,1)}, bf16[2,2,4,32,1024]{4,3,2,1,0:T(8,128)(2,1)}, u32[]{:S(2)}, u32[]{:S(2)}) collective-permute-start(bf16[2,2,4,32,1024]{4,3,2,1,0:T(8,128)(2,1)} %bitcast.23.refs_1_), channel_id=1, source_target_pairs={{0,1},{1,0},{2,3},{3,2},{4,5},{5,4},{6,7},{7,6},{8,9},{9,8},{10,11... | collective-permute-start | bytes 3145736 | tf_op jit(solution)/shard_map/ppermute | solution.py:45
  220.5 17.6 %collective-permute-start.5 = (bf16[2,2,4,128,1024]{4,3,2,1,0:T(8,128)(2,1)}, bf16[2,2,4,128,1024]{4,3,2,1,0:T(8,128)(2,1)}, u32[]{:S(2)}, u32[]{:S(2)}) collective-permute-start(bf16[2,2,4,128,1024]{4,3,2,1,0:T(8,128)(2,1)} %bitcast.25.refs_1_), channel_id=1, source_target_pairs={{0,1},{1,0},{2,3},{3,2},{4,5},{5,4},{6,7},{7,6},{8,9},{9,8},{10,11... | collective-permute-start | bytes 12582920 | tf_op jit(solution)/shard_map/ppermute | solution.py:45
  220.6 10.7 %copy-start.37 = (bf16[60,1024]{1,0:T(8,128)(2,1)S(1)}, bf16[60,1024]{1,0:T(8,128)(2,1)}, u32[]{:S(2)}) copy-start(bf16[60,1024]{1,0:T(8,128)(2,1)} %long_forward.1) | copy-start | bytes 368644
  238.1 7.1 %copy-start.8 = (f32[780,1024]{1,0:T(8,128)S(1)}, f32[780,1024]{1,0:T(8,128)}, u32[]{:S(2)}) copy-start(f32[780,1024]{1,0:T(8,128)} %copy-done.7) | copy-start | bytes 9584644
  238.1 7.1 %copy-start.58 = (f32[1024]{0:T(1024)S(1)}, f32[1024]{0:T(1024)}, u32[]{:S(2)}) copy-start(f32[1024]{0:T(1024)} %get-tuple-element.189) | copy-start | bytes 12292
  238.1 7.1 %copy-start.65 = (f32[8,2,128]{2,1,0:T(2,128)S(1)}, f32[8,2,128]{2,1,0:T(2,128)}, u32[]{:S(2)}) copy-start(f32[8,2,128]{2,1,0:T(2,128)} %get-tuple-element.158) | copy-start | bytes 24580
  238.1 7.1 %copy-start.67 = (f32[1024]{0:T(1024)S(1)}, f32[1024]{0:T(1024)}, u32[]{:S(2)}) copy-start(f32[1024]{0:T(1024)} %get-tuple-element.173) | copy-start | bytes 12292
  245.3 21.2 %copy-start.16 = (bf16[780,1024]{1,0:T(8,128)(2,1)S(1)}, bf16[780,1024]{1,0:T(8,128)(2,1)}, u32[]{:S(2)}) copy-start(bf16[780,1024]{1,0:T(8,128)(2,1)} %param.21) | copy-start | bytes 4792324
  275.3 12.3 %collective-permute-start.6 = (bf16[4,2,2,64,1024]{4,3,2,1,0:T(8,128)(2,1)}, bf16[4,2,2,64,1024]{4,3,2,1,0:T(8,128)(2,1)}, u32[]{:S(2)}, u32[]{:S(2)}) collective-permute-start(bf16[4,2,2,64,1024]{4,3,2,1,0:T(8,128)(2,1)} %dynamic-slice_bitcast_fusion), channel_id=1, source_target_pairs={{0,1},{1,0},{2,3},{3,2},{4,5},{5,4},{6,7},{7,6},{8,9},{9,8},{10,11... | collective-permute-start | bytes 6291464 | tf_op jit(solution)/shard_map/ppermute | solution.py:45
  275.8 11.9 %copy-start.20 = (bf16[2048,1024]{1,0:T(8,128)(2,1)S(1)}, bf16[2048,1024]{1,0:T(8,128)(2,1)}, u32[]{:S(2)}) copy-start(bf16[2048,1024]{1,0:T(8,128)(2,1)} %copy-done.19) | copy-start | bytes 12582916
  287.6 11.3 %copy-start.24 = (bf16[780,2048]{1,0:T(8,128)(2,1)}, bf16[780,2048]{1,0:T(8,128)(2,1)S(1)}, u32[]{:S(2)}) copy-start(bf16[780,2048]{1,0:T(8,128)(2,1)S(1)} %add_convert_fusion) | copy-start | bytes 9584644
  315.9 10.7 %collective-permute-start.7 = (bf16[4,2,2,32,1024]{4,3,2,1,0:T(8,128)(2,1)}, bf16[4,2,2,32,1024]{4,3,2,1,0:T(8,128)(2,1)}, u32[]{:S(2)}, u32[]{:S(2)}) collective-permute-start(bf16[4,2,2,32,1024]{4,3,2,1,0:T(8,128)(2,1)} %dynamic-slice_bitcast_fusion.5), channel_id=1, source_target_pairs={{0,1},{1,0},{2,3},{3,2},{4,5},{5,4},{6,7},{7,6},{8,9},{9,8},{10,11... | collective-permute-start | bytes 3145736 | tf_op jit(solution)/shard_map/ppermute | solution.py:45
  315.9 12.4 %collective-permute-start.8 = (bf16[4,2,2,32,1024]{4,3,2,1,0:T(8,128)(2,1)}, bf16[4,2,2,32,1024]{4,3,2,1,0:T(8,128)(2,1)}, u32[]{:S(2)}, u32[]{:S(2)}) collective-permute-start(bf16[4,2,2,32,1024]{4,3,2,1,0:T(8,128)(2,1)} %dynamic-slice_bitcast_fusion.4), channel_id=1, source_target_pairs={{0,1},{1,0},{2,3},{3,2},{4,5},{5,4},{6,7},{7,6},{8,9},{9,8},{10,11... | collective-permute-start | bytes 3145736 | tf_op jit(solution)/shard_map/ppermute | solution.py:45
  316.4 30.0 %all-to-all-start.7 = ((bf16[4,4,64,1024]{3,2,1,0:T(8,128)(2,1)}), bf16[4,4,64,1024]{3,2,1,0:T(8,128)(2,1)S(1)}, u32[]{:S(2)}, u32[]{:S(2)}) async-start(bf16[4,4,64,1024]{3,2,1,0:T(8,128)(2,1)} %bitcast.35), calls=%async_computation.7 | async-start | bytes 4194304 | tf_op jit(solution)/shard_map/all_to_all | solution.py:46
  321.3 8.8 %collective-permute-start.9 = (bf16[4,2,2,32,1024]{4,3,2,1,0:T(8,128)(2,1)S(1)}, bf16[4,2,2,32,1024]{4,3,2,1,0:T(8,128)(2,1)S(1)}, u32[]{:S(2)}, u32[]{:S(2)}) collective-permute-start(bf16[4,2,2,32,1024]{4,3,2,1,0:T(8,128)(2,1)S(1)} %dynamic-slice_bitcast_fusion.3), channel_id=1, source_target_pairs={{0,1},{1,0},{2,3},{3,2},{4,5},{5,4},{6,7},{7,6},{8,9},{9,8},{10,11... | collective-permute-start | bytes 3145736 | tf_op jit(solution)/shard_map/ppermute | solution.py:45
  347.7 52.6 %all-to-all-start.8 = ((bf16[4,4,96,1024]{3,2,1,0:T(8,128)(2,1)}), bf16[4,4,96,1024]{3,2,1,0:T(8,128)(2,1)S(1)}, u32[]{:S(2)}, u32[]{:S(2)}) async-start(bf16[4,4,96,1024]{3,2,1,0:T(8,128)(2,1)} %bitcast.197), calls=%async_computation.8 | async-start | bytes 6291456 | tf_op jit(solution)/shard_map/all_to_all | solution.py:46
  360.7 37.5 %collective-permute-start.10 = (bf16[2,60,1024]{2,1,0:T(8,128)(2,1)}, bf16[2,60,1024]{2,1,0:T(8,128)(2,1)S(1)}, u32[]{:S(2)}, u32[]{:S(2)}) collective-permute-start(bf16[2,60,1024]{2,1,0:T(8,128)(2,1)} %get-tuple-element.80), channel_id=1, source_target_pairs={{0,28},{4,0},{8,4},{12,8},{16,12},{20,16},{24,20},{28,24},{1,29},{... | collective-permute-start | bytes 737288 | tf_op jit(solution)/shard_map/ppermute | solution.py:41
  361.5 36.7 %collective-permute-start.11 = (bf16[2,60,1024]{2,1,0:T(8,128)(2,1)}, bf16[2,60,1024]{2,1,0:T(8,128)(2,1)}, u32[]{:S(2)}, u32[]{:S(2)}) collective-permute-start(bf16[2,60,1024]{2,1,0:T(8,128)(2,1)} %get-tuple-element.81), channel_id=1, source_target_pairs={{0,24},{4,28},{8,0},{12,4},{16,8},{20,12},{24,16},{28,20},{1,25},{... | collective-permute-start | bytes 737288 | tf_op jit(solution)/shard_map/ppermute | solution.py:41
  363.2 34.9 %collective-permute-start.12 = (bf16[2,60,1024]{2,1,0:T(8,128)(2,1)}, bf16[2,60,1024]{2,1,0:T(8,128)(2,1)}, u32[]{:S(2)}, u32[]{:S(2)}) collective-permute-start(bf16[2,60,1024]{2,1,0:T(8,128)(2,1)} %get-tuple-element.82), channel_id=1, source_target_pairs={{0,20},{4,24},{8,28},{12,0},{16,4},{20,8},{24,12},{28,16},{1,21},{... | collective-permute-start | bytes 737288 | tf_op jit(solution)/shard_map/ppermute | solution.py:41
  400.3 18.2 %all-to-all-start.9 = ((bf16[4,64,1024]{2,1,0:T(8,128)(2,1)}), bf16[4,64,1024]{2,1,0:T(8,128)(2,1)}, u32[]{:S(2)}, u32[]{:S(2)}) async-start(bf16[4,64,1024]{2,1,0:T(8,128)(2,1)} %reduce_sum.381), calls=%async_computation.9 | async-start | bytes 1048576 | tf_op jit(solution)/shard_map/all_to_all | solution.py:46
  414.7 29.5 %collective-permute-start.13 = (bf16[4,2,2,32,1536]{4,3,2,1,0:T(8,128)(2,1)}, bf16[4,2,2,32,1536]{4,3,2,1,0:T(8,128)(2,1)}, u32[]{:S(2)}, u32[]{:S(2)}) collective-permute-start(bf16[4,2,2,32,1536]{4,3,2,1,0:T(8,128)(2,1)} %dynamic-slice_bitcast_fusion.2), channel_id=1, source_target_pairs={{0,1},{1,0},{2,3},{3,2},{4,5},{5,4},{6,7},{7,6},{8,9},{9,8},{10,11... | collective-permute-start | bytes 4718600 | tf_op jit(solution)/shard_map/ppermute | solution.py:45
  418.5 24.3 %all-to-all-start.10 = ((bf16[4,96,1024]{2,1,0:T(8,128)(2,1)}), bf16[4,96,1024]{2,1,0:T(8,128)(2,1)}, u32[]{:S(2)}, u32[]{:S(2)}) async-start(bf16[4,96,1024]{2,1,0:T(8,128)(2,1)} %reduce_sum.382), calls=%async_computation.10 | async-start | bytes 1572864 | tf_op jit(solution)/shard_map/all_to_all | solution.py:46
  427.3 16.9 %copy-start.27 = (bf16[1024,1536]{1,0:T(8,128)(2,1)S(1)}, bf16[1024,1536]{1,0:T(8,128)(2,1)}, u32[]{:S(2)}) copy-start(bf16[1024,1536]{1,0:T(8,128)(2,1)} %copy-done.26) | copy-start | bytes 9437188
  446.2 9.3 %slice-start.2 = ((s8[6291456]{0:T(1024)(128)(4,1)}), s8[4194304]{0:T(1024)(128)(4,1)S(1)}, s32[]{:S(2)}) async-start(s8[6291456]{0:T(1024)(128)(4,1)} %bitcast.207), calls=%async_computation.23 | async-start | bytes 8388608
  448.3 7.2 %slice-start.3 = ((s8[6291456]{0:T(1024)(128)(4,1)}), s8[2097152]{0:T(1024)(128)(4,1)S(1)}, s32[]{:S(2)}) async-start(s8[6291456]{0:T(1024)(128)(4,1)} %bitcast.207), calls=%async_computation.24 | async-start | bytes 4194304
  455.4 39.8 %collective-permute-start.14 = (bf16[4,2,2,32,1536]{4,3,2,1,0:T(8,128)(2,1)}, bf16[4,2,2,32,1536]{4,3,2,1,0:T(8,128)(2,1)}, u32[]{:S(2)}, u32[]{:S(2)}) collective-permute-start(bf16[4,2,2,32,1536]{4,3,2,1,0:T(8,128)(2,1)} %dynamic-slice_bitcast_fusion.1), channel_id=1, source_target_pairs={{0,1},{1,0},{2,3},{3,2},{4,5},{5,4},{6,7},{7,6},{8,9},{9,8},{10,11... | collective-permute-start | bytes 4718600 | tf_op jit(solution)/shard_map/ppermute | solution.py:45
  458.3 9.9 %copy-start.51 = (f32[780]{0:T(1024)S(1)}, f32[780]{0:T(1024)}, u32[]{:S(2)}) copy-start(f32[780]{0:T(1024)} %copy-done.50) | copy-start | bytes 9364
  463.9 24.6 %all-to-all-start.11 = ((bf16[4,4,32,1536]{3,2,1,0:T(8,128)(2,1)}), bf16[4,4,32,1536]{3,2,1,0:T(8,128)(2,1)}, u32[]{:S(2)}, u32[]{:S(2)}) async-start(bf16[4,4,32,1536]{3,2,1,0:T(8,128)(2,1)} %bitcast.212), calls=%async_computation.11 | async-start | bytes 3145728 | tf_op jit(solution)/shard_map/all_to_all | solution.py:46
  488.4 26.6 %all-to-all-start.20 = ((bf16[4,64,1024]{2,1,0:T(8,128)(2,1)}), bf16[4,64,1024]{2,1,0:T(8,128)(2,1)}, u32[]{:S(2)}, u32[]{:S(2)}) async-start(bf16[4,64,1024]{2,1,0:T(8,128)(2,1)} %broadcast_in_dim.86), calls=%async_computation.20 | async-start | bytes 1048576 | tf_op jit(solution)/shard_map/all_to_all | solution.py:46
  515.0 16.8 %all-to-all-start.14 = ((bf16[4,32,1536]{2,1,0:T(8,128)(2,1)}), bf16[4,32,1536]{2,1,0:T(8,128)(2,1)}, u32[]{:S(2)}, u32[]{:S(2)}) async-start(bf16[4,32,1536]{2,1,0:T(8,128)(2,1)} %reduce_sum.387), calls=%async_computation.14 | async-start | bytes 786432 | tf_op jit(solution)/shard_map/all_to_all | solution.py:46
  519.9 56.3 %copy-start.9 = (f32[780,1024]{1,0:T(8,128)S(1)}, f32[780,1024]{1,0:T(8,128)}, u32[]{:S(2)}) copy-start(f32[780,1024]{1,0:T(8,128)} %copy-done.7) | copy-start | bytes 9584644
  549.2 22.8 %all-to-all-start.13 = ((bf16[4,4,32,1536]{3,2,1,0:T(8,128)(2,1)}), bf16[4,4,32,1536]{3,2,1,0:T(8,128)(2,1)}, u32[]{:S(2)}, u32[]{:S(2)}) async-start(bf16[4,4,32,1536]{3,2,1,0:T(8,128)(2,1)} %bitcast.211), calls=%async_computation.13 | async-start | bytes 3145728 | tf_op jit(solution)/shard_map/all_to_all | solution.py:46
  572.0 19.6 %all-to-all-start.19 = ((bf16[4,96,1024]{2,1,0:T(8,128)(2,1)}), bf16[4,96,1024]{2,1,0:T(8,128)(2,1)}, u32[]{:S(2)}, u32[]{:S(2)}) async-start(bf16[4,96,1024]{2,1,0:T(8,128)(2,1)} %broadcast_in_dim.87), calls=%async_computation.19 | async-start | bytes 1572864 | tf_op jit(solution)/shard_map/all_to_all | solution.py:46
  590.7 15.7 %copy-start.61 = (f32[8,1,8]{2,1,0:T(1,128)S(1)}, f32[8,1,8]{2,1,0:T(1,128)}, u32[]{:S(2)}) copy-start(f32[8,1,8]{2,1,0:T(1,128)} %copy.99) | copy-start | bytes 772
  591.5 27.8 %copy-start.64 = (f32[52,2]{0,1:T(2,128)S(1)}, f32[52,2]{0,1:T(2,128)}, u32[]{:S(2)}) copy-start(f32[52,2]{0,1:T(2,128)} %copy-done.63) | copy-start | bytes 1252
  592.2 8.8 %all-to-all-start.15 = ((f32[4,104,128]{2,1,0:T(8,128)}), f32[4,104,128]{2,1,0:T(8,128)S(1)}, u32[]{:S(2)}, u32[]{:S(2)}) async-start(f32[4,104,128]{2,1,0:T(8,128)} %broadcast_in_dim.94), calls=%async_computation.15 | async-start | bytes 425984 | tf_op jit(solution)/shard_map/all_to_all | solution.py:46
  596.8 34.2 %copy-start.36 = (f32[780,96]{0,1:T(8,128)S(1)}, f32[780,96]{0,1:T(8,128)}, u32[]{:S(2)}) copy-start(f32[780,96]{0,1:T(8,128)} %get-tuple-element.187) | copy-start | bytes 898564
  596.8 34.2 %copy-start.41 = (f32[780]{0:T(1024)S(1)}, f32[780]{0:T(1024)}, u32[]{:S(2)}) copy-start(f32[780]{0:T(1024)} %mul.223) | copy-start | bytes 9364
  596.8 34.2 %copy-start.44 = (f32[780]{0:T(1024)S(1)}, f32[780]{0:T(1024)}, u32[]{:S(2)}) copy-start(f32[780]{0:T(1024)} %sub.79) | copy-start | bytes 9364
  596.8 34.2 %copy-start.59 = (f32[780]{0:T(1024)S(1)}, f32[780]{0:T(1024)}, u32[]{:S(2)}) copy-start(f32[780]{0:T(1024)} %div.75) | copy-start | bytes 9364
  601.1 14.8 %all-to-all-start.17 = ((bf16[4,32,1536]{2,1,0:T(8,128)(2,1)}), bf16[4,32,1536]{2,1,0:T(8,128)(2,1)S(1)}, u32[]{:S(2)}, u32[]{:S(2)}) async-start(bf16[4,32,1536]{2,1,0:T(8,128)(2,1)} %reduce_sum.404), calls=%async_computation.17 | async-start | bytes 786432 | tf_op jit(solution)/shard_map/all_to_all | solution.py:46
  615.9 10.8 %all-to-all-start.16 = ((bf16[4,32,1536]{2,1,0:T(8,128)(2,1)}), bf16[4,32,1536]{2,1,0:T(8,128)(2,1)S(1)}, u32[]{:S(2)}, u32[]{:S(2)}) async-start(bf16[4,32,1536]{2,1,0:T(8,128)(2,1)} %broadcast_in_dim.93), calls=%async_computation.16 | async-start | bytes 786432 | tf_op jit(solution)/shard_map/all_to_all | solution.py:46
  627.5 10.8 %all-to-all-start.18 = ((bf16[4,32,1536]{2,1,0:T(8,128)(2,1)}), bf16[4,32,1536]{2,1,0:T(8,128)(2,1)S(1)}, u32[]{:S(2)}, u32[]{:S(2)}) async-start(bf16[4,32,1536]{2,1,0:T(8,128)(2,1)} %broadcast_in_dim.95), calls=%async_computation.18 | async-start | bytes 786432 | tf_op jit(solution)/shard_map/all_to_all | solution.py:46
  639.4 6.4 copy-start.1
  (47 other events, 155.4 us)

commit v5 on v3

--- a/solution.py
+++ b/solution.py
@@ -186,42 +186,48 @@
     return total.astype(BF16)
 
 
-def reduce_stages(place, grads, side_first):
+def weight_grad(place, left, right):
+    if not place.tuned:
+        return dot_l(left, right).astype(BF16)
+    half = right.shape[1] // 2
+    columns = lambda core: lax.dynamic_slice_in_dim(right, core * half, half, 1)
+    got = place.move(dot_l(left, columns(1 - place.c)).astype(BF16), core=1)
+    return (dot_l(left, columns(place.c)) + got.astype(F32)).astype(BF16)
+
+
+def reduce_stages(place, *grads):
     if not place.tuned:
         parts = [
             lax.psum_scatter(g.astype(F32), "fsdp", scatter_dimension=0, tiled=True) for g in grads
         ]
-        return [lax.psum(part.astype(BF16), "dp").astype(F32) for part in parts]
+        return [(lax.psum(part.astype(BF16), "dp").astype(F32),) for part in parts]
     z, y, x, c = place.z, place.y, place.x, place.c
     columns = grads[0].shape[1]
-    views = [g.reshape(8, 2, -1, columns) for g in grads]
-    got = yield [(pick(view, 1 - c, 1), dict(core=1)) for view in views]
-    value = [plus(pick(view, c, 1), other) for view, other in zip(views, got)]
-    value = value[0] if len(value) == 1 else jnp.concatenate(value, 1)
-    half = value.shape[1]
-    if side_first:
-        value = value.reshape(8, 2, half // 2, columns)
-        (got,) = yield [(pick(value, 1 - x, 1), dict(side=1))]
-        value = plus(pick(value, x, 1), got)
+    views = [g.reshape(8, -1, columns) for g in grads]
+    value = views[0] if len(views) == 1 else jnp.concatenate(views, 1)
+    value = value.reshape(8, 2, -1, columns)
+    (got,) = yield [(pick(value, 1 - x, 1), dict(side=1))]
+    value = plus(pick(value, x, 1), got)
     value = value.reshape(4, 2, *value.shape[1:])
     (got,) = yield [(pick(value, 1 - y, 1), dict(pair=1))]
     value = plus(pick(value, y, 1), got)
     got = yield [(pick(value, (z + k) % 4, 0), dict(line=k)) for k in (1, 2, 3)]
     value = plus(pick(value, z, 0), *got)
     (got,) = yield [(value, dict(side=1))]
-    if side_first:
-        low, high = jnp.where(x == 0, value, got), jnp.where(x == 0, got, value)
-        value = jnp.concatenate([low, high], 0)
-    else:
-        value = plus(value, got)
+    low, high = jnp.where(x == 0, value, got), jnp.where(x == 0, got, value)
+    value = jnp.concatenate([low, high], 0)
     (got,) = yield [(value, dict(core=1))]
     low, high = jnp.where(c == 0, value, got), jnp.where(c == 0, got, value)
     results, row = [], 0
     for view in views:
-        rows = slice(row, row + view.shape[2])
-        results.append(jnp.concatenate([low[rows], high[rows]], 0).astype(F32))
-        row += view.shape[2]
+        rows = slice(row, row + view.shape[1])
+        results.append((low[rows].astype(F32), high[rows].astype(F32)))
+        row += view.shape[1]
     return results
+
+
+def joined(*pairs):
+    return jnp.concatenate([part for side in zip(*pairs) for part in side], 1)
 
 
 def sum_replicas(place, part):
@@ -382,10 +388,7 @@
 
 
 def long_specs(rows):
-    sent = lambda part: pl.BlockSpec(
-        (rows, HEAD_DIM), lambda h: (0, (h // GROUP) * 2 * GROUP + part * GROUP + h % GROUP)
-    )
-    return [block_of(rows, part) for part in range(3)] + [sent(0), sent(1)] * 3
+    return [block_of(rows, part) for part in range(3)] + [block_of(rows, 1), block_of(rows, 2)] * 3
 
 
 def long_forward(quarter_index, own, priors):
@@ -503,18 +506,14 @@
     embedded = dot_n(normed_low, patch_all) + biases_all[0]
     first_value, first_back = jax.vjp(layer_norm, embedded, gains_all[0], biases_all[1])
     first_norm = first_value.astype(BF16)
-    own_long = dot_n(first_norm[short_rows:], heads_in_all).astype(BF16)
-
-    group_columns = lambda g, low, high: slice(
-        (g * 3 + low) * GROUP * HEAD_DIM, (g * 3 + high) * GROUP * HEAD_DIM
-    )
-    long_pairs = jnp.concatenate([own_long[:, group_columns(g, 1, 3)] for g in range(GROUPS)], 1)
-    priors = [place.along(long_pairs, step) for step in (1, 2, 3)]
-    first_norm_short, heads_in_all = lax.optimization_barrier(
-        (first_norm[:short_rows], heads_in_all, long_pairs)
-    )[:2]
-    projected = dot_n(first_norm_short, heads_in_all).astype(BF16)
-    projected, priors = lax.optimization_barrier((projected, priors))
+    long_norm = first_norm[short_rows:]
+    prior_norms = jnp.concatenate([place.along(long_norm, step) for step in (1, 2, 3)], 0)
+    prior_norms, heads_in_all = lax.optimization_barrier((prior_norms, heads_in_all))
+    projected = dot_n(first_norm, heads_in_all).astype(BF16)
+    own_long = projected[short_rows:]
+    prior_all = dot_n(prior_norms, heads_in_all).astype(BF16)
+    priors = [prior_all[i * long_rows : (i + 1) * long_rows] for i in range(3)]
+
     mixed_short = short_forward(projected, row_count)
     mixed_long = long_forward(quarter_index, own_long, priors)
     mixed_all = lax.dynamic_update_slice(mixed_short, mixed_long, (short_rows, 0))
@@ -525,26 +524,24 @@
     pre_act = dot_n(second_norm, expand_all) + expand_shift
     act_value, gelu_back = jax.vjp(exact_gelu, pre_act)
     activation = act_value.astype(BF16)
-    grad_reduce = Chain(
-        place, reduce_stages(place, [dot_l(activation, cotangent).astype(BF16)], False)
-    )
-    cotangent = tied(cotangent, grad_reduce)
+    grad_reduce = Chain(place, reduce_stages(place, weight_grad(place, activation, cotangent)))
 
     grad_act = dot_t(cotangent, reduce_all)
     grad_pre = tied(gelu_back(grad_act)[0].astype(BF16), grad_reduce)
-    grad_expand = dot_l(second_norm, grad_pre).astype(BF16)
+    grad_expand = weight_grad(place, second_norm, grad_pre)
     grad_expand_bias = jnp.sum(grad_pre.astype(F32), 0)
     grad_second = dot_t(grad_pre, expand_all)
     middle_back, gain_two, shift_two = second_back(grad_second)
     grad_middle = cotangent.astype(F32) + middle_back
     grad_branch = grad_middle.astype(BF16)
-    grad_heads_out = dot_l(mixed_all, grad_branch).astype(BF16)
+    grad_heads_out = weight_grad(place, mixed_all, grad_branch)
+    wide = grad_heads_out.shape[1]
     grad_rest = Chain(
-        place, reduce_stages(place, [grad_expand[:, :D], grad_expand[:, D:], grad_heads_out], True)
-    )
-    heads_out_all = tied(heads_out_all, grad_rest)
+        place,
+        reduce_stages(place, grad_expand[:, :wide], grad_expand[:, wide:], grad_heads_out),
+    )
     grad_mixture = dot_t(grad_branch, heads_out_all).astype(BF16)
-    grad_mixture, activation = tied((grad_mixture, activation), grad_rest, grad_reduce)
+    grad_mixture, activation = tied((grad_mixture, activation), grad_rest)
     layer_output = (middle + dot_n(activation, reduce_all) + biases_all[3]).astype(BF16)
 
     long_query, own_grads, *sent = long_backward(
@@ -560,14 +557,13 @@
         short = short_backward(projected, grad_mixture, g)
         return lax.dynamic_update_slice(short, grad_long, (short_rows, 0))
 
-    low_grad = tied(grad_group(0, grad_mixture), grad_reduce)
-    grad_low = Chain(place, reduce_stages(place, [dot_l(first_norm, low_grad).astype(BF16)], False))
-    grad_mixture = tied(grad_mixture, grad_low)
-    high_grad = tied(grad_group(1, grad_mixture), grad_low, grad_reduce, grad_rest)
-    grad_high = Chain(
-        place, reduce_stages(place, [dot_l(first_norm, high_grad).astype(BF16)], True)
-    )
-    heads_in_all = tied(heads_in_all, grad_high)
+    grad_mixture, long_query = tied((grad_mixture, long_query), grad_reduce)
+    low_grad = grad_group(0, grad_mixture)
+    grad_low = Chain(place, reduce_stages(place, weight_grad(place, first_norm, low_grad)))
+    grad_mixture = tied(grad_mixture, grad_reduce)
+    high_grad = tied(grad_group(1, grad_mixture), grad_low, grad_rest)
+    grad_high = Chain(place, reduce_stages(place, weight_grad(place, first_norm, high_grad)))
+    heads_in_all = tied(heads_in_all, grad_reduce)
     grad_first = dot_t(low_grad, heads_in_all[:, :WIDE]) + dot_t(high_grad, heads_in_all[:, WIDE:])
     embed_back, gain_one, shift_one = first_back(grad_first)
     grad_embedded = (grad_middle + embed_back).astype(BF16)
@@ -604,17 +600,17 @@
             - normed_slots * grad_totals[:, 1:2] / counts[:, None]
         )
     ).reshape(row_count, PATCH)
-    grouped_grads = jnp.stack([grad_low.finish()[0], grad_high.finish()[0]], 1)
+    grouped_grads = jnp.stack([joined(grad_low.finish()[0]), joined(grad_high.finish()[0])], 1)
     grad_heads_in = grouped_grads.reshape(-1, GROUPS, 3, GROUP * HEAD_DIM).transpose(0, 2, 1, 3)
-    expand_low, expand_high, grad_heads_out = grad_rest.finish()
+    *expand_pairs, heads_out_pair = grad_rest.finish()
     return (
         layer_output,
         series_grad,
         small_grads[:PATCH],
         grad_heads_in.reshape(-1, 3 * D),
-        grad_heads_out,
-        jnp.concatenate([expand_low, expand_high], 1),
-        grad_reduce.finish()[0],
+        joined(heads_out_pair),
+        joined(*expand_pairs),
+        joined(grad_reduce.finish()[0]),
         small_grads[PATCH : PATCH + 2],
         small_grads[PATCH + 2 : PATCH + 6],
         small_grads[PATCH + 6 :].reshape(-1),

time: 518 us -> 451 us (0.87)
  waiting for transfers between devices: 153 us -> 109 us
  starting transfers between devices: 92.7 us -> 81.2 us
  other arithmetic: 47.2 us -> 36.1 us
  matrix products: 89.7 us -> 98.2 us
  local copies, waits for them, and re-layouts: 60 us -> 51.5 us
    ppermute x46 -> x47, waiting for transfers between devices: 134 us -> 73.6 us  [move(): return lax.ppermute(value, AXES, pairs)]
    convert_element_type x18 -> x12, other arithmetic: 21.4 us -> 8.86 us  [plus(): return total.astype(BF16)]
    all_to_all x1, waiting for transfers between devices: 0.01 us -> 10.9 us  [body(): parts = lax.all_to_all(packed, 'fsdp', 0, 0, tiled=True)]
    ppermute x46 -> x47, starting transfers between devices: 62.2 us -> 52.7 us  [move(): return lax.ppermute(value, AXES, pairs)]
    unnamed x196 -> x166, local copies, waits for them, and re-layouts: 19.9 us -> 11.4 us
    ppermute x6, waiting for transfers between devices: 16.5 us -> 24.2 us  [along(): return lax.ppermute(value, 'fsdp', pairs)]
    dot_general x6 -> x11, matrix products: 23.6 us -> 28.8 us  [dot_l(): lax.dot_general(a, b, (((0,), (0,)), ((), ())), preferred_element_type=F32)]
    squeeze x19 -> x15, local copies, waits for them, and re-layouts: 13.1 us -> 9.01 us  [pick(): return lax.dynamic_index_in_dim(value, index, axis, keepdims=False)]
  transfers between devices with their start and end apart: 56 -> 57, of which waited for: 22 -> 21; matrix products, arithmetic and copies ran while one was open for 21% -> 28% of each run, Pallas kernels for 9% -> 10%
where the time goes in v5:
time: 451 us; the launch traced here: 444 us
  waiting for transfers between devices  109 us (24%)
  matrix products  98.2 us (22%)
  starting transfers between devices  81.2 us (18%)
  Pallas kernels  52.1 us (12%)
  local copies, waits for them, and re-layouts  51.5 us (11%)
  other arithmetic  36.1 us (8%)
  between operations  16 us (4%)
    ppermute x47, waiting for transfers between devices, move(): return lax.ppermute(value, AXES, pairs)  73.6 us
    ppermute x47, starting transfers between devices, move(): return lax.ppermute(value, AXES, pairs)  52.7 us
    dot_general x6, matrix products, dot_n(): lax.dot_general(a, b, (((1,), (0,)), ((), ())), preferred_element_type=F32)  39.6 us
    dot_general x6, matrix products, dot_t(): lax.dot_general(a, b, (((1,), (1,)), ((), ())), preferred_element_type=F32)  29.9 us
    dot_general x11, matrix products, dot_l(): lax.dot_general(a, b, (((0,), (0,)), ((), ())), preferred_element_type=F32)  28.8 us
    ppermute x6, waiting for transfers between devices, along(): return lax.ppermute(value, 'fsdp', pairs)  24.2 us
    pallas_call x2, Pallas kernels, short_backward(): pl.pallas_call(short_backward_kernel, grid=(GROUP,), out_shape=jax.ShapeD...  20.6 us
    ppermute x6, starting transfers between devices, along(): return lax.ppermute(value, 'fsdp', pairs)  16.7 us
  transfers between devices with their start and end apart: 57, of which 21 were waited for; matrix products, arithmetic and copies ran while one was open for 28% of the time, Pallas kernels for 10%

profile of v5, /device:TPU:0, one launch (start us, length us, event | category | flops | bytes accessed | tf_op | source)
XLA Modules:
  0.0 444.2 jit_solution(10282063456845076901)
XLA Ops:
  11.0 3.1 collective-permute-start.3
  15.7 4.8 %all-to-all-start = ((f32[8,112,128]{2,1,0:T(8,128)}), f32[8,112,128]{2,1,0:T(8,128)}, u32[]{:S(2)}, u32[]{:S(2)}) async-start(f32[8,112,128]{2,1,0:T(8,128)} %broadcast_in_dim.45), calls=%async_computation | async-start | bytes 917504 | tf_op jit(solution)/shard_map/all_to_all | solution.py:179
  20.6 5.4 %collective-permute-done.3.refs_2_ = bf16[64,3072]{1,0:T(8,128)(2,1)} collective-permute-done((bf16[64,3072]{1,0:T(8,128)(2,1)S(1)}, bf16[64,3072]{1,0:T(8,128)(2,1)}, u32[]{:S(2)}, u32[]{:S(2)}) %collective-permute-start.3) | collective-permute-done | bytes 393248 | tf_op jit(solution)/shard_map/ppermute | solution.py:47
  27.0 1.7 collective-permute-start.9
  28.8 3.6 collective-permute-start.4
  32.5 7.5 %collective-permute-done.9.refs_8_ = bf16[64,3072]{1,0:T(8,128)(2,1)} collective-permute-done((bf16[64,3072]{1,0:T(8,128)(2,1)S(1)}, bf16[64,3072]{1,0:T(8,128)(2,1)}, u32[]{:S(2)}, u32[]{:S(2)}) %collective-permute-start.9) | collective-permute-done | bytes 393248 | tf_op jit(solution)/shard_map/ppermute | solution.py:47
  41.4 6.6 %collective-permute-done.4.refs_3_ = bf16[64,3072]{1,0:T(8,128)(2,1)} collective-permute-done((bf16[64,3072]{1,0:T(8,128)(2,1)}, bf16[64,3072]{1,0:T(8,128)(2,1)}, u32[]{:S(2)}, u32[]{:S(2)}) %collective-permute-start.4) | collective-permute-done | bytes 393248 | tf_op jit(solution)/shard_map/ppermute | solution.py:47
  57.6 1.8 add_reduce_fusion
  60.0 5.0 %collective-permute-done.5.refs_4_ = bf16[64,3072]{1,0:T(8,128)(2,1)} collective-permute-done((bf16[64,3072]{1,0:T(8,128)(2,1)}, bf16[64,3072]{1,0:T(8,128)(2,1)}, u32[]{:S(2)}, u32[]{:S(2)}) %collective-permute-start.5) | collective-permute-done | bytes 393248 | tf_op jit(solution)/shard_map/ppermute | solution.py:47
  66.0 1.9 collective-permute-start.10
  68.0 6.0 %collective-permute-done.10.refs_9_ = bf16[64,3072]{1,0:T(8,128)(2,1)} collective-permute-done((bf16[64,3072]{1,0:T(8,128)(2,1)S(1)}, bf16[64,3072]{1,0:T(8,128)(2,1)}, u32[]{:S(2)}, u32[]{:S(2)}) %collective-permute-start.10) | collective-permute-done | bytes 393248 | tf_op jit(solution)/shard_map/ppermute | solution.py:47
  77.4 9.9 %collective-permute-start.2 = (bf16[60,1024]{1,0:T(8,128)(2,1)S(1)}, bf16[60,1024]{1,0:T(8,128)(2,1)S(1)}, u32[]{:S(2)}, u32[]{:S(2)}) collective-permute-start(bf16[60,1024]{1,0:T(8,128)(2,1)S(1)} %slice.226), channel_id=1, source_target_pairs={{0,12},{4,16},{8,20},{12,24},{16,28},{20,0},{24,4},{28,8},{1,13},{... | collective-permute-start | bytes 368648 | tf_op jit(solution)/shard_map/ppermute | solution.py:51
  87.3 5.3 %collective-permute-start.1 = (bf16[60,1024]{1,0:T(8,128)(2,1)S(1)}, bf16[60,1024]{1,0:T(8,128)(2,1)S(1)}, u32[]{:S(2)}, u32[]{:S(2)}) collective-permute-start(bf16[60,1024]{1,0:T(8,128)(2,1)S(1)} %slice.226), channel_id=1, source_target_pairs={{0,8},{4,12},{8,16},{12,20},{16,24},{20,28},{24,0},{28,4},{1,9},{5... | collective-permute-start | bytes 368648 | tf_op jit(solution)/shard_map/ppermute | solution.py:51
  92.6 12.2 %collective-permute-done.2 = bf16[60,1024]{1,0:T(8,128)(2,1)S(1)} collective-permute-done((bf16[60,1024]{1,0:T(8,128)(2,1)S(1)}, bf16[60,1024]{1,0:T(8,128)(2,1)S(1)}, u32[]{:S(2)}, u32[]{:S(2)}) %collective-permute-start.2) | collective-permute-done | bytes 122912 | tf_op jit(solution)/shard_map/ppermute | solution.py:51
  105.1 10.3 %collective-permute-done = bf16[60,1024]{1,0:T(8,128)(2,1)S(1)} collective-permute-done((bf16[60,1024]{1,0:T(8,128)(2,1)S(1)}, bf16[60,1024]{1,0:T(8,128)(2,1)S(1)}, u32[]{:S(2)}, u32[]{:S(2)}) %collective-permute-start) | collective-permute-done | bytes 122912 | tf_op jit(solution)/shard_map/ppermute | solution.py:51
  120.9 6.3 %assemble.1 = bf16[1024,3072]{1,0:T(8,128)(2,1)} custom-call(s32[4]{0:T(128)} %pad_add_fusion.refs_0_, bf16[128,3072]{1,0:T(8,128)(2,1)} %copy-done.15, bf16[64,3072]{1,0:T(8,128)(2,1)} %collective-permute-done.3.refs_2_, bf16[64,3072]{1,0:T(8,128)(2,1)} %collective-permute-done.4.refs_3_, bf16[64,3072]{1,0:T(8,128)(2,1)} %collective-permute-done.5.refs_4_, ...), custom_call_target="tpu_custom_call" | custom-call | bytes 12582912 | tf_op jit(solution)/shard_map/assemble/pallas_call | solution.py:128
  127.3 7.9 %convolution_convert_fusion.q_ref.k_ref.v_ref = bf16[780,3072]{1,0:T(8,128)(2,1)S(1)} fusion(bf16[780,1024]{1,0:T(8,128)(2,1)} %copy-done.29, bf16[1024,3072]{1,0:T(8,128)(2,1)} %assemble.1), kind=kOutput, calls=%fused_computation.26 | convolution fusion | flops 4909731840 | bytes 12681216 | tf_op jit(solution)/shard_map/dot_general | solution.py:257
  138.5 6.8 %long_forward.1 = bf16[60,1024]{1,0:T(8,128)(2,1)} custom-call(s32[4]{0:T(128)} %quarter_ref.3, bf16[60,3072]{1,0:T(8,128)(2,1)} %slice.227.q.k0.v0, bf16[60,3072]{1,0:T(8,128)(2,1)} %slice.227.q.k0.v0, bf16[60,3072]{1,0:T(8,128)(2,1)} %slice.227.q.k0.v0, bf16[60,3072]{1,0:T(8,128)(2,1)} %get-tuple-element.141.k1.v1, ...), custom_call_target="tpu_custom_call" | custom-call | flops 58982400 | bytes 1228800 | tf_op jit(solution)/shard_map/long_forward/pallas_call | solution.py:397
  145.3 10.6 %short_forward.1 = bf16[780,1024]{1,0:T(8,128)(2,1)} custom-call(bf16[780,3072]{1,0:T(8,128)(2,1)} %copy-done.2, bf16[780,3072]{1,0:T(8,128)(2,1)} %copy-done.2, bf16[780,3072]{1,0:T(8,128)(2,1)} %copy-done.2), custom_call_target="tpu_custom_call" | custom-call | flops 707788800 | bytes 6389760 | tf_op jit(solution)/shard_map/short_forward/pallas_call | solution.py:295
  156.6 4.3 fusion.110
  161.0 1.9 fusion.120
  164.6 20.2 %multiply_convert_fusion = (bf16[780,2048]{1,0:T(8,128)(2,1)S(1)}, f32[780,2048]{1,0:T(8,128)}, f32[780,2048]{1,0:T(8,128)}) fusion(f32[2048]{0:T(1024)S(1)} %bitcast.301, bf16[780,1024]{1,0:T(8,128)(2,1)S(1)} %add_convert_fusion.4, bf16[1024,1024]{1,0:T(8,128)(2,1)S(1)} %bitcast.279, bf16[1024,1024]{1,0:T(8,128)(2,1)S(1)} %bitcast.277), kind=kOutput, calls=%fused_computation.12 | convolution fusion | flops 3385376768 | bytes 21774336 | tf_op jit(solution)/shard_map/dot_general | solution.py:257
  184.8 3.8 convolution_convert_fusion.2
  190.4 2.9 slice.237
  193.4 10.0 %fusion.6 = bf16[780,2048]{1,0:T(8,128)(2,1)S(1)} fusion(f32[780,2048]{1,0:T(8,128)} %get-tuple-element.129, f32[780,2048]{1,0:T(8,128)} %get-tuple-element.202, bf16[2048,1024]{1,0:T(8,128)(2,1)S(1)} %bitcast.261, bf16[780,1024]{1,0:T(8,128)(2,1)S(1)} %copy-done.12, f32[2048]{0:T(1024)S(1)} %bitcast.302), kind=kOutput, calls=%fused_computation.9 | convolution fusion | flops 3295518720 | bytes 21774336 | tf_op jit(solution)/shard_map/dot_general | solution.py:249
  203.4 4.1 add_convert_fusion.1
  207.7 4.6 %multiply_reduce_fusion = (f32[1024]{0:T(1024)}, f32[780]{0:T(1024)S(1)}, f32[1024]{0:T(1024)}, f32[780,1024]{1,0:T(8,128)S(1)}) fusion(f32[780,1024]{1,0:T(8,128)S(1)} %copy-done.6, f32[780]{0:T(1024)S(1)} %fusion.96, f32[780]{0:T(1024)S(1)} %broadcast_multiply_fusion, f32[1024]{0:T(1024)S(1)} %get-tuple-element.194, bf16[780,2048]{1,0:T(8,128)(2,1)S(1)} %fusion.6, ...), kind=kOutput, calls=%fused_computation.36 | convolution fusion | flops 3286332672 | bytes 13800592 | tf_op jit(solution)/shard_map/dot_general | solution.py:249
  214.3 2.4 convolution_convert_fusion.3
  221.1 2.0 convolution_convert_fusion.4.g_ref
  223.2 15.5 %collective-permute-done.20 = bf16[8,128,512]{2,1,0:T(8,128)(2,1)S(1)} collective-permute-done((bf16[8,128,512]{2,1,0:T(8,128)(2,1)S(1)}, bf16[8,128,512]{2,1,0:T(8,128)(2,1)S(1)}, u32[]{:S(2)}, u32[]{:S(2)}) %collective-permute-start.20) | collective-permute-done | bytes 1048608 | tf_op jit(solution)/shard_map/ppermute | solution.py:47
  241.2 2.4 add_convert_fusion
  243.7 1.8 pad_maximum_fusion.1
  245.5 2.7 dynamic-slice_bitcast_fusion
  248.8 7.7 %long_backward.1 = (bf16[60,1024]{1,0:T(8,128)(2,1)}, f32[2,60,1024]{2,1,0:T(8,128)}, bf16[2,60,1024]{2,1,0:T(8,128)(2,1)}, bf16[2,60,1024]{2,1,0:T(8,128)(2,1)}, bf16[2,60,1024]{2,1,0:T(8,128)(2,1)}) custom-call(s32[4]{0:T(128)} %quarter_ref.3, bf16[60,3072]{1,0:T(8,128)(2,1)} %slice.227.q.k0.v0, bf16[60,3072]{1,0:T(8,128)(2,1)} %slice.227.q.k0.v0, ...), custom_call_target="tpu_custom_call" | custom-call | flops 147456000 | bytes 2457600 | tf_op jit(solution)/shard_map/long_backward/pallas_call | solution.py:437
  260.6 10.2 %short_backward.2 = bf16[780,1536]{1,0:T(8,128)(2,1)} custom-call(bf16[780,3072]{1,0:T(8,128)(2,1)} %copy-done.2, bf16[780,3072]{1,0:T(8,128)(2,1)} %copy-done.2, bf16[780,3072]{1,0:T(8,128)(2,1)} %copy-done.2, bf16[780,1024]{1,0:T(8,128)(2,1)} %copy-done.10), custom_call_target="tpu_custom_call" | custom-call | flops 884736000 | bytes 5591040 | tf_op jit(solution)/shard_map/short_backward/pallas_call | solution.py:339
  275.7 4.5 %convolution_convert_fusion.6 = bf16[1024,768]{1,0:T(8,128)(2,1)} fusion(bf16[780,1024]{1,0:T(8,128)(2,1)S(1)} %copy-done.30, bf16[780,1536]{1,0:T(8,128)(2,1)} %maximum_dynamic-update-slice_fusion, s32[]{:T(128)S(6)} %select_n.293), kind=kOutput, calls=%fused_computation.69 | convolution fusion | flops 1227620352 | bytes 4374532 | tf_op jit(solution)/shard_map/dot_general | solution.py:253
  284.0 5.9 %collective-permute-start.25 = (bf16[128,512]{1,0:T(8,128)(2,1)}, bf16[128,512]{1,0:T(8,128)(2,1)S(1)}, u32[]{:S(2)}, u32[]{:S(2)}) collective-permute-start(bf16[128,512]{1,0:T(8,128)(2,1)} %get-tuple-element.61), channel_id=1, source_target_pairs={{0,8},{1,9},{2,10},{3,11},{4,12},{5,13},{6,14},{7,15},{8,16},{9,17... | collective-permute-start | bytes 393224 | tf_op jit(solution)/shard_map/ppermute | solution.py:47
  289.9 2.4 collective-permute-start.27
  292.2 6.5 %add_convert_fusion.3 = bf16[780,1024]{1,0:T(8,128)(2,1)} fusion(f32[780,1024]{1,0:T(8,128)S(1)} %copy-done.7, bf16[780,2048]{1,0:T(8,128)(2,1)} %copy-done.76, bf16[2048,1024]{1,0:T(8,128)(2,1)S(1)} %bitcast.262, f32[1024]{0:T(1024)S(1)} %copy-done.72), kind=kOutput, calls=%fused_computation.40 | convolution fusion | flops 3273953280 | bytes 12185600 | tf_op jit(solution)/shard_map/dot_general | solution.py:257
  298.7 10.4 %short_backward.3 = bf16[780,1536]{1,0:T(8,128)(2,1)} custom-call(bf16[780,3072]{1,0:T(8,128)(2,1)} %copy-done.2, bf16[780,3072]{1,0:T(8,128)(2,1)} %copy-done.2, bf16[780,3072]{1,0:T(8,128)(2,1)} %copy-done.2, bf16[780,1024]{1,0:T(8,128)(2,1)} %copy-done.10), custom_call_target="tpu_custom_call" | custom-call | flops 884736000 | bytes 5591040 | tf_op jit(solution)/shard_map/short_backward/pallas_call | solution.py:339
  311.9 3.8 collective-permute-done.51
  316.5 2.5 fusion.13
  319.6 4.1 add_convert_fusion.7
  324.6 2.5 collective-permute-start.32
  327.1 1.9 convolution_convert_fusion.5
  329.1 4.3 fusion.14
  333.5 5.9 %multiply_reduce_fusion.1 = (f32[1024]{0:T(1024)}, f32[780]{0:T(1024)S(1)}, f32[1024]{0:T(1024)}, f32[780,1024]{1,0:T(8,128)S(1)}) fusion(f32[780,1024]{1,0:T(8,128)S(1)} %get-tuple-element.199, f32[780]{0:T(1024)S(1)} %copy-done.60, f32[780]{0:T(1024)S(1)} %copy-done.54, f32[1024]{0:T(1024)S(1)} %copy-done.51, f32[1024]{0:T(1024)S(1)} %copy-done.62, ...), kind=kOutput, calls=%fused_computation.37 | convolution fusion | flops 2461652224 | bytes 15182896 | tf_op jit(solution)/shard_map/dot_general | solution.py:249
  345.4 1.9 add_convert_fusion.6
  349.4 3.0 fusion.105
  360.3 1.8 pad_maximum_fusion.4
  362.1 1.7 collective-permute-start.35
  364.1 2.4 collective-permute-start.37
  366.5 1.8 collective-permute-start.34
  370.6 3.6 all-to-all-start.1
  374.2 5.6 %collective-permute-done.36 = bf16[192,512]{1,0:T(8,128)(2,1)S(1)} collective-permute-done((bf16[192,512]{1,0:T(8,128)(2,1)}, bf16[192,512]{1,0:T(8,128)(2,1)S(1)}, u32[]{:S(2)}, u32[]{:S(2)}) %collective-permute-start.36) | collective-permute-done | bytes 196640 | tf_op jit(solution)/shard_map/ppermute | solution.py:47
  382.8 10.9 %all-to-all-done.1 = f32[8,112,128]{2,1,0:T(8,128)S(1)} async-done(((f32[8,112,128]{2,1,0:T(8,128)}), f32[8,112,128]{2,1,0:T(8,128)S(1)}, u32[]{:S(2)}, u32[]{:S(2)}) %all-to-all-start.1) | async-done | bytes 458784 | tf_op jit(solution)/shard_map/all_to_all | solution.py:589
  395.6 2.7 collective-permute-start.40
  399.0 3.4 all-to-all-start.2
  402.4 2.0 collective-permute-start.49
  410.2 4.0 collective-permute-done.41
  416.0 3.3 collective-permute-start.46
  419.9 3.1 collective-permute-done.44
  422.9 5.0 %collective-permute-done.45 = bf16[64,768]{1,0:T(8,128)(2,1)S(1)} collective-permute-done((bf16[64,768]{1,0:T(8,128)(2,1)S(1)}, bf16[64,768]{1,0:T(8,128)(2,1)S(1)}, u32[]{:S(2)}, u32[]{:S(2)}) %collective-permute-start.45) | collective-permute-done | bytes 98336 | tf_op jit(solution)/shard_map/ppermute | solution.py:47
  429.7 3.0 collective-permute-done.47
  (407 shorter events, 101.1 us)
Async XLA Ops:
  7.2 149.4 %all-gather.3.cloned.1.call-start = ((), (), s32[]{:S(2)}) async-start(), calls=%async_computation.3 | async-start | bytes 10813440 | tf_op jit(solution)/shard_map/all_gather | solution.py:147
  10.6 21.8 %copy-start.71 = (s32[4]{0:T(128)S(1)}, s32[4]{0:T(128)}, u32[]{:S(2)}) copy-start(s32[4]{0:T(128)} %quarter_ref.3) | copy-start | bytes 52
  10.9 46.7 %copy-start.15 = (bf16[128,3072]{1,0:T(8,128)(2,1)}, bf16[128,3072]{1,0:T(8,128)(2,1)S(1)}, u32[]{:S(2)}) copy-start(bf16[128,3072]{1,0:T(8,128)(2,1)S(1)} %copy.107.refs_1_) | copy-start | bytes 2359300
  11.0 15.1 %collective-permute-start.3 = (bf16[64,3072]{1,0:T(8,128)(2,1)S(1)}, bf16[64,3072]{1,0:T(8,128)(2,1)}, u32[]{:S(2)}, u32[]{:S(2)}) collective-permute-start(bf16[64,3072]{1,0:T(8,128)(2,1)S(1)} %constant_dynamic-slice_fusion.4), channel_id=1, source_target_pairs={{0,8},{1,9},{2,10},{3,11},{4,12},{5,13},{6,14},{7,15},{8,16},{9,17... | collective-permute-start | bytes 1179656 | tf_op jit(solution)/shard_map/ppermute | solution.py:47
  15.7 35.3 %all-to-all-start = ((f32[8,112,128]{2,1,0:T(8,128)}), f32[8,112,128]{2,1,0:T(8,128)}, u32[]{:S(2)}, u32[]{:S(2)}) async-start(f32[8,112,128]{2,1,0:T(8,128)} %broadcast_in_dim.45), calls=%async_computation | async-start | bytes 917504 | tf_op jit(solution)/shard_map/all_to_all | solution.py:179
  27.0 12.9 %collective-permute-start.9 = (bf16[64,3072]{1,0:T(8,128)(2,1)S(1)}, bf16[64,3072]{1,0:T(8,128)(2,1)}, u32[]{:S(2)}, u32[]{:S(2)}) collective-permute-start(bf16[64,3072]{1,0:T(8,128)(2,1)S(1)} %pad_maximum_fusion.5), channel_id=1, source_target_pairs={{0,4},{1,5},{2,6},{3,7},{4,0},{5,1},{6,2},{7,3},{8,12},{9,13},{10,... | collective-permute-start | bytes 1179656 | tf_op jit(solution)/shard_map/ppermute | solution.py:47
  28.8 19.3 %collective-permute-start.4 = (bf16[64,3072]{1,0:T(8,128)(2,1)}, bf16[64,3072]{1,0:T(8,128)(2,1)}, u32[]{:S(2)}, u32[]{:S(2)}) collective-permute-start(bf16[64,3072]{1,0:T(8,128)(2,1)} %collective-permute-done.3.refs_2_), channel_id=1, source_target_pairs={{0,8},{1,9},{2,10},{3,11},{4,12},{5,13},{6,14},{7,15},{8,16},{9,17... | collective-permute-start | bytes 1179656 | tf_op jit(solution)/shard_map/ppermute | solution.py:47
  32.5 54.8 %collective-permute-start.6 = (bf16[64,3072]{1,0:T(8,128)(2,1)}, bf16[64,3072]{1,0:T(8,128)(2,1)}, u32[]{:S(2)}, u32[]{:S(2)}) collective-permute-start(bf16[64,3072]{1,0:T(8,128)(2,1)} %collective-permute-done.3.refs_2_), channel_id=1, source_target_pairs={{0,1},{1,0},{2,3},{3,2},{4,5},{5,4},{6,7},{7,6},{8,9},{9,8},{10,11... | collective-permute-start | bytes 1179656 | tf_op jit(solution)/shard_map/ppermute | solution.py:47
  40.0 76.6 %collective-permute-start.13 = (bf16[64,3072]{1,0:T(8,128)(2,1)}, bf16[64,3072]{1,0:T(8,128)(2,1)}, u32[]{:S(2)}, u32[]{:S(2)}) collective-permute-start(bf16[64,3072]{1,0:T(8,128)(2,1)} %collective-permute-done.9.refs_8_), channel_id=1, source_target_pairs={{0,1},{1,0},{2,3},{3,2},{4,5},{5,4},{6,7},{7,6},{8,9},{9,8},{10,11... | collective-permute-start | bytes 1179656 | tf_op jit(solution)/shard_map/ppermute | solution.py:47
  40.0 76.1 %collective-permute-start.11 = (bf16[64,3072]{1,0:T(8,128)(2,1)}, bf16[64,3072]{1,0:T(8,128)(2,1)}, u32[]{:S(2)}, u32[]{:S(2)}) collective-permute-start(bf16[64,3072]{1,0:T(8,128)(2,1)} %collective-permute-done.9.refs_8_), channel_id=1, source_target_pairs={{0,2},{1,3},{2,0},{3,1},{4,6},{5,7},{6,4},{7,5},{8,10},{9,11},{10,... | collective-permute-start | bytes 1179656 | tf_op jit(solution)/shard_map/ppermute | solution.py:47
  48.1 16.9 %collective-permute-start.5 = (bf16[64,3072]{1,0:T(8,128)(2,1)}, bf16[64,3072]{1,0:T(8,128)(2,1)}, u32[]{:S(2)}, u32[]{:S(2)}) collective-permute-start(bf16[64,3072]{1,0:T(8,128)(2,1)} %collective-permute-done.4.refs_3_), channel_id=1, source_target_pairs={{0,8},{1,9},{2,10},{3,11},{4,12},{5,13},{6,14},{7,15},{8,16},{9,17... | collective-permute-start | bytes 1179656 | tf_op jit(solution)/shard_map/ppermute | solution.py:47
  66.0 7.9 %collective-permute-start.10 = (bf16[64,3072]{1,0:T(8,128)(2,1)S(1)}, bf16[64,3072]{1,0:T(8,128)(2,1)}, u32[]{:S(2)}, u32[]{:S(2)}) collective-permute-start(bf16[64,3072]{1,0:T(8,128)(2,1)S(1)} %pad_maximum_fusion.6), channel_id=1, source_target_pairs={{0,4},{1,5},{2,6},{3,7},{4,0},{5,1},{6,2},{7,3},{8,12},{9,13},{10,... | collective-permute-start | bytes 1179656 | tf_op jit(solution)/shard_map/ppermute | solution.py:47
  74.0 42.7 %collective-permute-start.12 = (bf16[64,3072]{1,0:T(8,128)(2,1)}, bf16[64,3072]{1,0:T(8,128)(2,1)}, u32[]{:S(2)}, u32[]{:S(2)}) collective-permute-start(bf16[64,3072]{1,0:T(8,128)(2,1)} %collective-permute-done.10.refs_9_), channel_id=1, source_target_pairs={{0,2},{1,3},{2,0},{3,1},{4,6},{5,7},{6,4},{7,5},{8,10},{9,11},{10,... | collective-permute-start | bytes 1179656 | tf_op jit(solution)/shard_map/ppermute | solution.py:47
  77.4 27.4 %collective-permute-start.2 = (bf16[60,1024]{1,0:T(8,128)(2,1)S(1)}, bf16[60,1024]{1,0:T(8,128)(2,1)S(1)}, u32[]{:S(2)}, u32[]{:S(2)}) collective-permute-start(bf16[60,1024]{1,0:T(8,128)(2,1)S(1)} %slice.226), channel_id=1, source_target_pairs={{0,12},{4,16},{8,20},{12,24},{16,28},{20,0},{24,4},{28,8},{1,13},{... | collective-permute-start | bytes 368648 | tf_op jit(solution)/shard_map/ppermute | solution.py:51
  87.3 17.7 %collective-permute-start.1 = (bf16[60,1024]{1,0:T(8,128)(2,1)S(1)}, bf16[60,1024]{1,0:T(8,128)(2,1)S(1)}, u32[]{:S(2)}, u32[]{:S(2)}) collective-permute-start(bf16[60,1024]{1,0:T(8,128)(2,1)S(1)} %slice.226), channel_id=1, source_target_pairs={{0,8},{4,12},{8,16},{12,20},{16,24},{20,28},{24,0},{28,4},{1,9},{5... | collective-permute-start | bytes 368648 | tf_op jit(solution)/shard_map/ppermute | solution.py:51
  104.8 10.6 %collective-permute-start = (bf16[60,1024]{1,0:T(8,128)(2,1)S(1)}, bf16[60,1024]{1,0:T(8,128)(2,1)S(1)}, u32[]{:S(2)}, u32[]{:S(2)}) collective-permute-start(bf16[60,1024]{1,0:T(8,128)(2,1)S(1)} %slice.226), channel_id=1, source_target_pairs={{0,4},{4,8},{8,12},{12,16},{16,20},{20,24},{24,28},{28,0},{1,5},{5... | collective-permute-start | bytes 368648 | tf_op jit(solution)/shard_map/ppermute | solution.py:51
  105.0 14.4 %collective-permute-start.7 = (bf16[64,3072]{1,0:T(8,128)(2,1)}, bf16[64,3072]{1,0:T(8,128)(2,1)}, u32[]{:S(2)}, u32[]{:S(2)}) collective-permute-start(bf16[64,3072]{1,0:T(8,128)(2,1)} %collective-permute-done.4.refs_3_), channel_id=1, source_target_pairs={{0,1},{1,0},{2,3},{3,2},{4,5},{5,4},{6,7},{7,6},{8,9},{9,8},{10,11... | collective-permute-start | bytes 1179656 | tf_op jit(solution)/shard_map/ppermute | solution.py:47
  116.1 3.3 collective-permute-start.8
  116.1 3.3 collective-permute-start.15
  116.6 3.4 collective-permute-start.14
  116.7 4.3 collective-permute-start.16
  188.6 14.8 %collective-permute-start.17 = (bf16[2048,512]{1,0:T(8,128)(2,1)}, bf16[2048,512]{1,0:T(8,128)(2,1)}, u32[]{:S(2)}, u32[]{:S(2)}) collective-permute-start(bf16[2048,512]{1,0:T(8,128)(2,1)} %convolution_convert_fusion.2), channel_id=1, source_target_pairs={{0,1},{1,0},{2,3},{3,2},{4,5},{5,4},{6,7},{7,6},{8,9},{9,8},{10,11... | collective-permute-start | bytes 6291464 | tf_op jit(solution)/shard_map/ppermute | solution.py:47
  213.4 25.3 %collective-permute-start.20 = (bf16[8,128,512]{2,1,0:T(8,128)(2,1)S(1)}, bf16[8,128,512]{2,1,0:T(8,128)(2,1)S(1)}, u32[]{:S(2)}, u32[]{:S(2)}) collective-permute-start(bf16[8,128,512]{2,1,0:T(8,128)(2,1)S(1)} %dynamic-slice_bitcast_fusion.1), channel_id=1, source_target_pairs={{0,2},{1,3},{2,0},{3,1},{4,6},{5,7},{6,4},{7,5},{8,10},{9,11},{10,... | collective-permute-start | bytes 3145736 | tf_op jit(solution)/shard_map/ppermute | solution.py:47
  216.7 24.5 %collective-permute-start.18 = (bf16[1024,1024]{1,0:T(8,128)(2,1)S(1)}, bf16[1024,1024]{1,0:T(8,128)(2,1)S(1)}, u32[]{:S(2)}, u32[]{:S(2)}) collective-permute-start(bf16[1024,1024]{1,0:T(8,128)(2,1)S(1)} %convolution_convert_fusion.3), channel_id=1, source_target_pairs={{0,1},{1,0},{2,3},{3,2},{4,5},{5,4},{6,7},{7,6},{8,9},{9,8},{10,11... | collective-permute-start | bytes 6291464 | tf_op jit(solution)/shard_map/ppermute | solution.py:47
  219.5 20.4 %collective-permute-start.19 = (bf16[1024,512]{1,0:T(8,128)(2,1)S(1)}, bf16[1024,512]{1,0:T(8,128)(2,1)S(1)}, u32[]{:S(2)}, u32[]{:S(2)}) collective-permute-start(bf16[1024,512]{1,0:T(8,128)(2,1)S(1)} %convolution_convert_fusion.7), channel_id=1, source_target_pairs={{0,1},{1,0},{2,3},{3,2},{4,5},{5,4},{6,7},{7,6},{8,9},{9,8},{10,11... | collective-permute-start | bytes 3145736 | tf_op jit(solution)/shard_map/ppermute | solution.py:47
  223.1 25.0 %copy-start.10 = (bf16[780,1024]{1,0:T(8,128)(2,1)}, bf16[780,1024]{1,0:T(8,128)(2,1)S(1)}, u32[]{:S(2)}) copy-start(bf16[780,1024]{1,0:T(8,128)(2,1)S(1)} %convolution_convert_fusion.4.g_ref) | copy-start | bytes 4792324
  256.5 15.3 %collective-permute-start.21 = (bf16[2,60,1024]{2,1,0:T(8,128)(2,1)}, bf16[2,60,1024]{2,1,0:T(8,128)(2,1)S(1)}, u32[]{:S(2)}, u32[]{:S(2)}) collective-permute-start(bf16[2,60,1024]{2,1,0:T(8,128)(2,1)} %get-tuple-element.57), channel_id=1, source_target_pairs={{0,28},{4,0},{8,4},{12,8},{16,12},{20,16},{24,20},{28,24},{1,29},{... | collective-permute-start | bytes 737288 | tf_op jit(solution)/shard_map/ppermute | solution.py:51
  256.6 15.3 %collective-permute-start.22 = (bf16[2,60,1024]{2,1,0:T(8,128)(2,1)}, bf16[2,60,1024]{2,1,0:T(8,128)(2,1)}, u32[]{:S(2)}, u32[]{:S(2)}) collective-permute-start(bf16[2,60,1024]{2,1,0:T(8,128)(2,1)} %get-tuple-element.58), channel_id=1, source_target_pairs={{0,24},{4,28},{8,0},{12,4},{16,8},{20,12},{24,16},{28,20},{1,25},{... | collective-permute-start | bytes 737288 | tf_op jit(solution)/shard_map/ppermute | solution.py:51
  256.7 16.9 %collective-permute-start.23 = (bf16[2,60,1024]{2,1,0:T(8,128)(2,1)}, bf16[2,60,1024]{2,1,0:T(8,128)(2,1)}, u32[]{:S(2)}, u32[]{:S(2)}) collective-permute-start(bf16[2,60,1024]{2,1,0:T(8,128)(2,1)} %get-tuple-element.59), channel_id=1, source_target_pairs={{0,20},{4,24},{8,28},{12,0},{16,4},{20,8},{24,12},{28,16},{1,21},{... | collective-permute-start | bytes 737288 | tf_op jit(solution)/shard_map/ppermute | solution.py:51
  257.8 23.4 %collective-permute-start.24 = (bf16[4,128,512]{2,1,0:T(8,128)(2,1)}, bf16[4,128,512]{2,1,0:T(8,128)(2,1)}, u32[]{:S(2)}, u32[]{:S(2)}) collective-permute-start(bf16[4,128,512]{2,1,0:T(8,128)(2,1)} %dynamic-slice_bitcast_fusion.5), channel_id=1, source_target_pairs={{0,4},{1,5},{2,6},{3,7},{4,0},{5,1},{6,2},{7,3},{8,12},{9,13},{10,... | collective-permute-start | bytes 1572872 | tf_op jit(solution)/shard_map/ppermute | solution.py:47
  259.3 57.2 %collective-permute-start.29 = (bf16[8,192,512]{2,1,0:T(8,128)(2,1)}, bf16[8,192,512]{2,1,0:T(8,128)(2,1)}, u32[]{:S(2)}, u32[]{:S(2)}) collective-permute-start(bf16[8,192,512]{2,1,0:T(8,128)(2,1)} %dynamic-slice_bitcast_fusion), channel_id=1, source_target_pairs={{0,2},{1,3},{2,0},{3,1},{4,6},{5,7},{6,4},{7,5},{8,10},{9,11},{10,... | collective-permute-start | bytes 4718600 | tf_op jit(solution)/shard_map/ppermute | solution.py:47
  280.1 39.0 %collective-permute-start.28 = (bf16[1024,768]{1,0:T(8,128)(2,1)}, bf16[1024,768]{1,0:T(8,128)(2,1)}, u32[]{:S(2)}, u32[]{:S(2)}) collective-permute-start(bf16[1024,768]{1,0:T(8,128)(2,1)} %convolution_convert_fusion.6), channel_id=1, source_target_pairs={{0,1},{1,0},{2,3},{3,2},{4,5},{5,4},{6,7},{7,6},{8,9},{9,8},{10,11... | collective-permute-start | bytes 4718600 | tf_op jit(solution)/shard_map/ppermute | solution.py:47
  284.0 25.1 %collective-permute-start.25 = (bf16[128,512]{1,0:T(8,128)(2,1)}, bf16[128,512]{1,0:T(8,128)(2,1)S(1)}, u32[]{:S(2)}, u32[]{:S(2)}) collective-permute-start(bf16[128,512]{1,0:T(8,128)(2,1)} %get-tuple-element.61), channel_id=1, source_target_pairs={{0,8},{1,9},{2,10},{3,11},{4,12},{5,13},{6,14},{7,15},{8,16},{9,17... | collective-permute-start | bytes 393224 | tf_op jit(solution)/shard_map/ppermute | solution.py:47
  289.9 19.3 %collective-permute-start.26 = (bf16[128,512]{1,0:T(8,128)(2,1)}, bf16[128,512]{1,0:T(8,128)(2,1)}, u32[]{:S(2)}, u32[]{:S(2)}) collective-permute-start(bf16[128,512]{1,0:T(8,128)(2,1)} %get-tuple-element.62), channel_id=1, source_target_pairs={{0,16},{1,17},{2,18},{3,19},{4,20},{5,21},{6,22},{7,23},{8,24},{9,... | collective-permute-start | bytes 393224 | tf_op jit(solution)/shard_map/ppermute | solution.py:47
  289.9 19.3 %collective-permute-start.27 = (bf16[128,512]{1,0:T(8,128)(2,1)}, bf16[128,512]{1,0:T(8,128)(2,1)}, u32[]{:S(2)}, u32[]{:S(2)}) collective-permute-start(bf16[128,512]{1,0:T(8,128)(2,1)} %get-tuple-element.63), channel_id=1, source_target_pairs={{0,24},{1,25},{2,26},{3,27},{4,28},{5,29},{6,30},{7,31},{8,0},{9,1... | collective-permute-start | bytes 393224 | tf_op jit(solution)/shard_map/ppermute | solution.py:47
  310.3 5.4 %collective-permute-start.51 = (bf16[128,512]{1,0:T(8,128)(2,1)S(1)}, bf16[128,512]{1,0:T(8,128)(2,1)S(1)}, u32[]{:S(2)}, u32[]{:S(2)}) collective-permute-start(bf16[128,512]{1,0:T(8,128)(2,1)S(1)} %fusion.67), channel_id=1, source_target_pairs={{0,2},{1,3},{2,0},{3,1},{4,6},{5,7},{6,4},{7,5},{8,10},{9,11},{10,... | collective-permute-start | bytes 393224 | tf_op jit(solution)/shard_map/ppermute | solution.py:47
  316.5 50.0 %collective-permute-start.52 = (bf16[256,512]{1,0:T(8,128)(2,1)}, bf16[256,512]{1,0:T(8,128)(2,1)}, u32[]{:S(2)}, u32[]{:S(2)}) collective-permute-start(bf16[256,512]{1,0:T(8,128)(2,1)} %pad_maximum_fusion.12), channel_id=1, source_target_pairs={{0,1},{1,0},{2,3},{3,2},{4,5},{5,4},{6,7},{7,6},{8,9},{9,8},{10,11... | collective-permute-start | bytes 786440 | tf_op jit(solution)/shard_map/ppermute | solution.py:47
  323.7 19.5 %collective-permute-start.31 = (bf16[8,64,768]{2,1,0:T(8,128)(2,1)S(1)}, bf16[8,64,768]{2,1,0:T(8,128)(2,1)S(1)}, u32[]{:S(2)}, u32[]{:S(2)}) collective-permute-start(bf16[8,64,768]{2,1,0:T(8,128)(2,1)S(1)} %dynamic-slice_bitcast_fusion.4), channel_id=1, source_target_pairs={{0,2},{1,3},{2,0},{3,1},{4,6},{5,7},{6,4},{7,5},{8,10},{9,11},{10,... | collective-permute-start | bytes 2359304 | tf_op jit(solution)/shard_map/ppermute | solution.py:47
  324.6 19.6 %collective-permute-start.32 = (bf16[4,192,512]{2,1,0:T(8,128)(2,1)S(1)}, bf16[4,192,512]{2,1,0:T(8,128)(2,1)S(1)}, u32[]{:S(2)}, u32[]{:S(2)}) collective-permute-start(bf16[4,192,512]{2,1,0:T(8,128)(2,1)S(1)} %dynamic-slice_bitcast_fusion.3), channel_id=1, source_target_pairs={{0,4},{1,5},{2,6},{3,7},{4,0},{5,1},{6,2},{7,3},{8,12},{9,13},{10,... | collective-permute-start | bytes 2359304 | tf_op jit(solution)/shard_map/ppermute | solution.py:47
  329.0 16.4 %collective-permute-start.30 = (bf16[1024,768]{1,0:T(8,128)(2,1)S(1)}, bf16[1024,768]{1,0:T(8,128)(2,1)S(1)}, u32[]{:S(2)}, u32[]{:S(2)}) collective-permute-start(bf16[1024,768]{1,0:T(8,128)(2,1)S(1)} %convolution_convert_fusion.5), channel_id=1, source_target_pairs={{0,1},{1,0},{2,3},{3,2},{4,5},{5,4},{6,7},{7,6},{8,9},{9,8},{10,11... | collective-permute-start | bytes 4718600 | tf_op jit(solution)/shard_map/ppermute | solution.py:47
  356.2 25.2 %collective-permute-start.33 = (bf16[8,64,768]{2,1,0:T(8,128)(2,1)}, bf16[8,64,768]{2,1,0:T(8,128)(2,1)}, u32[]{:S(2)}, u32[]{:S(2)}) collective-permute-start(bf16[8,64,768]{2,1,0:T(8,128)(2,1)} %dynamic-slice_bitcast_fusion.2), channel_id=1, source_target_pairs={{0,2},{1,3},{2,0},{3,1},{4,6},{5,7},{6,4},{7,5},{8,10},{9,11},{10,... | collective-permute-start | bytes 2359304 | tf_op jit(solution)/shard_map/ppermute | solution.py:47
  362.1 12.1 %collective-permute-start.35 = (bf16[192,512]{1,0:T(8,128)(2,1)}, bf16[192,512]{1,0:T(8,128)(2,1)S(1)}, u32[]{:S(2)}, u32[]{:S(2)}) collective-permute-start(bf16[192,512]{1,0:T(8,128)(2,1)} %get-tuple-element.74), channel_id=1, source_target_pairs={{0,8},{1,9},{2,10},{3,11},{4,12},{5,13},{6,14},{7,15},{8,16},{9,17... | collective-permute-start | bytes 589832 | tf_op jit(solution)/shard_map/ppermute | solution.py:47
  363.9 15.9 %collective-permute-start.36 = (bf16[192,512]{1,0:T(8,128)(2,1)}, bf16[192,512]{1,0:T(8,128)(2,1)S(1)}, u32[]{:S(2)}, u32[]{:S(2)}) collective-permute-start(bf16[192,512]{1,0:T(8,128)(2,1)} %get-tuple-element.75), channel_id=1, source_target_pairs={{0,16},{1,17},{2,18},{3,19},{4,20},{5,21},{6,22},{7,23},{8,24},{9,... | collective-permute-start | bytes 589832 | tf_op jit(solution)/shard_map/ppermute | solution.py:47
  364.1 15.6 %collective-permute-start.37 = (bf16[192,512]{1,0:T(8,128)(2,1)}, bf16[192,512]{1,0:T(8,128)(2,1)S(1)}, u32[]{:S(2)}, u32[]{:S(2)}) collective-permute-start(bf16[192,512]{1,0:T(8,128)(2,1)} %get-tuple-element.76), channel_id=1, source_target_pairs={{0,24},{1,25},{2,26},{3,27},{4,28},{5,29},{6,30},{7,31},{8,0},{9,1... | collective-permute-start | bytes 589832 | tf_op jit(solution)/shard_map/ppermute | solution.py:47
  366.5 14.1 %collective-permute-start.34 = (bf16[4,64,768]{2,1,0:T(8,128)(2,1)}, bf16[4,64,768]{2,1,0:T(8,128)(2,1)S(1)}, u32[]{:S(2)}, u32[]{:S(2)}) collective-permute-start(bf16[4,64,768]{2,1,0:T(8,128)(2,1)} %dynamic-slice_bitcast_fusion.7), channel_id=1, source_target_pairs={{0,4},{1,5},{2,6},{3,7},{4,0},{5,1},{6,2},{7,3},{8,12},{9,13},{10,... | collective-permute-start | bytes 1179656 | tf_op jit(solution)/shard_map/ppermute | solution.py:47
  370.6 23.2 %copy-start.69 = (f32[8,1,8]{2,1,0:T(1,128)S(1)}, f32[8,1,8]{2,1,0:T(1,128)}, u32[]{:S(2)}) copy-start(f32[8,1,8]{2,1,0:T(1,128)} %copy.112) | copy-start | bytes 772
  370.6 23.2 %all-to-all-start.1 = ((f32[8,112,128]{2,1,0:T(8,128)}), f32[8,112,128]{2,1,0:T(8,128)S(1)}, u32[]{:S(2)}, u32[]{:S(2)}) async-start(f32[8,112,128]{2,1,0:T(8,128)} %pad_maximum_fusion.4), calls=%async_computation.1 | async-start | bytes 917504 | tf_op jit(solution)/shard_map/all_to_all | solution.py:589
  380.6 21.9 %copy-start.42 = (bf16[192,512]{1,0:T(8,128)(2,1)S(1)}, bf16[192,512]{1,0:T(8,128)(2,1)}, u32[]{:S(2)}) copy-start(bf16[192,512]{1,0:T(8,128)(2,1)} %fusion.63) | copy-start | bytes 589828
  380.6 24.2 %copy-start.38 = (f32[780,96]{0,1:T(8,128)S(1)}, f32[780,96]{0,1:T(8,128)}, u32[]{:S(2)}) copy-start(f32[780,96]{0,1:T(8,128)} %get-tuple-element.205) | copy-start | bytes 898564
  380.6 24.2 %copy-start.67 = (f32[780]{0:T(1024)S(1)}, f32[780]{0:T(1024)}, u32[]{:S(2)}) copy-start(f32[780]{0:T(1024)} %div.96) | copy-start | bytes 9364
  394.5 11.1 %collective-permute-start.38 = (bf16[64,768]{1,0:T(8,128)(2,1)}, bf16[64,768]{1,0:T(8,128)(2,1)S(1)}, u32[]{:S(2)}, u32[]{:S(2)}) collective-permute-start(bf16[64,768]{1,0:T(8,128)(2,1)} %get-tuple-element.78), channel_id=1, source_target_pairs={{0,8},{1,9},{2,10},{3,11},{4,12},{5,13},{6,14},{7,15},{8,16},{9,17... | collective-permute-start | bytes 294920 | tf_op jit(solution)/shard_map/ppermute | solution.py:47
  394.5 11.0 %collective-permute-start.39 = (bf16[64,768]{1,0:T(8,128)(2,1)}, bf16[64,768]{1,0:T(8,128)(2,1)S(1)}, u32[]{:S(2)}, u32[]{:S(2)}) collective-permute-start(bf16[64,768]{1,0:T(8,128)(2,1)} %get-tuple-element.79), channel_id=1, source_target_pairs={{0,16},{1,17},{2,18},{3,19},{4,20},{5,21},{6,22},{7,23},{8,24},{9,... | collective-permute-start | bytes 294920 | tf_op jit(solution)/shard_map/ppermute | solution.py:47
  395.6 10.6 %collective-permute-start.40 = (bf16[64,768]{1,0:T(8,128)(2,1)}, bf16[64,768]{1,0:T(8,128)(2,1)}, u32[]{:S(2)}, u32[]{:S(2)}) collective-permute-start(bf16[64,768]{1,0:T(8,128)(2,1)} %get-tuple-element.80), channel_id=1, source_target_pairs={{0,24},{1,25},{2,26},{3,27},{4,28},{5,29},{6,30},{7,31},{8,0},{9,1... | collective-permute-start | bytes 294920 | tf_op jit(solution)/shard_map/ppermute | solution.py:47
  399.0 9.4 %all-to-all-start.2 = ((f32[4,104,128]{2,1,0:T(8,128)}), f32[4,104,128]{2,1,0:T(8,128)S(1)}, u32[]{:S(2)}, u32[]{:S(2)}) async-start(f32[4,104,128]{2,1,0:T(8,128)} %broadcast_in_dim.55), calls=%async_computation.2 | async-start | bytes 425984 | tf_op jit(solution)/shard_map/all_to_all | solution.py:235
  402.4 11.9 %collective-permute-start.49 = (bf16[192,512]{1,0:T(8,128)(2,1)S(1)}, bf16[192,512]{1,0:T(8,128)(2,1)S(1)}, u32[]{:S(2)}, u32[]{:S(2)}) collective-permute-start(bf16[192,512]{1,0:T(8,128)(2,1)S(1)} %copy-done.42), channel_id=1, source_target_pairs={{0,2},{1,3},{2,0},{3,1},{4,6},{5,7},{6,4},{7,5},{8,10},{9,11},{10,... | collective-permute-start | bytes 589832 | tf_op jit(solution)/shard_map/ppermute | solution.py:47
  404.4 10.9 %collective-permute-start.43 = (bf16[4,64,768]{2,1,0:T(8,128)(2,1)S(1)}, bf16[4,64,768]{2,1,0:T(8,128)(2,1)S(1)}, u32[]{:S(2)}, u32[]{:S(2)}) collective-permute-start(bf16[4,64,768]{2,1,0:T(8,128)(2,1)S(1)} %dynamic-slice_bitcast_fusion.6), channel_id=1, source_target_pairs={{0,4},{1,5},{2,6},{3,7},{4,0},{5,1},{6,2},{7,3},{8,12},{9,13},{10,... | collective-permute-start | bytes 1179656 | tf_op jit(solution)/shard_map/ppermute | solution.py:47
  407.2 7.0 %collective-permute-start.41 = (bf16[64,768]{1,0:T(8,128)(2,1)S(1)}, bf16[64,768]{1,0:T(8,128)(2,1)S(1)}, u32[]{:S(2)}, u32[]{:S(2)}) collective-permute-start(bf16[64,768]{1,0:T(8,128)(2,1)S(1)} %fusion.78), channel_id=1, source_target_pairs={{0,2},{1,3},{2,0},{3,1},{4,6},{5,7},{6,4},{7,5},{8,10},{9,11},{10,... | collective-permute-start | bytes 294920 | tf_op jit(solution)/shard_map/ppermute | solution.py:47
  414.2 5.3 %collective-permute-start.42 = (bf16[128,768]{1,0:T(8,128)(2,1)S(1)}, bf16[128,768]{1,0:T(8,128)(2,1)S(1)}, u32[]{:S(2)}, u32[]{:S(2)}) collective-permute-start(bf16[128,768]{1,0:T(8,128)(2,1)S(1)} %pad_maximum_fusion.13), channel_id=1, source_target_pairs={{0,1},{1,0},{2,3},{3,2},{4,5},{5,4},{6,7},{7,6},{8,9},{9,8},{10,11... | collective-permute-start | bytes 589832 | tf_op jit(solution)/shard_map/ppermute | solution.py:47
  414.4 14.1 %collective-permute-start.50 = (bf16[384,512]{1,0:T(8,128)(2,1)S(1)}, bf16[384,512]{1,0:T(8,128)(2,1)}, u32[]{:S(2)}, u32[]{:S(2)}) collective-permute-start(bf16[384,512]{1,0:T(8,128)(2,1)S(1)} %pad_maximum_fusion.9), channel_id=1, source_target_pairs={{0,1},{1,0},{2,3},{3,2},{4,5},{5,4},{6,7},{7,6},{8,9},{9,8},{10,11... | collective-permute-start | bytes 1179656 | tf_op jit(solution)/shard_map/ppermute | solution.py:47
  415.4 7.5 %collective-permute-start.44 = (bf16[64,768]{1,0:T(8,128)(2,1)S(1)}, bf16[64,768]{1,0:T(8,128)(2,1)S(1)}, u32[]{:S(2)}, u32[]{:S(2)}) collective-permute-start(bf16[64,768]{1,0:T(8,128)(2,1)S(1)} %get-tuple-element.168), channel_id=1, source_target_pairs={{0,8},{1,9},{2,10},{3,11},{4,12},{5,13},{6,14},{7,15},{8,16},{9,17... | collective-permute-start | bytes 294920 | tf_op jit(solution)/shard_map/ppermute | solution.py:47
  416.0 6.9 %collective-permute-start.46 = (bf16[64,768]{1,0:T(8,128)(2,1)S(1)}, bf16[64,768]{1,0:T(8,128)(2,1)S(1)}, u32[]{:S(2)}, u32[]{:S(2)}) collective-permute-start(bf16[64,768]{1,0:T(8,128)(2,1)S(1)} %get-tuple-element.169), channel_id=1, source_target_pairs={{0,24},{1,25},{2,26},{3,27},{4,28},{5,29},{6,30},{7,31},{8,0},{9,1... | collective-permute-start | bytes 294920 | tf_op jit(solution)/shard_map/ppermute | solution.py:47
  419.3 8.6 %collective-permute-start.45 = (bf16[64,768]{1,0:T(8,128)(2,1)S(1)}, bf16[64,768]{1,0:T(8,128)(2,1)S(1)}, u32[]{:S(2)}, u32[]{:S(2)}) collective-permute-start(bf16[64,768]{1,0:T(8,128)(2,1)S(1)} %get-tuple-element.170), channel_id=1, source_target_pairs={{0,16},{1,17},{2,18},{3,19},{4,20},{5,21},{6,22},{7,23},{8,24},{9,... | collective-permute-start | bytes 294920 | tf_op jit(solution)/shard_map/ppermute | solution.py:47
  428.0 4.7 %collective-permute-start.47 = (bf16[64,768]{1,0:T(8,128)(2,1)S(1)}, bf16[64,768]{1,0:T(8,128)(2,1)S(1)}, u32[]{:S(2)}, u32[]{:S(2)}) collective-permute-start(bf16[64,768]{1,0:T(8,128)(2,1)S(1)} %fusion.75), channel_id=1, source_target_pairs={{0,2},{1,3},{2,0},{3,1},{4,6},{5,7},{6,4},{7,5},{8,10},{9,11},{10,... | collective-permute-start | bytes 294920 | tf_op jit(solution)/shard_map/ppermute | solution.py:47
  432.7 2.0 collective-permute-start.48
  (73 other events, 413.6 us)
Sparse Core Ops, SparseCore 0:
  11.4 109.4 all-gather.2
